TPU v7x, 256 devices: a whole 4x4x8 slice. The times are simulated.
256 devices in a mesh: seq: 256 (over z, x, y, core).
Axes of the slice: x: 4, y: 4, z: 8, core: 2. Of those that a mesh axis runs over, the one named last changes fastest.
Arguments:
- tokens: bfloat16 [32768, 1024], P('seq'), may hold values from -96 to 96
- query_weight: bfloat16 [1024, 1024], replicated, may hold values from -1 to 1
- key_weight: bfloat16 [1024, 512], replicated, may hold values from -1 to 1
- value_matrix: bfloat16 [1024, 512], replicated, may hold values from -0.1875 to 0.1875
- out_weight: bfloat16 [1024, 1024], replicated, may hold values from -0.1875 to 0.1875
- out_cotangent: bfloat16 [32768, 1024], P('seq'), may hold values from -24 to 24
Outputs:
- attn_out: bfloat16 [32768, 1024], P('seq')
- tokens_grad: bfloat16 [32768, 1024], P('seq')
- query_weight_grad: float32 [1024, 1024], P('seq')
- key_weight_grad: float32 [1024, 512], P('seq')
- value_weight_grad: float32 [1024, 512], P('seq')
- out_weight_grad: float32 [1024, 1024], P(None, 'seq')
All inputs are finite; a program needn't handle non-finite values.
Results may differ from a plain program's by a relative error of at most 0.015.
The roundings to bfloat16 on the way count: a program that leaves them out, or rounds other values in their place, can miss the bound.
Values may be sent and summed in bfloat16 or wider, within the bound.
No kernel may reach another device: no remote copies, remote signals or barrier semaphores. Data moves between devices by JAX's collectives and lax.ppermute only.
A program may use at most 128 MiB of HBM per device.

v0:
```python
import functools

import jax
import jax.numpy as jnp
from jax import lax
from jax.experimental import pallas as pl
from jax.experimental.pallas import tpu as pltpu
from jax.sharding import PartitionSpec as P

AXIS = "seq"
SHAPE = (8, 4, 4, 2)
ROWS = 128
MODEL = 1024
LANES = 128
STEPS = 4
QCOLS = 256
KCOLS = 128
GCOLS = 768
SCALE = 0.125
MASKED = -1e30
BF16 = jnp.bfloat16
SMALL = pl.CostEstimate(flops=1000, transcendentals=0, bytes_accessed=1000)
F32 = jnp.float32
NT = (((1,), (1,)), ((), ()))
TN = (((0,), (0,)), ((), ()))


def dot(a, b, dims=(((1,), (0,)), ((), ()))):
    return lax.dot_general(a, b, dims, preferred_element_type=F32)


def flat(z, x, y, c):
    return ((z * 4 + x) * 4 + y) * 2 + c


def moved(array, axis, distance):
    route = []
    for z in range(8):
        for x in range(4):
            for y in range(4):
                for c in range(2):
                    place = [z, x, y, c]
                    place[axis] = (place[axis] + distance) % SHAPE[axis]
                    route.append((flat(z, x, y, c), flat(*place)))
    return lax.ppermute(array, AXIS, route)


def passed_along(block, distance):
    devices = range(256)
    route = [(i - distance, i) for i in devices if i - distance in devices]
    return lax.ppermute(block, AXIS, route)


XY_GROUPS = [
    [flat(z, x, y, c) for x in range(4) for y in range(4)] for z in range(8) for c in range(2)
]
Z_GROUPS = [
    [flat(z, x, y, c) for z in range(8)] for x in range(4) for y in range(4) for c in range(2)
]


def prep_kernel(place, a_ref, b_ref, out_ref, t_ref):
    x, y, core = place[0], place[1], place[2]
    t_ref[:, :LANES] = a_ref[...].astype(F32).T
    t_ref[:, LANES:] = b_ref[...].astype(F32).T
    low = lax.broadcasted_iota(jnp.int32, (8, 2 * LANES), 0) < 4
    first = core == 0
    for dx in range(4):
        xs = lax.rem(x + dx, 4)
        for dy in range(4):
            ys = lax.rem(y + dy, 4)
            for z in range(0, 8, 4):
                keeps, sends = [], []
                for pair in range(2):
                    base = (z + 2 * pair) * 128 + xs * 32 + ys * 8
                    one = t_ref[pl.ds(pl.multiple_of(base, 8), 8), :]
                    two = t_ref[pl.ds(pl.multiple_of(base + 128, 8), 8), :]
                    c0 = jnp.where(low, one, pltpu.roll(two, 4, 0))
                    c1 = jnp.where(low, pltpu.roll(one, 4, 0), two)
                    keeps.append(jnp.where(first, c0, c1))
                    sends.append(jnp.where(first, c1, c0))
                row = (dx * 4 + dy) * 32 + z * 4
                out_ref[0, row : row + 16, :] = jnp.concatenate(sends, 0).astype(BF16)
                out_ref[1, row : row + 16, :] = jnp.concatenate(keeps, 0).astype(BF16)


def prepared(place, a, b):
    vmem = pl.BlockSpec(memory_space=pltpu.VMEM)
    return pl.pallas_call(
        prep_kernel,
        out_shape=jax.ShapeDtypeStruct((2, 512, 2 * LANES), BF16),
        in_specs=[pl.BlockSpec(memory_space=pltpu.SMEM), vmem, vmem],
        out_specs=vmem,
        scratch_shapes=[pltpu.VMEM((MODEL, 2 * LANES), F32)],
        compiler_params=pltpu.CompilerParams(vmem_limit_bytes=32 << 20),
        name="prep",
    )(place, a, b)


def swapped(a):
    return pltpu.roll(a, 64, 1)


def attention_kernel(
    place,
    far_ref,
    near_ref,
    own_ref,
    q_ref,
    da_ref,
    wk_ref,
    wv_ref,
    tp_ref,
    th_ref,
    att_ref,
    dq_ref,
    own_grad_ref,
    near_grad_ref,
    far_grad_ref,
    send_ref,
    keep_ref,
):
    window = jnp.concatenate([far_ref[...], near_ref[...], own_ref[...]], axis=0)
    keys = dot(window, wk_ref[...])
    values = dot(window, wv_ref[...])
    start = place[3]
    row = lax.rem(lax.broadcasted_iota(jnp.int32, (256, 384), 0), 128)
    col = lax.broadcasted_iota(jnp.int32, (256, 384), 1)
    allowed = (col <= row + 256) & (col >= start)
    low_k = lax.broadcasted_iota(jnp.int32, (384, LANES), 1) < 64
    low_q = lax.broadcasted_iota(jnp.int32, (ROWS, LANES), 1) < 64
    zero = jnp.zeros((ROWS, LANES), BF16)
    keys_swapped, values_swapped = swapped(keys), swapped(values)
    atts, dqs, dks, dvs = [], [], [], []
    for head in range(2):
        own_half = low_k if head == 0 else ~low_k
        key = jnp.where(own_half, keys, keys_swapped).astype(BF16)
        value = jnp.where(own_half, values, values_swapped).astype(BF16)
        cols = slice(head * LANES, (head + 1) * LANES)
        q = q_ref[:, cols]
        da = da_ref[:, cols]
        q2 = jnp.concatenate([jnp.where(low_q, q, zero), jnp.where(low_q, zero, q)], 0)
        da2 = jnp.concatenate([jnp.where(low_q, da, zero), jnp.where(low_q, zero, da)], 0)
        scores = jnp.where(allowed, dot(q2, key, NT) * SCALE, MASKED)
        highest = jnp.max(scores, axis=-1, keepdims=True)
        weights = jnp.exp(scores - highest)
        weights = weights * (1.0 / jnp.sum(weights, axis=-1, keepdims=True))
        probs = weights.astype(BF16)
        both = dot(probs, value)
        att = jnp.where(low_q, both[:ROWS], both[ROWS:]).astype(BF16)
        att_f = att.astype(F32)
        delta = jnp.sum(
            da2.astype(F32) * jnp.concatenate([att_f, att_f], 0), axis=-1, keepdims=True
        )
        dscores = (weights * (dot(da2, value, NT) - delta)).astype(BF16)
        both = dot(dscores, key) * SCALE
        dqs.append(jnp.where(low_q, both[:ROWS], both[ROWS:]).astype(BF16))
        dk = dot(dscores, q2, TN) * SCALE
        dv = dot(probs, da2, TN)
        dks.append(dk + swapped(dk))
        dvs.append(dv + swapped(dv))
        atts.append(att)
    att = jnp.concatenate(atts, 1)
    dq = jnp.concatenate(dqs, 1)
    dk = jnp.where(low_k, dks[0], dks[1])
    dv = jnp.where(low_k, dvs[0], dvs[1])
    att_ref[...] = att
    dq_ref[...] = dq
    own_grad_ref[0] = dk[256:]
    own_grad_ref[1] = dv[256:]
    dk, dv = dk.astype(BF16), dv.astype(BF16)
    far_grad_ref[0] = dk[:128]
    far_grad_ref[1] = dv[:128]
    near_grad_ref[0] = dk[128:256]
    near_grad_ref[1] = dv[128:256]
    rounded = jnp.concatenate([dk, dv], axis=1)
    for half, out in ((0, send_ref), (1, keep_ref)):
        tp = tp_ref[half]
        t_own, t_out = tp[:, :LANES], tp[:, LANES:]
        out[:, :256] = dot(t_out, att).astype(BF16)
        out[:, 256:512] = dot(t_own, dq).astype(BF16)
        out[:, 512:] = (dot(t_own, rounded[256:]) + dot(th_ref[half], rounded[:256])).astype(BF16)


def attention(first, steps, place, far, near, own, q, da, wk, wv, tp, th):
    def whole(shape):
        return pl.BlockSpec(shape, lambda i: (0,) * len(shape))

    def columns(rows, cols):
        return pl.BlockSpec((rows, cols), lambda i: (0, first + i))

    def fresh(rows, cols):
        return pl.BlockSpec((rows, cols), lambda i: (0, i))

    def struct(rows, cols, dtype):
        return jax.ShapeDtypeStruct((rows, cols * steps), dtype)

    return pl.pallas_call(
        attention_kernel,
        grid=(steps,),
        out_shape=(
            struct(ROWS, QCOLS, BF16),
            struct(ROWS, QCOLS, BF16),
            jax.ShapeDtypeStruct((2, ROWS, KCOLS * steps), F32),
            jax.ShapeDtypeStruct((2, ROWS, KCOLS * steps), BF16),
            jax.ShapeDtypeStruct((2, ROWS, KCOLS * steps), BF16),
            struct(512, GCOLS, BF16),
            struct(512, GCOLS, BF16),
        ),
        in_specs=[
            pl.BlockSpec(memory_space=pltpu.SMEM),
            whole((ROWS, MODEL)),
            whole((ROWS, MODEL)),
            whole((ROWS, MODEL)),
            columns(ROWS, QCOLS),
            columns(ROWS, QCOLS),
            columns(MODEL, KCOLS),
            columns(MODEL, KCOLS),
            whole((2, 512, 2 * LANES)),
            whole((2, 512, 2 * LANES)),
        ],
        out_specs=(
            fresh(ROWS, QCOLS),
            fresh(ROWS, QCOLS),
            pl.BlockSpec((2, ROWS, KCOLS), lambda i: (0, 0, i)),
            pl.BlockSpec((2, ROWS, KCOLS), lambda i: (0, 0, i)),
            pl.BlockSpec((2, ROWS, KCOLS), lambda i: (0, 0, i)),
            fresh(512, GCOLS),
            fresh(512, GCOLS),
        ),
        compiler_params=pltpu.CompilerParams(
            dimension_semantics=("arbitrary",), vmem_limit_bytes=48 << 20
        ),
        cost_estimate=SMALL,
        name="attention",
    )(place, far, near, own, q, da, wk, wv, tp, th)


VMEM_SPEC = pl.BlockSpec(memory_space=pltpu.VMEM)
SMEM_SPEC = pl.BlockSpec(memory_space=pltpu.SMEM)


XCOLS = 1152


def cut(addends, rows, cols):
    total = addends[0][rows, cols].astype(F32)
    for other in addends[1:]:
        total = total + other[rows, cols].astype(F32)
    return total


def first_fold_kernel(keep_one, got_one, keep_two, got_two, *outs):
    one, two = (keep_one, got_one), (keep_two, got_two)
    for d in range(4):
        out = outs[d]
        out[...] = cut(one, slice(d * 128, d * 128 + 128), slice(0, XCOLS)).astype(out.dtype)
        out = outs[4 + d]
        for g in range(4):
            rows, at = slice(g * 128 + d * 32, g * 128 + d * 32 + 32), slice(g * 32, g * 32 + 32)
            out[at, :384] = cut(one, rows, slice(XCOLS, 1536)).astype(out.dtype)
            out[at, 384:] = cut(two, rows, slice(0, 768)).astype(out.dtype)


def second_fold_kernel(*refs):
    addends, outs = refs[:8], refs[8:]
    for group in range(2):
        for d in range(4):
            out = outs[group * 4 + d]
            rows = slice(d * 32, d * 32 + 32)
            out[...] = cut(addends[group * 4 : group * 4 + 4], rows, slice(0, XCOLS)).astype(out.dtype)


def folded(kernel, rows, *addends):
    kinds = (F32, BF16, BF16, BF16) * 2
    outs = pl.pallas_call(
        kernel,
        out_shape=tuple(jax.ShapeDtypeStruct((rows, XCOLS), kind) for kind in kinds),
        in_specs=[VMEM_SPEC] * len(addends),
        out_specs=(VMEM_SPEC,) * 8,
        compiler_params=pltpu.CompilerParams(vmem_limit_bytes=32 << 20),
        cost_estimate=SMALL,
        name="fold",
    )(*addends)
    return outs[:4], outs[4:]


def plane_kernel(place, keep_ref, got_ref, out_ref):
    x, y = place[0], place[1]
    for xd in range(4):
        for yd in range(4):
            block = lax.rem(xd - x + 4, 4) * 4 + lax.rem(yd - y + 4, 4)
            rows = pl.ds(pl.multiple_of(block * 32, 32), 32)
            total = keep_ref[rows, :].astype(F32) + got_ref[rows, :].astype(F32)
            out_ref[xd * 4 + yd] = total.astype(BF16)


def in_plane_order(place, keep, got):
    return pl.pallas_call(
        plane_kernel,
        out_shape=jax.ShapeDtypeStruct((16, 32, keep.shape[1]), BF16),
        in_specs=[SMEM_SPEC, VMEM_SPEC, VMEM_SPEC],
        out_specs=VMEM_SPEC,
        compiler_params=pltpu.CompilerParams(vmem_limit_bytes=32 << 20),
        cost_estimate=SMALL,
        name="plane",
    )(place, keep, got)


def column_kernel(counts, *refs):
    out_ref, sum_ref = refs[-2], refs[-1]
    at, col = 0, 0
    for count in counts:
        if count:
            group = refs[at : at + count]
            at += count
            total = group[0][...].astype(F32)
            for other in group[1:]:
                total = total + other[...].astype(F32)
        else:
            stack = refs[at]
            at += 1
            total = stack[0].astype(F32)
            for i in range(1, stack.shape[0]):
                total = total + stack[i].astype(F32)
        sum_ref[:, col : col + total.shape[1]] = total
        col += total.shape[1]
    low = lax.broadcasted_iota(jnp.int32, (8, LANES), 0) < 4
    for z in range(4):
        for block in range(0, 24, 4):
            even, odd = [], []
            for pair in range(2):
                c = (block + 2 * pair) * LANES
                one = sum_ref[8 * z : 8 * z + 8, c : c + LANES]
                two = sum_ref[8 * z : 8 * z + 8, c + LANES : c + 2 * LANES]
                even.append(jnp.where(low, one, pltpu.roll(two, 4, 0)))
                odd.append(jnp.where(low, pltpu.roll(one, 4, 0), two))
            rows = slice(block * 4, block * 4 + 16)
            out_ref[2 * z, rows, :] = jnp.concatenate(even, 0).astype(BF16)
            out_ref[2 * z + 1, rows, :] = jnp.concatenate(odd, 0).astype(BF16)


def in_column_order(groups):
    counts, flat_args = [], []
    for group in groups:
        if isinstance(group, (tuple, list)):
            counts.append(len(group))
            flat_args.extend(group)
        else:
            counts.append(0)
            flat_args.append(group)
    return pl.pallas_call(
        functools.partial(column_kernel, tuple(counts)),
        out_shape=jax.ShapeDtypeStruct((8, 96, LANES), BF16),
        in_specs=[VMEM_SPEC] * len(flat_args),
        out_specs=VMEM_SPEC,
        scratch_shapes=[pltpu.VMEM((32, 4 * GCOLS), F32)],
        compiler_params=pltpu.CompilerParams(vmem_limit_bytes=32 << 20),
        cost_estimate=SMALL,
        name="column",
    )(*flat_args)


def last_kernel(got_ref, q_ref, k_ref, v_ref, o_ref):
    total = got_ref[0].astype(F32)
    for i in range(1, 8):
        total = total + got_ref[i].astype(F32)
    for step in range(STEPS):
        base = step * 24
        out, q, kv = (total[base + 8 * i : base + 8 * i + 8] for i in range(3))
        turned = out.T
        o_ref[step * 256 : step * 256 + 128, :] = turned[:, :4]
        o_ref[step * 256 + 128 : step * 256 + 256, :] = turned[:, 4:]
        q_ref[:, step * 256 : step * 256 + 128] = q[:4]
        q_ref[:, step * 256 + 128 : step * 256 + 256] = q[4:]
        k_ref[:, step * 128 : step * 128 + 128] = kv[:4]
        v_ref[:, step * 128 : step * 128 + 128] = kv[4:]


def summed_last(got):
    return pl.pallas_call(
        last_kernel,
        out_shape=(
            jax.ShapeDtypeStruct((4, 1024), F32),
            jax.ShapeDtypeStruct((4, 512), F32),
            jax.ShapeDtypeStruct((4, 512), F32),
            jax.ShapeDtypeStruct((1024, 4), F32),
        ),
        in_specs=[VMEM_SPEC],
        out_specs=(VMEM_SPEC,) * 4,
        name="last",
    )(got)


def after(value, *others):
    return lax.optimization_barrier((value, *others))[0]


def shards(tokens, query_weight, key_weight, value_matrix, out_weight, out_cotangent):
    near = passed_along(tokens, 1)
    far = passed_along(tokens, 2)
    me = lax.axis_index(AXIS)
    start = jnp.maximum(2 - me, 0) * ROWS
    place = jnp.stack([(me // 8) % 4, (me // 2) % 4, me % 2, start]).astype(jnp.int32)
    q = dot(tokens, query_weight).astype(BF16)
    da = dot(out_cotangent, out_weight, NT).astype(BF16)
    tp = prepared(place, tokens, out_cotangent)
    th = prepared(place, far, near)

    def attend(first, steps, place):
        return attention(
            first, steps, place, far, near, tokens, q, da, key_weight, value_matrix, tp, th
        )

    one = attend(0, 2, place)
    got_one = moved(one[-2], 3, 1)
    two = attend(2, 1, after(place, one[-1]))
    got_two = moved(two[-2], 3, 1)
    xs, ys = folded(first_fold_kernel, 128, one[-1], got_one, two[-1], got_two)
    ring_x = [moved(xs[1], 1, 1), moved(xs[3], 1, 3)]
    ring_y = [moved(ys[1], 2, 1), moved(ys[3], 2, 3)]
    three = attend(3, 1, after(place, xs[0]))
    got_three = moved(three[-2], 3, 1)
    blocks = in_plane_order(place, three[-1], got_three)
    ring_x.append(moved(after(xs[2], blocks), 1, 2))
    ring_y.append(moved(after(ys[2], blocks), 2, 2))
    plane = lax.all_to_all(blocks, AXIS, 0, 0, axis_index_groups=XY_GROUPS, tiled=True)
    xs, ys = folded(second_fold_kernel, 32, xs[0], *ring_x, ys[0], *ring_y)
    ring_x = [moved(xs[d], 2, d) for d in (1, 3, 2)]
    ring_y = [moved(ys[d], 1, d) for d in (1, 3, 2)]

    parts = zip(one[:-2], two[:-2], three[:-2])
    att, dq, own_kv, near_kv, far_kv = (jnp.concatenate(p, axis=-1) for p in parts)
    back_near = passed_along(after(near_kv, xs[0]), -1)
    back_far = passed_along(after(far_kv, xs[0]), -2)

    attn_out = dot(att, out_weight).astype(BF16)
    kv = (own_kv + back_near.astype(F32) + back_far.astype(F32)).astype(BF16)
    tokens_grad = (
        dot(dq, query_weight, NT) + dot(kv[0], key_weight, NT) + dot(kv[1], value_matrix, NT)
    ).astype(BF16)

    column = in_column_order([[xs[0], *ring_x], [ys[0], *ring_y], plane])
    got = lax.all_to_all(column, AXIS, 0, 0, axis_index_groups=Z_GROUPS, tiled=True)
    query_rows, key_rows, value_rows, out_columns = summed_last(got)
    return attn_out, tokens_grad, query_rows, key_rows, value_rows, out_columns


def solution(mesh):
    rows = P(AXIS, None)
    return jax.shard_map(
        shards,
        mesh=mesh,
        in_specs=(rows, P(), P(), P(), P(), rows),
        out_specs=(rows, rows, rows, rows, rows, P(None, AXIS)),
        check_vma=False,
    )
```

profile of v0, /device:TPU:24, one launch (start us, length us, event | category | flops | bytes accessed | tf_op | source)
XLA Modules:
  0.0 127.6 jit_solution(12838834804169173201)
XLA Ops:
  0.7 2.1 %collective-permute-start.1 = (bf16[128,1024]{1,0:T(8,128)(2,1)}, bf16[128,1024]{1,0:T(8,128)(2,1)}, u32[]{:S(2)}, u32[]{:S(2)}) collective-permute-start(bf16[128,1024]{1,0:T(8,128)(2,1)} %own_ref.5), channel_id=1, source_target_pairs={{0,1},{1,2},{2,3},{3,4},{4,5},{5,6},{6,7},{7,8},{8,9},{9,10},{10,1... | collective-permute-start | bytes 786440 | tf_op jit(solution)/shard_map/ppermute | solution.py:51
  2.7 3.1 %collective-permute-start = (bf16[128,1024]{1,0:T(8,128)(2,1)}, bf16[128,1024]{1,0:T(8,128)(2,1)}, u32[]{:S(2)}, u32[]{:S(2)}) collective-permute-start(bf16[128,1024]{1,0:T(8,128)(2,1)} %own_ref.5), channel_id=1, source_target_pairs={{0,2},{1,3},{2,4},{3,5},{4,6},{5,7},{6,8},{7,9},{8,10},{9,11},{10,... | collective-permute-start | bytes 786440 | tf_op jit(solution)/shard_map/ppermute | solution.py:51
  5.9 2.8 %convolution_convert_fusion.2.q_ref = bf16[128,1024]{1,0:T(8,128)(2,1)} fusion(bf16[128,1024]{1,0:T(8,128)(2,1)} %own_ref.5, bf16[1024,1024]{1,0:T(8,128)(2,1)} %param.7), kind=kOutput, calls=%fused_computation.5 | convolution fusion | flops 268566528 | bytes 2621440 | tf_op jit(solution)/shard_map/dot_general | solution.py:29
  9.7 1.9 %convolution_convert_fusion.1.da_ref = bf16[128,1024]{1,0:T(8,128)(2,1)S(1)} fusion(bf16[128,1024]{1,0:T(8,128)(2,1)} %b_ref.1, bf16[1024,1024]{1,0:T(8,128)(2,1)S(1)} %copy-done), kind=kOutput, calls=%fused_computation.4 | convolution fusion | flops 268566528 | bytes 2621440 | tf_op jit(solution)/shard_map/dot_general | solution.py:29
  11.7 2.5 %collective-permute-done.a_ref.far_ref = bf16[128,1024]{1,0:T(8,128)(2,1)} collective-permute-done((bf16[128,1024]{1,0:T(8,128)(2,1)}, bf16[128,1024]{1,0:T(8,128)(2,1)}, u32[]{:S(2)}, u32[]{:S(2)}) %collective-permute-start) | collective-permute-done | bytes 262176 | tf_op jit(solution)/shard_map/ppermute | solution.py:51
  15.6 8.7 %attention.3 = (bf16[128,512]{1,0:T(8,128)(2,1)S(1)}, bf16[128,512]{1,0:T(8,128)(2,1)S(1)}, f32[2,128,256]{2,1,0:T(8,128)S(1)}, bf16[2,128,256]{2,1,0:T(8,128)(2...) custom-call(s32[4]{0:T(128)S(1)} %pad_add_fusion.place, ...), custom_call_target="tpu_custom_call" | custom-call | flops 1000 | bytes 1000 | tf_op jit(solution)/shard_map/attention/pallas_call | solution.py:198
  26.4 4.3 %attention.4 = (bf16[128,256]{1,0:T(8,128)(2,1)S(1)}, bf16[128,256]{1,0:T(8,128)(2,1)S(1)}, f32[2,128,128]{2,1,0:T(8,128)S(1)}, bf16[2,128,128]{2,1,0:T(8,128)(2...) custom-call(s32[4]{0:T(128)S(1)} %pad_add_fusion.place, ...), custom_call_target="tpu_custom_call" | custom-call | flops 1000 | bytes 1000 | tf_op jit(solution)/shard_map/attention/pallas_call | solution.py:198
  31.7 1.9 %collective-permute-done.3.got_two = bf16[512,768]{1,0:T(8,128)(2,1)S(1)} collective-permute-done((bf16[512,768]{1,0:T(8,128)(2,1)S(1)}, bf16[512,768]{1,0:T(8,128)(2,1)S(1)}, u32[]{:S(2)}, u32[]{:S(2)}) %collective-permute-start.3) | collective-permute-done | bytes 786464 | tf_op jit(solution)/shard_map/ppermute | solution.py:45
  34.9 4.6 %attention.5 = (bf16[128,256]{1,0:T(8,128)(2,1)S(1)}, bf16[128,256]{1,0:T(8,128)(2,1)S(1)}, f32[2,128,128]{2,1,0:T(8,128)S(1)}, bf16[2,128,128]{2,1,0:T(8,128)(2...) custom-call(s32[4]{0:T(128)S(1)} %pad_add_fusion.place, ...), custom_call_target="tpu_custom_call" | custom-call | flops 1000 | bytes 1000 | tf_op jit(solution)/shard_map/attention/pallas_call | solution.py:198
  47.4 2.0 %collective-permute-start.7 = (bf16[128,1152]{1,0:T(8,128)(2,1)}, bf16[128,1152]{1,0:T(8,128)(2,1)}, u32[]{:S(2)}, u32[]{:S(2)}) collective-permute-start(bf16[128,1152]{1,0:T(8,128)(2,1)} %get-tuple-element.77), channel_id=1, source_target_pairs={{0,16},{1,17},{2,18},{3,19},{4,20},{5,21},{6,22},{7,23},{8,24},{9,... | collective-permute-start | bytes 884744 | tf_op jit(solution)/shard_map/ppermute | solution.py:45
  53.5 7.2 %all-to-all-start = ((bf16[16,32,768]{2,1,0:T(8,128)(2,1)}), bf16[16,32,768]{2,1,0:T(8,128)(2,1)}, u32[]{:S(2)}, u32[]{:S(2)}) async-start(bf16[16,32,768]{2,1,0:T(8,128)(2,1)} %copy-done.6), calls=%async_computation | async-start | bytes 1572864 | tf_op jit(solution)/shard_map/all_to_all | solution.py:427
  66.9 1.9 %collective-permute-start.11 = (bf16[2,128,512]{2,1,0:T(8,128)(2,1)S(1)}, bf16[2,128,512]{2,1,0:T(8,128)(2,1)S(1)}, u32[]{:S(2)}, u32[]{:S(2)}) collective-permute-start(bf16[2,128,512]{2,1,0:T(8,128)(2,1)S(1)} %copy-done.42), channel_id=1, source_target_pairs={{1,0},{2,1},{3,2},{4,3},{5,4},{6,5},{7,6},{8,7},{9,8},{10,9},{11,1... | collective-permute-start | bytes 786440 | tf_op jit(solution)/shard_map/ppermute | solution.py:51
  68.8 2.8 %collective-permute-start.12 = (bf16[2,128,512]{2,1,0:T(8,128)(2,1)S(1)}, bf16[2,128,512]{2,1,0:T(8,128)(2,1)S(1)}, u32[]{:S(2)}, u32[]{:S(2)}) collective-permute-start(bf16[2,128,512]{2,1,0:T(8,128)(2,1)S(1)} %copy-done.41), channel_id=1, source_target_pairs={{2,0},{3,1},{4,2},{5,3},{6,4},{7,5},{8,6},{9,7},{10,8},{11,9},{12,... | collective-permute-start | bytes 786440 | tf_op jit(solution)/shard_map/ppermute | solution.py:51
  71.6 2.1 %convolution_convert_fusion = bf16[128,1024]{1,0:T(8,128)(2,1)} fusion(bf16[1024,1024]{1,0:T(8,128)(2,1)S(1)} %copy-done, bf16[128,256]{1,0:T(8,128)(2,1)} %copy-done.36, bf16[128,256]{1,0:T(8,128)(2,1)} %copy-done.35, bf16[128,512]{1,0:T(8,128)(2,1)} %copy-done.19), kind=kOutput, calls=%fused_computation.3 | convolution fusion | flops 269352960 | bytes 2621440 | tf_op jit(solution)/shard_map/dot_general | solution.py:29
  73.7 2.0 %collective-permute-start.14 = (bf16[32,1152]{1,0:T(8,128)(2,1)S(1)}, bf16[32,1152]{1,0:T(8,128)(2,1)S(1)}, u32[]{:S(2)}, u32[]{:S(2)}) collective-permute-start(bf16[32,1152]{1,0:T(8,128)(2,1)S(1)} %get-tuple-element.90), channel_id=1, source_target_pairs={{0,6},{1,7},{2,0},{3,1},{4,2},{5,3},{6,4},{7,5},{8,14},{9,15},{10,... | collective-permute-start | bytes 221192 | tf_op jit(solution)/shard_map/ppermute | solution.py:45
  75.7 2.0 %collective-permute-start.15 = (bf16[32,1152]{1,0:T(8,128)(2,1)S(1)}, bf16[32,1152]{1,0:T(8,128)(2,1)S(1)}, u32[]{:S(2)}, u32[]{:S(2)}) collective-permute-start(bf16[32,1152]{1,0:T(8,128)(2,1)S(1)} %get-tuple-element.91), channel_id=1, source_target_pairs={{0,4},{1,5},{2,6},{3,7},{4,0},{5,1},{6,2},{7,3},{8,12},{9,13},{10,... | collective-permute-start | bytes 221192 | tf_op jit(solution)/shard_map/ppermute | solution.py:45
  79.0 2.6 %collective-permute-done.12 = bf16[2,128,512]{2,1,0:T(8,128)(2,1)S(1)} collective-permute-done((bf16[2,128,512]{2,1,0:T(8,128)(2,1)S(1)}, bf16[2,128,512]{2,1,0:T(8,128)(2,1)S(1)}, u32[]{:S(2)}, u32[]{:S(2)}) %collective-permute-start.12) | collective-permute-done | bytes 262176 | tf_op jit(solution)/shard_map/ppermute | solution.py:51
  81.6 9.3 %collective-permute-start.17 = (bf16[32,1152]{1,0:T(8,128)(2,1)S(1)}, bf16[32,1152]{1,0:T(8,128)(2,1)S(1)}, u32[]{:S(2)}, u32[]{:S(2)}) collective-permute-start(bf16[32,1152]{1,0:T(8,128)(2,1)S(1)} %get-tuple-element.94), channel_id=1, source_target_pairs={{0,24},{1,25},{2,26},{3,27},{4,28},{5,29},{6,30},{7,31},{8,0},{9,1... | collective-permute-start | bytes 221192 | tf_op jit(solution)/shard_map/ppermute | solution.py:45
  95.0 2.0 %collective-permute-done.18.refs_7_ = bf16[32,1152]{1,0:T(8,128)(2,1)S(1)} collective-permute-done((bf16[32,1152]{1,0:T(8,128)(2,1)S(1)}, bf16[32,1152]{1,0:T(8,128)(2,1)S(1)}, u32[]{:S(2)}, u32[]{:S(2)}) %collective-permute-start.18) | collective-permute-done | bytes 73760 | tf_op jit(solution)/shard_map/ppermute | solution.py:45
  103.0 2.0 %column.1 = bf16[8,96,128]{2,1,0:T(8,128)(2,1)} custom-call(f32[32,1152]{1,0:T(8,128)S(1)} %get-tuple-element.83.refs_0_, bf16[32,1152]{1,0:T(8,128)(2,1)S(1)} %copy-done.24, bf16[32,1152]{1,0:T(8,128)(2,1)S(1)} %copy-done.26, bf16[32,1152]{1,0:T(8,128)(2,1)S(1)} %copy-done.28, f32[32,1152]{1,0:T(8,128)S(1)} %get-tuple-element.92.refs_4_, ...), custom_call_target="tpu_custom_call" | custom-call | flops 1000 | bytes 1000 | tf_op jit(solution)/shard_map/column/pallas_call | solution.py:352
  105.0 8.9 %all-to-all-start.1 = ((bf16[8,96,128]{2,1,0:T(8,128)(2,1)}), bf16[8,96,128]{2,1,0:T(8,128)(2,1)}, u32[]{:S(2)}, u32[]{:S(2)}) async-start(bf16[8,96,128]{2,1,0:T(8,128)(2,1)} %column.1), calls=%async_computation.1 | async-start | bytes 393216 | tf_op jit(solution)/shard_map/all_to_all | solution.py:444
  113.9 2.6 %convolution_add_fusion.1 = f32[128,1024]{1,0:T(8,128)S(1)} fusion(f32[128,1024]{1,0:T(8,128)} %fusion.13, bf16[1024,1024]{1,0:T(8,128)(2,1)} %param.7, bf16[128,256]{1,0:T(8,128)(2,1)} %copy-done.38, bf16[128,256]{1,0:T(8,128)(2,1)} %copy-done.37, bf16[128,512]{1,0:T(8,128)(2,1)} %copy-done.22), kind=kOutput, calls=%fused_computation.1 | convolution fusion | flops 269352960 | bytes 3407872 | tf_op jit(solution)/shard_map/dot_general | solution.py:29
  117.7 6.1 %all-to-all-done.1.got_ref = bf16[8,96,128]{2,1,0:T(8,128)(2,1)} async-done(((bf16[8,96,128]{2,1,0:T(8,128)(2,1)}), bf16[8,96,128]{2,1,0:T(8,128)(2,1)}, u32[]{:S(2)}, u32[]{:S(2)}) %all-to-all-start.1) | async-done | bytes 196640 | tf_op jit(solution)/shard_map/all_to_all | solution.py:444
  123.8 2.0 %last.1 = (f32[4,1024]{1,0:T(4,128)}, f32[4,512]{1,0:T(4,128)}, f32[4,512]{1,0:T(4,128)}, f32[1024,4]{1,0:T(8,128)}) custom-call(bf16[8,96,128]{2,1,0:T(8,128)(2,1)} %all-to-all-done.1.got_ref), custom_call_target="tpu_custom_call" | custom-call | tf_op jit(solution)/shard_map/last/pallas_call | solution.py:381
  (124 shorter events, 39.1 us)
Async XLA Ops:
  0.7 11.0 %collective-permute-start.1 = (bf16[128,1024]{1,0:T(8,128)(2,1)}, bf16[128,1024]{1,0:T(8,128)(2,1)}, u32[]{:S(2)}, u32[]{:S(2)}) collective-permute-start(bf16[128,1024]{1,0:T(8,128)(2,1)} %own_ref.5), channel_id=1, source_target_pairs={{0,1},{1,2},{2,3},{3,4},{4,5},{5,6},{6,7},{7,8},{8,9},{9,10},{10,1... | collective-permute-start | bytes 786440 | tf_op jit(solution)/shard_map/ppermute | solution.py:51
  2.7 11.5 %collective-permute-start = (bf16[128,1024]{1,0:T(8,128)(2,1)}, bf16[128,1024]{1,0:T(8,128)(2,1)}, u32[]{:S(2)}, u32[]{:S(2)}) collective-permute-start(bf16[128,1024]{1,0:T(8,128)(2,1)} %own_ref.5), channel_id=1, source_target_pairs={{0,2},{1,3},{2,4},{3,5},{4,6},{5,7},{6,8},{7,9},{8,10},{9,11},{10,... | collective-permute-start | bytes 786440 | tf_op jit(solution)/shard_map/ppermute | solution.py:51
  26.3 7.4 %collective-permute-start.2 = (bf16[512,1536]{1,0:T(8,128)(2,1)}, bf16[512,1536]{1,0:T(8,128)(2,1)S(1)}, u32[]{:S(2)}, u32[]{:S(2)}) collective-permute-start(bf16[512,1536]{1,0:T(8,128)(2,1)} %get-tuple-element.57), channel_id=1, source_target_pairs={{0,1},{1,0},{2,3},{3,2},{4,5},{5,4},{6,7},{7,6},{8,9},{9,8},{10,11... | collective-permute-start | bytes 4718600 | tf_op jit(solution)/shard_map/ppermute | solution.py:45
  31.3 2.3 %collective-permute-start.3 = (bf16[512,768]{1,0:T(8,128)(2,1)S(1)}, bf16[512,768]{1,0:T(8,128)(2,1)S(1)}, u32[]{:S(2)}, u32[]{:S(2)}) collective-permute-start(bf16[512,768]{1,0:T(8,128)(2,1)S(1)} %get-tuple-element.59), channel_id=1, source_target_pairs={{0,1},{1,0},{2,3},{3,2},{4,5},{5,4},{6,7},{7,6},{8,9},{9,8},{10,11... | collective-permute-start | bytes 2359304 | tf_op jit(solution)/shard_map/ppermute | solution.py:45
  40.2 5.6 %collective-permute-start.6 = (bf16[512,768]{1,0:T(8,128)(2,1)S(1)}, bf16[512,768]{1,0:T(8,128)(2,1)S(1)}, u32[]{:S(2)}, u32[]{:S(2)}) collective-permute-start(bf16[512,768]{1,0:T(8,128)(2,1)S(1)} %get-tuple-element.76), channel_id=1, source_target_pairs={{0,1},{1,0},{2,3},{3,2},{4,5},{5,4},{6,7},{7,6},{8,9},{9,8},{10,11... | collective-permute-start | bytes 2359304 | tf_op jit(solution)/shard_map/ppermute | solution.py:45
  40.5 10.3 %collective-permute-start.4 = (bf16[128,1152]{1,0:T(8,128)(2,1)S(1)}, bf16[128,1152]{1,0:T(8,128)(2,1)S(1)}, u32[]{:S(2)}, u32[]{:S(2)}) collective-permute-start(bf16[128,1152]{1,0:T(8,128)(2,1)S(1)} %get-tuple-element.72), channel_id=1, source_target_pairs={{0,8},{1,9},{2,10},{3,11},{4,12},{5,13},{6,14},{7,15},{8,16},{9,17... | collective-permute-start | bytes 884744 | tf_op jit(solution)/shard_map/ppermute | solution.py:45
  42.0 18.7 %collective-permute-start.5 = (bf16[128,1152]{1,0:T(8,128)(2,1)}, bf16[128,1152]{1,0:T(8,128)(2,1)}, u32[]{:S(2)}, u32[]{:S(2)}) collective-permute-start(bf16[128,1152]{1,0:T(8,128)(2,1)} %get-tuple-element.73), channel_id=1, source_target_pairs={{0,24},{1,25},{2,26},{3,27},{4,28},{5,29},{6,30},{7,31},{8,0},{9,1... | collective-permute-start | bytes 884744 | tf_op jit(solution)/shard_map/ppermute | solution.py:45
  43.8 16.9 %collective-permute-start.8 = (bf16[128,1152]{1,0:T(8,128)(2,1)}, bf16[128,1152]{1,0:T(8,128)(2,1)}, u32[]{:S(2)}, u32[]{:S(2)}) collective-permute-start(bf16[128,1152]{1,0:T(8,128)(2,1)} %get-tuple-element.79), channel_id=1, source_target_pairs={{0,2},{1,3},{2,4},{3,5},{4,6},{5,7},{6,0},{7,1},{8,10},{9,11},{10,... | collective-permute-start | bytes 884744 | tf_op jit(solution)/shard_map/ppermute | solution.py:45
  45.5 16.6 %collective-permute-start.9 = (bf16[128,1152]{1,0:T(8,128)(2,1)}, bf16[128,1152]{1,0:T(8,128)(2,1)}, u32[]{:S(2)}, u32[]{:S(2)}) collective-permute-start(bf16[128,1152]{1,0:T(8,128)(2,1)} %get-tuple-element.80), channel_id=1, source_target_pairs={{0,6},{1,7},{2,0},{3,1},{4,2},{5,3},{6,4},{7,5},{8,14},{9,15},{10,... | collective-permute-start | bytes 884744 | tf_op jit(solution)/shard_map/ppermute | solution.py:45
  47.4 14.7 %collective-permute-start.7 = (bf16[128,1152]{1,0:T(8,128)(2,1)}, bf16[128,1152]{1,0:T(8,128)(2,1)}, u32[]{:S(2)}, u32[]{:S(2)}) collective-permute-start(bf16[128,1152]{1,0:T(8,128)(2,1)} %get-tuple-element.77), channel_id=1, source_target_pairs={{0,16},{1,17},{2,18},{3,19},{4,20},{5,21},{6,22},{7,23},{8,24},{9,... | collective-permute-start | bytes 884744 | tf_op jit(solution)/shard_map/ppermute | solution.py:45
  51.5 10.6 %collective-permute-start.10 = (bf16[128,1152]{1,0:T(8,128)(2,1)}, bf16[128,1152]{1,0:T(8,128)(2,1)}, u32[]{:S(2)}, u32[]{:S(2)}) collective-permute-start(bf16[128,1152]{1,0:T(8,128)(2,1)} %get-tuple-element.82), channel_id=1, source_target_pairs={{0,4},{1,5},{2,6},{3,7},{4,0},{5,1},{6,2},{7,3},{8,12},{9,13},{10,... | collective-permute-start | bytes 884744 | tf_op jit(solution)/shard_map/ppermute | solution.py:45
  53.5 44.1 %all-to-all-start = ((bf16[16,32,768]{2,1,0:T(8,128)(2,1)}), bf16[16,32,768]{2,1,0:T(8,128)(2,1)}, u32[]{:S(2)}, u32[]{:S(2)}) async-start(bf16[16,32,768]{2,1,0:T(8,128)(2,1)} %copy-done.6), calls=%async_computation | async-start | bytes 1572864 | tf_op jit(solution)/shard_map/all_to_all | solution.py:427
  65.2 25.8 %copy-start.16 = (f32[2,128,256]{2,1,0:T(8,128)S(1)}, f32[2,128,256]{2,1,0:T(8,128)}, u32[]{:S(2)}) copy-start(f32[2,128,256]{2,1,0:T(8,128)} %copy-done.15) | copy-start | bytes 786436
  65.2 25.8 %copy-start.18 = (f32[2,128,128]{2,1,0:T(8,128)S(1)}, f32[2,128,128]{2,1,0:T(8,128)}, u32[]{:S(2)}) copy-start(f32[2,128,128]{2,1,0:T(8,128)} %copy-done.17) | copy-start | bytes 393220
  65.2 25.8 %copy-start.21 = (f32[2,128,128]{2,1,0:T(8,128)S(1)}, f32[2,128,128]{2,1,0:T(8,128)}, u32[]{:S(2)}) copy-start(f32[2,128,128]{2,1,0:T(8,128)} %copy-done.20) | copy-start | bytes 393220
  66.9 10.9 %collective-permute-start.11 = (bf16[2,128,512]{2,1,0:T(8,128)(2,1)S(1)}, bf16[2,128,512]{2,1,0:T(8,128)(2,1)S(1)}, u32[]{:S(2)}, u32[]{:S(2)}) collective-permute-start(bf16[2,128,512]{2,1,0:T(8,128)(2,1)S(1)} %copy-done.42), channel_id=1, source_target_pairs={{1,0},{2,1},{3,2},{4,3},{5,4},{6,5},{7,6},{8,7},{9,8},{10,9},{11,1... | collective-permute-start | bytes 786440 | tf_op jit(solution)/shard_map/ppermute | solution.py:51
  68.8 12.8 %collective-permute-start.12 = (bf16[2,128,512]{2,1,0:T(8,128)(2,1)S(1)}, bf16[2,128,512]{2,1,0:T(8,128)(2,1)S(1)}, u32[]{:S(2)}, u32[]{:S(2)}) collective-permute-start(bf16[2,128,512]{2,1,0:T(8,128)(2,1)S(1)} %copy-done.41), channel_id=1, source_target_pairs={{2,0},{3,1},{4,2},{5,3},{6,4},{7,5},{8,6},{9,7},{10,8},{11,9},{12,... | collective-permute-start | bytes 786440 | tf_op jit(solution)/shard_map/ppermute | solution.py:51
  73.7 17.4 %collective-permute-start.13 = (bf16[32,1152]{1,0:T(8,128)(2,1)S(1)}, bf16[32,1152]{1,0:T(8,128)(2,1)S(1)}, u32[]{:S(2)}, u32[]{:S(2)}) collective-permute-start(bf16[32,1152]{1,0:T(8,128)(2,1)S(1)} %get-tuple-element.89), channel_id=1, source_target_pairs={{0,2},{1,3},{2,4},{3,5},{4,6},{5,7},{6,0},{7,1},{8,10},{9,11},{10,... | collective-permute-start | bytes 221192 | tf_op jit(solution)/shard_map/ppermute | solution.py:45
  73.7 18.8 %collective-permute-start.14 = (bf16[32,1152]{1,0:T(8,128)(2,1)S(1)}, bf16[32,1152]{1,0:T(8,128)(2,1)S(1)}, u32[]{:S(2)}, u32[]{:S(2)}) collective-permute-start(bf16[32,1152]{1,0:T(8,128)(2,1)S(1)} %get-tuple-element.90), channel_id=1, source_target_pairs={{0,6},{1,7},{2,0},{3,1},{4,2},{5,3},{6,4},{7,5},{8,14},{9,15},{10,... | collective-permute-start | bytes 221192 | tf_op jit(solution)/shard_map/ppermute | solution.py:45
  75.7 17.4 %collective-permute-start.15 = (bf16[32,1152]{1,0:T(8,128)(2,1)S(1)}, bf16[32,1152]{1,0:T(8,128)(2,1)S(1)}, u32[]{:S(2)}, u32[]{:S(2)}) collective-permute-start(bf16[32,1152]{1,0:T(8,128)(2,1)S(1)} %get-tuple-element.91), channel_id=1, source_target_pairs={{0,4},{1,5},{2,6},{3,7},{4,0},{5,1},{6,2},{7,3},{8,12},{9,13},{10,... | collective-permute-start | bytes 221192 | tf_op jit(solution)/shard_map/ppermute | solution.py:45
  77.7 16.0 %collective-permute-start.16 = (bf16[32,1152]{1,0:T(8,128)(2,1)S(1)}, bf16[32,1152]{1,0:T(8,128)(2,1)S(1)}, u32[]{:S(2)}, u32[]{:S(2)}) collective-permute-start(bf16[32,1152]{1,0:T(8,128)(2,1)S(1)} %get-tuple-element.93), channel_id=1, source_target_pairs={{0,8},{1,9},{2,10},{3,11},{4,12},{5,13},{6,14},{7,15},{8,16},{9,17... | collective-permute-start | bytes 221192 | tf_op jit(solution)/shard_map/ppermute | solution.py:45
  81.6 12.7 %collective-permute-start.17 = (bf16[32,1152]{1,0:T(8,128)(2,1)S(1)}, bf16[32,1152]{1,0:T(8,128)(2,1)S(1)}, u32[]{:S(2)}, u32[]{:S(2)}) collective-permute-start(bf16[32,1152]{1,0:T(8,128)(2,1)S(1)} %get-tuple-element.94), channel_id=1, source_target_pairs={{0,24},{1,25},{2,26},{3,27},{4,28},{5,29},{6,30},{7,31},{8,0},{9,1... | collective-permute-start | bytes 221192 | tf_op jit(solution)/shard_map/ppermute | solution.py:45
  91.1 5.9 %collective-permute-start.18 = (bf16[32,1152]{1,0:T(8,128)(2,1)S(1)}, bf16[32,1152]{1,0:T(8,128)(2,1)S(1)}, u32[]{:S(2)}, u32[]{:S(2)}) collective-permute-start(bf16[32,1152]{1,0:T(8,128)(2,1)S(1)} %get-tuple-element.95), channel_id=1, source_target_pairs={{0,16},{1,17},{2,18},{3,19},{4,20},{5,21},{6,22},{7,23},{8,24},{9,... | collective-permute-start | bytes 221192 | tf_op jit(solution)/shard_map/ppermute | solution.py:45
  105.0 18.8 %all-to-all-start.1 = ((bf16[8,96,128]{2,1,0:T(8,128)(2,1)}), bf16[8,96,128]{2,1,0:T(8,128)(2,1)}, u32[]{:S(2)}, u32[]{:S(2)}) async-start(bf16[8,96,128]{2,1,0:T(8,128)(2,1)} %column.1), calls=%async_computation.1 | async-start | bytes 393216 | tf_op jit(solution)/shard_map/all_to_all | solution.py:444
  (40 other events, 139.3 us)
where the time goes:
time: 129 us; the launch traced here: 128 us
  starting transfers between devices  49.9 us (39%)
  Pallas kernels  27.4 us (21%)
  local copies, waits for them, and re-layouts  18.3 us (14%)
  waiting for transfers between devices  17.9 us (14%)
  matrix products  12 us (9%)
    ppermute x15, starting transfers between devices, moved(): return lax.ppermute(array, AXIS, route)  24 us
    unnamed x87, local copies, waits for them, and re-layouts  18.3 us
    pallas_call x3, Pallas kernels, attention(): pl.pallas_call(attention_kernel, grid=(steps,), out_shape=(struct(ROWS, Q...  17.6 us
    dot_general x6, matrix products, dot(): return lax.dot_general(a, b, dims, preferred_element_type=F32)  12 us
    ppermute x4, starting transfers between devices, passed_along(): return lax.ppermute(block, AXIS, route)  9.79 us
    all_to_all x1, starting transfers between devices, shards(): lax.all_to_all(column, AXIS, 0, 0, axis_index_groups=Z_GROUPS, tiled=True)  8.93 us
    all_to_all x1, starting transfers between devices, shards(): lax.all_to_all(blocks, AXIS, 0, 0, axis_index_groups=XY_GROUPS, tiled=True)  7.16 us
    ppermute x15, waiting for transfers between devices, moved(): return lax.ppermute(array, AXIS, route)  6.73 us
  transfers between devices with their start and end apart: 21, of which 7 were waited for; matrix products, arithmetic and copies ran while one was open for 10% of the time, Pallas kernels for 6%

commit v1 on v0

v1 whole, which is shorter than its diff:
```python
import functools

import jax
import jax.numpy as jnp
from jax import lax
from jax.experimental import pallas as pl
from jax.experimental.pallas import tpu as pltpu
from jax.sharding import PartitionSpec as P

AXIS = "seq"
ROWS = 128
MODEL = 1024
LANES = 128
STEPS = 4
QCOLS = 256
KCOLS = 128
GCOLS = 768
SCALE = 0.125
MASKED = -1e30
BF16 = jnp.bfloat16
SMALL = pl.CostEstimate(flops=1000, transcendentals=0, bytes_accessed=1000)
F32 = jnp.float32
NT = (((1,), (1,)), ((), ()))
TN = (((0,), (0,)), ((), ()))


def dot(a, b, dims=(((1,), (0,)), ((), ()))):
    return lax.dot_general(a, b, dims, preferred_element_type=F32)


def flat(z, x, y, c):
    return ((z * 4 + x) * 4 + y) * 2 + c


def in_hbm(array):
    return pltpu.with_memory_space_constraint(array, pltpu.HBM)


def route_of(step):
    places = [(z, x, y, c) for z in range(8) for x in range(4) for y in range(4) for c in range(2)]
    return [(flat(*p), flat(*step(*p))) for p in places]


def to_mate(array):
    return lax.ppermute(array, AXIS, route_of(lambda z, x, y, c: (z, x, y, 1 - c)))


def ring(blocks, phase):
    def step(d, z, x, y, c):
        if c == phase:
            return z, (x + d) % 4, y, c
        return z, x, (y + d) % 4, c

    order = (1, 3, 2)
    return [
        lax.ppermute(blocks[d], AXIS, route_of(functools.partial(step, d))) for d in order
    ]


def passed_along(block, distance):
    devices = range(256)
    route = [(i - distance, i) for i in devices if i - distance in devices]
    return lax.ppermute(block, AXIS, route)


Z_GROUPS = [
    [flat(z, x, y, c) for z in range(8)] for x in range(4) for y in range(4) for c in range(2)
]


def reorder(place, t_ref, out_ref):
    x, y, core = place[0], place[1], place[2]
    low = lax.broadcasted_iota(jnp.int32, (8, 2 * LANES), 0) < 4
    for half in range(2):
        target = 1 - core if half == 0 else core
        zero = target == 0
        for d1 in range(4):
            for d2 in range(4):
                xs = lax.rem(x + jnp.where(zero, d1, d2), 4)
                ys = lax.rem(y + jnp.where(zero, d2, d1), 4)
                for z in range(0, 8, 4):
                    rows = []
                    for pair in range(2):
                        base = (z + 2 * pair) * 128 + xs * 32 + ys * 8
                        one = t_ref[pl.ds(pl.multiple_of(base, 8), 8), :]
                        two = t_ref[pl.ds(pl.multiple_of(base + 128, 8), 8), :]
                        c0 = jnp.where(low, one, pltpu.roll(two, 4, 0))
                        c1 = jnp.where(low, pltpu.roll(one, 4, 0), two)
                        rows.append(jnp.where(zero, c0, c1))
                    row = (d1 * 4 + d2) * 32 + z * 4
                    out_ref[half, row : row + 16, :] = jnp.concatenate(rows, 0).astype(BF16)


def early_kernel(place, tok_ref, cot_ref, wq_ref, wo_ref, q_ref, da_ref, out_ref, t_ref):
    q_ref[...] = dot(tok_ref[...], wq_ref[...]).astype(BF16)
    da_ref[...] = dot(cot_ref[...], wo_ref[...], NT).astype(BF16)

    @pl.when(pl.program_id(0) == 0)
    def _():
        t_ref[:, :LANES] = tok_ref[...].astype(F32).T
        t_ref[:, LANES:] = cot_ref[...].astype(F32).T
        reorder(place, t_ref, out_ref)


def whole(*shape):
    return pl.BlockSpec(shape, lambda i: (0,) * len(shape))


def early(place, tokens, cotangent, wq, wo):
    block = pl.BlockSpec((ROWS, QCOLS), lambda i: (0, i))
    return pl.pallas_call(
        early_kernel,
        grid=(STEPS,),
        out_shape=(
            jax.ShapeDtypeStruct((ROWS, MODEL), BF16),
            jax.ShapeDtypeStruct((ROWS, MODEL), BF16),
            jax.ShapeDtypeStruct((2, 512, 2 * LANES), BF16),
        ),
        in_specs=[
            pl.BlockSpec(memory_space=pltpu.SMEM),
            whole(ROWS, MODEL),
            whole(ROWS, MODEL),
            pl.BlockSpec((MODEL, QCOLS), lambda i: (0, i)),
            pl.BlockSpec((QCOLS, MODEL), lambda i: (i, 0)),
        ],
        out_specs=(block, block, whole(2, 512, 2 * LANES)),
        scratch_shapes=[pltpu.VMEM((MODEL, 2 * LANES), F32)],
        compiler_params=pltpu.CompilerParams(
            dimension_semantics=("arbitrary",), vmem_limit_bytes=20 << 20
        ),
        name="early",
    )(place, tokens, cotangent, wq, wo)


def prep_kernel(place, a_ref, b_ref, out_ref, t_ref):
    t_ref[:, :LANES] = a_ref[...].astype(F32).T
    t_ref[:, LANES:] = b_ref[...].astype(F32).T
    reorder(place, t_ref, out_ref)


def prepared(place, a, b):
    return pl.pallas_call(
        prep_kernel,
        grid=(1,),
        out_shape=jax.ShapeDtypeStruct((2, 512, 2 * LANES), BF16),
        in_specs=[pl.BlockSpec(memory_space=pltpu.SMEM), whole(ROWS, MODEL), whole(ROWS, MODEL)],
        out_specs=whole(2, 512, 2 * LANES),
        scratch_shapes=[pltpu.VMEM((MODEL, 2 * LANES), F32)],
        compiler_params=pltpu.CompilerParams(vmem_limit_bytes=12 << 20),
        name="prep",
    )(place, a, b)


def swapped(a):
    return pltpu.roll(a, 64, 1)


def attention_kernel(
    place,
    far_ref,
    near_ref,
    own_ref,
    q_ref,
    da_ref,
    wk_ref,
    wv_ref,
    tp_ref,
    th_ref,
    att_ref,
    dq_ref,
    own_grad_ref,
    near_grad_ref,
    far_grad_ref,
    send_ref,
    keep_ref,
):
    window = jnp.concatenate([far_ref[...], near_ref[...], own_ref[...]], axis=0)
    keys = dot(window, wk_ref[...])
    values = dot(window, wv_ref[...])
    start = place[3]
    row = lax.rem(lax.broadcasted_iota(jnp.int32, (256, 384), 0), 128)
    col = lax.broadcasted_iota(jnp.int32, (256, 384), 1)
    allowed = (col <= row + 256) & (col >= start)
    low_k = lax.broadcasted_iota(jnp.int32, (384, LANES), 1) < 64
    low_q = lax.broadcasted_iota(jnp.int32, (ROWS, LANES), 1) < 64
    zero = jnp.zeros((ROWS, LANES), BF16)
    keys_swapped, values_swapped = swapped(keys), swapped(values)
    atts, dqs, dks, dvs = [], [], [], []
    for head in range(2):
        own_half = low_k if head == 0 else ~low_k
        key = jnp.where(own_half, keys, keys_swapped).astype(BF16)
        value = jnp.where(own_half, values, values_swapped).astype(BF16)
        cols = slice(head * LANES, (head + 1) * LANES)
        q = q_ref[:, cols]
        da = da_ref[:, cols]
        q2 = jnp.concatenate([jnp.where(low_q, q, zero), jnp.where(low_q, zero, q)], 0)
        da2 = jnp.concatenate([jnp.where(low_q, da, zero), jnp.where(low_q, zero, da)], 0)
        scores = jnp.where(allowed, dot(q2, key, NT) * SCALE, MASKED)
        highest = jnp.max(scores, axis=-1, keepdims=True)
        weights = jnp.exp(scores - highest)
        weights = weights * (1.0 / jnp.sum(weights, axis=-1, keepdims=True))
        probs = weights.astype(BF16)
        both = dot(probs, value)
        att = jnp.where(low_q, both[:ROWS], both[ROWS:]).astype(BF16)
        att_f = att.astype(F32)
        delta = jnp.sum(
            da2.astype(F32) * jnp.concatenate([att_f, att_f], 0), axis=-1, keepdims=True
        )
        dscores = (weights * (dot(da2, value, NT) - delta)).astype(BF16)
        both = dot(dscores, key) * SCALE
        dqs.append(jnp.where(low_q, both[:ROWS], both[ROWS:]).astype(BF16))
        dk = dot(dscores, q2, TN) * SCALE
        dv = dot(probs, da2, TN)
        dks.append(dk + swapped(dk))
        dvs.append(dv + swapped(dv))
        atts.append(att)
    att = jnp.concatenate(atts, 1)
    dq = jnp.concatenate(dqs, 1)
    dk = jnp.where(low_k, dks[0], dks[1])
    dv = jnp.where(low_k, dvs[0], dvs[1])
    att_ref[...] = att
    dq_ref[...] = dq
    own_grad_ref[0] = dk[256:]
    own_grad_ref[1] = dv[256:]
    dk, dv = dk.astype(BF16), dv.astype(BF16)
    far_grad_ref[0] = dk[:128]
    far_grad_ref[1] = dv[:128]
    near_grad_ref[0] = dk[128:256]
    near_grad_ref[1] = dv[128:256]
    rounded = jnp.concatenate([dk, dv], axis=1)
    for half, out in ((0, send_ref), (1, keep_ref)):
        tp = tp_ref[half]
        t_own, t_out = tp[:, :LANES], tp[:, LANES:]
        out[:, :256] = dot(t_out, att).astype(BF16)
        out[:, 256:512] = dot(t_own, dq).astype(BF16)
        out[:, 512:] = (dot(t_own, rounded[256:]) + dot(th_ref[half], rounded[:256])).astype(BF16)


def attention(first, steps, place, far, near, own, q, da, wk, wv, tp, th):
    def columns(rows, cols):
        return pl.BlockSpec((rows, cols), lambda i: (0, first + i))

    def fresh(rows, cols):
        return pl.BlockSpec((rows, cols), lambda i: (0, i))

    def struct(rows, cols, dtype):
        return jax.ShapeDtypeStruct((rows, cols * steps), dtype)

    return pl.pallas_call(
        attention_kernel,
        grid=(steps,),
        out_shape=(
            struct(ROWS, QCOLS, BF16),
            struct(ROWS, QCOLS, BF16),
            jax.ShapeDtypeStruct((2, ROWS, KCOLS * steps), F32),
            jax.ShapeDtypeStruct((2, ROWS, KCOLS * steps), BF16),
            jax.ShapeDtypeStruct((2, ROWS, KCOLS * steps), BF16),
            struct(512, GCOLS, BF16),
            struct(512, GCOLS, BF16),
        ),
        in_specs=[
            pl.BlockSpec(memory_space=pltpu.SMEM),
            whole(ROWS, MODEL),
            whole(ROWS, MODEL),
            whole(ROWS, MODEL),
            columns(ROWS, QCOLS),
            columns(ROWS, QCOLS),
            columns(MODEL, KCOLS),
            columns(MODEL, KCOLS),
            whole(2, 512, 2 * LANES),
            whole(2, 512, 2 * LANES),
        ],
        out_specs=(
            fresh(ROWS, QCOLS),
            fresh(ROWS, QCOLS),
            pl.BlockSpec((2, ROWS, KCOLS), lambda i: (0, 0, i)),
            pl.BlockSpec((2, ROWS, KCOLS), lambda i: (0, 0, i)),
            pl.BlockSpec((2, ROWS, KCOLS), lambda i: (0, 0, i)),
            fresh(512, GCOLS),
            fresh(512, GCOLS),
        ),
        compiler_params=pltpu.CompilerParams(
            dimension_semantics=("arbitrary",), vmem_limit_bytes=28 << 20
        ),
        cost_estimate=SMALL,
        name="attention",
    )(place, far, near, own, q, da, wk, wv, tp, th)


def cut(addends, rows):
    total = addends[0][rows, :].astype(F32)
    for other in addends[1:]:
        total = total + other[rows, :].astype(F32)
    return total


def fold_kernel(count, quarter, *refs):
    addends, outs = refs[:count], refs[count:]
    for d in range(4):
        outs[d][...] = cut(addends, slice(d * quarter, (d + 1) * quarter)).astype(outs[d].dtype)


def folded(*addends):
    rows, cols = addends[0].shape
    quarter = rows // 4
    return pl.pallas_call(
        functools.partial(fold_kernel, len(addends), quarter),
        grid=(cols // GCOLS,),
        out_shape=tuple(
            jax.ShapeDtypeStruct((quarter, cols), BF16 if d else F32) for d in range(4)
        ),
        in_specs=[pl.BlockSpec((rows, GCOLS), lambda i: (0, i))] * len(addends),
        out_specs=(pl.BlockSpec((quarter, GCOLS), lambda i: (0, i)),) * 4,
        compiler_params=pltpu.CompilerParams(vmem_limit_bytes=12 << 20),
        name="fold",
    )(*addends)


def column_kernel(counts, *refs):
    out_ref, sum_ref = refs[-2], refs[-1]
    at, col = 0, 0
    for count in counts:
        total = cut(refs[at : at + count], slice(0, 32))
        at += count
        sum_ref[:, col : col + total.shape[1]] = total
        col += total.shape[1]
    low = lax.broadcasted_iota(jnp.int32, (8, LANES), 0) < 4
    for z in range(4):
        for block in range(0, 24, 4):
            even, odd = [], []
            for pair in range(2):
                c = (block + 2 * pair) * LANES
                one = sum_ref[8 * z : 8 * z + 8, c : c + LANES]
                two = sum_ref[8 * z : 8 * z + 8, c + LANES : c + 2 * LANES]
                even.append(jnp.where(low, one, pltpu.roll(two, 4, 0)))
                odd.append(jnp.where(low, pltpu.roll(one, 4, 0), two))
            rows = slice(block * 4, block * 4 + 16)
            out_ref[2 * z, rows, :] = jnp.concatenate(even, 0).astype(BF16)
            out_ref[2 * z + 1, rows, :] = jnp.concatenate(odd, 0).astype(BF16)


def in_column_order(*groups):
    args = [a for group in groups for a in group]
    return pl.pallas_call(
        functools.partial(column_kernel, tuple(len(group) for group in groups)),
        grid=(1,),
        out_shape=jax.ShapeDtypeStruct((8, 96, LANES), BF16),
        in_specs=[whole(*a.shape) for a in args],
        out_specs=whole(8, 96, LANES),
        scratch_shapes=[pltpu.VMEM((32, 4 * GCOLS), F32)],
        compiler_params=pltpu.CompilerParams(vmem_limit_bytes=8 << 20),
        name="column",
    )(*args)


def last_kernel(got_ref, q_ref, k_ref, v_ref, o_ref):
    total = got_ref[0].astype(F32)
    for i in range(1, 8):
        total = total + got_ref[i].astype(F32)
    for step in range(STEPS):
        base = step * 24
        out, q, kv = (total[base + 8 * i : base + 8 * i + 8] for i in range(3))
        for ref, pair in ((o_ref, out), (q_ref, q)):
            ref[:, step * 256 : step * 256 + 128] = pair[:4]
            ref[:, step * 256 + 128 : step * 256 + 256] = pair[4:]
        k_ref[:, step * 128 : step * 128 + 128] = kv[:4]
        v_ref[:, step * 128 : step * 128 + 128] = kv[4:]


def summed_last(got):
    shapes = [(4, 1024), (4, 512), (4, 512), (4, 1024)]
    return pl.pallas_call(
        last_kernel,
        grid=(1,),
        out_shape=tuple(jax.ShapeDtypeStruct(shape, F32) for shape in shapes),
        in_specs=[whole(8, 96, LANES)],
        out_specs=tuple(whole(*shape) for shape in shapes),
        compiler_params=pltpu.CompilerParams(vmem_limit_bytes=4 << 20),
        name="last",
    )(got)


def after(value, *others):
    return lax.optimization_barrier((value, *others))[0]


def shards(tokens, query_weight, key_weight, value_matrix, out_weight, out_cotangent):
    near = passed_along(tokens, 1)
    far = passed_along(tokens, 2)
    me = lax.axis_index(AXIS)
    start = jnp.maximum(2 - me, 0) * ROWS
    place = jnp.stack([(me // 8) % 4, (me // 2) % 4, me % 2, start]).astype(jnp.int32)
    q, da, tp = early(place, tokens, out_cotangent, in_hbm(query_weight), in_hbm(out_weight))
    th = prepared(place, far, near)

    wk, wv = in_hbm(key_weight), in_hbm(value_matrix)

    def attend(first, steps, place):
        return attention(
            first, steps, place, far, near, tokens, q, da, wk, wv, tp, th
        )

    one = attend(0, 3, place)
    got_one = to_mate(one[-2])
    two = attend(3, 1, after(place, one[-1]))
    got_two = to_mate(two[-2])
    own_one, *sends = folded(one[-1], after(got_one, two[-1]))
    ring_one = ring([None, *sends], 0)
    own_two, *sends = folded(two[-1], after(got_two, own_one))
    ring_two = ring([None, *(after(s, ring_one[0]) for s in sends)], 0)
    own_one, *sends = folded(own_one, *ring_one)
    ring_one = ring([None, *sends], 1)
    own_two, *sends = folded(own_two, *ring_two)
    ring_two = ring([None, *sends], 1)
    column = in_column_order([own_one, *ring_one], [own_two, *ring_two])
    got = lax.all_to_all(column, AXIS, 0, 0, axis_index_groups=Z_GROUPS, tiled=True)
    query_rows, key_rows, value_rows, out_rows = summed_last(got)

    parts = zip(one[:-2], two[:-2])
    att, dq, own_kv, near_kv, far_kv = (jnp.concatenate(p, axis=-1) for p in parts)
    back_near = passed_along(after(near_kv, own_two), -1)
    back_far = passed_along(after(far_kv, own_two), -2)
    attn_out = dot(att, out_weight).astype(BF16)
    kv = (own_kv + back_near.astype(F32) + back_far.astype(F32)).astype(BF16)
    tokens_grad = (
        dot(dq, query_weight, NT) + dot(kv[0], key_weight, NT) + dot(kv[1], value_matrix, NT)
    ).astype(BF16)

    return attn_out, tokens_grad, query_rows, key_rows, value_rows, out_rows.T


def solution(mesh):
    rows = P(AXIS, None)
    return jax.shard_map(
        shards,
        mesh=mesh,
        in_specs=(rows, P(), P(), P(), P(), rows),
        out_specs=(rows, rows, rows, rows, rows, P(None, AXIS)),
        check_vma=False,
    )
```

time: 129 us -> 100 us (0.78)
  the two profiles are of different devices: /device:TPU:24 before, /device:TPU:1 now
where the time goes in v1:
time: 100 us; the launch traced here: 99.4 us
  starting transfers between devices  55.9 us (56%)
  Pallas kernels  24.1 us (24%)
  waiting for transfers between devices  11.7 us (12%)
  matrix products  3.64 us (4%)
  local copies, waits for them, and re-layouts  2.89 us (3%)
    ppermute x12, starting transfers between devices, ring(): lax.ppermute(blocks[d], AXIS, route_of(functools.partial(step, d)))  25.5 us
    all_to_all x1, starting transfers between devices, shards(): lax.all_to_all(column, AXIS, 0, 0, axis_index_groups=Z_GROUPS, tiled=True)  18.7 us
    pallas_call x2, Pallas kernels, attention(): pl.pallas_call(attention_kernel, grid=(steps,), out_shape=(struct(ROWS, Q...  15 us
    ppermute x4, starting transfers between devices, passed_along(): return lax.ppermute(block, AXIS, route)  11 us
    all_to_all x1, waiting for transfers between devices, shards(): lax.all_to_all(column, AXIS, 0, 0, axis_index_groups=Z_GROUPS, tiled=True)  5.93 us
    ppermute x12, waiting for transfers between devices, ring(): lax.ppermute(blocks[d], AXIS, route_of(functools.partial(step, d)))  5.77 us
    pallas_call x1, Pallas kernels, early(): pl.pallas_call(early_kernel, grid=(STEPS,), out_shape=(jax.ShapeDtypeStru...  4.47 us
    dot_general x4, matrix products, dot(): return lax.dot_general(a, b, dims, preferred_element_type=F32)  3.64 us
  transfers between devices with their start and end apart: 19, of which 2 were waited for; matrix products, arithmetic and copies ran while one was open for 4% of the time, Pallas kernels for 11%

profile of v1, /device:TPU:1, one launch (start us, length us, event | category | flops | bytes accessed | tf_op | source)
XLA Modules:
  0.0 99.4 jit_solution(1071812559109458939)
XLA Ops:
  0.6 4.6 %collective-permute-start.1 = (bf16[128,1024]{1,0:T(8,128)(2,1)}, bf16[128,1024]{1,0:T(8,128)(2,1)S(1)}, u32[]{:S(2)}, u32[]{:S(2)}) collective-permute-start(bf16[128,1024]{1,0:T(8,128)(2,1)} %own_ref.3), channel_id=1, source_target_pairs={{0,1},{1,2},{2,3},{3,4},{4,5},{5,6},{6,7},{7,8},{8,9},{9,10},{10,1... | collective-permute-start | bytes 786440 | tf_op jit(solution)/shard_map/ppermute | solution.py:63
  5.2 3.2 %collective-permute-start = (bf16[128,1024]{1,0:T(8,128)(2,1)}, bf16[128,1024]{1,0:T(8,128)(2,1)S(1)}, u32[]{:S(2)}, u32[]{:S(2)}) collective-permute-start(bf16[128,1024]{1,0:T(8,128)(2,1)} %own_ref.3), channel_id=1, source_target_pairs={{0,2},{1,3},{2,4},{3,5},{4,6},{5,7},{6,8},{7,9},{8,10},{9,11},{10,... | collective-permute-start | bytes 786440 | tf_op jit(solution)/shard_map/ppermute | solution.py:63
  10.5 4.5 %early.1 = (bf16[128,1024]{1,0:T(8,128)(2,1)S(1)}, bf16[128,1024]{1,0:T(8,128)(2,1)S(1)}, bf16[2,512,256]{2,1,0:T(8,128)(2,1)S(1)}) custom-call(s32[4]{0:T(128)S(1)} %pad_add_fusion.place, bf16[128,1024]{1,0:T(8,128)(2,1)S(1)} %copy-done, bf16[128,1024]{1,0:T(8,128)(2,1)S(1)} %copy-done.2, bf16[1024,1024]{1,0:T(8,128)(2,1)} %wq_ref.1, bf16[1024,1024]{1,0:T(8,128)(2,1)} %wo_ref.1), custom_call_target="tpu_custom_call" | custom-call | tf_op jit(solution)/shard_map/early/pallas_call | solution.py:111
  15.0 1.2 %prep.1.th_ref = bf16[2,512,256]{2,1,0:T(8,128)(2,1)S(1)} custom-call(s32[4]{0:T(128)S(1)} %pad_add_fusion.place, bf16[128,1024]{1,0:T(8,128)(2,1)S(1)} %collective-permute-done.a_ref.far_ref, bf16[128,1024]{1,0:T(8,128)(2,1)S(1)} %collective-permute-done.1.b_ref.near_ref), custom_call_target="tpu_custom_call" | custom-call | tf_op jit(solution)/shard_map/prep/pallas_call | solution.py:142
  16.2 10.9 %attention.2 = (bf16[128,768]{1,0:T(8,128)(2,1)S(1)}, bf16[128,768]{1,0:T(8,128)(2,1)S(1)}, f32[2,128,384]{2,1,0:T(8,128)S(1)}, bf16[2,128,384]{2,1,0:T(8,128)(2...) custom-call(s32[4]{0:T(128)S(1)} %pad_add_fusion.place, ...), custom_call_target="tpu_custom_call" | custom-call | flops 1000 | bytes 1000 | tf_op jit(solution)/shard_map/attention/pallas_call | solution.py:249
  27.2 4.1 %attention.3 = (bf16[128,256]{1,0:T(8,128)(2,1)S(1)}, bf16[128,256]{1,0:T(8,128)(2,1)S(1)}, f32[2,128,128]{2,1,0:T(8,128)S(1)}, bf16[2,128,128]{2,1,0:T(8,128)(2...) custom-call(s32[4]{0:T(128)S(1)} %pad_add_fusion.place, ...), custom_call_target="tpu_custom_call" | custom-call | flops 1000 | bytes 1000 | tf_op jit(solution)/shard_map/attention/pallas_call | solution.py:249
  31.9 1.1 %fold.4 = (f32[128,2304]{1,0:T(8,128)S(1)}, bf16[128,2304]{1,0:T(8,128)(2,1)S(1)}, bf16[128,2304]{1,0:T(8,128)(2,1)S(1)}, bf16[128,2304]{1,0:T(8,128)(2,1)S(1)}) custom-call(bf16[512,2304]{1,0:T(8,128)(2,1)S(1)} %get-tuple-element.55.refs_0_, bf16[512,2304]{1,0:T(8,128)(2,1)S(1)} %collective-permute-done.3.refs_1_), custom_call_target="tpu_custom_call" | custom-call | tf_op jit(solution)/shard_map/fold/pallas_call | solution.py:306
  33.1 1.3 %collective-permute-start.4 = (bf16[128,2304]{1,0:T(8,128)(2,1)S(1)}, bf16[128,2304]{1,0:T(8,128)(2,1)S(1)}, u32[]{:S(2)}, u32[]{:S(2)}) collective-permute-start(bf16[128,2304]{1,0:T(8,128)(2,1)S(1)} %get-tuple-element.72), channel_id=1, source_target_pairs={{0,8},{1,3},{2,10},{3,5},{4,12},{5,7},{6,14},{7,1},{8,16},{9,11},{... | collective-permute-start | bytes 1769480 | tf_op jit(solution)/shard_map/ppermute | solution.py:56
  34.4 1.6 %collective-permute-start.10 = (bf16[128,2304]{1,0:T(8,128)(2,1)S(1)}, bf16[128,2304]{1,0:T(8,128)(2,1)S(1)}, u32[]{:S(2)}, u32[]{:S(2)}) collective-permute-start(bf16[128,2304]{1,0:T(8,128)(2,1)S(1)} %get-tuple-element.83), channel_id=1, source_target_pairs={{0,24},{1,7},{2,26},{3,1},{4,28},{5,3},{6,30},{7,5},{8,0},{9,15},{... | collective-permute-start | bytes 1769480 | tf_op jit(solution)/shard_map/ppermute | solution.py:56
  36.0 1.6 %collective-permute-start.11 = (bf16[128,2304]{1,0:T(8,128)(2,1)S(1)}, bf16[128,2304]{1,0:T(8,128)(2,1)S(1)}, u32[]{:S(2)}, u32[]{:S(2)}) collective-permute-start(bf16[128,2304]{1,0:T(8,128)(2,1)S(1)} %get-tuple-element.84), channel_id=1, source_target_pairs={{0,16},{1,5},{2,18},{3,7},{4,20},{5,1},{6,22},{7,3},{8,24},{9,13},... | collective-permute-start | bytes 1769480 | tf_op jit(solution)/shard_map/ppermute | solution.py:56
  37.7 5.7 %collective-permute-done.4.refs_1_ = bf16[128,2304]{1,0:T(8,128)(2,1)S(1)} collective-permute-done((bf16[128,2304]{1,0:T(8,128)(2,1)S(1)}, bf16[128,2304]{1,0:T(8,128)(2,1)S(1)}, u32[]{:S(2)}, u32[]{:S(2)}) %collective-permute-start.4) | collective-permute-done | bytes 589856 | tf_op jit(solution)/shard_map/ppermute | solution.py:56
  43.5 2.7 %collective-permute-start.6 = (bf16[128,768]{1,0:T(8,128)(2,1)S(1)}, bf16[128,768]{1,0:T(8,128)(2,1)S(1)}, u32[]{:S(2)}, u32[]{:S(2)}) collective-permute-start(bf16[128,768]{1,0:T(8,128)(2,1)S(1)} %get-tuple-element.75), channel_id=1, source_target_pairs={{0,24},{1,7},{2,26},{3,1},{4,28},{5,3},{6,30},{7,5},{8,0},{9,15},{... | collective-permute-start | bytes 589832 | tf_op jit(solution)/shard_map/ppermute | solution.py:56
  46.1 6.8 %collective-permute-start.7 = (bf16[128,768]{1,0:T(8,128)(2,1)S(1)}, bf16[128,768]{1,0:T(8,128)(2,1)S(1)}, u32[]{:S(2)}, u32[]{:S(2)}) collective-permute-start(bf16[128,768]{1,0:T(8,128)(2,1)S(1)} %get-tuple-element.77), channel_id=1, source_target_pairs={{0,16},{1,5},{2,18},{3,7},{4,20},{5,1},{6,22},{7,3},{8,24},{9,13},... | collective-permute-start | bytes 589832 | tf_op jit(solution)/shard_map/ppermute | solution.py:56
  53.5 2.7 %collective-permute-start.12 = (bf16[32,2304]{1,0:T(8,128)(2,1)S(1)}, bf16[32,2304]{1,0:T(8,128)(2,1)S(1)}, u32[]{:S(2)}, u32[]{:S(2)}) collective-permute-start(bf16[32,2304]{1,0:T(8,128)(2,1)S(1)} %get-tuple-element.86), channel_id=1, source_target_pairs={{0,2},{1,9},{2,4},{3,11},{4,6},{5,13},{6,0},{7,15},{8,10},{9,17},{... | collective-permute-start | bytes 442376 | tf_op jit(solution)/shard_map/ppermute | solution.py:56
  56.2 1.5 %collective-permute-start.13 = (bf16[32,2304]{1,0:T(8,128)(2,1)S(1)}, bf16[32,2304]{1,0:T(8,128)(2,1)S(1)}, u32[]{:S(2)}, u32[]{:S(2)}) collective-permute-start(bf16[32,2304]{1,0:T(8,128)(2,1)S(1)} %get-tuple-element.87), channel_id=1, source_target_pairs={{0,6},{1,25},{2,0},{3,27},{4,2},{5,29},{6,4},{7,31},{8,14},{9,1},{... | collective-permute-start | bytes 442376 | tf_op jit(solution)/shard_map/ppermute | solution.py:56
  57.7 3.1 %collective-permute-start.14 = (bf16[32,2304]{1,0:T(8,128)(2,1)S(1)}, bf16[32,2304]{1,0:T(8,128)(2,1)S(1)}, u32[]{:S(2)}, u32[]{:S(2)}) collective-permute-start(bf16[32,2304]{1,0:T(8,128)(2,1)S(1)} %get-tuple-element.88), channel_id=1, source_target_pairs={{0,4},{1,17},{2,6},{3,19},{4,0},{5,21},{6,2},{7,23},{8,12},{9,25},... | collective-permute-start | bytes 442376 | tf_op jit(solution)/shard_map/ppermute | solution.py:56
  61.0 2.1 %collective-permute-start.15 = (bf16[32,768]{1,0:T(8,128)(2,1)S(1)}, bf16[32,768]{1,0:T(8,128)(2,1)S(1)}, u32[]{:S(2)}, u32[]{:S(2)}) collective-permute-start(bf16[32,768]{1,0:T(8,128)(2,1)S(1)} %get-tuple-element.89), channel_id=1, source_target_pairs={{0,2},{1,9},{2,4},{3,11},{4,6},{5,13},{6,0},{7,15},{8,10},{9,17},{... | collective-permute-start | bytes 147464 | tf_op jit(solution)/shard_map/ppermute | solution.py:56
  64.0 1.3 %collective-permute-start.17 = (bf16[32,768]{1,0:T(8,128)(2,1)S(1)}, bf16[32,768]{1,0:T(8,128)(2,1)S(1)}, u32[]{:S(2)}, u32[]{:S(2)}) collective-permute-start(bf16[32,768]{1,0:T(8,128)(2,1)S(1)} %get-tuple-element.91), channel_id=1, source_target_pairs={{0,4},{1,17},{2,6},{3,19},{4,0},{5,21},{6,2},{7,23},{8,12},{9,25},... | collective-permute-start | bytes 147464 | tf_op jit(solution)/shard_map/ppermute | solution.py:56
  65.3 1.9 %collective-permute-start.8 = (bf16[2,128,512]{2,1,0:T(8,128)(2,1)S(1)}, bf16[2,128,512]{2,1,0:T(8,128)(2,1)S(1)}, u32[]{:S(2)}, u32[]{:S(2)}) collective-permute-start(bf16[2,128,512]{2,1,0:T(8,128)(2,1)S(1)} %get-tuple-element.79), channel_id=1, source_target_pairs={{1,0},{2,1},{3,2},{4,3},{5,4},{6,5},{7,6},{8,7},{9,8},{10,9},{11,1... | collective-permute-start | bytes 786440 | tf_op jit(solution)/shard_map/ppermute | solution.py:63
  67.3 1.3 %collective-permute-start.9 = (bf16[2,128,512]{2,1,0:T(8,128)(2,1)S(1)}, bf16[2,128,512]{2,1,0:T(8,128)(2,1)S(1)}, u32[]{:S(2)}, u32[]{:S(2)}) collective-permute-start(bf16[2,128,512]{2,1,0:T(8,128)(2,1)S(1)} %get-tuple-element.82), channel_id=1, source_target_pairs={{2,0},{3,1},{4,2},{5,3},{6,4},{7,5},{8,6},{9,7},{10,8},{11,9},{12,... | collective-permute-start | bytes 786440 | tf_op jit(solution)/shard_map/ppermute | solution.py:63
  68.6 1.2 %convolution_convert_fusion = bf16[128,1024]{1,0:T(8,128)(2,1)} fusion(bf16[1024,1024]{1,0:T(8,128)(2,1)S(1)} %copy-done.5, bf16[128,256]{1,0:T(8,128)(2,1)S(1)} %get-tuple-element.57, bf16[128,768]{1,0:T(8,128)(2,1)S(1)} %get-tuple-element.54), kind=kOutput, calls=%fused_computation.3 | convolution fusion | flops 269090816 | bytes 2621440 | tf_op jit(solution)/shard_map/dot_general | solution.py:28
  70.5 18.7 %all-to-all-start = ((bf16[8,96,128]{2,1,0:T(8,128)(2,1)}), bf16[8,96,128]{2,1,0:T(8,128)(2,1)S(1)}, u32[]{:S(2)}, u32[]{:S(2)}) async-start(bf16[8,96,128]{2,1,0:T(8,128)(2,1)} %column.1), calls=%async_computation | async-start | bytes 393216 | tf_op jit(solution)/shard_map/all_to_all | solution.py:416
  91.7 1.2 %fusion = bf16[128,1024]{1,0:T(8,128)(2,1)} fusion(f32[128,1024]{1,0:T(8,128)S(1)} %convolution_add_fusion.1, bf16[1024,512]{1,0:T(8,128)(2,1)S(1)} %copy-done.4, bf16[2,128,512]{2,1,0:T(8,128)(2,1)S(1)} %fusion.2), kind=kOutput, calls=%fused_computation.2 | convolution fusion | flops 134479872 | bytes 1966080 | tf_op jit(solution)/shard_map/dot_general | solution.py:28
  92.9 5.9 %all-to-all-done.got_ref = bf16[8,96,128]{2,1,0:T(8,128)(2,1)S(1)} async-done(((bf16[8,96,128]{2,1,0:T(8,128)(2,1)}), bf16[8,96,128]{2,1,0:T(8,128)(2,1)S(1)}, u32[]{:S(2)}, u32[]{:S(2)}) %all-to-all-start) | async-done | bytes 196640 | tf_op jit(solution)/shard_map/all_to_all | solution.py:416
  (45 shorter events, 8.3 us)
Async XLA Ops:
  0.6 14.4 %collective-permute-start.1 = (bf16[128,1024]{1,0:T(8,128)(2,1)}, bf16[128,1024]{1,0:T(8,128)(2,1)S(1)}, u32[]{:S(2)}, u32[]{:S(2)}) collective-permute-start(bf16[128,1024]{1,0:T(8,128)(2,1)} %own_ref.3), channel_id=1, source_target_pairs={{0,1},{1,2},{2,3},{3,4},{4,5},{5,6},{6,7},{7,8},{8,9},{9,10},{10,1... | collective-permute-start | bytes 786440 | tf_op jit(solution)/shard_map/ppermute | solution.py:63
  5.2 9.8 %collective-permute-start = (bf16[128,1024]{1,0:T(8,128)(2,1)}, bf16[128,1024]{1,0:T(8,128)(2,1)S(1)}, u32[]{:S(2)}, u32[]{:S(2)}) collective-permute-start(bf16[128,1024]{1,0:T(8,128)(2,1)} %own_ref.3), channel_id=1, source_target_pairs={{0,2},{1,3},{2,4},{3,5},{4,6},{5,7},{6,8},{7,9},{8,10},{9,11},{10,... | collective-permute-start | bytes 786440 | tf_op jit(solution)/shard_map/ppermute | solution.py:63
  10.5 5.7 %copy-start.1 = (bf16[128,1024]{1,0:T(8,128)(2,1)S(1)}, bf16[128,1024]{1,0:T(8,128)(2,1)}, u32[]{:S(2)}) copy-start(bf16[128,1024]{1,0:T(8,128)(2,1)} %own_ref.3) | copy-start | bytes 786436
  27.1 4.8 %collective-permute-start.3 = (bf16[512,2304]{1,0:T(8,128)(2,1)S(1)}, bf16[512,2304]{1,0:T(8,128)(2,1)S(1)}, u32[]{:S(2)}, u32[]{:S(2)}) collective-permute-start(bf16[512,2304]{1,0:T(8,128)(2,1)S(1)} %get-tuple-element.66), channel_id=1, source_target_pairs={{0,1},{1,0},{2,3},{3,2},{4,5},{5,4},{6,7},{7,6},{8,9},{9,8},{10,11... | collective-permute-start | bytes 7077896 | tf_op jit(solution)/shard_map/ppermute | solution.py:45
  31.4 6.2 %collective-permute-start.2 = (bf16[512,768]{1,0:T(8,128)(2,1)S(1)}, bf16[512,768]{1,0:T(8,128)(2,1)S(1)}, u32[]{:S(2)}, u32[]{:S(2)}) collective-permute-start(bf16[512,768]{1,0:T(8,128)(2,1)S(1)} %get-tuple-element.65), channel_id=1, source_target_pairs={{0,1},{1,0},{2,3},{3,2},{4,5},{5,4},{6,7},{7,6},{8,9},{9,8},{10,11... | collective-permute-start | bytes 2359304 | tf_op jit(solution)/shard_map/ppermute | solution.py:45
  33.1 10.4 %collective-permute-start.4 = (bf16[128,2304]{1,0:T(8,128)(2,1)S(1)}, bf16[128,2304]{1,0:T(8,128)(2,1)S(1)}, u32[]{:S(2)}, u32[]{:S(2)}) collective-permute-start(bf16[128,2304]{1,0:T(8,128)(2,1)S(1)} %get-tuple-element.72), channel_id=1, source_target_pairs={{0,8},{1,3},{2,10},{3,5},{4,12},{5,7},{6,14},{7,1},{8,16},{9,11},{... | collective-permute-start | bytes 1769480 | tf_op jit(solution)/shard_map/ppermute | solution.py:56
  34.4 18.5 %collective-permute-start.10 = (bf16[128,2304]{1,0:T(8,128)(2,1)S(1)}, bf16[128,2304]{1,0:T(8,128)(2,1)S(1)}, u32[]{:S(2)}, u32[]{:S(2)}) collective-permute-start(bf16[128,2304]{1,0:T(8,128)(2,1)S(1)} %get-tuple-element.83), channel_id=1, source_target_pairs={{0,24},{1,7},{2,26},{3,1},{4,28},{5,3},{6,30},{7,5},{8,0},{9,15},{... | collective-permute-start | bytes 1769480 | tf_op jit(solution)/shard_map/ppermute | solution.py:56
  36.0 16.9 %collective-permute-start.11 = (bf16[128,2304]{1,0:T(8,128)(2,1)S(1)}, bf16[128,2304]{1,0:T(8,128)(2,1)S(1)}, u32[]{:S(2)}, u32[]{:S(2)}) collective-permute-start(bf16[128,2304]{1,0:T(8,128)(2,1)S(1)} %get-tuple-element.84), channel_id=1, source_target_pairs={{0,16},{1,5},{2,18},{3,7},{4,20},{5,1},{6,22},{7,3},{8,24},{9,13},... | collective-permute-start | bytes 1769480 | tf_op jit(solution)/shard_map/ppermute | solution.py:56
  43.5 14.3 %collective-permute-start.5 = (bf16[128,768]{1,0:T(8,128)(2,1)S(1)}, bf16[128,768]{1,0:T(8,128)(2,1)S(1)}, u32[]{:S(2)}, u32[]{:S(2)}) collective-permute-start(bf16[128,768]{1,0:T(8,128)(2,1)S(1)} %get-tuple-element.73), channel_id=1, source_target_pairs={{0,8},{1,3},{2,10},{3,5},{4,12},{5,7},{6,14},{7,1},{8,16},{9,11},{... | collective-permute-start | bytes 589832 | tf_op jit(solution)/shard_map/ppermute | solution.py:56
  43.5 25.1 %copy-start.5 = (bf16[1024,1024]{1,0:T(8,128)(2,1)S(1)}, bf16[1024,1024]{1,0:T(8,128)(2,1)}, u32[]{:S(2)}) copy-start(bf16[1024,1024]{1,0:T(8,128)(2,1)} %wo_ref.1) | copy-start | bytes 6291460
  43.5 17.4 %collective-permute-start.6 = (bf16[128,768]{1,0:T(8,128)(2,1)S(1)}, bf16[128,768]{1,0:T(8,128)(2,1)S(1)}, u32[]{:S(2)}, u32[]{:S(2)}) collective-permute-start(bf16[128,768]{1,0:T(8,128)(2,1)S(1)} %get-tuple-element.75), channel_id=1, source_target_pairs={{0,24},{1,7},{2,26},{3,1},{4,28},{5,3},{6,30},{7,5},{8,0},{9,15},{... | collective-permute-start | bytes 589832 | tf_op jit(solution)/shard_map/ppermute | solution.py:56
  46.1 14.7 %collective-permute-start.7 = (bf16[128,768]{1,0:T(8,128)(2,1)S(1)}, bf16[128,768]{1,0:T(8,128)(2,1)S(1)}, u32[]{:S(2)}, u32[]{:S(2)}) collective-permute-start(bf16[128,768]{1,0:T(8,128)(2,1)S(1)} %get-tuple-element.77), channel_id=1, source_target_pairs={{0,16},{1,5},{2,18},{3,7},{4,20},{5,1},{6,22},{7,3},{8,24},{9,13},... | collective-permute-start | bytes 589832 | tf_op jit(solution)/shard_map/ppermute | solution.py:56
  53.5 10.5 %collective-permute-start.12 = (bf16[32,2304]{1,0:T(8,128)(2,1)S(1)}, bf16[32,2304]{1,0:T(8,128)(2,1)S(1)}, u32[]{:S(2)}, u32[]{:S(2)}) collective-permute-start(bf16[32,2304]{1,0:T(8,128)(2,1)S(1)} %get-tuple-element.86), channel_id=1, source_target_pairs={{0,2},{1,9},{2,4},{3,11},{4,6},{5,13},{6,0},{7,15},{8,10},{9,17},{... | collective-permute-start | bytes 442376 | tf_op jit(solution)/shard_map/ppermute | solution.py:56
  56.2 9.1 %collective-permute-start.13 = (bf16[32,2304]{1,0:T(8,128)(2,1)S(1)}, bf16[32,2304]{1,0:T(8,128)(2,1)S(1)}, u32[]{:S(2)}, u32[]{:S(2)}) collective-permute-start(bf16[32,2304]{1,0:T(8,128)(2,1)S(1)} %get-tuple-element.87), channel_id=1, source_target_pairs={{0,6},{1,25},{2,0},{3,27},{4,2},{5,29},{6,4},{7,31},{8,14},{9,1},{... | collective-permute-start | bytes 442376 | tf_op jit(solution)/shard_map/ppermute | solution.py:56
  57.7 9.5 %collective-permute-start.14 = (bf16[32,2304]{1,0:T(8,128)(2,1)S(1)}, bf16[32,2304]{1,0:T(8,128)(2,1)S(1)}, u32[]{:S(2)}, u32[]{:S(2)}) collective-permute-start(bf16[32,2304]{1,0:T(8,128)(2,1)S(1)} %get-tuple-element.88), channel_id=1, source_target_pairs={{0,4},{1,17},{2,6},{3,19},{4,0},{5,21},{6,2},{7,23},{8,12},{9,25},... | collective-permute-start | bytes 442376 | tf_op jit(solution)/shard_map/ppermute | solution.py:56
  61.0 8.7 %collective-permute-start.15 = (bf16[32,768]{1,0:T(8,128)(2,1)S(1)}, bf16[32,768]{1,0:T(8,128)(2,1)S(1)}, u32[]{:S(2)}, u32[]{:S(2)}) collective-permute-start(bf16[32,768]{1,0:T(8,128)(2,1)S(1)} %get-tuple-element.89), channel_id=1, source_target_pairs={{0,2},{1,9},{2,4},{3,11},{4,6},{5,13},{6,0},{7,15},{8,10},{9,17},{... | collective-permute-start | bytes 147464 | tf_op jit(solution)/shard_map/ppermute | solution.py:56
  63.1 6.6 %collective-permute-start.16 = (bf16[32,768]{1,0:T(8,128)(2,1)S(1)}, bf16[32,768]{1,0:T(8,128)(2,1)S(1)}, u32[]{:S(2)}, u32[]{:S(2)}) collective-permute-start(bf16[32,768]{1,0:T(8,128)(2,1)S(1)} %get-tuple-element.90), channel_id=1, source_target_pairs={{0,6},{1,25},{2,0},{3,27},{4,2},{5,29},{6,4},{7,31},{8,14},{9,1},{... | collective-permute-start | bytes 147464 | tf_op jit(solution)/shard_map/ppermute | solution.py:56
  64.0 5.8 %collective-permute-start.17 = (bf16[32,768]{1,0:T(8,128)(2,1)S(1)}, bf16[32,768]{1,0:T(8,128)(2,1)S(1)}, u32[]{:S(2)}, u32[]{:S(2)}) collective-permute-start(bf16[32,768]{1,0:T(8,128)(2,1)S(1)} %get-tuple-element.91), channel_id=1, source_target_pairs={{0,4},{1,17},{2,6},{3,19},{4,0},{5,21},{6,2},{7,23},{8,12},{9,25},... | collective-permute-start | bytes 147464 | tf_op jit(solution)/shard_map/ppermute | solution.py:56
  65.3 23.9 %collective-permute-start.8 = (bf16[2,128,512]{2,1,0:T(8,128)(2,1)S(1)}, bf16[2,128,512]{2,1,0:T(8,128)(2,1)S(1)}, u32[]{:S(2)}, u32[]{:S(2)}) collective-permute-start(bf16[2,128,512]{2,1,0:T(8,128)(2,1)S(1)} %get-tuple-element.79), channel_id=1, source_target_pairs={{1,0},{2,1},{3,2},{4,3},{5,4},{6,5},{7,6},{8,7},{9,8},{10,9},{11,1... | collective-permute-start | bytes 786440 | tf_op jit(solution)/shard_map/ppermute | solution.py:63
  67.3 22.0 %collective-permute-start.9 = (bf16[2,128,512]{2,1,0:T(8,128)(2,1)S(1)}, bf16[2,128,512]{2,1,0:T(8,128)(2,1)S(1)}, u32[]{:S(2)}, u32[]{:S(2)}) collective-permute-start(bf16[2,128,512]{2,1,0:T(8,128)(2,1)S(1)} %get-tuple-element.82), channel_id=1, source_target_pairs={{2,0},{3,1},{4,2},{5,3},{6,4},{7,5},{8,6},{9,7},{10,8},{11,9},{12,... | collective-permute-start | bytes 786440 | tf_op jit(solution)/shard_map/ppermute | solution.py:63
  69.7 19.7 %copy-start.3 = (bf16[1024,512]{1,0:T(8,128)(2,1)S(1)}, bf16[1024,512]{1,0:T(8,128)(2,1)}, u32[]{:S(2)}) copy-start(bf16[1024,512]{1,0:T(8,128)(2,1)} %wk_ref.3) | copy-start | bytes 3145732
  70.5 28.3 %all-to-all-start = ((bf16[8,96,128]{2,1,0:T(8,128)(2,1)}), bf16[8,96,128]{2,1,0:T(8,128)(2,1)S(1)}, u32[]{:S(2)}, u32[]{:S(2)}) async-start(bf16[8,96,128]{2,1,0:T(8,128)(2,1)} %column.1), calls=%async_computation | async-start | bytes 393216 | tf_op jit(solution)/shard_map/all_to_all | solution.py:416
  89.2 1.6 %copy-start.6 = (bf16[1024,1024]{1,0:T(8,128)(2,1)S(1)}, bf16[1024,1024]{1,0:T(8,128)(2,1)}, u32[]{:S(2)}) copy-start(bf16[1024,1024]{1,0:T(8,128)(2,1)} %wq_ref.1) | copy-start | bytes 6291460
  89.8 1.8 %copy-start.4 = (bf16[1024,512]{1,0:T(8,128)(2,1)S(1)}, bf16[1024,512]{1,0:T(8,128)(2,1)}, u32[]{:S(2)}) copy-start(bf16[1024,512]{1,0:T(8,128)(2,1)} %wv_ref.3) | copy-start | bytes 3145732
  (2 other events, 1.9 us)

commit v2 on v1

--- a/solution.py
+++ b/solution.py
@@ -45,16 +45,23 @@
     return lax.ppermute(array, AXIS, route_of(lambda z, x, y, c: (z, x, y, 1 - c)))
 
 
+def plane_step(phase, d, z, x, y, c):
+    if c == phase:
+        return z, (x + d) % 4, y, c
+    return z, x, (y + d) % 4, c
+
+
 def ring(blocks, phase):
-    def step(d, z, x, y, c):
-        if c == phase:
-            return z, (x + d) % 4, y, c
-        return z, x, (y + d) % 4, c
-
-    order = (1, 3, 2)
     return [
-        lax.ppermute(blocks[d], AXIS, route_of(functools.partial(step, d))) for d in order
+        lax.ppermute(blocks[d], AXIS, route_of(functools.partial(plane_step, phase, d)))
+        for d in (1, 3, 2)
     ]
+
+
+def along_z(block, distance):
+    return lax.ppermute(
+        block, AXIS, route_of(lambda z, x, y, c: ((z + distance) % 8, x, y, c))
+    )
 
 
 def passed_along(block, distance):
@@ -63,13 +70,8 @@
     return lax.ppermute(block, AXIS, route)
 
 
-Z_GROUPS = [
-    [flat(z, x, y, c) for z in range(8)] for x in range(4) for y in range(4) for c in range(2)
-]
-
-
 def reorder(place, t_ref, out_ref):
-    x, y, core = place[0], place[1], place[2]
+    x, y, core, mine = place[0], place[1], place[2], place[3]
     low = lax.broadcasted_iota(jnp.int32, (8, 2 * LANES), 0) < 4
     for half in range(2):
         target = 1 - core if half == 0 else core
@@ -81,9 +83,11 @@
                 for z in range(0, 8, 4):
                     rows = []
                     for pair in range(2):
-                        base = (z + 2 * pair) * 128 + xs * 32 + ys * 8
-                        one = t_ref[pl.ds(pl.multiple_of(base, 8), 8), :]
-                        two = t_ref[pl.ds(pl.multiple_of(base + 128, 8), 8), :]
+                        base = xs * 32 + ys * 8
+                        at = base + lax.rem(mine + z + 2 * pair, 8) * 128
+                        one = t_ref[pl.ds(pl.multiple_of(at, 8), 8), :]
+                        at = base + lax.rem(mine + z + 2 * pair + 1, 8) * 128
+                        two = t_ref[pl.ds(pl.multiple_of(at, 8), 8), :]
                         c0 = jnp.where(low, one, pltpu.roll(two, 4, 0))
                         c1 = jnp.where(low, pltpu.roll(one, 4, 0), two)
                         rows.append(jnp.where(zero, c0, c1))
@@ -177,7 +181,7 @@
     window = jnp.concatenate([far_ref[...], near_ref[...], own_ref[...]], axis=0)
     keys = dot(window, wk_ref[...])
     values = dot(window, wv_ref[...])
-    start = place[3]
+    start = place[4]
     row = lax.rem(lax.broadcasted_iota(jnp.int32, (256, 384), 0), 128)
     col = lax.broadcasted_iota(jnp.int32, (256, 384), 1)
     allowed = (col <= row + 256) & (col >= start)
@@ -303,81 +307,88 @@
 def folded(*addends):
     rows, cols = addends[0].shape
     quarter = rows // 4
+    width = GCOLS if rows > 128 else cols
     return pl.pallas_call(
         functools.partial(fold_kernel, len(addends), quarter),
-        grid=(cols // GCOLS,),
+        grid=(cols // width,),
         out_shape=tuple(
             jax.ShapeDtypeStruct((quarter, cols), BF16 if d else F32) for d in range(4)
         ),
-        in_specs=[pl.BlockSpec((rows, GCOLS), lambda i: (0, i))] * len(addends),
-        out_specs=(pl.BlockSpec((quarter, GCOLS), lambda i: (0, i)),) * 4,
+        in_specs=[pl.BlockSpec((rows, width), lambda i: (0, i))] * len(addends),
+        out_specs=(pl.BlockSpec((quarter, width), lambda i: (0, i)),) * 4,
         compiler_params=pltpu.CompilerParams(vmem_limit_bytes=12 << 20),
         name="fold",
     )(*addends)
 
 
-def column_kernel(counts, *refs):
-    out_ref, sum_ref = refs[-2], refs[-1]
-    at, col = 0, 0
-    for count in counts:
-        total = cut(refs[at : at + count], slice(0, 32))
-        at += count
-        sum_ref[:, col : col + total.shape[1]] = total
-        col += total.shape[1]
-    low = lax.broadcasted_iota(jnp.int32, (8, LANES), 0) < 4
-    for z in range(4):
-        for block in range(0, 24, 4):
-            even, odd = [], []
-            for pair in range(2):
-                c = (block + 2 * pair) * LANES
-                one = sum_ref[8 * z : 8 * z + 8, c : c + LANES]
-                two = sum_ref[8 * z : 8 * z + 8, c + LANES : c + 2 * LANES]
-                even.append(jnp.where(low, one, pltpu.roll(two, 4, 0)))
-                odd.append(jnp.where(low, pltpu.roll(one, 4, 0), two))
-            rows = slice(block * 4, block * 4 + 16)
-            out_ref[2 * z, rows, :] = jnp.concatenate(even, 0).astype(BF16)
-            out_ref[2 * z + 1, rows, :] = jnp.concatenate(odd, 0).astype(BF16)
-
-
-def in_column_order(*groups):
-    args = [a for group in groups for a in group]
-    return pl.pallas_call(
-        functools.partial(column_kernel, tuple(len(group) for group in groups)),
+def join_kernel(*refs):
+    one, two, outs = refs[:4], refs[4:8], refs[8:]
+    split = one[0].shape[1]
+    for d in range(4):
+        rows = slice(d * 32, (d + 1) * 32)
+        outs[d][:, :split] = cut(one, rows).astype(outs[d].dtype)
+        outs[d][:, split:] = cut(two, rows).astype(outs[d].dtype)
+
+
+def joined(one, two):
+    args = [*one, *two]
+    cols = one[0].shape[1] + two[0].shape[1]
+    return pl.pallas_call(
+        join_kernel,
         grid=(1,),
-        out_shape=jax.ShapeDtypeStruct((8, 96, LANES), BF16),
+        out_shape=tuple(jax.ShapeDtypeStruct((32, cols), BF16 if d else F32) for d in range(4)),
         in_specs=[whole(*a.shape) for a in args],
-        out_specs=whole(8, 96, LANES),
-        scratch_shapes=[pltpu.VMEM((32, 4 * GCOLS), F32)],
-        compiler_params=pltpu.CompilerParams(vmem_limit_bytes=8 << 20),
-        name="column",
+        out_specs=(whole(32, cols),) * 4,
+        compiler_params=pltpu.CompilerParams(vmem_limit_bytes=16 << 20),
+        name="join",
     )(*args)
 
 
-def last_kernel(got_ref, q_ref, k_ref, v_ref, o_ref):
-    total = got_ref[0].astype(F32)
-    for i in range(1, 8):
-        total = total + got_ref[i].astype(F32)
+def halve_kernel(own_ref, a_ref, b_ref, c_ref, keep_ref, send_ref):
+    total = cut((own_ref, a_ref, b_ref, c_ref), slice(0, 8))
+    keep_ref[...] = total[:4]
+    send_ref[...] = total[4:].astype(BF16)
+
+
+def halved(*addends):
+    cols = addends[0].shape[1]
+    return pl.pallas_call(
+        halve_kernel,
+        grid=(1,),
+        out_shape=(
+            jax.ShapeDtypeStruct((4, cols), F32),
+            jax.ShapeDtypeStruct((4, cols), BF16),
+        ),
+        in_specs=[whole(8, cols)] * 4,
+        out_specs=(whole(4, cols),) * 2,
+        compiler_params=pltpu.CompilerParams(vmem_limit_bytes=4 << 20),
+        name="halve",
+    )(*addends)
+
+
+def last_kernel(own_ref, got_ref, q_ref, k_ref, v_ref, o_ref):
+    total = own_ref[...] + got_ref[...].astype(F32)
     for step in range(STEPS):
-        base = step * 24
-        out, q, kv = (total[base + 8 * i : base + 8 * i + 8] for i in range(3))
-        for ref, pair in ((o_ref, out), (q_ref, q)):
-            ref[:, step * 256 : step * 256 + 128] = pair[:4]
-            ref[:, step * 256 + 128 : step * 256 + 256] = pair[4:]
-        k_ref[:, step * 128 : step * 128 + 128] = kv[:4]
-        v_ref[:, step * 128 : step * 128 + 128] = kv[4:]
-
-
-def summed_last(got):
+        base = step * GCOLS
+        at = slice(step * 256, step * 256 + 256)
+        o_ref[:, at] = total[:, base : base + 256]
+        q_ref[:, at] = total[:, base + 256 : base + 512]
+        at = slice(step * 128, step * 128 + 128)
+        k_ref[:, at] = total[:, base + 512 : base + 640]
+        v_ref[:, at] = total[:, base + 640 : base + 768]
+
+
+def summed_last(own, got):
     shapes = [(4, 1024), (4, 512), (4, 512), (4, 1024)]
     return pl.pallas_call(
         last_kernel,
         grid=(1,),
         out_shape=tuple(jax.ShapeDtypeStruct(shape, F32) for shape in shapes),
-        in_specs=[whole(8, 96, LANES)],
+        in_specs=[whole(*own.shape)] * 2,
         out_specs=tuple(whole(*shape) for shape in shapes),
         compiler_params=pltpu.CompilerParams(vmem_limit_bytes=4 << 20),
         name="last",
-    )(got)
+    )(own, got)
 
 
 def after(value, *others):
@@ -389,7 +400,7 @@
     far = passed_along(tokens, 2)
     me = lax.axis_index(AXIS)
     start = jnp.maximum(2 - me, 0) * ROWS
-    place = jnp.stack([(me // 8) % 4, (me // 2) % 4, me % 2, start]).astype(jnp.int32)
+    place = jnp.stack([(me // 8) % 4, (me // 2) % 4, me % 2, me // 32, start]).astype(jnp.int32)
     q, da, tp = early(place, tokens, out_cotangent, in_hbm(query_weight), in_hbm(out_weight))
     th = prepared(place, far, near)
 
@@ -408,18 +419,19 @@
     ring_one = ring([None, *sends], 0)
     own_two, *sends = folded(two[-1], after(got_two, own_one))
     ring_two = ring([None, *(after(s, ring_one[0]) for s in sends)], 0)
-    own_one, *sends = folded(own_one, *ring_one)
-    ring_one = ring([None, *sends], 1)
-    own_two, *sends = folded(own_two, *ring_two)
-    ring_two = ring([None, *sends], 1)
-    column = in_column_order([own_one, *ring_one], [own_two, *ring_two])
-    got = lax.all_to_all(column, AXIS, 0, 0, axis_index_groups=Z_GROUPS, tiled=True)
-    query_rows, key_rows, value_rows, out_rows = summed_last(got)
+    own, *sends = joined([own_one, *ring_one], [own_two, *ring_two])
+    ring_three = ring([None, *sends], 1)
+    own, *sends = folded(own, *ring_three)
+    ring_four = [along_z(block, 2 * d) for d, block in ((1, sends[0]), (3, sends[2]), (2, sends[1]))]
+    z_own = own
+    own, send = halved(own, *ring_four)
+    got = along_z(send, 1)
+    query_rows, key_rows, value_rows, out_rows = summed_last(own, got)
 
     parts = zip(one[:-2], two[:-2])
     att, dq, own_kv, near_kv, far_kv = (jnp.concatenate(p, axis=-1) for p in parts)
-    back_near = passed_along(after(near_kv, own_two), -1)
-    back_far = passed_along(after(far_kv, own_two), -2)
+    back_near = passed_along(after(near_kv, z_own), -1)
+    back_far = passed_along(after(far_kv, z_own), -2)
     attn_out = dot(att, out_weight).astype(BF16)
     kv = (own_kv + back_near.astype(F32) + back_far.astype(F32)).astype(BF16)
     tokens_grad = (

time: 100 us -> 106 us (1.060)
  the two profiles are of different devices: /device:TPU:1 before, /device:TPU:24 now
where the time goes in v2:
time: 106 us; the launch traced here: 105 us
  starting transfers between devices  42.9 us (40%)
  waiting for transfers between devices  31.5 us (30%)
  Pallas kernels  23.1 us (22%)
  matrix products  3.65 us (3%)
  local copies, waits for them, and re-layouts  2.38 us (2%)
    ppermute x9, waiting for transfers between devices, ring(): lax.ppermute(blocks[d], AXIS, route_of(functools.partial(plane_step, phas...  20.9 us
    ppermute x4, starting transfers between devices, along_z(): lax.ppermute(block, AXIS, route_of(lambda z, x, y, c: ((z + distance) % 8...  20.4 us
    pallas_call x2, Pallas kernels, attention(): pl.pallas_call(attention_kernel, grid=(steps,), out_shape=(struct(ROWS, Q...  15 us
    ppermute x9, starting transfers between devices, ring(): lax.ppermute(blocks[d], AXIS, route_of(functools.partial(plane_step, phas...  12.9 us
    ppermute x4, starting transfers between devices, passed_along(): return lax.ppermute(block, AXIS, route)  8.96 us
    ppermute x4, waiting for transfers between devices, passed_along(): return lax.ppermute(block, AXIS, route)  6.68 us
    pallas_call x1, Pallas kernels, early(): pl.pallas_call(early_kernel, grid=(STEPS,), out_shape=(jax.ShapeDtypeStru...  4.51 us
    ppermute x4, waiting for transfers between devices, along_z(): lax.ppermute(block, AXIS, route_of(lambda z, x, y, c: ((z + distance) % 8...  3.85 us
  transfers between devices with their start and end apart: 19, of which 10 were waited for; matrix products, arithmetic and copies ran while one was open for 1% of the time, Pallas kernels for 10%

profile of v2, /device:TPU:24, one launch (start us, length us, event | category | flops | bytes accessed | tf_op | source)
XLA Modules:
  0.0 104.6 jit_solution(13914152635716380715)
XLA Ops:
  0.6 1.9 %collective-permute-start.1 = (bf16[128,1024]{1,0:T(8,128)(2,1)}, bf16[128,1024]{1,0:T(8,128)(2,1)S(1)}, u32[]{:S(2)}, u32[]{:S(2)}) collective-permute-start(bf16[128,1024]{1,0:T(8,128)(2,1)} %own_ref.3), channel_id=1, source_target_pairs={{0,1},{1,2},{2,3},{3,4},{4,5},{5,6},{6,7},{7,8},{8,9},{9,10},{10,1... | collective-permute-start | bytes 786440 | tf_op jit(solution)/shard_map/ppermute | solution.py:70
  2.6 3.1 %collective-permute-start = (bf16[128,1024]{1,0:T(8,128)(2,1)}, bf16[128,1024]{1,0:T(8,128)(2,1)S(1)}, u32[]{:S(2)}, u32[]{:S(2)}) collective-permute-start(bf16[128,1024]{1,0:T(8,128)(2,1)} %own_ref.3), channel_id=1, source_target_pairs={{0,2},{1,3},{2,4},{3,5},{4,6},{5,7},{6,8},{7,9},{8,10},{9,11},{10,... | collective-permute-start | bytes 786440 | tf_op jit(solution)/shard_map/ppermute | solution.py:70
  7.7 4.5 %early.1 = (bf16[128,1024]{1,0:T(8,128)(2,1)S(1)}, bf16[128,1024]{1,0:T(8,128)(2,1)S(1)}, bf16[2,512,256]{2,1,0:T(8,128)(2,1)S(1)}) custom-call(s32[5]{0:T(128)S(1)} %stack.23.place, bf16[128,1024]{1,0:T(8,128)(2,1)S(1)} %copy-done, bf16[128,1024]{1,0:T(8,128)(2,1)S(1)} %copy-done.2, bf16[1024,1024]{1,0:T(8,128)(2,1)} %wq_ref.1, bf16[1024,1024]{1,0:T(8,128)(2,1)} %wo_ref.1), custom_call_target="tpu_custom_call" | custom-call | tf_op jit(solution)/shard_map/early/pallas_call | solution.py:115
  12.2 1.7 %collective-permute-done.a_ref.far_ref = bf16[128,1024]{1,0:T(8,128)(2,1)S(1)} collective-permute-done((bf16[128,1024]{1,0:T(8,128)(2,1)}, bf16[128,1024]{1,0:T(8,128)(2,1)S(1)}, u32[]{:S(2)}, u32[]{:S(2)}) %collective-permute-start) | collective-permute-done | bytes 262176 | tf_op jit(solution)/shard_map/ppermute | solution.py:70
  15.1 10.9 %attention.2 = (bf16[128,768]{1,0:T(8,128)(2,1)S(1)}, bf16[128,768]{1,0:T(8,128)(2,1)S(1)}, f32[2,128,384]{2,1,0:T(8,128)S(1)}, bf16[2,128,384]{2,1,0:T(8,128)(2...) custom-call(s32[5]{0:T(128)S(1)} %stack.23.place, ...), custom_call_target="tpu_custom_call" | custom-call | flops 1000 | bytes 1000 | tf_op jit(solution)/shard_map/attention/pallas_call | solution.py:253
  26.2 4.1 %attention.3 = (bf16[128,256]{1,0:T(8,128)(2,1)S(1)}, bf16[128,256]{1,0:T(8,128)(2,1)S(1)}, f32[2,128,128]{2,1,0:T(8,128)S(1)}, bf16[2,128,128]{2,1,0:T(8,128)(2...) custom-call(s32[5]{0:T(128)S(1)} %stack.23.place, ...), custom_call_target="tpu_custom_call" | custom-call | flops 1000 | bytes 1000 | tf_op jit(solution)/shard_map/attention/pallas_call | solution.py:253
  32.0 1.6 %collective-permute-start.3 = (bf16[128,2304]{1,0:T(8,128)(2,1)S(1)}, bf16[128,2304]{1,0:T(8,128)(2,1)S(1)}, u32[]{:S(2)}, u32[]{:S(2)}) collective-permute-start(bf16[128,2304]{1,0:T(8,128)(2,1)S(1)} %get-tuple-element.70), channel_id=1, source_target_pairs={{0,8},{1,3},{2,10},{3,5},{4,12},{5,7},{6,14},{7,1},{8,16},{9,11},{... | collective-permute-start | bytes 1769480 | tf_op jit(solution)/shard_map/ppermute | solution.py:56
  33.6 1.7 %collective-permute-start.4 = (bf16[128,2304]{1,0:T(8,128)(2,1)S(1)}, bf16[128,2304]{1,0:T(8,128)(2,1)S(1)}, u32[]{:S(2)}, u32[]{:S(2)}) collective-permute-start(bf16[128,2304]{1,0:T(8,128)(2,1)S(1)} %get-tuple-element.71), channel_id=1, source_target_pairs={{0,24},{1,7},{2,26},{3,1},{4,28},{5,3},{6,30},{7,5},{8,0},{9,15},{... | collective-permute-start | bytes 1769480 | tf_op jit(solution)/shard_map/ppermute | solution.py:56
  35.3 1.8 %collective-permute-start.5 = (bf16[128,2304]{1,0:T(8,128)(2,1)S(1)}, bf16[128,2304]{1,0:T(8,128)(2,1)S(1)}, u32[]{:S(2)}, u32[]{:S(2)}) collective-permute-start(bf16[128,2304]{1,0:T(8,128)(2,1)S(1)} %get-tuple-element.72), channel_id=1, source_target_pairs={{0,16},{1,5},{2,18},{3,7},{4,20},{5,1},{6,22},{7,3},{8,24},{9,13},... | collective-permute-start | bytes 1769480 | tf_op jit(solution)/shard_map/ppermute | solution.py:56
  37.3 5.9 %collective-permute-done.3.refs_1_ = bf16[128,2304]{1,0:T(8,128)(2,1)S(1)} collective-permute-done((bf16[128,2304]{1,0:T(8,128)(2,1)S(1)}, bf16[128,2304]{1,0:T(8,128)(2,1)S(1)}, u32[]{:S(2)}, u32[]{:S(2)}) %collective-permute-start.3) | collective-permute-done | bytes 589856 | tf_op jit(solution)/shard_map/ppermute | solution.py:56
  43.4 3.0 %collective-permute-start.8 = (bf16[128,768]{1,0:T(8,128)(2,1)S(1)}, bf16[128,768]{1,0:T(8,128)(2,1)S(1)}, u32[]{:S(2)}, u32[]{:S(2)}) collective-permute-start(bf16[128,768]{1,0:T(8,128)(2,1)S(1)} %get-tuple-element.79), channel_id=1, source_target_pairs={{0,24},{1,7},{2,26},{3,1},{4,28},{5,3},{6,30},{7,5},{8,0},{9,15},{... | collective-permute-start | bytes 589832 | tf_op jit(solution)/shard_map/ppermute | solution.py:56
  47.0 2.0 %collective-permute-done.4.refs_2_ = bf16[128,2304]{1,0:T(8,128)(2,1)S(1)} collective-permute-done((bf16[128,2304]{1,0:T(8,128)(2,1)S(1)}, bf16[128,2304]{1,0:T(8,128)(2,1)S(1)}, u32[]{:S(2)}, u32[]{:S(2)}) %collective-permute-start.4) | collective-permute-done | bytes 589856 | tf_op jit(solution)/shard_map/ppermute | solution.py:56
  50.5 2.0 %collective-permute-done.7.refs_5_ = bf16[128,768]{1,0:T(8,128)(2,1)S(1)} collective-permute-done((bf16[128,768]{1,0:T(8,128)(2,1)S(1)}, bf16[128,768]{1,0:T(8,128)(2,1)S(1)}, u32[]{:S(2)}, u32[]{:S(2)}) %collective-permute-start.7) | collective-permute-done | bytes 196640 | tf_op jit(solution)/shard_map/ppermute | solution.py:56
  52.5 2.1 %collective-permute-done.9.refs_7_ = bf16[128,768]{1,0:T(8,128)(2,1)S(1)} collective-permute-done((bf16[128,768]{1,0:T(8,128)(2,1)S(1)}, bf16[128,768]{1,0:T(8,128)(2,1)S(1)}, u32[]{:S(2)}, u32[]{:S(2)}) %collective-permute-start.9) | collective-permute-done | bytes 196640 | tf_op jit(solution)/shard_map/ppermute | solution.py:56
  55.0 2.4 %collective-permute-start.10 = (bf16[32,3072]{1,0:T(8,128)(2,1)S(1)}, bf16[32,3072]{1,0:T(8,128)(2,1)S(1)}, u32[]{:S(2)}, u32[]{:S(2)}) collective-permute-start(bf16[32,3072]{1,0:T(8,128)(2,1)S(1)} %get-tuple-element.83), channel_id=1, source_target_pairs={{0,2},{1,9},{2,4},{3,11},{4,6},{5,13},{6,0},{7,15},{8,10},{9,17},{... | collective-permute-start | bytes 589832 | tf_op jit(solution)/shard_map/ppermute | solution.py:56
  58.9 1.8 %collective-permute-done.10.refs_1_ = bf16[32,3072]{1,0:T(8,128)(2,1)S(1)} collective-permute-done((bf16[32,3072]{1,0:T(8,128)(2,1)S(1)}, bf16[32,3072]{1,0:T(8,128)(2,1)S(1)}, u32[]{:S(2)}, u32[]{:S(2)}) %collective-permute-start.10) | collective-permute-done | bytes 196640 | tf_op jit(solution)/shard_map/ppermute | solution.py:56
  60.7 5.6 %collective-permute-done.11.refs_2_ = bf16[32,3072]{1,0:T(8,128)(2,1)S(1)} collective-permute-done((bf16[32,3072]{1,0:T(8,128)(2,1)S(1)}, bf16[32,3072]{1,0:T(8,128)(2,1)S(1)}, u32[]{:S(2)}, u32[]{:S(2)}) %collective-permute-start.11) | collective-permute-done | bytes 196640 | tf_op jit(solution)/shard_map/ppermute | solution.py:56
  66.4 10.6 %collective-permute-start.15 = (bf16[8,3072]{1,0:T(8,128)(2,1)S(1)}, bf16[8,3072]{1,0:T(8,128)(2,1)S(1)}, u32[]{:S(2)}, u32[]{:S(2)}) collective-permute-start(bf16[8,3072]{1,0:T(8,128)(2,1)S(1)} %get-tuple-element.91), channel_id=1, source_target_pairs={{0,64},{1,65},{2,66},{3,67},{4,68},{5,69},{6,70},{7,71},{8,72},{9,... | collective-permute-start | bytes 147464 | tf_op jit(solution)/shard_map/ppermute | solution.py:62
  77.1 3.1 %collective-permute-start.16 = (bf16[8,3072]{1,0:T(8,128)(2,1)S(1)}, bf16[8,3072]{1,0:T(8,128)(2,1)S(1)}, u32[]{:S(2)}, u32[]{:S(2)}) collective-permute-start(bf16[8,3072]{1,0:T(8,128)(2,1)S(1)} %get-tuple-element.92), channel_id=1, source_target_pairs={{0,192},{1,193},{2,194},{3,195},{4,196},{5,197},{6,198},{7,199},{8... | collective-permute-start | bytes 147464 | tf_op jit(solution)/shard_map/ppermute | solution.py:62
  80.2 6.6 %collective-permute-start.17 = (bf16[8,3072]{1,0:T(8,128)(2,1)S(1)}, bf16[8,3072]{1,0:T(8,128)(2,1)S(1)}, u32[]{:S(2)}, u32[]{:S(2)}) collective-permute-start(bf16[8,3072]{1,0:T(8,128)(2,1)S(1)} %get-tuple-element.93), channel_id=1, source_target_pairs={{0,128},{1,129},{2,130},{3,131},{4,132},{5,133},{6,134},{7,135},{8... | collective-permute-start | bytes 147464 | tf_op jit(solution)/shard_map/ppermute | solution.py:62
  86.8 2.1 %collective-permute-start.13 = (bf16[2,128,512]{2,1,0:T(8,128)(2,1)S(1)}, bf16[2,128,512]{2,1,0:T(8,128)(2,1)S(1)}, u32[]{:S(2)}, u32[]{:S(2)}) collective-permute-start(bf16[2,128,512]{2,1,0:T(8,128)(2,1)S(1)} %get-tuple-element.87), channel_id=1, source_target_pairs={{1,0},{2,1},{3,2},{4,3},{5,4},{6,5},{7,6},{8,7},{9,8},{10,9},{11,1... | collective-permute-start | bytes 786440 | tf_op jit(solution)/shard_map/ppermute | solution.py:70
  88.9 1.9 %collective-permute-start.14 = (bf16[2,128,512]{2,1,0:T(8,128)(2,1)S(1)}, bf16[2,128,512]{2,1,0:T(8,128)(2,1)S(1)}, u32[]{:S(2)}, u32[]{:S(2)}) collective-permute-start(bf16[2,128,512]{2,1,0:T(8,128)(2,1)S(1)} %get-tuple-element.90), channel_id=1, source_target_pairs={{2,0},{3,1},{4,2},{5,3},{6,4},{7,5},{8,6},{9,7},{10,8},{11,9},{12,... | collective-permute-start | bytes 786440 | tf_op jit(solution)/shard_map/ppermute | solution.py:70
  92.2 3.8 %collective-permute-done.18.got_ref = bf16[4,3072]{1,0:T(4,128)(2,1)S(1)} collective-permute-done((bf16[4,3072]{1,0:T(4,128)(2,1)S(1)}, bf16[4,3072]{1,0:T(4,128)(2,1)S(1)}, u32[]{:S(2)}, u32[]{:S(2)}) %collective-permute-start.18) | collective-permute-done | bytes 24608 | tf_op jit(solution)/shard_map/ppermute | solution.py:62
  96.6 5.0 %collective-permute-done.14 = bf16[2,128,512]{2,1,0:T(8,128)(2,1)S(1)} collective-permute-done((bf16[2,128,512]{2,1,0:T(8,128)(2,1)S(1)}, bf16[2,128,512]{2,1,0:T(8,128)(2,1)S(1)}, u32[]{:S(2)}, u32[]{:S(2)}) %collective-permute-start.14) | collective-permute-done | bytes 262176 | tf_op jit(solution)/shard_map/ppermute | solution.py:70
  (45 shorter events, 14.4 us)
Async XLA Ops:
  0.6 11.6 %collective-permute-start.1 = (bf16[128,1024]{1,0:T(8,128)(2,1)}, bf16[128,1024]{1,0:T(8,128)(2,1)S(1)}, u32[]{:S(2)}, u32[]{:S(2)}) collective-permute-start(bf16[128,1024]{1,0:T(8,128)(2,1)} %own_ref.3), channel_id=1, source_target_pairs={{0,1},{1,2},{2,3},{3,4},{4,5},{5,6},{6,7},{7,8},{8,9},{9,10},{10,1... | collective-permute-start | bytes 786440 | tf_op jit(solution)/shard_map/ppermute | solution.py:70
  2.6 11.3 %collective-permute-start = (bf16[128,1024]{1,0:T(8,128)(2,1)}, bf16[128,1024]{1,0:T(8,128)(2,1)S(1)}, u32[]{:S(2)}, u32[]{:S(2)}) collective-permute-start(bf16[128,1024]{1,0:T(8,128)(2,1)} %own_ref.3), channel_id=1, source_target_pairs={{0,2},{1,3},{2,4},{3,5},{4,6},{5,7},{6,8},{7,9},{8,10},{9,11},{10,... | collective-permute-start | bytes 786440 | tf_op jit(solution)/shard_map/ppermute | solution.py:70
  7.7 7.4 %copy-start.1 = (bf16[128,1024]{1,0:T(8,128)(2,1)S(1)}, bf16[128,1024]{1,0:T(8,128)(2,1)}, u32[]{:S(2)}) copy-start(bf16[128,1024]{1,0:T(8,128)(2,1)} %own_ref.3) | copy-start | bytes 786436
  26.0 4.8 %collective-permute-start.2 = (bf16[512,2304]{1,0:T(8,128)(2,1)S(1)}, bf16[512,2304]{1,0:T(8,128)(2,1)S(1)}, u32[]{:S(2)}, u32[]{:S(2)}) collective-permute-start(bf16[512,2304]{1,0:T(8,128)(2,1)S(1)} %get-tuple-element.66), channel_id=1, source_target_pairs={{0,1},{1,0},{2,3},{3,2},{4,5},{5,4},{6,7},{7,6},{8,9},{9,8},{10,11... | collective-permute-start | bytes 7077896 | tf_op jit(solution)/shard_map/ppermute | solution.py:45
  30.4 6.7 %collective-permute-start.6 = (bf16[512,768]{1,0:T(8,128)(2,1)S(1)}, bf16[512,768]{1,0:T(8,128)(2,1)S(1)}, u32[]{:S(2)}, u32[]{:S(2)}) collective-permute-start(bf16[512,768]{1,0:T(8,128)(2,1)S(1)} %get-tuple-element.73), channel_id=1, source_target_pairs={{0,1},{1,0},{2,3},{3,2},{4,5},{5,4},{6,7},{7,6},{8,9},{9,8},{10,11... | collective-permute-start | bytes 2359304 | tf_op jit(solution)/shard_map/ppermute | solution.py:45
  32.0 11.2 %collective-permute-start.3 = (bf16[128,2304]{1,0:T(8,128)(2,1)S(1)}, bf16[128,2304]{1,0:T(8,128)(2,1)S(1)}, u32[]{:S(2)}, u32[]{:S(2)}) collective-permute-start(bf16[128,2304]{1,0:T(8,128)(2,1)S(1)} %get-tuple-element.70), channel_id=1, source_target_pairs={{0,8},{1,3},{2,10},{3,5},{4,12},{5,7},{6,14},{7,1},{8,16},{9,11},{... | collective-permute-start | bytes 1769480 | tf_op jit(solution)/shard_map/ppermute | solution.py:56
  33.6 15.5 %collective-permute-start.4 = (bf16[128,2304]{1,0:T(8,128)(2,1)S(1)}, bf16[128,2304]{1,0:T(8,128)(2,1)S(1)}, u32[]{:S(2)}, u32[]{:S(2)}) collective-permute-start(bf16[128,2304]{1,0:T(8,128)(2,1)S(1)} %get-tuple-element.71), channel_id=1, source_target_pairs={{0,24},{1,7},{2,26},{3,1},{4,28},{5,3},{6,30},{7,5},{8,0},{9,15},{... | collective-permute-start | bytes 1769480 | tf_op jit(solution)/shard_map/ppermute | solution.py:56
  35.3 15.2 %collective-permute-start.5 = (bf16[128,2304]{1,0:T(8,128)(2,1)S(1)}, bf16[128,2304]{1,0:T(8,128)(2,1)S(1)}, u32[]{:S(2)}, u32[]{:S(2)}) collective-permute-start(bf16[128,2304]{1,0:T(8,128)(2,1)S(1)} %get-tuple-element.72), channel_id=1, source_target_pairs={{0,16},{1,5},{2,18},{3,7},{4,20},{5,1},{6,22},{7,3},{8,24},{9,13},... | collective-permute-start | bytes 1769480 | tf_op jit(solution)/shard_map/ppermute | solution.py:56
  43.2 9.3 %collective-permute-start.7 = (bf16[128,768]{1,0:T(8,128)(2,1)S(1)}, bf16[128,768]{1,0:T(8,128)(2,1)S(1)}, u32[]{:S(2)}, u32[]{:S(2)}) collective-permute-start(bf16[128,768]{1,0:T(8,128)(2,1)S(1)} %get-tuple-element.77), channel_id=1, source_target_pairs={{0,8},{1,3},{2,10},{3,5},{4,12},{5,7},{6,14},{7,1},{8,16},{9,11},{... | collective-permute-start | bytes 589832 | tf_op jit(solution)/shard_map/ppermute | solution.py:56
  43.4 9.1 %collective-permute-start.8 = (bf16[128,768]{1,0:T(8,128)(2,1)S(1)}, bf16[128,768]{1,0:T(8,128)(2,1)S(1)}, u32[]{:S(2)}, u32[]{:S(2)}) collective-permute-start(bf16[128,768]{1,0:T(8,128)(2,1)S(1)} %get-tuple-element.79), channel_id=1, source_target_pairs={{0,24},{1,7},{2,26},{3,1},{4,28},{5,3},{6,30},{7,5},{8,0},{9,15},{... | collective-permute-start | bytes 589832 | tf_op jit(solution)/shard_map/ppermute | solution.py:56
  46.4 8.2 %collective-permute-start.9 = (bf16[128,768]{1,0:T(8,128)(2,1)S(1)}, bf16[128,768]{1,0:T(8,128)(2,1)S(1)}, u32[]{:S(2)}, u32[]{:S(2)}) collective-permute-start(bf16[128,768]{1,0:T(8,128)(2,1)S(1)} %get-tuple-element.81), channel_id=1, source_target_pairs={{0,16},{1,5},{2,18},{3,7},{4,20},{5,1},{6,22},{7,3},{8,24},{9,13},... | collective-permute-start | bytes 589832 | tf_op jit(solution)/shard_map/ppermute | solution.py:56
  55.0 36.0 %copy-start.5 = (bf16[1024,1024]{1,0:T(8,128)(2,1)S(1)}, bf16[1024,1024]{1,0:T(8,128)(2,1)}, u32[]{:S(2)}) copy-start(bf16[1024,1024]{1,0:T(8,128)(2,1)} %wo_ref.1) | copy-start | bytes 6291460
  55.0 5.7 %collective-permute-start.10 = (bf16[32,3072]{1,0:T(8,128)(2,1)S(1)}, bf16[32,3072]{1,0:T(8,128)(2,1)S(1)}, u32[]{:S(2)}, u32[]{:S(2)}) collective-permute-start(bf16[32,3072]{1,0:T(8,128)(2,1)S(1)} %get-tuple-element.83), channel_id=1, source_target_pairs={{0,2},{1,9},{2,4},{3,11},{4,6},{5,13},{6,0},{7,15},{8,10},{9,17},{... | collective-permute-start | bytes 589832 | tf_op jit(solution)/shard_map/ppermute | solution.py:56
  57.3 9.0 %collective-permute-start.11 = (bf16[32,3072]{1,0:T(8,128)(2,1)S(1)}, bf16[32,3072]{1,0:T(8,128)(2,1)S(1)}, u32[]{:S(2)}, u32[]{:S(2)}) collective-permute-start(bf16[32,3072]{1,0:T(8,128)(2,1)S(1)} %get-tuple-element.84), channel_id=1, source_target_pairs={{0,6},{1,25},{2,0},{3,27},{4,2},{5,29},{6,4},{7,31},{8,14},{9,1},{... | collective-permute-start | bytes 589832 | tf_op jit(solution)/shard_map/ppermute | solution.py:56
  57.4 9.0 %collective-permute-start.12 = (bf16[32,3072]{1,0:T(8,128)(2,1)S(1)}, bf16[32,3072]{1,0:T(8,128)(2,1)S(1)}, u32[]{:S(2)}, u32[]{:S(2)}) collective-permute-start(bf16[32,3072]{1,0:T(8,128)(2,1)S(1)} %get-tuple-element.85), channel_id=1, source_target_pairs={{0,4},{1,17},{2,6},{3,19},{4,0},{5,21},{6,2},{7,23},{8,12},{9,25},... | collective-permute-start | bytes 589832 | tf_op jit(solution)/shard_map/ppermute | solution.py:56
  66.4 24.4 %collective-permute-start.15 = (bf16[8,3072]{1,0:T(8,128)(2,1)S(1)}, bf16[8,3072]{1,0:T(8,128)(2,1)S(1)}, u32[]{:S(2)}, u32[]{:S(2)}) collective-permute-start(bf16[8,3072]{1,0:T(8,128)(2,1)S(1)} %get-tuple-element.91), channel_id=1, source_target_pairs={{0,64},{1,65},{2,66},{3,67},{4,68},{5,69},{6,70},{7,71},{8,72},{9,... | collective-permute-start | bytes 147464 | tf_op jit(solution)/shard_map/ppermute | solution.py:62
  77.1 13.8 %collective-permute-start.16 = (bf16[8,3072]{1,0:T(8,128)(2,1)S(1)}, bf16[8,3072]{1,0:T(8,128)(2,1)S(1)}, u32[]{:S(2)}, u32[]{:S(2)}) collective-permute-start(bf16[8,3072]{1,0:T(8,128)(2,1)S(1)} %get-tuple-element.92), channel_id=1, source_target_pairs={{0,192},{1,193},{2,194},{3,195},{4,196},{5,197},{6,198},{7,199},{8... | collective-permute-start | bytes 147464 | tf_op jit(solution)/shard_map/ppermute | solution.py:62
  80.2 10.7 %collective-permute-start.17 = (bf16[8,3072]{1,0:T(8,128)(2,1)S(1)}, bf16[8,3072]{1,0:T(8,128)(2,1)S(1)}, u32[]{:S(2)}, u32[]{:S(2)}) collective-permute-start(bf16[8,3072]{1,0:T(8,128)(2,1)S(1)} %get-tuple-element.93), channel_id=1, source_target_pairs={{0,128},{1,129},{2,130},{3,131},{4,132},{5,133},{6,134},{7,135},{8... | collective-permute-start | bytes 147464 | tf_op jit(solution)/shard_map/ppermute | solution.py:62
  86.8 14.9 %copy-start.3 = (bf16[1024,512]{1,0:T(8,128)(2,1)S(1)}, bf16[1024,512]{1,0:T(8,128)(2,1)}, u32[]{:S(2)}) copy-start(bf16[1024,512]{1,0:T(8,128)(2,1)} %wk_ref.3) | copy-start | bytes 3145732
  86.8 9.8 %collective-permute-start.13 = (bf16[2,128,512]{2,1,0:T(8,128)(2,1)S(1)}, bf16[2,128,512]{2,1,0:T(8,128)(2,1)S(1)}, u32[]{:S(2)}, u32[]{:S(2)}) collective-permute-start(bf16[2,128,512]{2,1,0:T(8,128)(2,1)S(1)} %get-tuple-element.87), channel_id=1, source_target_pairs={{1,0},{2,1},{3,2},{4,3},{5,4},{6,5},{7,6},{8,7},{9,8},{10,9},{11,1... | collective-permute-start | bytes 786440 | tf_op jit(solution)/shard_map/ppermute | solution.py:70
  88.9 12.7 %collective-permute-start.14 = (bf16[2,128,512]{2,1,0:T(8,128)(2,1)S(1)}, bf16[2,128,512]{2,1,0:T(8,128)(2,1)S(1)}, u32[]{:S(2)}, u32[]{:S(2)}) collective-permute-start(bf16[2,128,512]{2,1,0:T(8,128)(2,1)S(1)} %get-tuple-element.90), channel_id=1, source_target_pairs={{2,0},{3,1},{4,2},{5,3},{6,4},{7,5},{8,6},{9,7},{10,8},{11,9},{12,... | collective-permute-start | bytes 786440 | tf_op jit(solution)/shard_map/ppermute | solution.py:70
  90.9 5.1 %collective-permute-start.18 = (bf16[4,3072]{1,0:T(4,128)(2,1)S(1)}, bf16[4,3072]{1,0:T(4,128)(2,1)S(1)}, u32[]{:S(2)}, u32[]{:S(2)}) collective-permute-start(bf16[4,3072]{1,0:T(4,128)(2,1)S(1)} %get-tuple-element.95), channel_id=1, source_target_pairs={{0,32},{1,33},{2,34},{3,35},{4,36},{5,37},{6,38},{7,39},{8,40},{9,... | collective-permute-start | bytes 73736 | tf_op jit(solution)/shard_map/ppermute | solution.py:62
  92.1 10.0 %copy-start.6 = (bf16[1024,1024]{1,0:T(8,128)(2,1)S(1)}, bf16[1024,1024]{1,0:T(8,128)(2,1)}, u32[]{:S(2)}) copy-start(bf16[1024,1024]{1,0:T(8,128)(2,1)} %wq_ref.1) | copy-start | bytes 6291460
  102.2 1.2 %copy-start.4 = (bf16[1024,512]{1,0:T(8,128)(2,1)S(1)}, bf16[1024,512]{1,0:T(8,128)(2,1)}, u32[]{:S(2)}) copy-start(bf16[1024,512]{1,0:T(8,128)(2,1)} %wv_ref.3) | copy-start | bytes 3145732
  (2 other events, 1.9 us)

commit v3 on v2

--- a/solution.py
+++ b/solution.py
@@ -306,42 +306,38 @@
 
 def folded(*addends):
     rows, cols = addends[0].shape
-    quarter = rows // 4
-    width = GCOLS if rows > 128 else cols
-    return pl.pallas_call(
-        functools.partial(fold_kernel, len(addends), quarter),
-        grid=(cols // width,),
+    return pl.pallas_call(
+        functools.partial(fold_kernel, len(addends), rows // 4),
+        grid=(1,),
         out_shape=tuple(
-            jax.ShapeDtypeStruct((quarter, cols), BF16 if d else F32) for d in range(4)
-        ),
-        in_specs=[pl.BlockSpec((rows, width), lambda i: (0, i))] * len(addends),
-        out_specs=(pl.BlockSpec((quarter, width), lambda i: (0, i)),) * 4,
-        compiler_params=pltpu.CompilerParams(vmem_limit_bytes=12 << 20),
+            jax.ShapeDtypeStruct((rows // 4, cols), BF16 if d else F32) for d in range(4)
+        ),
+        in_specs=[whole(rows, cols)] * len(addends),
+        out_specs=(whole(rows // 4, cols),) * 4,
+        compiler_params=pltpu.CompilerParams(vmem_limit_bytes=20 << 20),
         name="fold",
     )(*addends)
 
 
-def join_kernel(*refs):
-    one, two, outs = refs[:4], refs[4:8], refs[8:]
-    split = one[0].shape[1]
-    for d in range(4):
-        rows = slice(d * 32, (d + 1) * 32)
-        outs[d][:, :split] = cut(one, rows).astype(outs[d].dtype)
-        outs[d][:, split:] = cut(two, rows).astype(outs[d].dtype)
-
-
-def joined(one, two):
-    args = [*one, *two]
-    cols = one[0].shape[1] + two[0].shape[1]
-    return pl.pallas_call(
-        join_kernel,
-        grid=(1,),
-        out_shape=tuple(jax.ShapeDtypeStruct((32, cols), BF16 if d else F32) for d in range(4)),
-        in_specs=[whole(*a.shape) for a in args],
-        out_specs=(whole(32, cols),) * 4,
-        compiler_params=pltpu.CompilerParams(vmem_limit_bytes=16 << 20),
-        name="join",
-    )(*args)
+def place_kernel(count, *refs):
+    fold_kernel(2, 128, *refs[:2], *refs[2 + count :])
+
+
+def folded_into(first, keep, got, wide=()):
+    rows, cols = keep.shape
+    given = pl.BlockSpec((rows, GCOLS), lambda i: (0, i))
+    return pl.pallas_call(
+        functools.partial(place_kernel, len(wide)),
+        grid=(cols // GCOLS,),
+        out_shape=tuple(
+            jax.ShapeDtypeStruct((rows // 4, STEPS * GCOLS), BF16 if d else F32) for d in range(4)
+        ),
+        in_specs=[given, given] + [pl.BlockSpec(memory_space=pl.ANY)] * len(wide),
+        out_specs=(pl.BlockSpec((rows // 4, GCOLS), lambda i: (0, first + i)),) * 4,
+        input_output_aliases={2 + d: d for d in range(len(wide))},
+        compiler_params=pltpu.CompilerParams(vmem_limit_bytes=12 << 20),
+        name="place",
+    )(keep, got, *wide)
 
 
 def halve_kernel(own_ref, a_ref, b_ref, c_ref, keep_ref, send_ref):
@@ -391,53 +387,93 @@
     )(own, got)
 
 
+def middle_kernel(att_ref, dq_ref, wo_ref, wq_ref, out_ref, base_ref):
+    out_ref[...] = dot(att_ref[...], wo_ref[...]).astype(BF16)
+    base_ref[...] = dot(dq_ref[...], wq_ref[...], NT)
+
+
+def middle(att, dq, wo, wq):
+    block = pl.BlockSpec((ROWS, QCOLS), lambda i: (0, i))
+    return pl.pallas_call(
+        middle_kernel,
+        grid=(STEPS,),
+        out_shape=(
+            jax.ShapeDtypeStruct((ROWS, MODEL), BF16),
+            jax.ShapeDtypeStruct((ROWS, MODEL), F32),
+        ),
+        in_specs=[
+            whole(ROWS, MODEL),
+            whole(ROWS, MODEL),
+            pl.BlockSpec((MODEL, QCOLS), lambda i: (0, i)),
+            pl.BlockSpec((QCOLS, MODEL), lambda i: (i, 0)),
+        ],
+        out_specs=(block, block),
+        compiler_params=pltpu.CompilerParams(vmem_limit_bytes=12 << 20),
+        name="middle",
+    )(att, dq, wo, wq)
+
+
+def tail_kernel(base_ref, own_ref, near_ref, far_ref, wk_ref, wv_ref, out_ref):
+    total = base_ref[...]
+    for i, w_ref in enumerate((wk_ref, wv_ref)):
+        grad = own_ref[i] + near_ref[i].astype(F32) + far_ref[i].astype(F32)
+        total = total + dot(grad.astype(BF16), w_ref[...], NT)
+    out_ref[...] = total.astype(BF16)
+
+
+def tail(base, own, near, far, wk, wv):
+    block = pl.BlockSpec((ROWS, QCOLS), lambda i: (0, i))
+    return pl.pallas_call(
+        tail_kernel,
+        grid=(STEPS,),
+        out_shape=jax.ShapeDtypeStruct((ROWS, MODEL), BF16),
+        in_specs=[block, *[whole(2, ROWS, 512)] * 3]
+        + [pl.BlockSpec((QCOLS, 512), lambda i: (i, 0))] * 2,
+        out_specs=block,
+        compiler_params=pltpu.CompilerParams(vmem_limit_bytes=12 << 20),
+        name="tail",
+    )(base, own, near, far, wk, wv)
+
+
 def after(value, *others):
     return lax.optimization_barrier((value, *others))[0]
 
 
 def shards(tokens, query_weight, key_weight, value_matrix, out_weight, out_cotangent):
+    far = passed_along(tokens, 2)
     near = passed_along(tokens, 1)
-    far = passed_along(tokens, 2)
     me = lax.axis_index(AXIS)
     start = jnp.maximum(2 - me, 0) * ROWS
     place = jnp.stack([(me // 8) % 4, (me // 2) % 4, me % 2, me // 32, start]).astype(jnp.int32)
-    q, da, tp = early(place, tokens, out_cotangent, in_hbm(query_weight), in_hbm(out_weight))
+    wq, wk, wv, wo = map(in_hbm, (query_weight, key_weight, value_matrix, out_weight))
+    q, da, tp = early(place, in_hbm(tokens), in_hbm(out_cotangent), wq, wo)
     th = prepared(place, far, near)
 
-    wk, wv = in_hbm(key_weight), in_hbm(value_matrix)
-
     def attend(first, steps, place):
-        return attention(
-            first, steps, place, far, near, tokens, q, da, wk, wv, tp, th
-        )
+        return attention(first, steps, place, far, near, tokens, q, da, wk, wv, tp, th)
 
     one = attend(0, 3, place)
     got_one = to_mate(one[-2])
     two = attend(3, 1, after(place, one[-1]))
     got_two = to_mate(two[-2])
-    own_one, *sends = folded(one[-1], after(got_one, two[-1]))
+    sums = folded_into(0, one[-1], after(got_one, two[-1]))
+    own, *sends = folded_into(3, two[-1], after(got_two, sums[0]), sums)
     ring_one = ring([None, *sends], 0)
-    own_two, *sends = folded(two[-1], after(got_two, own_one))
-    ring_two = ring([None, *(after(s, ring_one[0]) for s in sends)], 0)
-    own, *sends = joined([own_one, *ring_one], [own_two, *ring_two])
-    ring_three = ring([None, *sends], 1)
-    own, *sends = folded(own, *ring_three)
-    ring_four = [along_z(block, 2 * d) for d, block in ((1, sends[0]), (3, sends[2]), (2, sends[1]))]
-    z_own = own
-    own, send = halved(own, *ring_four)
-    got = along_z(send, 1)
-    query_rows, key_rows, value_rows, out_rows = summed_last(own, got)
 
     parts = zip(one[:-2], two[:-2])
     att, dq, own_kv, near_kv, far_kv = (jnp.concatenate(p, axis=-1) for p in parts)
-    back_near = passed_along(after(near_kv, z_own), -1)
-    back_far = passed_along(after(far_kv, z_own), -2)
-    attn_out = dot(att, out_weight).astype(BF16)
-    kv = (own_kv + back_near.astype(F32) + back_far.astype(F32)).astype(BF16)
-    tokens_grad = (
-        dot(dq, query_weight, NT) + dot(kv[0], key_weight, NT) + dot(kv[1], value_matrix, NT)
-    ).astype(BF16)
-
+    back_near = passed_along(after(near_kv, ring_one[0]), -1)
+    back_far = passed_along(after(far_kv, ring_one[0]), -2)
+    attn_out, base = middle(after(att, own), after(dq, own), wo, wq)
+
+    own, *sends = folded(after(own, base), *ring_one)
+    ring_two = ring([None, *sends], 1)
+    own, *sends = folded(own, *ring_two)
+    ring_three = [along_z(sends[d - 1], 2 * d) for d in (1, 3, 2)]
+    own, send = halved(own, *ring_three)
+    got = along_z(send, 1)
+    tokens_grad = tail(base, own_kv, back_near, back_far, wk, wv)
+    query_rows, key_rows, value_rows, out_rows = summed_last(after(own, tokens_grad), got)
     return attn_out, tokens_grad, query_rows, key_rows, value_rows, out_rows.T
 
 

time: 106 us -> 99.2 us (0.936)
  waiting for transfers between devices: 31.5 us -> 20.6 us
  Pallas kernels: 23.1 us -> 31.5 us
  matrix products: 3.65 us -> 0 us
  local copies, waits for them, and re-layouts: 2.38 us -> 0.09 us
  starting transfers between devices: 42.9 us -> 44.2 us
    pallas_call x4 -> x6, Pallas kernels: 1.69 us -> 10.1 us  [the longest x1 4.37 us: middle(): pl.pallas_call(middle_kernel, grid=(STEPS,), out_shape=(jax.ShapeDtypeStr...]
    ppermute x9 -> x6, waiting for transfers between devices: 20.9 us -> 14 us  [ring(): lax.ppermute(blocks[d], AXIS, route_of(functools.partial(plane_step, phas...]
    dot_general x4 -> x0, matrix products: 3.65 us -> none  [dot(): return lax.dot_general(a, b, dims, preferred_element_type=F32)]
    ppermute x9 -> x6, starting transfers between devices: 12.9 us -> 9.27 us  [ring(): lax.ppermute(blocks[d], AXIS, route_of(functools.partial(plane_step, phas...]
    ppermute x4, waiting for transfers between devices: 6.68 us -> 3.57 us  [passed_along(): return lax.ppermute(block, AXIS, route)]
    ppermute x4, starting transfers between devices: 20.4 us -> 23.1 us  [along_z(): lax.ppermute(block, AXIS, route_of(lambda z, x, y, c: ((z + distance) % 8...]
    unnamed x14 -> x2, local copies, waits for them, and re-layouts: 2.29 us -> 0.01 us
    ppermute x4, starting transfers between devices: 8.96 us -> 11.2 us  [passed_along(): return lax.ppermute(block, AXIS, route)]
  transfers between devices with their start and end apart: 19 -> 16, of which waited for: 10 -> 8; matrix products, arithmetic and copies ran while one was open for 1% -> 0% of each run, Pallas kernels for 10% -> 19%
where the time goes in v3:
time: 99.2 us; the launch traced here: 97.5 us
  starting transfers between devices  44.2 us (45%)
  Pallas kernels  31.5 us (32%)
  waiting for transfers between devices  20.6 us (21%)
    ppermute x4, starting transfers between devices, along_z(): lax.ppermute(block, AXIS, route_of(lambda z, x, y, c: ((z + distance) % 8...  23.1 us
    pallas_call x2, Pallas kernels, attention(): pl.pallas_call(attention_kernel, grid=(steps,), out_shape=(struct(ROWS, Q...  15 us
    ppermute x6, waiting for transfers between devices, ring(): lax.ppermute(blocks[d], AXIS, route_of(functools.partial(plane_step, phas...  14 us
    ppermute x4, starting transfers between devices, passed_along(): return lax.ppermute(block, AXIS, route)  11.2 us
    ppermute x6, starting transfers between devices, ring(): lax.ppermute(blocks[d], AXIS, route_of(functools.partial(plane_step, phas...  9.27 us
    pallas_call x1, Pallas kernels, early(): pl.pallas_call(early_kernel, grid=(STEPS,), out_shape=(jax.ShapeDtypeStru...  4.55 us
    pallas_call x1, Pallas kernels, middle(): pl.pallas_call(middle_kernel, grid=(STEPS,), out_shape=(jax.ShapeDtypeStr...  4.37 us
    pallas_call x1, Pallas kernels, tail(): pl.pallas_call(tail_kernel, grid=(STEPS,), out_shape=jax.ShapeDtypeStruct...  4.02 us
  transfers between devices with their start and end apart: 16, of which 8 were waited for; matrix products, arithmetic and copies ran while one was open for 0% of the time, Pallas kernels for 19%

profile of v3, /device:TPU:24, one launch (start us, length us, event | category | flops | bytes accessed | tf_op | source)
XLA Modules:
  0.0 97.5 jit_solution(16931281486631114077)
XLA Ops:
  0.6 1.9 %collective-permute-start.1 = (bf16[128,1024]{1,0:T(8,128)(2,1)}, bf16[128,1024]{1,0:T(8,128)(2,1)S(1)}, u32[]{:S(2)}, u32[]{:S(2)}) collective-permute-start(bf16[128,1024]{1,0:T(8,128)(2,1)} %own_ref.3), channel_id=1, source_target_pairs={{0,1},{1,2},{2,3},{3,4},{4,5},{5,6},{6,7},{7,8},{8,9},{9,10},{10,1... | collective-permute-start | bytes 786440 | tf_op jit(solution)/shard_map/ppermute | solution.py:70
  2.6 3.1 %collective-permute-start = (bf16[128,1024]{1,0:T(8,128)(2,1)}, bf16[128,1024]{1,0:T(8,128)(2,1)S(1)}, u32[]{:S(2)}, u32[]{:S(2)}) collective-permute-start(bf16[128,1024]{1,0:T(8,128)(2,1)} %own_ref.3), channel_id=1, source_target_pairs={{0,2},{1,3},{2,4},{3,5},{4,6},{5,7},{6,8},{7,9},{8,10},{9,11},{10,... | collective-permute-start | bytes 786440 | tf_op jit(solution)/shard_map/ppermute | solution.py:70
  5.8 4.5 %early.1 = (bf16[128,1024]{1,0:T(8,128)(2,1)S(1)}, bf16[128,1024]{1,0:T(8,128)(2,1)S(1)}, bf16[2,512,256]{2,1,0:T(8,128)(2,1)S(1)}) custom-call(s32[5]{0:T(128)S(1)} %stack.23.place, bf16[128,1024]{1,0:T(8,128)(2,1)} %own_ref.3, bf16[128,1024]{1,0:T(8,128)(2,1)} %cot_ref.1, bf16[1024,1024]{1,0:T(8,128)(2,1)} %wq_ref.3, bf16[1024,1024]{1,0:T(8,128)(2,1)} %wo_ref.3), custom_call_target="tpu_custom_call" | custom-call | tf_op jit(solution)/shard_map/early/pallas_call | solution.py:115
  10.3 3.6 %collective-permute-done.a_ref.far_ref = bf16[128,1024]{1,0:T(8,128)(2,1)S(1)} collective-permute-done((bf16[128,1024]{1,0:T(8,128)(2,1)}, bf16[128,1024]{1,0:T(8,128)(2,1)S(1)}, u32[]{:S(2)}, u32[]{:S(2)}) %collective-permute-start) | collective-permute-done | bytes 262176 | tf_op jit(solution)/shard_map/ppermute | solution.py:70
  13.9 1.2 %prep.1.th_ref = bf16[2,512,256]{2,1,0:T(8,128)(2,1)S(1)} custom-call(s32[5]{0:T(128)S(1)} %stack.23.place, bf16[128,1024]{1,0:T(8,128)(2,1)S(1)} %collective-permute-done.a_ref.far_ref, bf16[128,1024]{1,0:T(8,128)(2,1)S(1)} %collective-permute-done.1.b_ref.near_ref), custom_call_target="tpu_custom_call" | custom-call | tf_op jit(solution)/shard_map/prep/pallas_call | solution.py:146
  15.1 10.9 %attention.2 = (bf16[128,768]{1,0:T(8,128)(2,1)S(1)}, bf16[128,768]{1,0:T(8,128)(2,1)S(1)}, f32[2,128,384]{2,1,0:T(8,128)S(1)}, bf16[2,128,384]{2,1,0:T(8,128)(2...) custom-call(s32[5]{0:T(128)S(1)} %stack.23.place, ...), custom_call_target="tpu_custom_call" | custom-call | flops 1000 | bytes 1000 | tf_op jit(solution)/shard_map/attention/pallas_call | solution.py:253
  26.2 4.1 %attention.3 = (bf16[128,256]{1,0:T(8,128)(2,1)S(1)}, bf16[128,256]{1,0:T(8,128)(2,1)S(1)}, f32[2,128,128]{2,1,0:T(8,128)S(1)}, bf16[2,128,128]{2,1,0:T(8,128)(2...) custom-call(s32[5]{0:T(128)S(1)} %stack.23.place, ...), custom_call_target="tpu_custom_call" | custom-call | flops 1000 | bytes 1000 | tf_op jit(solution)/shard_map/attention/pallas_call | solution.py:253
  30.9 1.1 %place.2 = (f32[128,3072]{1,0:T(8,128)S(1)}, bf16[128,3072]{1,0:T(8,128)(2,1)S(1)}, bf16[128,3072]{1,0:T(8,128)(2,1)S(1)}, bf16[128,3072]{1,0:T(8,128)(2,1)S(1)}) custom-call(bf16[512,2304]{1,0:T(8,128)(2,1)S(1)} %get-tuple-element.60.refs_0_, bf16[512,2304]{1,0:T(8,128)(2,1)S(1)} %collective-permute-done.3.refs_1_), custom_call_target="tpu_custom_call" | custom-call | tf_op jit(solution)/shard_map/place/pallas_call | solution.py:329
  33.0 1.6 %collective-permute-start.4 = (bf16[128,3072]{1,0:T(8,128)(2,1)S(1)}, bf16[128,3072]{1,0:T(8,128)(2,1)S(1)}, u32[]{:S(2)}, u32[]{:S(2)}) collective-permute-start(bf16[128,3072]{1,0:T(8,128)(2,1)S(1)} %get-tuple-element.83), channel_id=1, source_target_pairs={{0,8},{1,3},{2,10},{3,5},{4,12},{5,7},{6,14},{7,1},{8,16},{9,11},{... | collective-permute-start | bytes 2359304 | tf_op jit(solution)/shard_map/ppermute | solution.py:56
  34.5 1.7 %collective-permute-start.7 = (bf16[128,3072]{1,0:T(8,128)(2,1)S(1)}, bf16[128,3072]{1,0:T(8,128)(2,1)S(1)}, u32[]{:S(2)}, u32[]{:S(2)}) collective-permute-start(bf16[128,3072]{1,0:T(8,128)(2,1)S(1)} %get-tuple-element.89), channel_id=1, source_target_pairs={{0,24},{1,7},{2,26},{3,1},{4,28},{5,3},{6,30},{7,5},{8,0},{9,15},{... | collective-permute-start | bytes 2359304 | tf_op jit(solution)/shard_map/ppermute | solution.py:56
  36.3 1.8 %collective-permute-start.8 = (bf16[128,3072]{1,0:T(8,128)(2,1)S(1)}, bf16[128,3072]{1,0:T(8,128)(2,1)S(1)}, u32[]{:S(2)}, u32[]{:S(2)}) collective-permute-start(bf16[128,3072]{1,0:T(8,128)(2,1)S(1)} %get-tuple-element.90), channel_id=1, source_target_pairs={{0,16},{1,5},{2,18},{3,7},{4,20},{5,1},{6,22},{7,3},{8,24},{9,13},... | collective-permute-start | bytes 2359304 | tf_op jit(solution)/shard_map/ppermute | solution.py:56
  38.1 4.4 %middle.1 = (bf16[128,1024]{1,0:T(8,128)(2,1)}, f32[128,1024]{1,0:T(8,128)S(1)}) custom-call(bf16[128,1024]{1,0:T(8,128)(2,1)S(1)} %get-tuple-element.73.att_ref, bf16[128,1024]{1,0:T(8,128)(2,1)S(1)} %get-tuple-element.76.dq_ref, bf16[1024,1024]{1,0:T(8,128)(2,1)} %wo_ref.3, bf16[1024,1024]{1,0:T(8,128)(2,1)} %wq_ref.3), custom_call_target="tpu_custom_call" | custom-call | tf_op jit(solution)/shard_map/middle/pallas_call | solution.py:397
  42.5 3.7 %collective-permute-done.4.refs_1_ = bf16[128,3072]{1,0:T(8,128)(2,1)S(1)} collective-permute-done((bf16[128,3072]{1,0:T(8,128)(2,1)S(1)}, bf16[128,3072]{1,0:T(8,128)(2,1)S(1)}, u32[]{:S(2)}, u32[]{:S(2)}) %collective-permute-start.4) | collective-permute-done | bytes 786464 | tf_op jit(solution)/shard_map/ppermute | solution.py:56
  46.2 8.0 %collective-permute-done.7.refs_2_ = bf16[128,3072]{1,0:T(8,128)(2,1)S(1)} collective-permute-done((bf16[128,3072]{1,0:T(8,128)(2,1)S(1)}, bf16[128,3072]{1,0:T(8,128)(2,1)S(1)}, u32[]{:S(2)}, u32[]{:S(2)}) %collective-permute-start.7) | collective-permute-done | bytes 786464 | tf_op jit(solution)/shard_map/ppermute | solution.py:56
  54.2 1.3 %collective-permute-done.8.refs_3_ = bf16[128,3072]{1,0:T(8,128)(2,1)S(1)} collective-permute-done((bf16[128,3072]{1,0:T(8,128)(2,1)S(1)}, bf16[128,3072]{1,0:T(8,128)(2,1)S(1)}, u32[]{:S(2)}, u32[]{:S(2)}) %collective-permute-start.8) | collective-permute-done | bytes 786464 | tf_op jit(solution)/shard_map/ppermute | solution.py:56
  55.9 2.4 %collective-permute-start.9 = (bf16[32,3072]{1,0:T(8,128)(2,1)S(1)}, bf16[32,3072]{1,0:T(8,128)(2,1)S(1)}, u32[]{:S(2)}, u32[]{:S(2)}) collective-permute-start(bf16[32,3072]{1,0:T(8,128)(2,1)S(1)} %get-tuple-element.92), channel_id=1, source_target_pairs={{0,2},{1,9},{2,4},{3,11},{4,6},{5,13},{6,0},{7,15},{8,10},{9,17},{... | collective-permute-start | bytes 589832 | tf_op jit(solution)/shard_map/ppermute | solution.py:56
  58.3 1.7 %collective-permute-start.11 = (bf16[32,3072]{1,0:T(8,128)(2,1)S(1)}, bf16[32,3072]{1,0:T(8,128)(2,1)S(1)}, u32[]{:S(2)}, u32[]{:S(2)}) collective-permute-start(bf16[32,3072]{1,0:T(8,128)(2,1)S(1)} %get-tuple-element.94), channel_id=1, source_target_pairs={{0,4},{1,17},{2,6},{3,19},{4,0},{5,21},{6,2},{7,23},{8,12},{9,25},... | collective-permute-start | bytes 589832 | tf_op jit(solution)/shard_map/ppermute | solution.py:56
  60.1 1.9 %collective-permute-start.5 = (bf16[2,128,512]{2,1,0:T(8,128)(2,1)S(1)}, bf16[2,128,512]{2,1,0:T(8,128)(2,1)S(1)}, u32[]{:S(2)}, u32[]{:S(2)}) collective-permute-start(bf16[2,128,512]{2,1,0:T(8,128)(2,1)S(1)} %get-tuple-element.84), channel_id=1, source_target_pairs={{1,0},{2,1},{3,2},{4,3},{5,4},{6,5},{7,6},{8,7},{9,8},{10,9},{11,1... | collective-permute-start | bytes 786440 | tf_op jit(solution)/shard_map/ppermute | solution.py:70
  62.0 4.3 %collective-permute-start.6 = (bf16[2,128,512]{2,1,0:T(8,128)(2,1)S(1)}, bf16[2,128,512]{2,1,0:T(8,128)(2,1)S(1)}, u32[]{:S(2)}, u32[]{:S(2)}) collective-permute-start(bf16[2,128,512]{2,1,0:T(8,128)(2,1)S(1)} %get-tuple-element.87), channel_id=1, source_target_pairs={{2,0},{3,1},{4,2},{5,3},{6,4},{7,5},{8,6},{9,7},{10,8},{11,9},{12,... | collective-permute-start | bytes 786440 | tf_op jit(solution)/shard_map/ppermute | solution.py:70
  67.4 12.9 %collective-permute-start.12 = (bf16[8,3072]{1,0:T(8,128)(2,1)S(1)}, bf16[8,3072]{1,0:T(8,128)(2,1)S(1)}, u32[]{:S(2)}, u32[]{:S(2)}) collective-permute-start(bf16[8,3072]{1,0:T(8,128)(2,1)S(1)} %get-tuple-element.96), channel_id=1, source_target_pairs={{0,64},{1,65},{2,66},{3,67},{4,68},{5,69},{6,70},{7,71},{8,72},{9,... | collective-permute-start | bytes 147464 | tf_op jit(solution)/shard_map/ppermute | solution.py:62
  80.3 3.1 %collective-permute-start.13 = (bf16[8,3072]{1,0:T(8,128)(2,1)S(1)}, bf16[8,3072]{1,0:T(8,128)(2,1)S(1)}, u32[]{:S(2)}, u32[]{:S(2)}) collective-permute-start(bf16[8,3072]{1,0:T(8,128)(2,1)S(1)} %get-tuple-element.97), channel_id=1, source_target_pairs={{0,192},{1,193},{2,194},{3,195},{4,196},{5,197},{6,198},{7,199},{8... | collective-permute-start | bytes 147464 | tf_op jit(solution)/shard_map/ppermute | solution.py:62
  83.4 6.1 %collective-permute-start.14 = (bf16[8,3072]{1,0:T(8,128)(2,1)S(1)}, bf16[8,3072]{1,0:T(8,128)(2,1)S(1)}, u32[]{:S(2)}, u32[]{:S(2)}) collective-permute-start(bf16[8,3072]{1,0:T(8,128)(2,1)S(1)} %get-tuple-element.98), channel_id=1, source_target_pairs={{0,128},{1,129},{2,130},{3,131},{4,132},{5,133},{6,134},{7,135},{8... | collective-permute-start | bytes 147464 | tf_op jit(solution)/shard_map/ppermute | solution.py:62
  89.6 2.1 %collective-permute-done.14.c_ref = bf16[8,3072]{1,0:T(8,128)(2,1)S(1)} collective-permute-done((bf16[8,3072]{1,0:T(8,128)(2,1)S(1)}, bf16[8,3072]{1,0:T(8,128)(2,1)S(1)}, u32[]{:S(2)}, u32[]{:S(2)}) %collective-permute-start.14) | collective-permute-done | bytes 49184 | tf_op jit(solution)/shard_map/ppermute | solution.py:62
  92.7 4.0 %tail.1 = bf16[128,1024]{1,0:T(8,128)(2,1)} custom-call(f32[128,1024]{1,0:T(8,128)S(1)} %get-tuple-element.78.base_ref, f32[2,128,512]{2,1,0:T(8,128)S(1)} %pad_maximum_fusion.own_ref, bf16[2,128,512]{2,1,0:T(8,128)(2,1)S(1)} %collective-permute-done.5.near_ref, bf16[2,128,512]{2,1,0:T(8,128)(2,1)S(1)} %collective-permute-done.6.far_ref, ...), custom_call_target="tpu_custom_call" | custom-call | tf_op jit(solution)/shard_map/tail/pallas_call | solution.py:426
  (26 shorter events, 5.0 us)
Async XLA Ops:
  0.6 9.7 %collective-permute-start.1 = (bf16[128,1024]{1,0:T(8,128)(2,1)}, bf16[128,1024]{1,0:T(8,128)(2,1)S(1)}, u32[]{:S(2)}, u32[]{:S(2)}) collective-permute-start(bf16[128,1024]{1,0:T(8,128)(2,1)} %own_ref.3), channel_id=1, source_target_pairs={{0,1},{1,2},{2,3},{3,4},{4,5},{5,6},{6,7},{7,8},{8,9},{9,10},{10,1... | collective-permute-start | bytes 786440 | tf_op jit(solution)/shard_map/ppermute | solution.py:70
  2.6 11.3 %collective-permute-start = (bf16[128,1024]{1,0:T(8,128)(2,1)}, bf16[128,1024]{1,0:T(8,128)(2,1)S(1)}, u32[]{:S(2)}, u32[]{:S(2)}) collective-permute-start(bf16[128,1024]{1,0:T(8,128)(2,1)} %own_ref.3), channel_id=1, source_target_pairs={{0,2},{1,3},{2,4},{3,5},{4,6},{5,7},{6,8},{7,9},{8,10},{9,11},{10,... | collective-permute-start | bytes 786440 | tf_op jit(solution)/shard_map/ppermute | solution.py:70
  5.8 9.3 %copy-start = (bf16[128,1024]{1,0:T(8,128)(2,1)S(1)}, bf16[128,1024]{1,0:T(8,128)(2,1)}, u32[]{:S(2)}) copy-start(bf16[128,1024]{1,0:T(8,128)(2,1)} %own_ref.3) | copy-start | bytes 786436
  26.0 4.8 %collective-permute-start.3 = (bf16[512,2304]{1,0:T(8,128)(2,1)S(1)}, bf16[512,2304]{1,0:T(8,128)(2,1)S(1)}, u32[]{:S(2)}, u32[]{:S(2)}) collective-permute-start(bf16[512,2304]{1,0:T(8,128)(2,1)S(1)} %get-tuple-element.65), channel_id=1, source_target_pairs={{0,1},{1,0},{2,3},{3,2},{4,5},{5,4},{6,7},{7,6},{8,9},{9,8},{10,11... | collective-permute-start | bytes 7077896 | tf_op jit(solution)/shard_map/ppermute | solution.py:45
  30.4 2.4 %collective-permute-start.2 = (bf16[512,768]{1,0:T(8,128)(2,1)S(1)}, bf16[512,768]{1,0:T(8,128)(2,1)S(1)}, u32[]{:S(2)}, u32[]{:S(2)}) collective-permute-start(bf16[512,768]{1,0:T(8,128)(2,1)S(1)} %get-tuple-element.64), channel_id=1, source_target_pairs={{0,1},{1,0},{2,3},{3,2},{4,5},{5,4},{6,7},{7,6},{8,9},{9,8},{10,11... | collective-permute-start | bytes 2359304 | tf_op jit(solution)/shard_map/ppermute | solution.py:45
  33.0 13.3 %collective-permute-start.4 = (bf16[128,3072]{1,0:T(8,128)(2,1)S(1)}, bf16[128,3072]{1,0:T(8,128)(2,1)S(1)}, u32[]{:S(2)}, u32[]{:S(2)}) collective-permute-start(bf16[128,3072]{1,0:T(8,128)(2,1)S(1)} %get-tuple-element.83), channel_id=1, source_target_pairs={{0,8},{1,3},{2,10},{3,5},{4,12},{5,7},{6,14},{7,1},{8,16},{9,11},{... | collective-permute-start | bytes 2359304 | tf_op jit(solution)/shard_map/ppermute | solution.py:56
  34.5 19.7 %collective-permute-start.7 = (bf16[128,3072]{1,0:T(8,128)(2,1)S(1)}, bf16[128,3072]{1,0:T(8,128)(2,1)S(1)}, u32[]{:S(2)}, u32[]{:S(2)}) collective-permute-start(bf16[128,3072]{1,0:T(8,128)(2,1)S(1)} %get-tuple-element.89), channel_id=1, source_target_pairs={{0,24},{1,7},{2,26},{3,1},{4,28},{5,3},{6,30},{7,5},{8,0},{9,15},{... | collective-permute-start | bytes 2359304 | tf_op jit(solution)/shard_map/ppermute | solution.py:56
  36.3 19.3 %collective-permute-start.8 = (bf16[128,3072]{1,0:T(8,128)(2,1)S(1)}, bf16[128,3072]{1,0:T(8,128)(2,1)S(1)}, u32[]{:S(2)}, u32[]{:S(2)}) collective-permute-start(bf16[128,3072]{1,0:T(8,128)(2,1)S(1)} %get-tuple-element.90), channel_id=1, source_target_pairs={{0,16},{1,5},{2,18},{3,7},{4,20},{5,1},{6,22},{7,3},{8,24},{9,13},... | collective-permute-start | bytes 2359304 | tf_op jit(solution)/shard_map/ppermute | solution.py:56
  55.9 10.4 %collective-permute-start.9 = (bf16[32,3072]{1,0:T(8,128)(2,1)S(1)}, bf16[32,3072]{1,0:T(8,128)(2,1)S(1)}, u32[]{:S(2)}, u32[]{:S(2)}) collective-permute-start(bf16[32,3072]{1,0:T(8,128)(2,1)S(1)} %get-tuple-element.92), channel_id=1, source_target_pairs={{0,2},{1,9},{2,4},{3,11},{4,6},{5,13},{6,0},{7,15},{8,10},{9,17},{... | collective-permute-start | bytes 589832 | tf_op jit(solution)/shard_map/ppermute | solution.py:56
  58.3 9.0 %collective-permute-start.10 = (bf16[32,3072]{1,0:T(8,128)(2,1)S(1)}, bf16[32,3072]{1,0:T(8,128)(2,1)S(1)}, u32[]{:S(2)}, u32[]{:S(2)}) collective-permute-start(bf16[32,3072]{1,0:T(8,128)(2,1)S(1)} %get-tuple-element.93), channel_id=1, source_target_pairs={{0,6},{1,25},{2,0},{3,27},{4,2},{5,29},{6,4},{7,31},{8,14},{9,1},{... | collective-permute-start | bytes 589832 | tf_op jit(solution)/shard_map/ppermute | solution.py:56
  58.3 9.0 %collective-permute-start.11 = (bf16[32,3072]{1,0:T(8,128)(2,1)S(1)}, bf16[32,3072]{1,0:T(8,128)(2,1)S(1)}, u32[]{:S(2)}, u32[]{:S(2)}) collective-permute-start(bf16[32,3072]{1,0:T(8,128)(2,1)S(1)} %get-tuple-element.94), channel_id=1, source_target_pairs={{0,4},{1,17},{2,6},{3,19},{4,0},{5,21},{6,2},{7,23},{8,12},{9,25},... | collective-permute-start | bytes 589832 | tf_op jit(solution)/shard_map/ppermute | solution.py:56
  60.1 32.6 %collective-permute-start.5 = (bf16[2,128,512]{2,1,0:T(8,128)(2,1)S(1)}, bf16[2,128,512]{2,1,0:T(8,128)(2,1)S(1)}, u32[]{:S(2)}, u32[]{:S(2)}) collective-permute-start(bf16[2,128,512]{2,1,0:T(8,128)(2,1)S(1)} %get-tuple-element.84), channel_id=1, source_target_pairs={{1,0},{2,1},{3,2},{4,3},{5,4},{6,5},{7,6},{8,7},{9,8},{10,9},{11,1... | collective-permute-start | bytes 786440 | tf_op jit(solution)/shard_map/ppermute | solution.py:70
  62.0 30.7 %collective-permute-start.6 = (bf16[2,128,512]{2,1,0:T(8,128)(2,1)S(1)}, bf16[2,128,512]{2,1,0:T(8,128)(2,1)S(1)}, u32[]{:S(2)}, u32[]{:S(2)}) collective-permute-start(bf16[2,128,512]{2,1,0:T(8,128)(2,1)S(1)} %get-tuple-element.87), channel_id=1, source_target_pairs={{2,0},{3,1},{4,2},{5,3},{6,4},{7,5},{8,6},{9,7},{10,8},{11,9},{12,... | collective-permute-start | bytes 786440 | tf_op jit(solution)/shard_map/ppermute | solution.py:70
  67.4 22.2 %collective-permute-start.12 = (bf16[8,3072]{1,0:T(8,128)(2,1)S(1)}, bf16[8,3072]{1,0:T(8,128)(2,1)S(1)}, u32[]{:S(2)}, u32[]{:S(2)}) collective-permute-start(bf16[8,3072]{1,0:T(8,128)(2,1)S(1)} %get-tuple-element.96), channel_id=1, source_target_pairs={{0,64},{1,65},{2,66},{3,67},{4,68},{5,69},{6,70},{7,71},{8,72},{9,... | collective-permute-start | bytes 147464 | tf_op jit(solution)/shard_map/ppermute | solution.py:62
  80.3 9.3 %collective-permute-start.13 = (bf16[8,3072]{1,0:T(8,128)(2,1)S(1)}, bf16[8,3072]{1,0:T(8,128)(2,1)S(1)}, u32[]{:S(2)}, u32[]{:S(2)}) collective-permute-start(bf16[8,3072]{1,0:T(8,128)(2,1)S(1)} %get-tuple-element.97), channel_id=1, source_target_pairs={{0,192},{1,193},{2,194},{3,195},{4,196},{5,197},{6,198},{7,199},{8... | collective-permute-start | bytes 147464 | tf_op jit(solution)/shard_map/ppermute | solution.py:62
  83.4 8.3 %collective-permute-start.14 = (bf16[8,3072]{1,0:T(8,128)(2,1)S(1)}, bf16[8,3072]{1,0:T(8,128)(2,1)S(1)}, u32[]{:S(2)}, u32[]{:S(2)}) collective-permute-start(bf16[8,3072]{1,0:T(8,128)(2,1)S(1)} %get-tuple-element.98), channel_id=1, source_target_pairs={{0,128},{1,129},{2,130},{3,131},{4,132},{5,133},{6,134},{7,135},{8... | collective-permute-start | bytes 147464 | tf_op jit(solution)/shard_map/ppermute | solution.py:62
  91.7 5.1 %collective-permute-start.15 = (bf16[4,3072]{1,0:T(4,128)(2,1)S(1)}, bf16[4,3072]{1,0:T(4,128)(2,1)S(1)}, u32[]{:S(2)}, u32[]{:S(2)}) collective-permute-start(bf16[4,3072]{1,0:T(4,128)(2,1)S(1)} %get-tuple-element.101), channel_id=1, source_target_pairs={{0,32},{1,33},{2,34},{3,35},{4,36},{5,37},{6,38},{7,39},{8,40},{9,... | collective-permute-start | bytes 73736 | tf_op jit(solution)/shard_map/ppermute | solution.py:62

commit v4 on v3

--- a/solution.py
+++ b/solution.py
@@ -64,10 +64,10 @@
     )
 
 
-def passed_along(block, distance):
-    devices = range(256)
-    route = [(i - distance, i) for i in devices if i - distance in devices]
-    return lax.ppermute(block, AXIS, route)
+def passed_along(block, distance, sources=range(256)):
+    return lax.ppermute(
+        block, AXIS, [(i, i + distance) for i in sources if i + distance in range(256)]
+    )
 
 
 def reorder(place, t_ref, out_ref):
@@ -95,45 +95,33 @@
                     out_ref[half, row : row + 16, :] = jnp.concatenate(rows, 0).astype(BF16)
 
 
-def early_kernel(place, tok_ref, cot_ref, wq_ref, wo_ref, q_ref, da_ref, out_ref, t_ref):
+def early_kernel(tok_ref, cot_ref, wq_ref, wo_ref, q_ref, da_ref):
     q_ref[...] = dot(tok_ref[...], wq_ref[...]).astype(BF16)
     da_ref[...] = dot(cot_ref[...], wo_ref[...], NT).astype(BF16)
 
-    @pl.when(pl.program_id(0) == 0)
-    def _():
-        t_ref[:, :LANES] = tok_ref[...].astype(F32).T
-        t_ref[:, LANES:] = cot_ref[...].astype(F32).T
-        reorder(place, t_ref, out_ref)
-
 
 def whole(*shape):
     return pl.BlockSpec(shape, lambda i: (0,) * len(shape))
 
 
-def early(place, tokens, cotangent, wq, wo):
+def early(tokens, cotangent, wq, wo):
     block = pl.BlockSpec((ROWS, QCOLS), lambda i: (0, i))
     return pl.pallas_call(
         early_kernel,
         grid=(STEPS,),
-        out_shape=(
-            jax.ShapeDtypeStruct((ROWS, MODEL), BF16),
-            jax.ShapeDtypeStruct((ROWS, MODEL), BF16),
-            jax.ShapeDtypeStruct((2, 512, 2 * LANES), BF16),
-        ),
+        out_shape=(jax.ShapeDtypeStruct((ROWS, MODEL), BF16),) * 2,
         in_specs=[
-            pl.BlockSpec(memory_space=pltpu.SMEM),
             whole(ROWS, MODEL),
             whole(ROWS, MODEL),
             pl.BlockSpec((MODEL, QCOLS), lambda i: (0, i)),
             pl.BlockSpec((QCOLS, MODEL), lambda i: (i, 0)),
         ],
-        out_specs=(block, block, whole(2, 512, 2 * LANES)),
-        scratch_shapes=[pltpu.VMEM((MODEL, 2 * LANES), F32)],
+        out_specs=(block, block),
         compiler_params=pltpu.CompilerParams(
-            dimension_semantics=("arbitrary",), vmem_limit_bytes=20 << 20
+            dimension_semantics=("arbitrary",), vmem_limit_bytes=12 << 20
         ),
         name="early",
-    )(place, tokens, cotangent, wq, wo)
+    )(tokens, cotangent, wq, wo)
 
 
 def prep_kernel(place, a_ref, b_ref, out_ref, t_ref):
@@ -142,17 +130,31 @@
     reorder(place, t_ref, out_ref)
 
 
-def prepared(place, a, b):
-    return pl.pallas_call(
-        prep_kernel,
+def halo_kernel(place, far_ref, mate_ref, near_ref, out_ref, got_ref, t_ref):
+    @pl.when(place[2] == 0)
+    def _():
+        got_ref[...] = far_ref[...]
+
+    @pl.when(place[2] == 1)
+    def _():
+        got_ref[...] = mate_ref[...]
+
+    prep_kernel(place, got_ref, near_ref, out_ref, t_ref)
+
+
+def prepared(kernel, place, *blocks):
+    order = jax.ShapeDtypeStruct((2, 512, 2 * LANES), BF16), whole(2, 512, 2 * LANES)
+    outs = [order] if len(blocks) == 2 else [order, (jax.ShapeDtypeStruct((ROWS, MODEL), BF16), whole(ROWS, MODEL))]
+    return pl.pallas_call(
+        kernel,
         grid=(1,),
-        out_shape=jax.ShapeDtypeStruct((2, 512, 2 * LANES), BF16),
-        in_specs=[pl.BlockSpec(memory_space=pltpu.SMEM), whole(ROWS, MODEL), whole(ROWS, MODEL)],
-        out_specs=whole(2, 512, 2 * LANES),
+        out_shape=[o[0] for o in outs],
+        in_specs=[pl.BlockSpec(memory_space=pltpu.SMEM)] + [whole(ROWS, MODEL)] * len(blocks),
+        out_specs=[o[1] for o in outs],
         scratch_shapes=[pltpu.VMEM((MODEL, 2 * LANES), F32)],
         compiler_params=pltpu.CompilerParams(vmem_limit_bytes=12 << 20),
         name="prep",
-    )(place, a, b)
+    )(place, *blocks)
 
 
 def swapped(a):
@@ -387,12 +389,14 @@
     )(own, got)
 
 
-def middle_kernel(att_ref, dq_ref, wo_ref, wq_ref, out_ref, base_ref):
-    out_ref[...] = dot(att_ref[...], wo_ref[...]).astype(BF16)
-    base_ref[...] = dot(dq_ref[...], wq_ref[...], NT)
-
-
-def middle(att, dq, wo, wq):
+def middle_kernel(att_one, att_two, dq_one, dq_two, wo_ref, wq_ref, out_ref, base_ref):
+    att = jnp.concatenate([att_one[...], att_two[...]], axis=1)
+    out_ref[...] = dot(att, wo_ref[...]).astype(BF16)
+    dq = jnp.concatenate([dq_one[...], dq_two[...]], axis=1)
+    base_ref[...] = dot(dq, wq_ref[...], NT)
+
+
+def middle(atts, dqs, wo, wq):
     block = pl.BlockSpec((ROWS, QCOLS), lambda i: (0, i))
     return pl.pallas_call(
         middle_kernel,
@@ -401,38 +405,37 @@
             jax.ShapeDtypeStruct((ROWS, MODEL), BF16),
             jax.ShapeDtypeStruct((ROWS, MODEL), F32),
         ),
-        in_specs=[
-            whole(ROWS, MODEL),
-            whole(ROWS, MODEL),
+        in_specs=[whole(*a.shape) for a in (*atts, *dqs)]
+        + [
             pl.BlockSpec((MODEL, QCOLS), lambda i: (0, i)),
             pl.BlockSpec((QCOLS, MODEL), lambda i: (i, 0)),
         ],
         out_specs=(block, block),
         compiler_params=pltpu.CompilerParams(vmem_limit_bytes=12 << 20),
         name="middle",
-    )(att, dq, wo, wq)
-
-
-def tail_kernel(base_ref, own_ref, near_ref, far_ref, wk_ref, wv_ref, out_ref):
+    )(*atts, *dqs, wo, wq)
+
+
+def tail_kernel(base_ref, own_one, own_two, handed, near, far, wk_ref, wv_ref, out_ref):
     total = base_ref[...]
     for i, w_ref in enumerate((wk_ref, wv_ref)):
-        grad = own_ref[i] + near_ref[i].astype(F32) + far_ref[i].astype(F32)
+        grad = jnp.concatenate([own_one[i], own_two[i]], axis=1)
+        for part in (handed[0, i], near[i], far[i]):
+            grad = grad + part.astype(F32)
         total = total + dot(grad.astype(BF16), w_ref[...], NT)
     out_ref[...] = total.astype(BF16)
 
 
-def tail(base, own, near, far, wk, wv):
-    block = pl.BlockSpec((ROWS, QCOLS), lambda i: (0, i))
+def tail(*args):
     return pl.pallas_call(
         tail_kernel,
-        grid=(STEPS,),
+        grid=(1,),
         out_shape=jax.ShapeDtypeStruct((ROWS, MODEL), BF16),
-        in_specs=[block, *[whole(2, ROWS, 512)] * 3]
-        + [pl.BlockSpec((QCOLS, 512), lambda i: (i, 0))] * 2,
-        out_specs=block,
-        compiler_params=pltpu.CompilerParams(vmem_limit_bytes=12 << 20),
+        in_specs=[whole(*a.shape) for a in args],
+        out_specs=whole(ROWS, MODEL),
+        compiler_params=pltpu.CompilerParams(vmem_limit_bytes=20 << 20),
         name="tail",
-    )(base, own, near, far, wk, wv)
+    )(*args)
 
 
 def after(value, *others):
@@ -440,14 +443,16 @@
 
 
 def shards(tokens, query_weight, key_weight, value_matrix, out_weight, out_cotangent):
-    far = passed_along(tokens, 2)
     near = passed_along(tokens, 1)
+    far = passed_along(tokens, 2, range(0, 256, 2))
+    mate = passed_along(near, 1, range(0, 256, 2))
     me = lax.axis_index(AXIS)
     start = jnp.maximum(2 - me, 0) * ROWS
     place = jnp.stack([(me // 8) % 4, (me // 2) % 4, me % 2, me // 32, start]).astype(jnp.int32)
     wq, wk, wv, wo = map(in_hbm, (query_weight, key_weight, value_matrix, out_weight))
-    q, da, tp = early(place, in_hbm(tokens), in_hbm(out_cotangent), wq, wo)
-    th = prepared(place, far, near)
+    q, da = early(in_hbm(tokens), in_hbm(out_cotangent), wq, wo)
+    (tp,) = prepared(prep_kernel, after(place, q, near), tokens, out_cotangent)
+    th, far = prepared(halo_kernel, after(place, tp), far, mate, near)
 
     def attend(first, steps, place):
         return attention(first, steps, place, far, near, tokens, q, da, wk, wv, tp, th)
@@ -460,19 +465,23 @@
     own, *sends = folded_into(3, two[-1], after(got_two, sums[0]), sums)
     ring_one = ring([None, *sends], 0)
 
-    parts = zip(one[:-2], two[:-2])
-    att, dq, own_kv, near_kv, far_kv = (jnp.concatenate(p, axis=-1) for p in parts)
-    back_near = passed_along(after(near_kv, ring_one[0]), -1)
-    back_far = passed_along(after(far_kv, ring_one[0]), -2)
-    attn_out, base = middle(after(att, own), after(dq, own), wo, wq)
+    near_grad = jnp.concatenate([one[3], after(two[3], own)], axis=-1)
+    far_grad = jnp.concatenate([one[4], after(two[4], own)], axis=-1)
+    handed = passed_along(jnp.stack([near_grad, far_grad]), -1, range(1, 256, 2))
+    attn_out, base = middle((one[0], after(two[0], own)), (one[1], two[1]), wo, wq)
+    summed = (near_grad.astype(F32) + handed[1].astype(F32)).astype(BF16)
+    base, summed = lax.optimization_barrier((base, summed))
 
     own, *sends = folded(after(own, base), *ring_one)
     ring_two = ring([None, *sends], 1)
     own, *sends = folded(own, *ring_two)
+    z_own = own
     ring_three = [along_z(sends[d - 1], 2 * d) for d in (1, 3, 2)]
     own, send = halved(own, *ring_three)
     got = along_z(send, 1)
-    tokens_grad = tail(base, own_kv, back_near, back_far, wk, wv)
+    back_near = passed_along(after(summed, z_own), -1, range(0, 256, 2))
+    back_far = passed_along(after(far_grad, z_own), -2, range(0, 256, 2))
+    tokens_grad = tail(base, one[2], two[2], handed, back_near, back_far, key_weight, value_matrix)
     query_rows, key_rows, value_rows, out_rows = summed_last(after(own, tokens_grad), got)
     return attn_out, tokens_grad, query_rows, key_rows, value_rows, out_rows.T
 

time: 99.2 us -> 97.8 us (0.986)
  the two profiles are of different devices: /device:TPU:24 before, /device:TPU:32 now
where the time goes in v4:
time: 97.8 us; the launch traced here: 97.4 us
  starting transfers between devices  33.4 us (34%)
  waiting for transfers between devices  33 us (34%)
  Pallas kernels  29.7 us (30%)
    ppermute x6, waiting for transfers between devices, ring(): lax.ppermute(blocks[d], AXIS, route_of(functools.partial(plane_step, phas...  19.9 us
    pallas_call x2, Pallas kernels, attention(): pl.pallas_call(attention_kernel, grid=(steps,), out_shape=(struct(ROWS, Q...  15 us
    ppermute x4, starting transfers between devices, along_z(): lax.ppermute(block, AXIS, route_of(lambda z, x, y, c: ((z + distance) % 8...  14.5 us
    ppermute x6, starting transfers between devices, passed_along(): lax.ppermute(block, AXIS, [(i, i + distance) for i in sources if i + dist...  12.7 us
    ppermute x6, waiting for transfers between devices, passed_along(): lax.ppermute(block, AXIS, [(i, i + distance) for i in sources if i + dist...  6.95 us
    ppermute x6, starting transfers between devices, ring(): lax.ppermute(blocks[d], AXIS, route_of(functools.partial(plane_step, phas...  5.59 us
    ppermute x4, waiting for transfers between devices, along_z(): lax.ppermute(block, AXIS, route_of(lambda z, x, y, c: ((z + distance) % 8...  5.43 us
    pallas_call x1, Pallas kernels, middle(): pl.pallas_call(middle_kernel, grid=(STEPS,), out_shape=(jax.ShapeDtypeStr...  4.37 us
  transfers between devices with their start and end apart: 18, of which 8 were waited for; matrix products, arithmetic and copies ran while one was open for 0% of the time, Pallas kernels for 17%

profile of v4, /device:TPU:32, one launch (start us, length us, event | category | flops | bytes accessed | tf_op | source)
XLA Modules:
  0.0 97.4 jit_solution(17955272542941325469)
XLA Ops:
  0.6 1.9 %collective-permute-start = (bf16[128,1024]{1,0:T(8,128)(2,1)}, bf16[128,1024]{1,0:T(8,128)(2,1)S(1)}, u32[]{:S(2)}, u32[]{:S(2)}) collective-permute-start(bf16[128,1024]{1,0:T(8,128)(2,1)} %own_ref.3), channel_id=1, source_target_pairs={{0,1},{1,2},{2,3},{3,4},{4,5},{5,6},{6,7},{7,8},{8,9},{9,10},{10,1... | collective-permute-start | bytes 786440 | tf_op jit(solution)/shard_map/ppermute | solution.py:68
  2.6 3.5 %collective-permute-start.1 = (bf16[128,1024]{1,0:T(8,128)(2,1)}, bf16[128,1024]{1,0:T(8,128)(2,1)S(1)}, u32[]{:S(2)}, u32[]{:S(2)}) collective-permute-start(bf16[128,1024]{1,0:T(8,128)(2,1)} %own_ref.3), channel_id=1, source_target_pairs={{0,2},{2,4},{4,6},{6,8},{8,10},{10,12},{12,14},{14,16},{16,18},{18... | collective-permute-start | bytes 786440 | tf_op jit(solution)/shard_map/ppermute | solution.py:68
  6.1 6.9 %collective-permute-done.near_ref = bf16[128,1024]{1,0:T(8,128)(2,1)S(1)} collective-permute-done((bf16[128,1024]{1,0:T(8,128)(2,1)}, bf16[128,1024]{1,0:T(8,128)(2,1)S(1)}, u32[]{:S(2)}, u32[]{:S(2)}) %collective-permute-start) | collective-permute-done | bytes 262176 | tf_op jit(solution)/shard_map/ppermute | solution.py:68
  13.0 1.3 %collective-permute-start.2 = (bf16[128,1024]{1,0:T(8,128)(2,1)S(1)}, bf16[128,1024]{1,0:T(8,128)(2,1)S(1)}, u32[]{:S(2)}, u32[]{:S(2)}) collective-permute-start(bf16[128,1024]{1,0:T(8,128)(2,1)S(1)} %collective-permute-done.near_ref), channel_id=1, source_target_pairs={{0,1},{2,3},{4,5},{6,7},{8,9},{10,11},{12,13},{14,15},{16,17},{18,... | collective-permute-start | bytes 786440 | tf_op jit(solution)/shard_map/ppermute | solution.py:68
  14.4 4.0 %early.1 = (bf16[128,1024]{1,0:T(8,128)(2,1)S(1)}, bf16[128,1024]{1,0:T(8,128)(2,1)S(1)}) custom-call(bf16[128,1024]{1,0:T(8,128)(2,1)} %own_ref.3, bf16[128,1024]{1,0:T(8,128)(2,1)} %b_ref.1, bf16[1024,1024]{1,0:T(8,128)(2,1)} %wq_ref.3, bf16[1024,1024]{1,0:T(8,128)(2,1)} %wo_ref.3), custom_call_target="tpu_custom_call" | custom-call | tf_op jit(solution)/shard_map/early/pallas_call | solution.py:109
  19.7 1.2 %prep.3 = (bf16[2,512,256]{2,1,0:T(8,128)(2,1)S(1)}, bf16[128,1024]{1,0:T(8,128)(2,1)S(1)}) custom-call(s32[5]{0:T(128)S(1)} %stack.32.place, bf16[128,1024]{1,0:T(8,128)(2,1)S(1)} %collective-permute-done.1.far_ref, bf16[128,1024]{1,0:T(8,128)(2,1)S(1)} %collective-permute-done.2.mate_ref, bf16[128,1024]{1,0:T(8,128)(2,1)S(1)} %collective-permute-done.near_ref), custom_call_target="tpu_custom_call" | custom-call | tf_op jit(solution)/shard_map/prep/pallas_call | solution.py:148
  20.9 10.9 %attention.2 = (bf16[128,768]{1,0:T(8,128)(2,1)S(1)}, bf16[128,768]{1,0:T(8,128)(2,1)S(1)}, f32[2,128,384]{2,1,0:T(8,128)S(1)}, bf16[2,128,384]{2,1,0:T(8,128)(2...) custom-call(s32[5]{0:T(128)S(1)} %stack.32.place, ...), custom_call_target="tpu_custom_call" | custom-call | flops 1000 | bytes 1000 | tf_op jit(solution)/shard_map/attention/pallas_call | solution.py:255
  31.9 4.1 %attention.3 = (bf16[128,256]{1,0:T(8,128)(2,1)S(1)}, bf16[128,256]{1,0:T(8,128)(2,1)S(1)}, f32[2,128,128]{2,1,0:T(8,128)S(1)}, bf16[2,128,128]{2,1,0:T(8,128)(2...) custom-call(s32[5]{0:T(128)S(1)} %stack.32.place, ...), custom_call_target="tpu_custom_call" | custom-call | flops 1000 | bytes 1000 | tf_op jit(solution)/shard_map/attention/pallas_call | solution.py:255
  38.8 3.2 %collective-permute-start.7 = (bf16[128,3072]{1,0:T(8,128)(2,1)S(1)}, bf16[128,3072]{1,0:T(8,128)(2,1)S(1)}, u32[]{:S(2)}, u32[]{:S(2)}) collective-permute-start(bf16[128,3072]{1,0:T(8,128)(2,1)S(1)} %get-tuple-element.99), channel_id=1, source_target_pairs={{0,24},{1,7},{2,26},{3,1},{4,28},{5,3},{6,30},{7,5},{8,0},{9,15},{... | collective-permute-start | bytes 2359304 | tf_op jit(solution)/shard_map/ppermute | solution.py:56
  42.2 1.3 %collective-permute-start.5 = (bf16[2,2,128,512]{3,2,1,0:T(8,128)(2,1)S(1)}, bf16[2,2,128,512]{3,2,1,0:T(8,128)(2,1)S(1)}, u32[]{:S(2)}, u32[]{:S(2)}) collective-permute-start(bf16[2,2,128,512]{3,2,1,0:T(8,128)(2,1)S(1)} %pad_maximum_fusion), channel_id=1, source_target_pairs={{1,0},{3,2},{5,4},{7,6},{9,8},{11,10},{13,12},{15,14},{17,16},{19,... | collective-permute-start | bytes 1572872 | tf_op jit(solution)/shard_map/ppermute | solution.py:68
  43.5 4.4 %middle.1 = (bf16[128,1024]{1,0:T(8,128)(2,1)}, f32[128,1024]{1,0:T(8,128)S(1)}) custom-call(bf16[128,768]{1,0:T(8,128)(2,1)S(1)} %get-tuple-element.68.att_one, bf16[128,256]{1,0:T(8,128)(2,1)S(1)} %get-tuple-element.82.att_two, bf16[128,768]{1,0:T(8,128)(2,1)S(1)} %get-tuple-element.83.dq_one, bf16[128,256]{1,0:T(8,128)(2,1)S(1)} %get-tuple-element.84.dq_two, ...), custom_call_target="tpu_custom_call" | custom-call | tf_op jit(solution)/shard_map/middle/pallas_call | solution.py:401
  47.9 12.5 %collective-permute-done.6.refs_1_ = bf16[128,3072]{1,0:T(8,128)(2,1)S(1)} collective-permute-done((bf16[128,3072]{1,0:T(8,128)(2,1)S(1)}, bf16[128,3072]{1,0:T(8,128)(2,1)S(1)}, u32[]{:S(2)}, u32[]{:S(2)}) %collective-permute-start.6) | collective-permute-done | bytes 786464 | tf_op jit(solution)/shard_map/ppermute | solution.py:56
  61.4 1.6 %collective-permute-start.9 = (bf16[32,3072]{1,0:T(8,128)(2,1)S(1)}, bf16[32,3072]{1,0:T(8,128)(2,1)S(1)}, u32[]{:S(2)}, u32[]{:S(2)}) collective-permute-start(bf16[32,3072]{1,0:T(8,128)(2,1)S(1)} %get-tuple-element.102), channel_id=1, source_target_pairs={{0,2},{1,9},{2,4},{3,11},{4,6},{5,13},{6,0},{7,15},{8,10},{9,17},{... | collective-permute-start | bytes 589832 | tf_op jit(solution)/shard_map/ppermute | solution.py:56
  63.1 3.6 %collective-permute-done.10.refs_2_ = bf16[32,3072]{1,0:T(8,128)(2,1)S(1)} collective-permute-done((bf16[32,3072]{1,0:T(8,128)(2,1)S(1)}, bf16[32,3072]{1,0:T(8,128)(2,1)S(1)}, u32[]{:S(2)}, u32[]{:S(2)}) %collective-permute-start.10) | collective-permute-done | bytes 196640 | tf_op jit(solution)/shard_map/ppermute | solution.py:56
  66.7 1.7 %collective-permute-done.11.refs_3_ = bf16[32,3072]{1,0:T(8,128)(2,1)S(1)} collective-permute-done((bf16[32,3072]{1,0:T(8,128)(2,1)S(1)}, bf16[32,3072]{1,0:T(8,128)(2,1)S(1)}, u32[]{:S(2)}, u32[]{:S(2)}) %collective-permute-start.11) | collective-permute-done | bytes 196640 | tf_op jit(solution)/shard_map/ppermute | solution.py:56
  68.4 2.0 %collective-permute-done.9.refs_1_ = bf16[32,3072]{1,0:T(8,128)(2,1)S(1)} collective-permute-done((bf16[32,3072]{1,0:T(8,128)(2,1)S(1)}, bf16[32,3072]{1,0:T(8,128)(2,1)S(1)}, u32[]{:S(2)}, u32[]{:S(2)}) %collective-permute-start.9) | collective-permute-done | bytes 196640 | tf_op jit(solution)/shard_map/ppermute | solution.py:56
  70.5 3.4 %collective-permute-start.13 = (bf16[2,128,512]{2,1,0:T(8,128)(2,1)S(1)}, bf16[2,128,512]{2,1,0:T(8,128)(2,1)S(1)}, u32[]{:S(2)}, u32[]{:S(2)}) collective-permute-start(bf16[2,128,512]{2,1,0:T(8,128)(2,1)S(1)} %constant_dynamic-update-slice_fusion.2), channel_id=1, source_target_pairs={{2,0},{4,2},{6,4},{8,6},{10,8},{12,10},{14,12},{16,14},{18,16},{20... | collective-permute-start | bytes 786440 | tf_op jit(solution)/shard_map/ppermute | solution.py:68
  73.9 1.3 %collective-permute-start.12 = (bf16[2,128,512]{2,1,0:T(8,128)(2,1)S(1)}, bf16[2,128,512]{2,1,0:T(8,128)(2,1)S(1)}, u32[]{:S(2)}, u32[]{:S(2)}) collective-permute-start(bf16[2,128,512]{2,1,0:T(8,128)(2,1)S(1)} %fusion), channel_id=1, source_target_pairs={{2,1},{4,3},{6,5},{8,7},{10,9},{12,11},{14,13},{16,15},{18,17},{20... | collective-permute-start | bytes 786440 | tf_op jit(solution)/shard_map/ppermute | solution.py:68
  75.2 5.1 %collective-permute-start.14 = (bf16[8,3072]{1,0:T(8,128)(2,1)S(1)}, bf16[8,3072]{1,0:T(8,128)(2,1)S(1)}, u32[]{:S(2)}, u32[]{:S(2)}) collective-permute-start(bf16[8,3072]{1,0:T(8,128)(2,1)S(1)} %get-tuple-element.108), channel_id=1, source_target_pairs={{0,64},{1,65},{2,66},{3,67},{4,68},{5,69},{6,70},{7,71},{8,72},{9,... | collective-permute-start | bytes 147464 | tf_op jit(solution)/shard_map/ppermute | solution.py:62
  80.4 3.1 %collective-permute-start.15 = (bf16[8,3072]{1,0:T(8,128)(2,1)S(1)}, bf16[8,3072]{1,0:T(8,128)(2,1)S(1)}, u32[]{:S(2)}, u32[]{:S(2)}) collective-permute-start(bf16[8,3072]{1,0:T(8,128)(2,1)S(1)} %get-tuple-element.109), channel_id=1, source_target_pairs={{0,192},{1,193},{2,194},{3,195},{4,196},{5,197},{6,198},{7,199},{8... | collective-permute-start | bytes 147464 | tf_op jit(solution)/shard_map/ppermute | solution.py:62
  83.5 6.1 %collective-permute-start.16 = (bf16[8,3072]{1,0:T(8,128)(2,1)S(1)}, bf16[8,3072]{1,0:T(8,128)(2,1)S(1)}, u32[]{:S(2)}, u32[]{:S(2)}) collective-permute-start(bf16[8,3072]{1,0:T(8,128)(2,1)S(1)} %get-tuple-element.110), channel_id=1, source_target_pairs={{0,128},{1,129},{2,130},{3,131},{4,132},{5,133},{6,134},{7,135},{8... | collective-permute-start | bytes 147464 | tf_op jit(solution)/shard_map/ppermute | solution.py:62
  89.6 3.2 %collective-permute-done.16.c_ref = bf16[8,3072]{1,0:T(8,128)(2,1)S(1)} collective-permute-done((bf16[8,3072]{1,0:T(8,128)(2,1)S(1)}, bf16[8,3072]{1,0:T(8,128)(2,1)S(1)}, u32[]{:S(2)}, u32[]{:S(2)}) %collective-permute-start.16) | collective-permute-done | bytes 49184 | tf_op jit(solution)/shard_map/ppermute | solution.py:62
  93.0 1.5 %tail.1 = bf16[128,1024]{1,0:T(8,128)(2,1)} custom-call(f32[128,1024]{1,0:T(8,128)S(1)} %get-tuple-element.93.base_ref, f32[2,128,384]{2,1,0:T(8,128)S(1)} %get-tuple-element.94.own_one, f32[2,128,128]{2,1,0:T(8,128)S(1)} %get-tuple-element.95.own_two, bf16[2,2,128,512]{3,2,1,0:T(8,128)(2,1)S(1)} %collective-permute-done.5.handed, ...), custom_call_target="tpu_custom_call" | custom-call | tf_op jit(solution)/shard_map/tail/pallas_call | solution.py:430
  94.5 2.2 %collective-permute-done.17.got_ref = bf16[4,3072]{1,0:T(4,128)(2,1)S(1)} collective-permute-done((bf16[4,3072]{1,0:T(4,128)(2,1)S(1)}, bf16[4,3072]{1,0:T(4,128)(2,1)S(1)}, u32[]{:S(2)}, u32[]{:S(2)}) %collective-permute-start.17) | collective-permute-done | bytes 24608 | tf_op jit(solution)/shard_map/ppermute | solution.py:62
  (39 shorter events, 6.1 us)
Async XLA Ops:
  0.6 12.4 %collective-permute-start = (bf16[128,1024]{1,0:T(8,128)(2,1)}, bf16[128,1024]{1,0:T(8,128)(2,1)S(1)}, u32[]{:S(2)}, u32[]{:S(2)}) collective-permute-start(bf16[128,1024]{1,0:T(8,128)(2,1)} %own_ref.3), channel_id=1, source_target_pairs={{0,1},{1,2},{2,3},{3,4},{4,5},{5,6},{6,7},{7,8},{8,9},{9,10},{10,1... | collective-permute-start | bytes 786440 | tf_op jit(solution)/shard_map/ppermute | solution.py:68
  2.6 17.1 %collective-permute-start.1 = (bf16[128,1024]{1,0:T(8,128)(2,1)}, bf16[128,1024]{1,0:T(8,128)(2,1)S(1)}, u32[]{:S(2)}, u32[]{:S(2)}) collective-permute-start(bf16[128,1024]{1,0:T(8,128)(2,1)} %own_ref.3), channel_id=1, source_target_pairs={{0,2},{2,4},{4,6},{6,8},{8,10},{10,12},{12,14},{14,16},{16,18},{18... | collective-permute-start | bytes 786440 | tf_op jit(solution)/shard_map/ppermute | solution.py:68
  13.0 6.7 %collective-permute-start.2 = (bf16[128,1024]{1,0:T(8,128)(2,1)S(1)}, bf16[128,1024]{1,0:T(8,128)(2,1)S(1)}, u32[]{:S(2)}, u32[]{:S(2)}) collective-permute-start(bf16[128,1024]{1,0:T(8,128)(2,1)S(1)} %collective-permute-done.near_ref), channel_id=1, source_target_pairs={{0,1},{2,3},{4,5},{6,7},{8,9},{10,11},{12,13},{14,15},{16,17},{18,... | collective-permute-start | bytes 786440 | tf_op jit(solution)/shard_map/ppermute | solution.py:68
  14.4 4.1 %copy-start.2 = (bf16[128,1024]{1,0:T(8,128)(2,1)S(1)}, bf16[128,1024]{1,0:T(8,128)(2,1)}, u32[]{:S(2)}) copy-start(bf16[128,1024]{1,0:T(8,128)(2,1)} %own_ref.3) | copy-start | bytes 786436
  14.4 4.1 %copy-start.3 = (bf16[128,1024]{1,0:T(8,128)(2,1)S(1)}, bf16[128,1024]{1,0:T(8,128)(2,1)}, u32[]{:S(2)}) copy-start(bf16[128,1024]{1,0:T(8,128)(2,1)} %b_ref.1) | copy-start | bytes 786436
  31.8 4.9 %collective-permute-start.4 = (bf16[512,2304]{1,0:T(8,128)(2,1)S(1)}, bf16[512,2304]{1,0:T(8,128)(2,1)S(1)}, u32[]{:S(2)}, u32[]{:S(2)}) collective-permute-start(bf16[512,2304]{1,0:T(8,128)(2,1)S(1)} %get-tuple-element.74), channel_id=1, source_target_pairs={{0,1},{1,0},{2,3},{3,2},{4,5},{5,4},{6,7},{7,6},{8,9},{9,8},{10,11... | collective-permute-start | bytes 7077896 | tf_op jit(solution)/shard_map/ppermute | solution.py:45
  36.1 2.5 %collective-permute-start.3 = (bf16[512,768]{1,0:T(8,128)(2,1)S(1)}, bf16[512,768]{1,0:T(8,128)(2,1)S(1)}, u32[]{:S(2)}, u32[]{:S(2)}) collective-permute-start(bf16[512,768]{1,0:T(8,128)(2,1)S(1)} %get-tuple-element.73), channel_id=1, source_target_pairs={{0,1},{1,0},{2,3},{3,2},{4,5},{5,4},{6,7},{7,6},{8,9},{9,8},{10,11... | collective-permute-start | bytes 2359304 | tf_op jit(solution)/shard_map/ppermute | solution.py:45
  38.7 21.7 %collective-permute-start.6 = (bf16[128,3072]{1,0:T(8,128)(2,1)S(1)}, bf16[128,3072]{1,0:T(8,128)(2,1)S(1)}, u32[]{:S(2)}, u32[]{:S(2)}) collective-permute-start(bf16[128,3072]{1,0:T(8,128)(2,1)S(1)} %get-tuple-element.98), channel_id=1, source_target_pairs={{0,8},{1,3},{2,10},{3,5},{4,12},{5,7},{6,14},{7,1},{8,16},{9,11},{... | collective-permute-start | bytes 2359304 | tf_op jit(solution)/shard_map/ppermute | solution.py:56
  38.8 21.6 %collective-permute-start.7 = (bf16[128,3072]{1,0:T(8,128)(2,1)S(1)}, bf16[128,3072]{1,0:T(8,128)(2,1)S(1)}, u32[]{:S(2)}, u32[]{:S(2)}) collective-permute-start(bf16[128,3072]{1,0:T(8,128)(2,1)S(1)} %get-tuple-element.99), channel_id=1, source_target_pairs={{0,24},{1,7},{2,26},{3,1},{4,28},{5,3},{6,30},{7,5},{8,0},{9,15},{... | collective-permute-start | bytes 2359304 | tf_op jit(solution)/shard_map/ppermute | solution.py:56
  42.0 18.4 %collective-permute-start.8 = (bf16[128,3072]{1,0:T(8,128)(2,1)S(1)}, bf16[128,3072]{1,0:T(8,128)(2,1)S(1)}, u32[]{:S(2)}, u32[]{:S(2)}) collective-permute-start(bf16[128,3072]{1,0:T(8,128)(2,1)S(1)} %get-tuple-element.100), channel_id=1, source_target_pairs={{0,16},{1,5},{2,18},{3,7},{4,20},{5,1},{6,22},{7,3},{8,24},{9,13},... | collective-permute-start | bytes 2359304 | tf_op jit(solution)/shard_map/ppermute | solution.py:56
  42.2 5.7 %collective-permute-start.5 = (bf16[2,2,128,512]{3,2,1,0:T(8,128)(2,1)S(1)}, bf16[2,2,128,512]{3,2,1,0:T(8,128)(2,1)S(1)}, u32[]{:S(2)}, u32[]{:S(2)}) collective-permute-start(bf16[2,2,128,512]{3,2,1,0:T(8,128)(2,1)S(1)} %pad_maximum_fusion), channel_id=1, source_target_pairs={{1,0},{3,2},{5,4},{7,6},{9,8},{11,10},{13,12},{15,14},{17,16},{19,... | collective-permute-start | bytes 1572872 | tf_op jit(solution)/shard_map/ppermute | solution.py:68
  47.9 45.1 %copy-start = (bf16[1024,512]{1,0:T(8,128)(2,1)S(1)}, bf16[1024,512]{1,0:T(8,128)(2,1)}, u32[]{:S(2)}) copy-start(bf16[1024,512]{1,0:T(8,128)(2,1)} %wk_ref.5) | copy-start | bytes 3145732
  47.9 45.1 %copy-start.1 = (bf16[1024,512]{1,0:T(8,128)(2,1)S(1)}, bf16[1024,512]{1,0:T(8,128)(2,1)}, u32[]{:S(2)}) copy-start(bf16[1024,512]{1,0:T(8,128)(2,1)} %wv_ref.5) | copy-start | bytes 3145732
  60.8 5.9 %collective-permute-start.10 = (bf16[32,3072]{1,0:T(8,128)(2,1)S(1)}, bf16[32,3072]{1,0:T(8,128)(2,1)S(1)}, u32[]{:S(2)}, u32[]{:S(2)}) collective-permute-start(bf16[32,3072]{1,0:T(8,128)(2,1)S(1)} %get-tuple-element.103), channel_id=1, source_target_pairs={{0,6},{1,25},{2,0},{3,27},{4,2},{5,29},{6,4},{7,31},{8,14},{9,1},{... | collective-permute-start | bytes 589832 | tf_op jit(solution)/shard_map/ppermute | solution.py:56
  61.0 7.4 %collective-permute-start.11 = (bf16[32,3072]{1,0:T(8,128)(2,1)S(1)}, bf16[32,3072]{1,0:T(8,128)(2,1)S(1)}, u32[]{:S(2)}, u32[]{:S(2)}) collective-permute-start(bf16[32,3072]{1,0:T(8,128)(2,1)S(1)} %get-tuple-element.104), channel_id=1, source_target_pairs={{0,4},{1,17},{2,6},{3,19},{4,0},{5,21},{6,2},{7,23},{8,12},{9,25},... | collective-permute-start | bytes 589832 | tf_op jit(solution)/shard_map/ppermute | solution.py:56
  61.4 9.0 %collective-permute-start.9 = (bf16[32,3072]{1,0:T(8,128)(2,1)S(1)}, bf16[32,3072]{1,0:T(8,128)(2,1)S(1)}, u32[]{:S(2)}, u32[]{:S(2)}) collective-permute-start(bf16[32,3072]{1,0:T(8,128)(2,1)S(1)} %get-tuple-element.102), channel_id=1, source_target_pairs={{0,2},{1,9},{2,4},{3,11},{4,6},{5,13},{6,0},{7,15},{8,10},{9,17},{... | collective-permute-start | bytes 589832 | tf_op jit(solution)/shard_map/ppermute | solution.py:56
  70.5 22.4 %collective-permute-start.13 = (bf16[2,128,512]{2,1,0:T(8,128)(2,1)S(1)}, bf16[2,128,512]{2,1,0:T(8,128)(2,1)S(1)}, u32[]{:S(2)}, u32[]{:S(2)}) collective-permute-start(bf16[2,128,512]{2,1,0:T(8,128)(2,1)S(1)} %constant_dynamic-update-slice_fusion.2), channel_id=1, source_target_pairs={{2,0},{4,2},{6,4},{8,6},{10,8},{12,10},{14,12},{16,14},{18,16},{20... | collective-permute-start | bytes 786440 | tf_op jit(solution)/shard_map/ppermute | solution.py:68
  73.9 19.0 %collective-permute-start.12 = (bf16[2,128,512]{2,1,0:T(8,128)(2,1)S(1)}, bf16[2,128,512]{2,1,0:T(8,128)(2,1)S(1)}, u32[]{:S(2)}, u32[]{:S(2)}) collective-permute-start(bf16[2,128,512]{2,1,0:T(8,128)(2,1)S(1)} %fusion), channel_id=1, source_target_pairs={{2,1},{4,3},{6,5},{8,7},{10,9},{12,11},{14,13},{16,15},{18,17},{20... | collective-permute-start | bytes 786440 | tf_op jit(solution)/shard_map/ppermute | solution.py:68
  75.2 14.4 %collective-permute-start.14 = (bf16[8,3072]{1,0:T(8,128)(2,1)S(1)}, bf16[8,3072]{1,0:T(8,128)(2,1)S(1)}, u32[]{:S(2)}, u32[]{:S(2)}) collective-permute-start(bf16[8,3072]{1,0:T(8,128)(2,1)S(1)} %get-tuple-element.108), channel_id=1, source_target_pairs={{0,64},{1,65},{2,66},{3,67},{4,68},{5,69},{6,70},{7,71},{8,72},{9,... | collective-permute-start | bytes 147464 | tf_op jit(solution)/shard_map/ppermute | solution.py:62
  80.4 9.3 %collective-permute-start.15 = (bf16[8,3072]{1,0:T(8,128)(2,1)S(1)}, bf16[8,3072]{1,0:T(8,128)(2,1)S(1)}, u32[]{:S(2)}, u32[]{:S(2)}) collective-permute-start(bf16[8,3072]{1,0:T(8,128)(2,1)S(1)} %get-tuple-element.109), channel_id=1, source_target_pairs={{0,192},{1,193},{2,194},{3,195},{4,196},{5,197},{6,198},{7,199},{8... | collective-permute-start | bytes 147464 | tf_op jit(solution)/shard_map/ppermute | solution.py:62
  83.5 9.3 %collective-permute-start.16 = (bf16[8,3072]{1,0:T(8,128)(2,1)S(1)}, bf16[8,3072]{1,0:T(8,128)(2,1)S(1)}, u32[]{:S(2)}, u32[]{:S(2)}) collective-permute-start(bf16[8,3072]{1,0:T(8,128)(2,1)S(1)} %get-tuple-element.110), channel_id=1, source_target_pairs={{0,128},{1,129},{2,130},{3,131},{4,132},{5,133},{6,134},{7,135},{8... | collective-permute-start | bytes 147464 | tf_op jit(solution)/shard_map/ppermute | solution.py:62
  92.9 3.9 %collective-permute-start.17 = (bf16[4,3072]{1,0:T(4,128)(2,1)S(1)}, bf16[4,3072]{1,0:T(4,128)(2,1)S(1)}, u32[]{:S(2)}, u32[]{:S(2)}) collective-permute-start(bf16[4,3072]{1,0:T(4,128)(2,1)S(1)} %get-tuple-element.113), channel_id=1, source_target_pairs={{0,32},{1,33},{2,34},{3,35},{4,36},{5,37},{6,38},{7,39},{8,40},{9,... | collective-permute-start | bytes 73736 | tf_op jit(solution)/shard_map/ppermute | solution.py:62

commit v5 on v4

--- a/solution.py
+++ b/solution.py
@@ -445,13 +445,14 @@
 def shards(tokens, query_weight, key_weight, value_matrix, out_weight, out_cotangent):
     near = passed_along(tokens, 1)
     far = passed_along(tokens, 2, range(0, 256, 2))
-    mate = passed_along(near, 1, range(0, 256, 2))
     me = lax.axis_index(AXIS)
     start = jnp.maximum(2 - me, 0) * ROWS
     place = jnp.stack([(me // 8) % 4, (me // 2) % 4, me % 2, me // 32, start]).astype(jnp.int32)
     wq, wk, wv, wo = map(in_hbm, (query_weight, key_weight, value_matrix, out_weight))
     q, da = early(in_hbm(tokens), in_hbm(out_cotangent), wq, wo)
-    (tp,) = prepared(prep_kernel, after(place, q, near), tokens, out_cotangent)
+    near = after(near, q)
+    mate = passed_along(near, 1, range(0, 256, 2))
+    (tp,) = prepared(prep_kernel, after(place, near), tokens, out_cotangent)
     th, far = prepared(halo_kernel, after(place, tp), far, mate, near)
 
     def attend(first, steps, place):
@@ -465,24 +466,26 @@
     own, *sends = folded_into(3, two[-1], after(got_two, sums[0]), sums)
     ring_one = ring([None, *sends], 0)
 
-    near_grad = jnp.concatenate([one[3], after(two[3], own)], axis=-1)
-    far_grad = jnp.concatenate([one[4], after(two[4], own)], axis=-1)
+    attn_out, base = middle((one[0], after(two[0], own)), (one[1], two[1]), wo, wq)
+    grads = lax.optimization_barrier((one[3], two[3], one[4], two[4], base))
+    near_grad = jnp.concatenate(grads[0:2], axis=-1)
+    far_grad = jnp.concatenate(grads[2:4], axis=-1)
     handed = passed_along(jnp.stack([near_grad, far_grad]), -1, range(1, 256, 2))
-    attn_out, base = middle((one[0], after(two[0], own)), (one[1], two[1]), wo, wq)
     summed = (near_grad.astype(F32) + handed[1].astype(F32)).astype(BF16)
-    base, summed = lax.optimization_barrier((base, summed))
-
-    own, *sends = folded(after(own, base), *ring_one)
+
+    back_near = passed_along(after(summed, ring_one[0]), -1, range(0, 256, 2))
+    back_far = passed_along(after(far_grad, ring_one[0]), -2, range(0, 256, 2))
+
+    own, *sends = folded(after(own, base, back_near, back_far), *ring_one)
     ring_two = ring([None, *sends], 1)
-    own, *sends = folded(own, *ring_two)
-    z_own = own
+    tokens_grad = tail(
+        after(base, own), one[2], two[2], handed, back_near, back_far, key_weight, value_matrix
+    )
+    own, *sends = folded(after(own, tokens_grad), *ring_two)
     ring_three = [along_z(sends[d - 1], 2 * d) for d in (1, 3, 2)]
     own, send = halved(own, *ring_three)
     got = along_z(send, 1)
-    back_near = passed_along(after(summed, z_own), -1, range(0, 256, 2))
-    back_far = passed_along(after(far_grad, z_own), -2, range(0, 256, 2))
-    tokens_grad = tail(base, one[2], two[2], handed, back_near, back_far, key_weight, value_matrix)
-    query_rows, key_rows, value_rows, out_rows = summed_last(after(own, tokens_grad), got)
+    query_rows, key_rows, value_rows, out_rows = summed_last(own, got)
     return attn_out, tokens_grad, query_rows, key_rows, value_rows, out_rows.T
 
 

time: 97.8 us -> 102 us (1.043)
  the two profiles are of different devices: /device:TPU:32 before, /device:TPU:24 now
where the time goes in v5:
time: 102 us
  waiting for transfers between devices  35.7 us (35%)
  starting transfers between devices  35.1 us (34%)
  Pallas kernels  29.6 us (29%)
    ppermute x6, waiting for transfers between devices, passed_along(): lax.ppermute(block, AXIS, [(i, i + distance) for i in sources if i + dist...  16.1 us
    ppermute x4, starting transfers between devices, along_z(): lax.ppermute(block, AXIS, route_of(lambda z, x, y, c: ((z + distance) % 8...  15.4 us
    pallas_call x2, Pallas kernels, attention(): pl.pallas_call(attention_kernel, grid=(steps,), out_shape=(struct(ROWS, Q...  15 us
    ppermute x6, waiting for transfers between devices, ring(): lax.ppermute(blocks[d], AXIS, route_of(functools.partial(plane_step, phas...  12.5 us
    ppermute x6, starting transfers between devices, passed_along(): lax.ppermute(block, AXIS, [(i, i + distance) for i in sources if i + dist...  11.8 us
    ppermute x6, starting transfers between devices, ring(): lax.ppermute(blocks[d], AXIS, route_of(functools.partial(plane_step, phas...  7.19 us
    ppermute x4, waiting for transfers between devices, along_z(): lax.ppermute(block, AXIS, route_of(lambda z, x, y, c: ((z + distance) % 8...  6.28 us
    pallas_call x1, Pallas kernels, middle(): pl.pallas_call(middle_kernel, grid=(STEPS,), out_shape=(jax.ShapeDtypeStr...  4.37 us
  transfers between devices with their start and end apart: 18, of which 9 were waited for; matrix products, arithmetic and copies ran while one was open for 0% of the time, Pallas kernels for 12%

profile of v5, /device:TPU:24, one launch (start us, length us, event | category | flops | bytes accessed | tf_op | source)
XLA Modules:
  0.0 101.6 jit_solution(11466753032910966085)
XLA Ops:
  0.7 2.1 %collective-permute-start = (bf16[128,1024]{1,0:T(8,128)(2,1)}, bf16[128,1024]{1,0:T(8,128)(2,1)S(1)}, u32[]{:S(2)}, u32[]{:S(2)}) collective-permute-start(bf16[128,1024]{1,0:T(8,128)(2,1)} %own_ref.3), channel_id=1, source_target_pairs={{0,1},{1,2},{2,3},{3,4},{4,5},{5,6},{6,7},{7,8},{8,9},{9,10},{10,1... | collective-permute-start | bytes 786440 | tf_op jit(solution)/shard_map/ppermute | solution.py:68
  2.7 3.1 %collective-permute-start.1 = (bf16[128,1024]{1,0:T(8,128)(2,1)}, bf16[128,1024]{1,0:T(8,128)(2,1)S(1)}, u32[]{:S(2)}, u32[]{:S(2)}) collective-permute-start(bf16[128,1024]{1,0:T(8,128)(2,1)} %own_ref.3), channel_id=1, source_target_pairs={{0,2},{2,4},{4,6},{6,8},{8,10},{10,12},{12,14},{14,16},{16,18},{18... | collective-permute-start | bytes 786440 | tf_op jit(solution)/shard_map/ppermute | solution.py:68
  5.8 3.9 %early.1 = (bf16[128,1024]{1,0:T(8,128)(2,1)S(1)}, bf16[128,1024]{1,0:T(8,128)(2,1)S(1)}) custom-call(bf16[128,1024]{1,0:T(8,128)(2,1)} %own_ref.3, bf16[128,1024]{1,0:T(8,128)(2,1)} %b_ref.1, bf16[1024,1024]{1,0:T(8,128)(2,1)} %wq_ref.3, bf16[1024,1024]{1,0:T(8,128)(2,1)} %wo_ref.3), custom_call_target="tpu_custom_call" | custom-call | tf_op jit(solution)/shard_map/early/pallas_call | solution.py:109
  9.7 1.3 %collective-permute-start.2 = (bf16[128,1024]{1,0:T(8,128)(2,1)S(1)}, bf16[128,1024]{1,0:T(8,128)(2,1)S(1)}, u32[]{:S(2)}, u32[]{:S(2)}) collective-permute-start(bf16[128,1024]{1,0:T(8,128)(2,1)S(1)} %collective-permute-done.near_ref), channel_id=1, source_target_pairs={{0,1},{2,3},{4,5},{6,7},{8,9},{10,11},{12,13},{14,15},{16,17},{18,... | collective-permute-start | bytes 786440 | tf_op jit(solution)/shard_map/ppermute | solution.py:68
  13.6 10.9 %attention.2 = (bf16[128,768]{1,0:T(8,128)(2,1)S(1)}, bf16[128,768]{1,0:T(8,128)(2,1)S(1)}, f32[2,128,384]{2,1,0:T(8,128)S(1)}, bf16[2,128,384]{2,1,0:T(8,128)(2...) custom-call(s32[5]{0:T(128)S(1)} %stack.32.place, ...), custom_call_target="tpu_custom_call" | custom-call | flops 1000 | bytes 1000 | tf_op jit(solution)/shard_map/attention/pallas_call | solution.py:255
  24.8 4.1 %attention.3 = (bf16[128,256]{1,0:T(8,128)(2,1)S(1)}, bf16[128,256]{1,0:T(8,128)(2,1)S(1)}, f32[2,128,128]{2,1,0:T(8,128)S(1)}, bf16[2,128,128]{2,1,0:T(8,128)(2...) custom-call(s32[5]{0:T(128)S(1)} %stack.32.place, ...), custom_call_target="tpu_custom_call" | custom-call | flops 1000 | bytes 1000 | tf_op jit(solution)/shard_map/attention/pallas_call | solution.py:255
  31.5 4.4 %middle.1 = (bf16[128,1024]{1,0:T(8,128)(2,1)}, f32[128,1024]{1,0:T(8,128)S(1)}) custom-call(bf16[128,768]{1,0:T(8,128)(2,1)S(1)} %get-tuple-element.71.att_one, bf16[128,256]{1,0:T(8,128)(2,1)S(1)} %get-tuple-element.85.att_two, bf16[128,768]{1,0:T(8,128)(2,1)S(1)} %get-tuple-element.86.dq_one, bf16[128,256]{1,0:T(8,128)(2,1)S(1)} %get-tuple-element.87.dq_two, ...), custom_call_target="tpu_custom_call" | custom-call | tf_op jit(solution)/shard_map/middle/pallas_call | solution.py:401
  35.9 1.6 %collective-permute-start.6 = (bf16[128,3072]{1,0:T(8,128)(2,1)S(1)}, bf16[128,3072]{1,0:T(8,128)(2,1)S(1)}, u32[]{:S(2)}, u32[]{:S(2)}) collective-permute-start(bf16[128,3072]{1,0:T(8,128)(2,1)S(1)} %get-tuple-element.98), channel_id=1, source_target_pairs={{0,8},{1,3},{2,10},{3,5},{4,12},{5,7},{6,14},{7,1},{8,16},{9,11},{... | collective-permute-start | bytes 2359304 | tf_op jit(solution)/shard_map/ppermute | solution.py:56
  38.9 1.8 %collective-permute-start.9 = (bf16[128,3072]{1,0:T(8,128)(2,1)S(1)}, bf16[128,3072]{1,0:T(8,128)(2,1)S(1)}, u32[]{:S(2)}, u32[]{:S(2)}) collective-permute-start(bf16[128,3072]{1,0:T(8,128)(2,1)S(1)} %get-tuple-element.102), channel_id=1, source_target_pairs={{0,24},{1,7},{2,26},{3,1},{4,28},{5,3},{6,30},{7,5},{8,0},{9,15},{... | collective-permute-start | bytes 2359304 | tf_op jit(solution)/shard_map/ppermute | solution.py:56
  40.7 1.5 %collective-permute-start.10 = (bf16[128,3072]{1,0:T(8,128)(2,1)S(1)}, bf16[128,3072]{1,0:T(8,128)(2,1)S(1)}, u32[]{:S(2)}, u32[]{:S(2)}) collective-permute-start(bf16[128,3072]{1,0:T(8,128)(2,1)S(1)} %get-tuple-element.103), channel_id=1, source_target_pairs={{0,16},{1,5},{2,18},{3,7},{4,20},{5,1},{6,22},{7,3},{8,24},{9,13},... | collective-permute-start | bytes 2359304 | tf_op jit(solution)/shard_map/ppermute | solution.py:56
  42.3 6.9 %collective-permute-done.6.refs_1_ = bf16[128,3072]{1,0:T(8,128)(2,1)S(1)} collective-permute-done((bf16[128,3072]{1,0:T(8,128)(2,1)S(1)}, bf16[128,3072]{1,0:T(8,128)(2,1)S(1)}, u32[]{:S(2)}, u32[]{:S(2)}) %collective-permute-start.6) | collective-permute-done | bytes 786464 | tf_op jit(solution)/shard_map/ppermute | solution.py:56
  50.5 2.8 %collective-permute-start.8 = (bf16[2,128,512]{2,1,0:T(8,128)(2,1)S(1)}, bf16[2,128,512]{2,1,0:T(8,128)(2,1)S(1)}, u32[]{:S(2)}, u32[]{:S(2)}) collective-permute-start(bf16[2,128,512]{2,1,0:T(8,128)(2,1)S(1)} %get-tuple-element.100), channel_id=1, source_target_pairs={{2,0},{4,2},{6,4},{8,6},{10,8},{12,10},{14,12},{16,14},{18,16},{20... | collective-permute-start | bytes 786440 | tf_op jit(solution)/shard_map/ppermute | solution.py:68
  53.3 3.9 %collective-permute-done.7.near = bf16[2,128,512]{2,1,0:T(8,128)(2,1)S(1)} collective-permute-done((bf16[2,128,512]{2,1,0:T(8,128)(2,1)S(1)}, bf16[2,128,512]{2,1,0:T(8,128)(2,1)S(1)}, u32[]{:S(2)}, u32[]{:S(2)}) %collective-permute-start.7) | collective-permute-done | bytes 262176 | tf_op jit(solution)/shard_map/ppermute | solution.py:68
  57.2 12.2 %collective-permute-done.8.far = bf16[2,128,512]{2,1,0:T(8,128)(2,1)S(1)} collective-permute-done((bf16[2,128,512]{2,1,0:T(8,128)(2,1)S(1)}, bf16[2,128,512]{2,1,0:T(8,128)(2,1)S(1)}, u32[]{:S(2)}, u32[]{:S(2)}) %collective-permute-start.8) | collective-permute-done | bytes 262176 | tf_op jit(solution)/shard_map/ppermute | solution.py:68
  70.0 2.0 %collective-permute-start.12 = (bf16[32,3072]{1,0:T(8,128)(2,1)S(1)}, bf16[32,3072]{1,0:T(8,128)(2,1)S(1)}, u32[]{:S(2)}, u32[]{:S(2)}) collective-permute-start(bf16[32,3072]{1,0:T(8,128)(2,1)S(1)} %get-tuple-element.110), channel_id=1, source_target_pairs={{0,6},{1,25},{2,0},{3,27},{4,2},{5,29},{6,4},{7,31},{8,14},{9,1},{... | collective-permute-start | bytes 589832 | tf_op jit(solution)/shard_map/ppermute | solution.py:56
  72.0 1.5 %tail.1 = bf16[128,1024]{1,0:T(8,128)(2,1)} custom-call(f32[128,1024]{1,0:T(8,128)S(1)} %get-tuple-element.105.base_ref, f32[2,128,384]{2,1,0:T(8,128)S(1)} %get-tuple-element.106.own_one, f32[2,128,128]{2,1,0:T(8,128)S(1)} %get-tuple-element.107.own_two, bf16[2,2,128,512]{3,2,1,0:T(8,128)(2,1)S(1)} %collective-permute-done.5.handed, ...), custom_call_target="tpu_custom_call" | custom-call | tf_op jit(solution)/shard_map/tail/pallas_call | solution.py:430
  73.6 2.1 %collective-permute-done.11.refs_1_ = bf16[32,3072]{1,0:T(8,128)(2,1)S(1)} collective-permute-done((bf16[32,3072]{1,0:T(8,128)(2,1)S(1)}, bf16[32,3072]{1,0:T(8,128)(2,1)S(1)}, u32[]{:S(2)}, u32[]{:S(2)}) %collective-permute-start.11) | collective-permute-done | bytes 196640 | tf_op jit(solution)/shard_map/ppermute | solution.py:56
  75.7 1.3 %collective-permute-done.12.refs_2_ = bf16[32,3072]{1,0:T(8,128)(2,1)S(1)} collective-permute-done((bf16[32,3072]{1,0:T(8,128)(2,1)S(1)}, bf16[32,3072]{1,0:T(8,128)(2,1)S(1)}, u32[]{:S(2)}, u32[]{:S(2)}) %collective-permute-start.12) | collective-permute-done | bytes 196640 | tf_op jit(solution)/shard_map/ppermute | solution.py:56
  77.0 2.2 %collective-permute-done.13.refs_3_ = bf16[32,3072]{1,0:T(8,128)(2,1)S(1)} collective-permute-done((bf16[32,3072]{1,0:T(8,128)(2,1)S(1)}, bf16[32,3072]{1,0:T(8,128)(2,1)S(1)}, u32[]{:S(2)}, u32[]{:S(2)}) %collective-permute-start.13) | collective-permute-done | bytes 196640 | tf_op jit(solution)/shard_map/ppermute | solution.py:56
  79.3 5.2 %collective-permute-start.14 = (bf16[8,3072]{1,0:T(8,128)(2,1)S(1)}, bf16[8,3072]{1,0:T(8,128)(2,1)S(1)}, u32[]{:S(2)}, u32[]{:S(2)}) collective-permute-start(bf16[8,3072]{1,0:T(8,128)(2,1)S(1)} %get-tuple-element.113), channel_id=1, source_target_pairs={{0,64},{1,65},{2,66},{3,67},{4,68},{5,69},{6,70},{7,71},{8,72},{9,... | collective-permute-start | bytes 147464 | tf_op jit(solution)/shard_map/ppermute | solution.py:62
  84.5 3.1 %collective-permute-start.15 = (bf16[8,3072]{1,0:T(8,128)(2,1)S(1)}, bf16[8,3072]{1,0:T(8,128)(2,1)S(1)}, u32[]{:S(2)}, u32[]{:S(2)}) collective-permute-start(bf16[8,3072]{1,0:T(8,128)(2,1)S(1)} %get-tuple-element.114), channel_id=1, source_target_pairs={{0,192},{1,193},{2,194},{3,195},{4,196},{5,197},{6,198},{7,199},{8... | collective-permute-start | bytes 147464 | tf_op jit(solution)/shard_map/ppermute | solution.py:62
  87.6 6.2 %collective-permute-start.16 = (bf16[8,3072]{1,0:T(8,128)(2,1)S(1)}, bf16[8,3072]{1,0:T(8,128)(2,1)S(1)}, u32[]{:S(2)}, u32[]{:S(2)}) collective-permute-start(bf16[8,3072]{1,0:T(8,128)(2,1)S(1)} %get-tuple-element.115), channel_id=1, source_target_pairs={{0,128},{1,129},{2,130},{3,131},{4,132},{5,133},{6,134},{7,135},{8... | collective-permute-start | bytes 147464 | tf_op jit(solution)/shard_map/ppermute | solution.py:62
  93.7 2.1 %collective-permute-done.16.c_ref = bf16[8,3072]{1,0:T(8,128)(2,1)S(1)} collective-permute-done((bf16[8,3072]{1,0:T(8,128)(2,1)S(1)}, bf16[8,3072]{1,0:T(8,128)(2,1)S(1)}, u32[]{:S(2)}, u32[]{:S(2)}) %collective-permute-start.16) | collective-permute-done | bytes 49184 | tf_op jit(solution)/shard_map/ppermute | solution.py:62
  96.8 4.2 %collective-permute-done.17.got_ref = bf16[4,3072]{1,0:T(4,128)(2,1)S(1)} collective-permute-done((bf16[4,3072]{1,0:T(4,128)(2,1)S(1)}, bf16[4,3072]{1,0:T(4,128)(2,1)S(1)}, u32[]{:S(2)}, u32[]{:S(2)}) %collective-permute-start.17) | collective-permute-done | bytes 24608 | tf_op jit(solution)/shard_map/ppermute | solution.py:62
  (39 shorter events, 10.4 us)
Async XLA Ops:
  0.6 10.5 %copy-start.2 = (bf16[128,1024]{1,0:T(8,128)(2,1)S(1)}, bf16[128,1024]{1,0:T(8,128)(2,1)}, u32[]{:S(2)}) copy-start(bf16[128,1024]{1,0:T(8,128)(2,1)} %own_ref.3) | copy-start | bytes 786436
  0.6 10.5 %copy-start.3 = (bf16[128,1024]{1,0:T(8,128)(2,1)S(1)}, bf16[128,1024]{1,0:T(8,128)(2,1)}, u32[]{:S(2)}) copy-start(bf16[128,1024]{1,0:T(8,128)(2,1)} %b_ref.1) | copy-start | bytes 786436
  0.7 9.0 %collective-permute-start = (bf16[128,1024]{1,0:T(8,128)(2,1)}, bf16[128,1024]{1,0:T(8,128)(2,1)S(1)}, u32[]{:S(2)}, u32[]{:S(2)}) collective-permute-start(bf16[128,1024]{1,0:T(8,128)(2,1)} %own_ref.3), channel_id=1, source_target_pairs={{0,1},{1,2},{2,3},{3,4},{4,5},{5,6},{6,7},{7,8},{8,9},{9,10},{10,1... | collective-permute-start | bytes 786440 | tf_op jit(solution)/shard_map/ppermute | solution.py:68
  2.7 9.7 %collective-permute-start.1 = (bf16[128,1024]{1,0:T(8,128)(2,1)}, bf16[128,1024]{1,0:T(8,128)(2,1)S(1)}, u32[]{:S(2)}, u32[]{:S(2)}) collective-permute-start(bf16[128,1024]{1,0:T(8,128)(2,1)} %own_ref.3), channel_id=1, source_target_pairs={{0,2},{2,4},{4,6},{6,8},{8,10},{10,12},{12,14},{14,16},{16,18},{18... | collective-permute-start | bytes 786440 | tf_op jit(solution)/shard_map/ppermute | solution.py:68
  9.7 2.7 %collective-permute-start.2 = (bf16[128,1024]{1,0:T(8,128)(2,1)S(1)}, bf16[128,1024]{1,0:T(8,128)(2,1)S(1)}, u32[]{:S(2)}, u32[]{:S(2)}) collective-permute-start(bf16[128,1024]{1,0:T(8,128)(2,1)S(1)} %collective-permute-done.near_ref), channel_id=1, source_target_pairs={{0,1},{2,3},{4,5},{6,7},{8,9},{10,11},{12,13},{14,15},{16,17},{18,... | collective-permute-start | bytes 786440 | tf_op jit(solution)/shard_map/ppermute | solution.py:68
  24.6 4.8 %collective-permute-start.4 = (bf16[512,2304]{1,0:T(8,128)(2,1)S(1)}, bf16[512,2304]{1,0:T(8,128)(2,1)S(1)}, u32[]{:S(2)}, u32[]{:S(2)}) collective-permute-start(bf16[512,2304]{1,0:T(8,128)(2,1)S(1)} %get-tuple-element.77), channel_id=1, source_target_pairs={{0,1},{1,0},{2,3},{3,2},{4,5},{5,4},{6,7},{7,6},{8,9},{9,8},{10,11... | collective-permute-start | bytes 7077896 | tf_op jit(solution)/shard_map/ppermute | solution.py:45
  28.9 2.4 %collective-permute-start.3 = (bf16[512,768]{1,0:T(8,128)(2,1)S(1)}, bf16[512,768]{1,0:T(8,128)(2,1)S(1)}, u32[]{:S(2)}, u32[]{:S(2)}) collective-permute-start(bf16[512,768]{1,0:T(8,128)(2,1)S(1)} %get-tuple-element.76), channel_id=1, source_target_pairs={{0,1},{1,0},{2,3},{3,2},{4,5},{5,4},{6,7},{7,6},{8,9},{9,8},{10,11... | collective-permute-start | bytes 2359304 | tf_op jit(solution)/shard_map/ppermute | solution.py:45
  35.9 13.3 %collective-permute-start.6 = (bf16[128,3072]{1,0:T(8,128)(2,1)S(1)}, bf16[128,3072]{1,0:T(8,128)(2,1)S(1)}, u32[]{:S(2)}, u32[]{:S(2)}) collective-permute-start(bf16[128,3072]{1,0:T(8,128)(2,1)S(1)} %get-tuple-element.98), channel_id=1, source_target_pairs={{0,8},{1,3},{2,10},{3,5},{4,12},{5,7},{6,14},{7,1},{8,16},{9,11},{... | collective-permute-start | bytes 2359304 | tf_op jit(solution)/shard_map/ppermute | solution.py:56
  37.6 4.6 %collective-permute-start.5 = (bf16[2,2,128,512]{3,2,1,0:T(8,128)(2,1)S(1)}, bf16[2,2,128,512]{3,2,1,0:T(8,128)(2,1)S(1)}, u32[]{:S(2)}, u32[]{:S(2)}) collective-permute-start(bf16[2,2,128,512]{3,2,1,0:T(8,128)(2,1)S(1)} %pad_maximum_fusion), channel_id=1, source_target_pairs={{1,0},{3,2},{5,4},{7,6},{9,8},{11,10},{13,12},{15,14},{17,16},{19,... | collective-permute-start | bytes 1572872 | tf_op jit(solution)/shard_map/ppermute | solution.py:68
  38.9 30.5 %collective-permute-start.9 = (bf16[128,3072]{1,0:T(8,128)(2,1)S(1)}, bf16[128,3072]{1,0:T(8,128)(2,1)S(1)}, u32[]{:S(2)}, u32[]{:S(2)}) collective-permute-start(bf16[128,3072]{1,0:T(8,128)(2,1)S(1)} %get-tuple-element.102), channel_id=1, source_target_pairs={{0,24},{1,7},{2,26},{3,1},{4,28},{5,3},{6,30},{7,5},{8,0},{9,15},{... | collective-permute-start | bytes 2359304 | tf_op jit(solution)/shard_map/ppermute | solution.py:56
  40.7 28.7 %collective-permute-start.10 = (bf16[128,3072]{1,0:T(8,128)(2,1)S(1)}, bf16[128,3072]{1,0:T(8,128)(2,1)S(1)}, u32[]{:S(2)}, u32[]{:S(2)}) collective-permute-start(bf16[128,3072]{1,0:T(8,128)(2,1)S(1)} %get-tuple-element.103), channel_id=1, source_target_pairs={{0,16},{1,5},{2,18},{3,7},{4,20},{5,1},{6,22},{7,3},{8,24},{9,13},... | collective-permute-start | bytes 2359304 | tf_op jit(solution)/shard_map/ppermute | solution.py:56
  42.3 29.7 %copy-start = (bf16[1024,512]{1,0:T(8,128)(2,1)S(1)}, bf16[1024,512]{1,0:T(8,128)(2,1)}, u32[]{:S(2)}) copy-start(bf16[1024,512]{1,0:T(8,128)(2,1)} %wk_ref.5) | copy-start | bytes 3145732
  42.3 29.7 %copy-start.1 = (bf16[1024,512]{1,0:T(8,128)(2,1)S(1)}, bf16[1024,512]{1,0:T(8,128)(2,1)}, u32[]{:S(2)}) copy-start(bf16[1024,512]{1,0:T(8,128)(2,1)} %wv_ref.5) | copy-start | bytes 3145732
  49.2 8.0 %collective-permute-start.7 = (bf16[2,128,512]{2,1,0:T(8,128)(2,1)S(1)}, bf16[2,128,512]{2,1,0:T(8,128)(2,1)S(1)}, u32[]{:S(2)}, u32[]{:S(2)}) collective-permute-start(bf16[2,128,512]{2,1,0:T(8,128)(2,1)S(1)} %fusion), channel_id=1, source_target_pairs={{2,1},{4,3},{6,5},{8,7},{10,9},{12,11},{14,13},{16,15},{18,17},{20... | collective-permute-start | bytes 786440 | tf_op jit(solution)/shard_map/ppermute | solution.py:68
  50.5 18.9 %collective-permute-start.8 = (bf16[2,128,512]{2,1,0:T(8,128)(2,1)S(1)}, bf16[2,128,512]{2,1,0:T(8,128)(2,1)S(1)}, u32[]{:S(2)}, u32[]{:S(2)}) collective-permute-start(bf16[2,128,512]{2,1,0:T(8,128)(2,1)S(1)} %get-tuple-element.100), channel_id=1, source_target_pairs={{2,0},{4,2},{6,4},{8,6},{10,8},{12,10},{14,12},{16,14},{18,16},{20... | collective-permute-start | bytes 786440 | tf_op jit(solution)/shard_map/ppermute | solution.py:68
  69.7 5.9 %collective-permute-start.11 = (bf16[32,3072]{1,0:T(8,128)(2,1)S(1)}, bf16[32,3072]{1,0:T(8,128)(2,1)S(1)}, u32[]{:S(2)}, u32[]{:S(2)}) collective-permute-start(bf16[32,3072]{1,0:T(8,128)(2,1)S(1)} %get-tuple-element.109), channel_id=1, source_target_pairs={{0,2},{1,9},{2,4},{3,11},{4,6},{5,13},{6,0},{7,15},{8,10},{9,17},{... | collective-permute-start | bytes 589832 | tf_op jit(solution)/shard_map/ppermute | solution.py:56
  70.0 7.0 %collective-permute-start.12 = (bf16[32,3072]{1,0:T(8,128)(2,1)S(1)}, bf16[32,3072]{1,0:T(8,128)(2,1)S(1)}, u32[]{:S(2)}, u32[]{:S(2)}) collective-permute-start(bf16[32,3072]{1,0:T(8,128)(2,1)S(1)} %get-tuple-element.110), channel_id=1, source_target_pairs={{0,6},{1,25},{2,0},{3,27},{4,2},{5,29},{6,4},{7,31},{8,14},{9,1},{... | collective-permute-start | bytes 589832 | tf_op jit(solution)/shard_map/ppermute | solution.py:56
  72.0 7.2 %collective-permute-start.13 = (bf16[32,3072]{1,0:T(8,128)(2,1)S(1)}, bf16[32,3072]{1,0:T(8,128)(2,1)S(1)}, u32[]{:S(2)}, u32[]{:S(2)}) collective-permute-start(bf16[32,3072]{1,0:T(8,128)(2,1)S(1)} %get-tuple-element.111), channel_id=1, source_target_pairs={{0,4},{1,17},{2,6},{3,19},{4,0},{5,21},{6,2},{7,23},{8,12},{9,25},... | collective-permute-start | bytes 589832 | tf_op jit(solution)/shard_map/ppermute | solution.py:56
  79.3 14.5 %collective-permute-start.14 = (bf16[8,3072]{1,0:T(8,128)(2,1)S(1)}, bf16[8,3072]{1,0:T(8,128)(2,1)S(1)}, u32[]{:S(2)}, u32[]{:S(2)}) collective-permute-start(bf16[8,3072]{1,0:T(8,128)(2,1)S(1)} %get-tuple-element.113), channel_id=1, source_target_pairs={{0,64},{1,65},{2,66},{3,67},{4,68},{5,69},{6,70},{7,71},{8,72},{9,... | collective-permute-start | bytes 147464 | tf_op jit(solution)/shard_map/ppermute | solution.py:62
  84.5 9.3 %collective-permute-start.15 = (bf16[8,3072]{1,0:T(8,128)(2,1)S(1)}, bf16[8,3072]{1,0:T(8,128)(2,1)S(1)}, u32[]{:S(2)}, u32[]{:S(2)}) collective-permute-start(bf16[8,3072]{1,0:T(8,128)(2,1)S(1)} %get-tuple-element.114), channel_id=1, source_target_pairs={{0,192},{1,193},{2,194},{3,195},{4,196},{5,197},{6,198},{7,199},{8... | collective-permute-start | bytes 147464 | tf_op jit(solution)/shard_map/ppermute | solution.py:62
  87.6 8.3 %collective-permute-start.16 = (bf16[8,3072]{1,0:T(8,128)(2,1)S(1)}, bf16[8,3072]{1,0:T(8,128)(2,1)S(1)}, u32[]{:S(2)}, u32[]{:S(2)}) collective-permute-start(bf16[8,3072]{1,0:T(8,128)(2,1)S(1)} %get-tuple-element.115), channel_id=1, source_target_pairs={{0,128},{1,129},{2,130},{3,131},{4,132},{5,133},{6,134},{7,135},{8... | collective-permute-start | bytes 147464 | tf_op jit(solution)/shard_map/ppermute | solution.py:62
  95.9 5.1 %collective-permute-start.17 = (bf16[4,3072]{1,0:T(4,128)(2,1)S(1)}, bf16[4,3072]{1,0:T(4,128)(2,1)S(1)}, u32[]{:S(2)}, u32[]{:S(2)}) collective-permute-start(bf16[4,3072]{1,0:T(4,128)(2,1)S(1)} %get-tuple-element.117), channel_id=1, source_target_pairs={{0,32},{1,33},{2,34},{3,35},{4,36},{5,37},{6,38},{7,39},{8,40},{9,... | collective-permute-start | bytes 73736 | tf_op jit(solution)/shard_map/ppermute | solution.py:62

commit v6 on v5

--- a/solution.py
+++ b/solution.py
@@ -467,25 +467,21 @@
     ring_one = ring([None, *sends], 0)
 
     attn_out, base = middle((one[0], after(two[0], own)), (one[1], two[1]), wo, wq)
-    grads = lax.optimization_barrier((one[3], two[3], one[4], two[4], base))
+    grads = lax.optimization_barrier((one[3], two[3], one[4], two[4], ring_one[0]))
     near_grad = jnp.concatenate(grads[0:2], axis=-1)
     far_grad = jnp.concatenate(grads[2:4], axis=-1)
     handed = passed_along(jnp.stack([near_grad, far_grad]), -1, range(1, 256, 2))
     summed = (near_grad.astype(F32) + handed[1].astype(F32)).astype(BF16)
-
-    back_near = passed_along(after(summed, ring_one[0]), -1, range(0, 256, 2))
-    back_far = passed_along(after(far_grad, ring_one[0]), -2, range(0, 256, 2))
-
-    own, *sends = folded(after(own, base, back_near, back_far), *ring_one)
+    own, *sends = folded(after(own, base, summed), *ring_one)
     ring_two = ring([None, *sends], 1)
-    tokens_grad = tail(
-        after(base, own), one[2], two[2], handed, back_near, back_far, key_weight, value_matrix
-    )
-    own, *sends = folded(after(own, tokens_grad), *ring_two)
+    back_near = passed_along(after(summed, own), -1, range(0, 256, 2))
+    back_far = passed_along(after(far_grad, own), -2, range(0, 256, 2))
+    own, *sends = folded(own, *ring_two)
     ring_three = [along_z(sends[d - 1], 2 * d) for d in (1, 3, 2)]
     own, send = halved(own, *ring_three)
     got = along_z(send, 1)
-    query_rows, key_rows, value_rows, out_rows = summed_last(own, got)
+    tokens_grad = tail(base, one[2], two[2], handed, back_near, back_far, key_weight, value_matrix)
+    query_rows, key_rows, value_rows, out_rows = summed_last(after(own, tokens_grad), got)
     return attn_out, tokens_grad, query_rows, key_rows, value_rows, out_rows.T
 
 

time: 102 us -> 99 us (0.971)
  waiting for transfers between devices: 35.7 us -> 19.5 us
  starting transfers between devices: 35.1 us -> 48.2 us
    ppermute x6, waiting for transfers between devices: 16.1 us -> 0.02 us  [passed_along(): lax.ppermute(block, AXIS, [(i, i + distance) for i in sources if i + dist...]
    ppermute x4, starting transfers between devices: 15.4 us -> 26.3 us  [along_z(): lax.ppermute(block, AXIS, route_of(lambda z, x, y, c: ((z + distance) % 8...]
    ppermute x4, waiting for transfers between devices: 6.28 us -> 4.74 us  [along_z(): lax.ppermute(block, AXIS, route_of(lambda z, x, y, c: ((z + distance) % 8...]
    ppermute x6, waiting for transfers between devices: 12.5 us -> 13.9 us  [ring(): lax.ppermute(blocks[d], AXIS, route_of(functools.partial(plane_step, phas...]
    ppermute x6, starting transfers between devices: 7.19 us -> 8.44 us  [ring(): lax.ppermute(blocks[d], AXIS, route_of(functools.partial(plane_step, phas...]
    ppermute x6, starting transfers between devices: 11.8 us -> 12.9 us  [passed_along(): lax.ppermute(block, AXIS, [(i, i + distance) for i in sources if i + dist...]
  transfers between devices with their start and end apart: 18 -> 18, of which waited for: 9 -> 6; matrix products, arithmetic and copies ran while one was open for 0% -> 0% of each run, Pallas kernels for 12% -> 17%
where the time goes in v6:
time: 99 us; the launch traced here: 98.6 us
  starting transfers between devices  48.2 us (49%)
  Pallas kernels  29.6 us (30%)
  waiting for transfers between devices  19.5 us (20%)
    ppermute x4, starting transfers between devices, along_z(): lax.ppermute(block, AXIS, route_of(lambda z, x, y, c: ((z + distance) % 8...  26.3 us
    pallas_call x2, Pallas kernels, attention(): pl.pallas_call(attention_kernel, grid=(steps,), out_shape=(struct(ROWS, Q...  15 us
    ppermute x6, waiting for transfers between devices, ring(): lax.ppermute(blocks[d], AXIS, route_of(functools.partial(plane_step, phas...  13.9 us
    ppermute x6, starting transfers between devices, passed_along(): lax.ppermute(block, AXIS, [(i, i + distance) for i in sources if i + dist...  12.9 us
    ppermute x6, starting transfers between devices, ring(): lax.ppermute(blocks[d], AXIS, route_of(functools.partial(plane_step, phas...  8.44 us
    ppermute x4, waiting for transfers between devices, along_z(): lax.ppermute(block, AXIS, route_of(lambda z, x, y, c: ((z + distance) % 8...  4.74 us
    pallas_call x1, Pallas kernels, middle(): pl.pallas_call(middle_kernel, grid=(STEPS,), out_shape=(jax.ShapeDtypeStr...  4.37 us
    pallas_call x1, Pallas kernels, early(): pl.pallas_call(early_kernel, grid=(STEPS,), out_shape=(jax.ShapeDtypeStru...  3.9 us
  transfers between devices with their start and end apart: 18, of which 6 were waited for; matrix products, arithmetic and copies ran while one was open for 0% of the time, Pallas kernels for 17%

profile of v6, /device:TPU:24, one launch (start us, length us, event | category | flops | bytes accessed | tf_op | source)
XLA Modules:
  0.0 98.6 jit_solution(15690374688111019737)
XLA Ops:
  0.7 2.1 %collective-permute-start = (bf16[128,1024]{1,0:T(8,128)(2,1)}, bf16[128,1024]{1,0:T(8,128)(2,1)S(1)}, u32[]{:S(2)}, u32[]{:S(2)}) collective-permute-start(bf16[128,1024]{1,0:T(8,128)(2,1)} %own_ref.3), channel_id=1, source_target_pairs={{0,1},{1,2},{2,3},{3,4},{4,5},{5,6},{6,7},{7,8},{8,9},{9,10},{10,1... | collective-permute-start | bytes 786440 | tf_op jit(solution)/shard_map/ppermute | solution.py:68
  2.7 3.1 %collective-permute-start.1 = (bf16[128,1024]{1,0:T(8,128)(2,1)}, bf16[128,1024]{1,0:T(8,128)(2,1)S(1)}, u32[]{:S(2)}, u32[]{:S(2)}) collective-permute-start(bf16[128,1024]{1,0:T(8,128)(2,1)} %own_ref.3), channel_id=1, source_target_pairs={{0,2},{2,4},{4,6},{6,8},{8,10},{10,12},{12,14},{14,16},{16,18},{18... | collective-permute-start | bytes 786440 | tf_op jit(solution)/shard_map/ppermute | solution.py:68
  5.8 3.9 %early.1 = (bf16[128,1024]{1,0:T(8,128)(2,1)S(1)}, bf16[128,1024]{1,0:T(8,128)(2,1)S(1)}) custom-call(bf16[128,1024]{1,0:T(8,128)(2,1)} %own_ref.3, bf16[128,1024]{1,0:T(8,128)(2,1)} %b_ref.1, bf16[1024,1024]{1,0:T(8,128)(2,1)} %wq_ref.3, bf16[1024,1024]{1,0:T(8,128)(2,1)} %wo_ref.3), custom_call_target="tpu_custom_call" | custom-call | tf_op jit(solution)/shard_map/early/pallas_call | solution.py:109
  9.7 1.3 %collective-permute-start.2 = (bf16[128,1024]{1,0:T(8,128)(2,1)S(1)}, bf16[128,1024]{1,0:T(8,128)(2,1)S(1)}, u32[]{:S(2)}, u32[]{:S(2)}) collective-permute-start(bf16[128,1024]{1,0:T(8,128)(2,1)S(1)} %collective-permute-done.near_ref), channel_id=1, source_target_pairs={{0,1},{2,3},{4,5},{6,7},{8,9},{10,11},{12,13},{14,15},{16,17},{18,... | collective-permute-start | bytes 786440 | tf_op jit(solution)/shard_map/ppermute | solution.py:68
  13.6 10.9 %attention.2 = (bf16[128,768]{1,0:T(8,128)(2,1)S(1)}, bf16[128,768]{1,0:T(8,128)(2,1)S(1)}, f32[2,128,384]{2,1,0:T(8,128)S(1)}, bf16[2,128,384]{2,1,0:T(8,128)(2...) custom-call(s32[5]{0:T(128)S(1)} %stack.32.place, ...), custom_call_target="tpu_custom_call" | custom-call | flops 1000 | bytes 1000 | tf_op jit(solution)/shard_map/attention/pallas_call | solution.py:255
  24.8 4.1 %attention.3 = (bf16[128,256]{1,0:T(8,128)(2,1)S(1)}, bf16[128,256]{1,0:T(8,128)(2,1)S(1)}, f32[2,128,128]{2,1,0:T(8,128)S(1)}, bf16[2,128,128]{2,1,0:T(8,128)(2...) custom-call(s32[5]{0:T(128)S(1)} %stack.32.place, ...), custom_call_target="tpu_custom_call" | custom-call | flops 1000 | bytes 1000 | tf_op jit(solution)/shard_map/attention/pallas_call | solution.py:255
  31.5 1.6 %collective-permute-start.5 = (bf16[128,3072]{1,0:T(8,128)(2,1)S(1)}, bf16[128,3072]{1,0:T(8,128)(2,1)S(1)}, u32[]{:S(2)}, u32[]{:S(2)}) collective-permute-start(bf16[128,3072]{1,0:T(8,128)(2,1)S(1)} %get-tuple-element.95), channel_id=1, source_target_pairs={{0,8},{1,3},{2,10},{3,5},{4,12},{5,7},{6,14},{7,1},{8,16},{9,11},{... | collective-permute-start | bytes 2359304 | tf_op jit(solution)/shard_map/ppermute | solution.py:56
  33.0 1.7 %collective-permute-start.7 = (bf16[128,3072]{1,0:T(8,128)(2,1)S(1)}, bf16[128,3072]{1,0:T(8,128)(2,1)S(1)}, u32[]{:S(2)}, u32[]{:S(2)}) collective-permute-start(bf16[128,3072]{1,0:T(8,128)(2,1)S(1)} %get-tuple-element.101), channel_id=1, source_target_pairs={{0,24},{1,7},{2,26},{3,1},{4,28},{5,3},{6,30},{7,5},{8,0},{9,15},{... | collective-permute-start | bytes 2359304 | tf_op jit(solution)/shard_map/ppermute | solution.py:56
  34.8 1.5 %collective-permute-start.8 = (bf16[128,3072]{1,0:T(8,128)(2,1)S(1)}, bf16[128,3072]{1,0:T(8,128)(2,1)S(1)}, u32[]{:S(2)}, u32[]{:S(2)}) collective-permute-start(bf16[128,3072]{1,0:T(8,128)(2,1)S(1)} %get-tuple-element.102), channel_id=1, source_target_pairs={{0,16},{1,5},{2,18},{3,7},{4,20},{5,1},{6,22},{7,3},{8,24},{9,13},... | collective-permute-start | bytes 2359304 | tf_op jit(solution)/shard_map/ppermute | solution.py:56
  36.3 8.4 %collective-permute-done.5.refs_1_ = bf16[128,3072]{1,0:T(8,128)(2,1)S(1)} collective-permute-done((bf16[128,3072]{1,0:T(8,128)(2,1)S(1)}, bf16[128,3072]{1,0:T(8,128)(2,1)S(1)}, u32[]{:S(2)}, u32[]{:S(2)}) %collective-permute-start.5) | collective-permute-done | bytes 786464 | tf_op jit(solution)/shard_map/ppermute | solution.py:56
  44.9 1.3 %collective-permute-start.6 = (bf16[2,2,128,512]{3,2,1,0:T(8,128)(2,1)S(1)}, bf16[2,2,128,512]{3,2,1,0:T(8,128)(2,1)S(1)}, u32[]{:S(2)}, u32[]{:S(2)}) collective-permute-start(bf16[2,2,128,512]{3,2,1,0:T(8,128)(2,1)S(1)} %pad_maximum_fusion), channel_id=1, source_target_pairs={{1,0},{3,2},{5,4},{7,6},{9,8},{11,10},{13,12},{15,14},{17,16},{19,... | collective-permute-start | bytes 1572872 | tf_op jit(solution)/shard_map/ppermute | solution.py:68
  46.2 4.4 %middle.1 = (bf16[128,1024]{1,0:T(8,128)(2,1)}, f32[128,1024]{1,0:T(8,128)S(1)}) custom-call(bf16[128,768]{1,0:T(8,128)(2,1)S(1)} %get-tuple-element.70.att_one, bf16[128,256]{1,0:T(8,128)(2,1)S(1)} %get-tuple-element.84.att_two, bf16[128,768]{1,0:T(8,128)(2,1)S(1)} %get-tuple-element.85.dq_one, bf16[128,256]{1,0:T(8,128)(2,1)S(1)} %get-tuple-element.86.dq_two, ...), custom_call_target="tpu_custom_call" | custom-call | tf_op jit(solution)/shard_map/middle/pallas_call | solution.py:401
  50.7 3.8 %collective-permute-done.8.refs_3_ = bf16[128,3072]{1,0:T(8,128)(2,1)S(1)} collective-permute-done((bf16[128,3072]{1,0:T(8,128)(2,1)S(1)}, bf16[128,3072]{1,0:T(8,128)(2,1)S(1)}, u32[]{:S(2)}, u32[]{:S(2)}) %collective-permute-start.8) | collective-permute-done | bytes 786464 | tf_op jit(solution)/shard_map/ppermute | solution.py:56
  54.8 1.5 %collective-permute-start.11 = (bf16[32,3072]{1,0:T(8,128)(2,1)S(1)}, bf16[32,3072]{1,0:T(8,128)(2,1)S(1)}, u32[]{:S(2)}, u32[]{:S(2)}) collective-permute-start(bf16[32,3072]{1,0:T(8,128)(2,1)S(1)} %get-tuple-element.106), channel_id=1, source_target_pairs={{0,2},{1,9},{2,4},{3,11},{4,6},{5,13},{6,0},{7,15},{8,10},{9,17},{... | collective-permute-start | bytes 589832 | tf_op jit(solution)/shard_map/ppermute | solution.py:56
  57.1 1.3 %collective-permute-start.13 = (bf16[32,3072]{1,0:T(8,128)(2,1)S(1)}, bf16[32,3072]{1,0:T(8,128)(2,1)S(1)}, u32[]{:S(2)}, u32[]{:S(2)}) collective-permute-start(bf16[32,3072]{1,0:T(8,128)(2,1)S(1)} %get-tuple-element.108), channel_id=1, source_target_pairs={{0,4},{1,17},{2,6},{3,19},{4,0},{5,21},{6,2},{7,23},{8,12},{9,25},... | collective-permute-start | bytes 589832 | tf_op jit(solution)/shard_map/ppermute | solution.py:56
  58.4 1.3 %collective-permute-start.9 = (bf16[2,128,512]{2,1,0:T(8,128)(2,1)S(1)}, bf16[2,128,512]{2,1,0:T(8,128)(2,1)S(1)}, u32[]{:S(2)}, u32[]{:S(2)}) collective-permute-start(bf16[2,128,512]{2,1,0:T(8,128)(2,1)S(1)} %fusion), channel_id=1, source_target_pairs={{2,1},{4,3},{6,5},{8,7},{10,9},{12,11},{14,13},{16,15},{18,17},{20... | collective-permute-start | bytes 786440 | tf_op jit(solution)/shard_map/ppermute | solution.py:68
  59.7 3.9 %collective-permute-start.10 = (bf16[2,128,512]{2,1,0:T(8,128)(2,1)S(1)}, bf16[2,128,512]{2,1,0:T(8,128)(2,1)S(1)}, u32[]{:S(2)}, u32[]{:S(2)}) collective-permute-start(bf16[2,128,512]{2,1,0:T(8,128)(2,1)S(1)} %get-tuple-element.105), channel_id=1, source_target_pairs={{2,0},{4,2},{6,4},{8,6},{10,8},{12,10},{14,12},{16,14},{18,16},{20... | collective-permute-start | bytes 786440 | tf_op jit(solution)/shard_map/ppermute | solution.py:68
  63.6 1.7 %collective-permute-done.12.refs_2_ = bf16[32,3072]{1,0:T(8,128)(2,1)S(1)} collective-permute-done((bf16[32,3072]{1,0:T(8,128)(2,1)S(1)}, bf16[32,3072]{1,0:T(8,128)(2,1)S(1)}, u32[]{:S(2)}, u32[]{:S(2)}) %collective-permute-start.12) | collective-permute-done | bytes 196640 | tf_op jit(solution)/shard_map/ppermute | solution.py:56
  65.4 16.1 %collective-permute-start.14 = (bf16[8,3072]{1,0:T(8,128)(2,1)S(1)}, bf16[8,3072]{1,0:T(8,128)(2,1)S(1)}, u32[]{:S(2)}, u32[]{:S(2)}) collective-permute-start(bf16[8,3072]{1,0:T(8,128)(2,1)S(1)} %get-tuple-element.110), channel_id=1, source_target_pairs={{0,64},{1,65},{2,66},{3,67},{4,68},{5,69},{6,70},{7,71},{8,72},{9,... | collective-permute-start | bytes 147464 | tf_op jit(solution)/shard_map/ppermute | solution.py:62
  81.4 3.1 %collective-permute-start.15 = (bf16[8,3072]{1,0:T(8,128)(2,1)S(1)}, bf16[8,3072]{1,0:T(8,128)(2,1)S(1)}, u32[]{:S(2)}, u32[]{:S(2)}) collective-permute-start(bf16[8,3072]{1,0:T(8,128)(2,1)S(1)} %get-tuple-element.111), channel_id=1, source_target_pairs={{0,192},{1,193},{2,194},{3,195},{4,196},{5,197},{6,198},{7,199},{8... | collective-permute-start | bytes 147464 | tf_op jit(solution)/shard_map/ppermute | solution.py:62
  84.5 6.1 %collective-permute-start.16 = (bf16[8,3072]{1,0:T(8,128)(2,1)S(1)}, bf16[8,3072]{1,0:T(8,128)(2,1)S(1)}, u32[]{:S(2)}, u32[]{:S(2)}) collective-permute-start(bf16[8,3072]{1,0:T(8,128)(2,1)S(1)} %get-tuple-element.112), channel_id=1, source_target_pairs={{0,128},{1,129},{2,130},{3,131},{4,132},{5,133},{6,134},{7,135},{8... | collective-permute-start | bytes 147464 | tf_op jit(solution)/shard_map/ppermute | solution.py:62
  90.7 2.1 %collective-permute-done.16.c_ref = bf16[8,3072]{1,0:T(8,128)(2,1)S(1)} collective-permute-done((bf16[8,3072]{1,0:T(8,128)(2,1)S(1)}, bf16[8,3072]{1,0:T(8,128)(2,1)S(1)}, u32[]{:S(2)}, u32[]{:S(2)}) %collective-permute-start.16) | collective-permute-done | bytes 49184 | tf_op jit(solution)/shard_map/ppermute | solution.py:62
  93.8 1.5 %tail.1 = bf16[128,1024]{1,0:T(8,128)(2,1)} custom-call(f32[128,1024]{1,0:T(8,128)S(1)} %get-tuple-element.88.base_ref, f32[2,128,384]{2,1,0:T(8,128)S(1)} %get-tuple-element.89.own_one, f32[2,128,128]{2,1,0:T(8,128)S(1)} %get-tuple-element.90.own_two, bf16[2,2,128,512]{3,2,1,0:T(8,128)(2,1)S(1)} %collective-permute-done.6.handed, ...), custom_call_target="tpu_custom_call" | custom-call | tf_op jit(solution)/shard_map/tail/pallas_call | solution.py:430
  95.3 2.6 %collective-permute-done.17.got_ref = bf16[4,3072]{1,0:T(4,128)(2,1)S(1)} collective-permute-done((bf16[4,3072]{1,0:T(4,128)(2,1)S(1)}, bf16[4,3072]{1,0:T(4,128)(2,1)S(1)}, u32[]{:S(2)}, u32[]{:S(2)}) %collective-permute-start.17) | collective-permute-done | bytes 24608 | tf_op jit(solution)/shard_map/ppermute | solution.py:62
  (39 shorter events, 8.4 us)
Async XLA Ops:
  0.6 10.5 %copy-start.2 = (bf16[128,1024]{1,0:T(8,128)(2,1)S(1)}, bf16[128,1024]{1,0:T(8,128)(2,1)}, u32[]{:S(2)}) copy-start(bf16[128,1024]{1,0:T(8,128)(2,1)} %own_ref.3) | copy-start | bytes 786436
  0.6 10.5 %copy-start.3 = (bf16[128,1024]{1,0:T(8,128)(2,1)S(1)}, bf16[128,1024]{1,0:T(8,128)(2,1)}, u32[]{:S(2)}) copy-start(bf16[128,1024]{1,0:T(8,128)(2,1)} %b_ref.1) | copy-start | bytes 786436
  0.7 9.0 %collective-permute-start = (bf16[128,1024]{1,0:T(8,128)(2,1)}, bf16[128,1024]{1,0:T(8,128)(2,1)S(1)}, u32[]{:S(2)}, u32[]{:S(2)}) collective-permute-start(bf16[128,1024]{1,0:T(8,128)(2,1)} %own_ref.3), channel_id=1, source_target_pairs={{0,1},{1,2},{2,3},{3,4},{4,5},{5,6},{6,7},{7,8},{8,9},{9,10},{10,1... | collective-permute-start | bytes 786440 | tf_op jit(solution)/shard_map/ppermute | solution.py:68
  2.7 9.7 %collective-permute-start.1 = (bf16[128,1024]{1,0:T(8,128)(2,1)}, bf16[128,1024]{1,0:T(8,128)(2,1)S(1)}, u32[]{:S(2)}, u32[]{:S(2)}) collective-permute-start(bf16[128,1024]{1,0:T(8,128)(2,1)} %own_ref.3), channel_id=1, source_target_pairs={{0,2},{2,4},{4,6},{6,8},{8,10},{10,12},{12,14},{14,16},{16,18},{18... | collective-permute-start | bytes 786440 | tf_op jit(solution)/shard_map/ppermute | solution.py:68
  9.7 2.7 %collective-permute-start.2 = (bf16[128,1024]{1,0:T(8,128)(2,1)S(1)}, bf16[128,1024]{1,0:T(8,128)(2,1)S(1)}, u32[]{:S(2)}, u32[]{:S(2)}) collective-permute-start(bf16[128,1024]{1,0:T(8,128)(2,1)S(1)} %collective-permute-done.near_ref), channel_id=1, source_target_pairs={{0,1},{2,3},{4,5},{6,7},{8,9},{10,11},{12,13},{14,15},{16,17},{18,... | collective-permute-start | bytes 786440 | tf_op jit(solution)/shard_map/ppermute | solution.py:68
  24.6 4.8 %collective-permute-start.4 = (bf16[512,2304]{1,0:T(8,128)(2,1)S(1)}, bf16[512,2304]{1,0:T(8,128)(2,1)S(1)}, u32[]{:S(2)}, u32[]{:S(2)}) collective-permute-start(bf16[512,2304]{1,0:T(8,128)(2,1)S(1)} %get-tuple-element.76), channel_id=1, source_target_pairs={{0,1},{1,0},{2,3},{3,2},{4,5},{5,4},{6,7},{7,6},{8,9},{9,8},{10,11... | collective-permute-start | bytes 7077896 | tf_op jit(solution)/shard_map/ppermute | solution.py:45
  28.9 2.4 %collective-permute-start.3 = (bf16[512,768]{1,0:T(8,128)(2,1)S(1)}, bf16[512,768]{1,0:T(8,128)(2,1)S(1)}, u32[]{:S(2)}, u32[]{:S(2)}) collective-permute-start(bf16[512,768]{1,0:T(8,128)(2,1)S(1)} %get-tuple-element.75), channel_id=1, source_target_pairs={{0,1},{1,0},{2,3},{3,2},{4,5},{5,4},{6,7},{7,6},{8,9},{9,8},{10,11... | collective-permute-start | bytes 2359304 | tf_op jit(solution)/shard_map/ppermute | solution.py:45
  31.5 13.3 %collective-permute-start.5 = (bf16[128,3072]{1,0:T(8,128)(2,1)S(1)}, bf16[128,3072]{1,0:T(8,128)(2,1)S(1)}, u32[]{:S(2)}, u32[]{:S(2)}) collective-permute-start(bf16[128,3072]{1,0:T(8,128)(2,1)S(1)} %get-tuple-element.95), channel_id=1, source_target_pairs={{0,8},{1,3},{2,10},{3,5},{4,12},{5,7},{6,14},{7,1},{8,16},{9,11},{... | collective-permute-start | bytes 2359304 | tf_op jit(solution)/shard_map/ppermute | solution.py:56
  33.0 17.6 %collective-permute-start.7 = (bf16[128,3072]{1,0:T(8,128)(2,1)S(1)}, bf16[128,3072]{1,0:T(8,128)(2,1)S(1)}, u32[]{:S(2)}, u32[]{:S(2)}) collective-permute-start(bf16[128,3072]{1,0:T(8,128)(2,1)S(1)} %get-tuple-element.101), channel_id=1, source_target_pairs={{0,24},{1,7},{2,26},{3,1},{4,28},{5,3},{6,30},{7,5},{8,0},{9,15},{... | collective-permute-start | bytes 2359304 | tf_op jit(solution)/shard_map/ppermute | solution.py:56
  34.8 19.7 %collective-permute-start.8 = (bf16[128,3072]{1,0:T(8,128)(2,1)S(1)}, bf16[128,3072]{1,0:T(8,128)(2,1)S(1)}, u32[]{:S(2)}, u32[]{:S(2)}) collective-permute-start(bf16[128,3072]{1,0:T(8,128)(2,1)S(1)} %get-tuple-element.102), channel_id=1, source_target_pairs={{0,16},{1,5},{2,18},{3,7},{4,20},{5,1},{6,22},{7,3},{8,24},{9,13},... | collective-permute-start | bytes 2359304 | tf_op jit(solution)/shard_map/ppermute | solution.py:56
  44.9 5.7 %collective-permute-start.6 = (bf16[2,2,128,512]{3,2,1,0:T(8,128)(2,1)S(1)}, bf16[2,2,128,512]{3,2,1,0:T(8,128)(2,1)S(1)}, u32[]{:S(2)}, u32[]{:S(2)}) collective-permute-start(bf16[2,2,128,512]{3,2,1,0:T(8,128)(2,1)S(1)} %pad_maximum_fusion), channel_id=1, source_target_pairs={{1,0},{3,2},{5,4},{7,6},{9,8},{11,10},{13,12},{15,14},{17,16},{19,... | collective-permute-start | bytes 1572872 | tf_op jit(solution)/shard_map/ppermute | solution.py:68
  50.6 43.2 %copy-start = (bf16[1024,512]{1,0:T(8,128)(2,1)S(1)}, bf16[1024,512]{1,0:T(8,128)(2,1)}, u32[]{:S(2)}) copy-start(bf16[1024,512]{1,0:T(8,128)(2,1)} %wk_ref.5) | copy-start | bytes 3145732
  50.7 43.1 %copy-start.1 = (bf16[1024,512]{1,0:T(8,128)(2,1)S(1)}, bf16[1024,512]{1,0:T(8,128)(2,1)}, u32[]{:S(2)}) copy-start(bf16[1024,512]{1,0:T(8,128)(2,1)} %wv_ref.5) | copy-start | bytes 3145732
  54.8 8.8 %collective-permute-start.11 = (bf16[32,3072]{1,0:T(8,128)(2,1)S(1)}, bf16[32,3072]{1,0:T(8,128)(2,1)S(1)}, u32[]{:S(2)}, u32[]{:S(2)}) collective-permute-start(bf16[32,3072]{1,0:T(8,128)(2,1)S(1)} %get-tuple-element.106), channel_id=1, source_target_pairs={{0,2},{1,9},{2,4},{3,11},{4,6},{5,13},{6,0},{7,15},{8,10},{9,17},{... | collective-permute-start | bytes 589832 | tf_op jit(solution)/shard_map/ppermute | solution.py:56
  56.3 9.0 %collective-permute-start.12 = (bf16[32,3072]{1,0:T(8,128)(2,1)S(1)}, bf16[32,3072]{1,0:T(8,128)(2,1)S(1)}, u32[]{:S(2)}, u32[]{:S(2)}) collective-permute-start(bf16[32,3072]{1,0:T(8,128)(2,1)S(1)} %get-tuple-element.107), channel_id=1, source_target_pairs={{0,6},{1,25},{2,0},{3,27},{4,2},{5,29},{6,4},{7,31},{8,14},{9,1},{... | collective-permute-start | bytes 589832 | tf_op jit(solution)/shard_map/ppermute | solution.py:56
  57.1 8.2 %collective-permute-start.13 = (bf16[32,3072]{1,0:T(8,128)(2,1)S(1)}, bf16[32,3072]{1,0:T(8,128)(2,1)S(1)}, u32[]{:S(2)}, u32[]{:S(2)}) collective-permute-start(bf16[32,3072]{1,0:T(8,128)(2,1)S(1)} %get-tuple-element.108), channel_id=1, source_target_pairs={{0,4},{1,17},{2,6},{3,19},{4,0},{5,21},{6,2},{7,23},{8,12},{9,25},... | collective-permute-start | bytes 589832 | tf_op jit(solution)/shard_map/ppermute | solution.py:56
  58.4 35.4 %collective-permute-start.9 = (bf16[2,128,512]{2,1,0:T(8,128)(2,1)S(1)}, bf16[2,128,512]{2,1,0:T(8,128)(2,1)S(1)}, u32[]{:S(2)}, u32[]{:S(2)}) collective-permute-start(bf16[2,128,512]{2,1,0:T(8,128)(2,1)S(1)} %fusion), channel_id=1, source_target_pairs={{2,1},{4,3},{6,5},{8,7},{10,9},{12,11},{14,13},{16,15},{18,17},{20... | collective-permute-start | bytes 786440 | tf_op jit(solution)/shard_map/ppermute | solution.py:68
  59.7 34.1 %collective-permute-start.10 = (bf16[2,128,512]{2,1,0:T(8,128)(2,1)S(1)}, bf16[2,128,512]{2,1,0:T(8,128)(2,1)S(1)}, u32[]{:S(2)}, u32[]{:S(2)}) collective-permute-start(bf16[2,128,512]{2,1,0:T(8,128)(2,1)S(1)} %get-tuple-element.105), channel_id=1, source_target_pairs={{2,0},{4,2},{6,4},{8,6},{10,8},{12,10},{14,12},{16,14},{18,16},{20... | collective-permute-start | bytes 786440 | tf_op jit(solution)/shard_map/ppermute | solution.py:68
  65.4 25.3 %collective-permute-start.14 = (bf16[8,3072]{1,0:T(8,128)(2,1)S(1)}, bf16[8,3072]{1,0:T(8,128)(2,1)S(1)}, u32[]{:S(2)}, u32[]{:S(2)}) collective-permute-start(bf16[8,3072]{1,0:T(8,128)(2,1)S(1)} %get-tuple-element.110), channel_id=1, source_target_pairs={{0,64},{1,65},{2,66},{3,67},{4,68},{5,69},{6,70},{7,71},{8,72},{9,... | collective-permute-start | bytes 147464 | tf_op jit(solution)/shard_map/ppermute | solution.py:62
  81.4 9.3 %collective-permute-start.15 = (bf16[8,3072]{1,0:T(8,128)(2,1)S(1)}, bf16[8,3072]{1,0:T(8,128)(2,1)S(1)}, u32[]{:S(2)}, u32[]{:S(2)}) collective-permute-start(bf16[8,3072]{1,0:T(8,128)(2,1)S(1)} %get-tuple-element.111), channel_id=1, source_target_pairs={{0,192},{1,193},{2,194},{3,195},{4,196},{5,197},{6,198},{7,199},{8... | collective-permute-start | bytes 147464 | tf_op jit(solution)/shard_map/ppermute | solution.py:62
  84.5 8.3 %collective-permute-start.16 = (bf16[8,3072]{1,0:T(8,128)(2,1)S(1)}, bf16[8,3072]{1,0:T(8,128)(2,1)S(1)}, u32[]{:S(2)}, u32[]{:S(2)}) collective-permute-start(bf16[8,3072]{1,0:T(8,128)(2,1)S(1)} %get-tuple-element.112), channel_id=1, source_target_pairs={{0,128},{1,129},{2,130},{3,131},{4,132},{5,133},{6,134},{7,135},{8... | collective-permute-start | bytes 147464 | tf_op jit(solution)/shard_map/ppermute | solution.py:62
  92.8 5.1 %collective-permute-start.17 = (bf16[4,3072]{1,0:T(4,128)(2,1)S(1)}, bf16[4,3072]{1,0:T(4,128)(2,1)S(1)}, u32[]{:S(2)}, u32[]{:S(2)}) collective-permute-start(bf16[4,3072]{1,0:T(4,128)(2,1)S(1)} %get-tuple-element.115), channel_id=1, source_target_pairs={{0,32},{1,33},{2,34},{3,35},{4,36},{5,37},{6,38},{7,39},{8,40},{9,... | collective-permute-start | bytes 73736 | tf_op jit(solution)/shard_map/ppermute | solution.py:62

commit v7 on v6

--- a/solution.py
+++ b/solution.py
@@ -416,26 +416,89 @@
     )(*atts, *dqs, wo, wq)
 
 
-def tail_kernel(base_ref, own_one, own_two, handed, near, far, wk_ref, wv_ref, out_ref):
+def tail_kernel(place, base_ref, own_one, own_two, mine_ref, other_ref, wk_ref, wv_ref, out_ref):
     total = base_ref[...]
     for i, w_ref in enumerate((wk_ref, wv_ref)):
         grad = jnp.concatenate([own_one[i], own_two[i]], axis=1)
-        for part in (handed[0, i], near[i], far[i]):
-            grad = grad + part.astype(F32)
+        grad = grad + jnp.where(place[2] == i, mine_ref[...], other_ref[...].astype(F32))
         total = total + dot(grad.astype(BF16), w_ref[...], NT)
     out_ref[...] = total.astype(BF16)
 
 
-def tail(*args):
+def tail(place, *args):
     return pl.pallas_call(
         tail_kernel,
         grid=(1,),
         out_shape=jax.ShapeDtypeStruct((ROWS, MODEL), BF16),
-        in_specs=[whole(*a.shape) for a in args],
+        in_specs=[pl.BlockSpec(memory_space=pltpu.SMEM)] + [whole(*a.shape) for a in args],
         out_specs=whole(ROWS, MODEL),
         compiler_params=pltpu.CompilerParams(vmem_limit_bytes=20 << 20),
         name="tail",
+    )(place, *args)
+
+
+def on_place(kernel, name, outs, *args):
+    return pl.pallas_call(
+        kernel,
+        grid=(1,),
+        out_shape=tuple(jax.ShapeDtypeStruct(shape, kind) for shape, kind in outs),
+        in_specs=[pl.BlockSpec(memory_space=pltpu.SMEM)] + [whole(*a.shape) for a in args[1:]],
+        out_specs=tuple(whole(*shape) for shape, _ in outs),
+        compiler_params=pltpu.CompilerParams(vmem_limit_bytes=8 << 20),
+        name=name,
     )(*args)
+
+
+def hand_kernel(place, near_one, near_two, far_one, far_two, give_ref, keep_ref):
+    core = place[2]
+    for i, (one, two) in enumerate(((near_one, near_two), (far_one, far_two))):
+        split = one.shape[2]
+        give_ref[i, :, :split] = one[1 - core]
+        give_ref[i, :, split:] = two[1 - core]
+        keep_ref[i, :, :split] = one[core]
+        keep_ref[i, :, split:] = two[core]
+
+
+def handed(*args):
+    return on_place(hand_kernel, "hand", [((2, ROWS, 512), BF16)] * 2, *args)
+
+
+def met_kernel(place, keep_ref, got_ref, back_ref, near_ref):
+    def fill(zero, one):
+        back_ref[0] = (zero[0].astype(F32) + one[1].astype(F32)).astype(BF16)
+        back_ref[1] = zero[1]
+        near_ref[...] = one[0]
+
+    @pl.when(place[2] == 0)
+    def _():
+        fill(keep_ref, got_ref)
+
+    @pl.when(place[2] == 1)
+    def _():
+        fill(got_ref, keep_ref)
+
+
+def met(*args):
+    return on_place(met_kernel, "met", [((2, ROWS, 512), BF16), ((ROWS, 512), BF16)], *args)
+
+
+def turn_kernel(place, back_ref, near_ref, mine_ref, other_ref):
+    at_zero = back_ref[1].astype(F32) + near_ref[...].astype(F32)
+    at_one = back_ref[0].astype(F32)
+
+    @pl.when(place[2] == 0)
+    def _():
+        mine_ref[...] = at_zero
+        other_ref[...] = at_one.astype(BF16)
+
+    @pl.when(place[2] == 1)
+    def _():
+        mine_ref[...] = at_one
+        other_ref[...] = at_zero.astype(BF16)
+
+
+def turned(*args):
+    return on_place(turn_kernel, "turn", [((ROWS, 512), F32), ((ROWS, 512), BF16)], *args)
 
 
 def after(value, *others):
@@ -463,24 +526,22 @@
     two = attend(3, 1, after(place, one[-1]))
     got_two = to_mate(two[-2])
     sums = folded_into(0, one[-1], after(got_one, two[-1]))
-    own, *sends = folded_into(3, two[-1], after(got_two, sums[0]), sums)
+    hand_give, hand_keep = handed(after(place, sums[0]), one[3], two[3], one[4], two[4])
+    own, *sends = folded_into(3, two[-1], after(got_two, hand_keep), sums)
     ring_one = ring([None, *sends], 0)
 
     attn_out, base = middle((one[0], after(two[0], own)), (one[1], two[1]), wo, wq)
-    grads = lax.optimization_barrier((one[3], two[3], one[4], two[4], ring_one[0]))
-    near_grad = jnp.concatenate(grads[0:2], axis=-1)
-    far_grad = jnp.concatenate(grads[2:4], axis=-1)
-    handed = passed_along(jnp.stack([near_grad, far_grad]), -1, range(1, 256, 2))
-    summed = (near_grad.astype(F32) + handed[1].astype(F32)).astype(BF16)
-    own, *sends = folded(after(own, base, summed), *ring_one)
+    back, near_one = met(after(place, base), hand_keep, to_mate(hand_give))
+    own, *sends = folded(after(own, base, back), *ring_one)
     ring_two = ring([None, *sends], 1)
-    back_near = passed_along(after(summed, own), -1, range(0, 256, 2))
-    back_far = passed_along(after(far_grad, own), -2, range(0, 256, 2))
     own, *sends = folded(own, *ring_two)
+    back = passed_along(after(back, own), -2)
     ring_three = [along_z(sends[d - 1], 2 * d) for d in (1, 3, 2)]
     own, send = halved(own, *ring_three)
     got = along_z(send, 1)
-    tokens_grad = tail(base, one[2], two[2], handed, back_near, back_far, key_weight, value_matrix)
+    mine, other = turned(after(place, own), back, near_one)
+    other = to_mate(other)
+    tokens_grad = tail(place, base, one[2], two[2], mine, other, key_weight, value_matrix)
     query_rows, key_rows, value_rows, out_rows = summed_last(after(own, tokens_grad), got)
     return attn_out, tokens_grad, query_rows, key_rows, value_rows, out_rows.T
 

time: 99 us -> 96.5 us (0.975)
  the two profiles are of different devices: /device:TPU:24 before, /device:TPU:1 now
where the time goes in v7:
time: 96.5 us; the launch traced here: 96.2 us
  starting transfers between devices  41.9 us (43%)
  Pallas kernels  32.1 us (33%)
  waiting for transfers between devices  21.1 us (22%)
    ppermute x4, starting transfers between devices, along_z(): lax.ppermute(block, AXIS, route_of(lambda z, x, y, c: ((z + distance) % 8...  19.1 us
    ppermute x6, waiting for transfers between devices, ring(): lax.ppermute(blocks[d], AXIS, route_of(functools.partial(plane_step, phas...  15.5 us
    pallas_call x2, Pallas kernels, attention(): pl.pallas_call(attention_kernel, grid=(steps,), out_shape=(struct(ROWS, Q...  15 us
    ppermute x6, starting transfers between devices, ring(): lax.ppermute(blocks[d], AXIS, route_of(functools.partial(plane_step, phas...  8.24 us
    ppermute x4, starting transfers between devices, passed_along(): lax.ppermute(block, AXIS, [(i, i + distance) for i in sources if i + dist...  7.99 us
    ppermute x4, starting transfers between devices, to_mate(): lax.ppermute(array, AXIS, route_of(lambda z, x, y, c: (z, x, y, 1 - c)))  6.58 us
    pallas_call x1, Pallas kernels, middle(): pl.pallas_call(middle_kernel, grid=(STEPS,), out_shape=(jax.ShapeDtypeStr...  4.35 us
    ppermute x4, waiting for transfers between devices, along_z(): lax.ppermute(block, AXIS, route_of(lambda z, x, y, c: ((z + distance) % 8...  3.91 us
  transfers between devices with their start and end apart: 18, of which 9 were waited for; matrix products, arithmetic and copies ran while one was open for 0% of the time, Pallas kernels for 19%

profile of v7, /device:TPU:1, one launch (start us, length us, event | category | flops | bytes accessed | tf_op | source)
XLA Modules:
  0.0 96.2 jit_solution(14031974599653246848)
XLA Ops:
  0.7 4.7 %collective-permute-start = (bf16[128,1024]{1,0:T(8,128)(2,1)}, bf16[128,1024]{1,0:T(8,128)(2,1)S(1)}, u32[]{:S(2)}, u32[]{:S(2)}) collective-permute-start(bf16[128,1024]{1,0:T(8,128)(2,1)} %own_ref.3), channel_id=1, source_target_pairs={{0,1},{1,2},{2,3},{3,4},{4,5},{5,6},{6,7},{7,8},{8,9},{9,10},{10,1... | collective-permute-start | bytes 786440 | tf_op jit(solution)/shard_map/ppermute | solution.py:68
  6.1 3.9 %early.1 = (bf16[128,1024]{1,0:T(8,128)(2,1)S(1)}, bf16[128,1024]{1,0:T(8,128)(2,1)S(1)}) custom-call(bf16[128,1024]{1,0:T(8,128)(2,1)} %own_ref.3, bf16[128,1024]{1,0:T(8,128)(2,1)} %b_ref.1, bf16[1024,1024]{1,0:T(8,128)(2,1)} %wq_ref.3, bf16[1024,1024]{1,0:T(8,128)(2,1)} %wo_ref.3), custom_call_target="tpu_custom_call" | custom-call | tf_op jit(solution)/shard_map/early/pallas_call | solution.py:109
  10.0 1.3 %collective-permute-start.2 = (bf16[128,1024]{1,0:T(8,128)(2,1)S(1)}, bf16[128,1024]{1,0:T(8,128)(2,1)S(1)}, u32[]{:S(2)}, u32[]{:S(2)}) collective-permute-start(bf16[128,1024]{1,0:T(8,128)(2,1)S(1)} %collective-permute-done.near_ref), channel_id=1, source_target_pairs={{0,1},{2,3},{4,5},{6,7},{8,9},{10,11},{12,13},{14,15},{16,17},{18,... | collective-permute-start | bytes 786440 | tf_op jit(solution)/shard_map/ppermute | solution.py:68
  12.7 1.3 %collective-permute-done.2.mate_ref = bf16[128,1024]{1,0:T(8,128)(2,1)S(1)} collective-permute-done((bf16[128,1024]{1,0:T(8,128)(2,1)S(1)}, bf16[128,1024]{1,0:T(8,128)(2,1)S(1)}, u32[]{:S(2)}, u32[]{:S(2)}) %collective-permute-start.2) | collective-permute-done | bytes 262176 | tf_op jit(solution)/shard_map/ppermute | solution.py:68
  15.2 10.9 %attention.2 = (bf16[128,768]{1,0:T(8,128)(2,1)S(1)}, bf16[128,768]{1,0:T(8,128)(2,1)S(1)}, f32[2,128,384]{2,1,0:T(8,128)S(1)}, bf16[2,128,384]{2,1,0:T(8,128)(2...) custom-call(s32[5]{0:T(128)S(1)} %stack.23.place, ...), custom_call_target="tpu_custom_call" | custom-call | flops 1000 | bytes 1000 | tf_op jit(solution)/shard_map/attention/pallas_call | solution.py:255
  26.6 4.1 %attention.3 = (bf16[128,256]{1,0:T(8,128)(2,1)S(1)}, bf16[128,256]{1,0:T(8,128)(2,1)S(1)}, f32[2,128,128]{2,1,0:T(8,128)S(1)}, bf16[2,128,128]{2,1,0:T(8,128)(2...) custom-call(s32[5]{0:T(128)S(1)} %stack.23.place, ...), custom_call_target="tpu_custom_call" | custom-call | flops 1000 | bytes 1000 | tf_op jit(solution)/shard_map/attention/pallas_call | solution.py:255
  33.3 1.4 %collective-permute-start.6 = (bf16[128,3072]{1,0:T(8,128)(2,1)S(1)}, bf16[128,3072]{1,0:T(8,128)(2,1)S(1)}, u32[]{:S(2)}, u32[]{:S(2)}) collective-permute-start(bf16[128,3072]{1,0:T(8,128)(2,1)S(1)} %get-tuple-element.105), channel_id=1, source_target_pairs={{0,8},{1,3},{2,10},{3,5},{4,12},{5,7},{6,14},{7,1},{8,16},{9,11},{... | collective-permute-start | bytes 2359304 | tf_op jit(solution)/shard_map/ppermute | solution.py:56
  34.6 1.4 %collective-permute-start.7 = (bf16[128,3072]{1,0:T(8,128)(2,1)S(1)}, bf16[128,3072]{1,0:T(8,128)(2,1)S(1)}, u32[]{:S(2)}, u32[]{:S(2)}) collective-permute-start(bf16[128,3072]{1,0:T(8,128)(2,1)S(1)} %get-tuple-element.106), channel_id=1, source_target_pairs={{0,24},{1,7},{2,26},{3,1},{4,28},{5,3},{6,30},{7,5},{8,0},{9,15},{... | collective-permute-start | bytes 2359304 | tf_op jit(solution)/shard_map/ppermute | solution.py:56
  36.0 1.4 %collective-permute-start.8 = (bf16[128,3072]{1,0:T(8,128)(2,1)S(1)}, bf16[128,3072]{1,0:T(8,128)(2,1)S(1)}, u32[]{:S(2)}, u32[]{:S(2)}) collective-permute-start(bf16[128,3072]{1,0:T(8,128)(2,1)S(1)} %get-tuple-element.107), channel_id=1, source_target_pairs={{0,16},{1,5},{2,18},{3,7},{4,20},{5,1},{6,22},{7,3},{8,24},{9,13},... | collective-permute-start | bytes 2359304 | tf_op jit(solution)/shard_map/ppermute | solution.py:56
  37.4 2.0 %collective-permute-start.5 = (bf16[2,128,512]{2,1,0:T(8,128)(2,1)S(1)}, bf16[2,128,512]{2,1,0:T(8,128)(2,1)S(1)}, u32[]{:S(2)}, u32[]{:S(2)}) collective-permute-start(bf16[2,128,512]{2,1,0:T(8,128)(2,1)S(1)} %get-tuple-element.102), channel_id=1, source_target_pairs={{0,1},{1,0},{2,3},{3,2},{4,5},{5,4},{6,7},{7,6},{8,9},{9,8},{10,11... | collective-permute-start | bytes 786440 | tf_op jit(solution)/shard_map/ppermute | solution.py:45
  39.4 4.4 %middle.1 = (bf16[128,1024]{1,0:T(8,128)(2,1)}, f32[128,1024]{1,0:T(8,128)S(1)}) custom-call(bf16[128,768]{1,0:T(8,128)(2,1)S(1)} %get-tuple-element.74.att_one, bf16[128,256]{1,0:T(8,128)(2,1)S(1)} %get-tuple-element.94.att_two, bf16[128,768]{1,0:T(8,128)(2,1)S(1)} %get-tuple-element.95.dq_one, bf16[128,256]{1,0:T(8,128)(2,1)S(1)} %get-tuple-element.96.dq_two, ...), custom_call_target="tpu_custom_call" | custom-call | tf_op jit(solution)/shard_map/middle/pallas_call | solution.py:401
  45.8 9.2 %collective-permute-done.8.refs_3_ = bf16[128,3072]{1,0:T(8,128)(2,1)S(1)} collective-permute-done((bf16[128,3072]{1,0:T(8,128)(2,1)S(1)}, bf16[128,3072]{1,0:T(8,128)(2,1)S(1)}, u32[]{:S(2)}, u32[]{:S(2)}) %collective-permute-start.8) | collective-permute-done | bytes 786464 | tf_op jit(solution)/shard_map/ppermute | solution.py:56
  56.3 1.9 %collective-permute-start.10 = (bf16[32,3072]{1,0:T(8,128)(2,1)S(1)}, bf16[32,3072]{1,0:T(8,128)(2,1)S(1)}, u32[]{:S(2)}, u32[]{:S(2)}) collective-permute-start(bf16[32,3072]{1,0:T(8,128)(2,1)S(1)} %get-tuple-element.110), channel_id=1, source_target_pairs={{0,6},{1,25},{2,0},{3,27},{4,2},{5,29},{6,4},{7,31},{8,14},{9,1},{... | collective-permute-start | bytes 589832 | tf_op jit(solution)/shard_map/ppermute | solution.py:56
  59.3 1.9 %collective-permute-done.9.refs_1_ = bf16[32,3072]{1,0:T(8,128)(2,1)S(1)} collective-permute-done((bf16[32,3072]{1,0:T(8,128)(2,1)S(1)}, bf16[32,3072]{1,0:T(8,128)(2,1)S(1)}, u32[]{:S(2)}, u32[]{:S(2)}) %collective-permute-start.9) | collective-permute-done | bytes 196640 | tf_op jit(solution)/shard_map/ppermute | solution.py:56
  61.2 1.8 %collective-permute-done.10.refs_2_ = bf16[32,3072]{1,0:T(8,128)(2,1)S(1)} collective-permute-done((bf16[32,3072]{1,0:T(8,128)(2,1)S(1)}, bf16[32,3072]{1,0:T(8,128)(2,1)S(1)}, u32[]{:S(2)}, u32[]{:S(2)}) %collective-permute-start.10) | collective-permute-done | bytes 196640 | tf_op jit(solution)/shard_map/ppermute | solution.py:56
  63.0 1.5 %collective-permute-done.11.refs_3_ = bf16[32,3072]{1,0:T(8,128)(2,1)S(1)} collective-permute-done((bf16[32,3072]{1,0:T(8,128)(2,1)S(1)}, bf16[32,3072]{1,0:T(8,128)(2,1)S(1)}, u32[]{:S(2)}, u32[]{:S(2)}) %collective-permute-start.11) | collective-permute-done | bytes 196640 | tf_op jit(solution)/shard_map/ppermute | solution.py:56
  64.6 1.3 %collective-permute-start.15 = (bf16[2,128,512]{2,1,0:T(8,128)(2,1)S(1)}, bf16[2,128,512]{2,1,0:T(8,128)(2,1)S(1)}, u32[]{:S(2)}, u32[]{:S(2)}) collective-permute-start(bf16[2,128,512]{2,1,0:T(8,128)(2,1)S(1)} %get-tuple-element.118), channel_id=1, source_target_pairs={{2,0},{3,1},{4,2},{5,3},{6,4},{7,5},{8,6},{9,7},{10,8},{11,9},{12,... | collective-permute-start | bytes 786440 | tf_op jit(solution)/shard_map/ppermute | solution.py:68
  65.9 9.2 %collective-permute-start.12 = (bf16[8,3072]{1,0:T(8,128)(2,1)S(1)}, bf16[8,3072]{1,0:T(8,128)(2,1)S(1)}, u32[]{:S(2)}, u32[]{:S(2)}) collective-permute-start(bf16[8,3072]{1,0:T(8,128)(2,1)S(1)} %get-tuple-element.113), channel_id=1, source_target_pairs={{0,64},{1,65},{2,66},{3,67},{4,68},{5,69},{6,70},{7,71},{8,72},{9,... | collective-permute-start | bytes 147464 | tf_op jit(solution)/shard_map/ppermute | solution.py:62
  75.1 4.0 %collective-permute-start.13 = (bf16[8,3072]{1,0:T(8,128)(2,1)S(1)}, bf16[8,3072]{1,0:T(8,128)(2,1)S(1)}, u32[]{:S(2)}, u32[]{:S(2)}) collective-permute-start(bf16[8,3072]{1,0:T(8,128)(2,1)S(1)} %get-tuple-element.114), channel_id=1, source_target_pairs={{0,192},{1,193},{2,194},{3,195},{4,196},{5,197},{6,198},{7,199},{8... | collective-permute-start | bytes 147464 | tf_op jit(solution)/shard_map/ppermute | solution.py:62
  79.1 3.5 %collective-permute-start.14 = (bf16[8,3072]{1,0:T(8,128)(2,1)S(1)}, bf16[8,3072]{1,0:T(8,128)(2,1)S(1)}, u32[]{:S(2)}, u32[]{:S(2)}) collective-permute-start(bf16[8,3072]{1,0:T(8,128)(2,1)S(1)} %get-tuple-element.115), channel_id=1, source_target_pairs={{0,128},{1,129},{2,130},{3,131},{4,132},{5,133},{6,134},{7,135},{8... | collective-permute-start | bytes 147464 | tf_op jit(solution)/shard_map/ppermute | solution.py:62
  82.6 3.9 %collective-permute-done.14.c_ref = bf16[8,3072]{1,0:T(8,128)(2,1)S(1)} collective-permute-done((bf16[8,3072]{1,0:T(8,128)(2,1)S(1)}, bf16[8,3072]{1,0:T(8,128)(2,1)S(1)}, u32[]{:S(2)}, u32[]{:S(2)}) %collective-permute-start.14) | collective-permute-done | bytes 49184 | tf_op jit(solution)/shard_map/ppermute | solution.py:62
  87.2 3.9 %collective-permute-start.16 = (bf16[128,512]{1,0:T(8,128)(2,1)S(1)}, bf16[128,512]{1,0:T(8,128)(2,1)S(1)}, u32[]{:S(2)}, u32[]{:S(2)}) collective-permute-start(bf16[128,512]{1,0:T(8,128)(2,1)S(1)} %get-tuple-element.121), channel_id=1, source_target_pairs={{0,1},{1,0},{2,3},{3,2},{4,5},{5,4},{6,7},{7,6},{8,9},{9,8},{10,11... | collective-permute-start | bytes 393224 | tf_op jit(solution)/shard_map/ppermute | solution.py:45
  91.1 2.4 %collective-permute-start.17 = (bf16[4,3072]{1,0:T(4,128)(2,1)S(1)}, bf16[4,3072]{1,0:T(4,128)(2,1)S(1)}, u32[]{:S(2)}, u32[]{:S(2)}) collective-permute-start(bf16[4,3072]{1,0:T(4,128)(2,1)S(1)} %get-tuple-element.123), channel_id=1, source_target_pairs={{0,32},{1,33},{2,34},{3,35},{4,36},{5,37},{6,38},{7,39},{8,40},{9,... | collective-permute-start | bytes 73736 | tf_op jit(solution)/shard_map/ppermute | solution.py:62
  93.5 2.1 %tail.1 = bf16[128,1024]{1,0:T(8,128)(2,1)} custom-call(s32[5]{0:T(128)S(1)} %stack.23.place, f32[128,1024]{1,0:T(8,128)S(1)} %get-tuple-element.98.base_ref, f32[2,128,384]{2,1,0:T(8,128)S(1)} %get-tuple-element.99.own_one, f32[2,128,128]{2,1,0:T(8,128)S(1)} %get-tuple-element.100.own_two, f32[128,512]{1,0:T(8,128)S(1)} %get-tuple-element.120.mine_ref, ...), custom_call_target="tpu_custom_call" | custom-call | tf_op jit(solution)/shard_map/tail/pallas_call | solution.py:429
  (37 shorter events, 12.1 us)
Async XLA Ops:
  0.6 10.8 %copy-start.2 = (bf16[128,1024]{1,0:T(8,128)(2,1)S(1)}, bf16[128,1024]{1,0:T(8,128)(2,1)}, u32[]{:S(2)}) copy-start(bf16[128,1024]{1,0:T(8,128)(2,1)} %own_ref.3) | copy-start | bytes 786436
  0.6 10.8 %copy-start.3 = (bf16[128,1024]{1,0:T(8,128)(2,1)S(1)}, bf16[128,1024]{1,0:T(8,128)(2,1)}, u32[]{:S(2)}) copy-start(bf16[128,1024]{1,0:T(8,128)(2,1)} %b_ref.1) | copy-start | bytes 786436
  0.7 9.3 %collective-permute-start = (bf16[128,1024]{1,0:T(8,128)(2,1)}, bf16[128,1024]{1,0:T(8,128)(2,1)S(1)}, u32[]{:S(2)}, u32[]{:S(2)}) collective-permute-start(bf16[128,1024]{1,0:T(8,128)(2,1)} %own_ref.3), channel_id=1, source_target_pairs={{0,1},{1,2},{2,3},{3,4},{4,5},{5,6},{6,7},{7,8},{8,9},{9,10},{10,1... | collective-permute-start | bytes 786440 | tf_op jit(solution)/shard_map/ppermute | solution.py:68
  5.4 7.3 %collective-permute-start.1 = (bf16[128,1024]{1,0:T(8,128)(2,1)}, bf16[128,1024]{1,0:T(8,128)(2,1)S(1)}, u32[]{:S(2)}, u32[]{:S(2)}) collective-permute-start(bf16[128,1024]{1,0:T(8,128)(2,1)} %own_ref.3), channel_id=1, source_target_pairs={{0,2},{2,4},{4,6},{6,8},{8,10},{10,12},{12,14},{14,16},{16,18},{18... | collective-permute-start | bytes 786440 | tf_op jit(solution)/shard_map/ppermute | solution.py:68
  10.0 4.0 %collective-permute-start.2 = (bf16[128,1024]{1,0:T(8,128)(2,1)S(1)}, bf16[128,1024]{1,0:T(8,128)(2,1)S(1)}, u32[]{:S(2)}, u32[]{:S(2)}) collective-permute-start(bf16[128,1024]{1,0:T(8,128)(2,1)S(1)} %collective-permute-done.near_ref), channel_id=1, source_target_pairs={{0,1},{2,3},{4,5},{6,7},{8,9},{10,11},{12,13},{14,15},{16,17},{18,... | collective-permute-start | bytes 786440 | tf_op jit(solution)/shard_map/ppermute | solution.py:68
  26.1 4.8 %collective-permute-start.4 = (bf16[512,2304]{1,0:T(8,128)(2,1)S(1)}, bf16[512,2304]{1,0:T(8,128)(2,1)S(1)}, u32[]{:S(2)}, u32[]{:S(2)}) collective-permute-start(bf16[512,2304]{1,0:T(8,128)(2,1)S(1)} %get-tuple-element.80), channel_id=1, source_target_pairs={{0,1},{1,0},{2,3},{3,2},{4,5},{5,4},{6,7},{7,6},{8,9},{9,8},{10,11... | collective-permute-start | bytes 7077896 | tf_op jit(solution)/shard_map/ppermute | solution.py:45
  30.7 2.4 %collective-permute-start.3 = (bf16[512,768]{1,0:T(8,128)(2,1)S(1)}, bf16[512,768]{1,0:T(8,128)(2,1)S(1)}, u32[]{:S(2)}, u32[]{:S(2)}) collective-permute-start(bf16[512,768]{1,0:T(8,128)(2,1)S(1)} %get-tuple-element.79), channel_id=1, source_target_pairs={{0,1},{1,0},{2,3},{3,2},{4,5},{5,4},{6,7},{7,6},{8,9},{9,8},{10,11... | collective-permute-start | bytes 2359304 | tf_op jit(solution)/shard_map/ppermute | solution.py:45
  33.3 12.4 %collective-permute-start.6 = (bf16[128,3072]{1,0:T(8,128)(2,1)S(1)}, bf16[128,3072]{1,0:T(8,128)(2,1)S(1)}, u32[]{:S(2)}, u32[]{:S(2)}) collective-permute-start(bf16[128,3072]{1,0:T(8,128)(2,1)S(1)} %get-tuple-element.105), channel_id=1, source_target_pairs={{0,8},{1,3},{2,10},{3,5},{4,12},{5,7},{6,14},{7,1},{8,16},{9,11},{... | collective-permute-start | bytes 2359304 | tf_op jit(solution)/shard_map/ppermute | solution.py:56
  34.6 11.1 %collective-permute-start.7 = (bf16[128,3072]{1,0:T(8,128)(2,1)S(1)}, bf16[128,3072]{1,0:T(8,128)(2,1)S(1)}, u32[]{:S(2)}, u32[]{:S(2)}) collective-permute-start(bf16[128,3072]{1,0:T(8,128)(2,1)S(1)} %get-tuple-element.106), channel_id=1, source_target_pairs={{0,24},{1,7},{2,26},{3,1},{4,28},{5,3},{6,30},{7,5},{8,0},{9,15},{... | collective-permute-start | bytes 2359304 | tf_op jit(solution)/shard_map/ppermute | solution.py:56
  36.0 18.9 %collective-permute-start.8 = (bf16[128,3072]{1,0:T(8,128)(2,1)S(1)}, bf16[128,3072]{1,0:T(8,128)(2,1)S(1)}, u32[]{:S(2)}, u32[]{:S(2)}) collective-permute-start(bf16[128,3072]{1,0:T(8,128)(2,1)S(1)} %get-tuple-element.107), channel_id=1, source_target_pairs={{0,16},{1,5},{2,18},{3,7},{4,20},{5,1},{6,22},{7,3},{8,24},{9,13},... | collective-permute-start | bytes 2359304 | tf_op jit(solution)/shard_map/ppermute | solution.py:56
  37.4 6.4 %collective-permute-start.5 = (bf16[2,128,512]{2,1,0:T(8,128)(2,1)S(1)}, bf16[2,128,512]{2,1,0:T(8,128)(2,1)S(1)}, u32[]{:S(2)}, u32[]{:S(2)}) collective-permute-start(bf16[2,128,512]{2,1,0:T(8,128)(2,1)S(1)} %get-tuple-element.102), channel_id=1, source_target_pairs={{0,1},{1,0},{2,3},{3,2},{4,5},{5,4},{6,7},{7,6},{8,9},{9,8},{10,11... | collective-permute-start | bytes 786440 | tf_op jit(solution)/shard_map/ppermute | solution.py:45
  44.6 48.9 %copy-start = (bf16[1024,512]{1,0:T(8,128)(2,1)S(1)}, bf16[1024,512]{1,0:T(8,128)(2,1)}, u32[]{:S(2)}) copy-start(bf16[1024,512]{1,0:T(8,128)(2,1)} %wk_ref.5) | copy-start | bytes 3145732
  44.6 48.9 %copy-start.1 = (bf16[1024,512]{1,0:T(8,128)(2,1)S(1)}, bf16[1024,512]{1,0:T(8,128)(2,1)}, u32[]{:S(2)}) copy-start(bf16[1024,512]{1,0:T(8,128)(2,1)} %wv_ref.5) | copy-start | bytes 3145732
  55.3 6.0 %collective-permute-start.9 = (bf16[32,3072]{1,0:T(8,128)(2,1)S(1)}, bf16[32,3072]{1,0:T(8,128)(2,1)S(1)}, u32[]{:S(2)}, u32[]{:S(2)}) collective-permute-start(bf16[32,3072]{1,0:T(8,128)(2,1)S(1)} %get-tuple-element.109), channel_id=1, source_target_pairs={{0,2},{1,9},{2,4},{3,11},{4,6},{5,13},{6,0},{7,15},{8,10},{9,17},{... | collective-permute-start | bytes 589832 | tf_op jit(solution)/shard_map/ppermute | solution.py:56
  56.3 6.6 %collective-permute-start.10 = (bf16[32,3072]{1,0:T(8,128)(2,1)S(1)}, bf16[32,3072]{1,0:T(8,128)(2,1)S(1)}, u32[]{:S(2)}, u32[]{:S(2)}) collective-permute-start(bf16[32,3072]{1,0:T(8,128)(2,1)S(1)} %get-tuple-element.110), channel_id=1, source_target_pairs={{0,6},{1,25},{2,0},{3,27},{4,2},{5,29},{6,4},{7,31},{8,14},{9,1},{... | collective-permute-start | bytes 589832 | tf_op jit(solution)/shard_map/ppermute | solution.py:56
  58.3 6.3 %collective-permute-start.11 = (bf16[32,3072]{1,0:T(8,128)(2,1)S(1)}, bf16[32,3072]{1,0:T(8,128)(2,1)S(1)}, u32[]{:S(2)}, u32[]{:S(2)}) collective-permute-start(bf16[32,3072]{1,0:T(8,128)(2,1)S(1)} %get-tuple-element.111), channel_id=1, source_target_pairs={{0,4},{1,17},{2,6},{3,19},{4,0},{5,21},{6,2},{7,23},{8,12},{9,25},... | collective-permute-start | bytes 589832 | tf_op jit(solution)/shard_map/ppermute | solution.py:56
  64.6 22.0 %collective-permute-start.15 = (bf16[2,128,512]{2,1,0:T(8,128)(2,1)S(1)}, bf16[2,128,512]{2,1,0:T(8,128)(2,1)S(1)}, u32[]{:S(2)}, u32[]{:S(2)}) collective-permute-start(bf16[2,128,512]{2,1,0:T(8,128)(2,1)S(1)} %get-tuple-element.118), channel_id=1, source_target_pairs={{2,0},{3,1},{4,2},{5,3},{6,4},{7,5},{8,6},{9,7},{10,8},{11,9},{12,... | collective-permute-start | bytes 786440 | tf_op jit(solution)/shard_map/ppermute | solution.py:68
  65.9 16.7 %collective-permute-start.12 = (bf16[8,3072]{1,0:T(8,128)(2,1)S(1)}, bf16[8,3072]{1,0:T(8,128)(2,1)S(1)}, u32[]{:S(2)}, u32[]{:S(2)}) collective-permute-start(bf16[8,3072]{1,0:T(8,128)(2,1)S(1)} %get-tuple-element.113), channel_id=1, source_target_pairs={{0,64},{1,65},{2,66},{3,67},{4,68},{5,69},{6,70},{7,71},{8,72},{9,... | collective-permute-start | bytes 147464 | tf_op jit(solution)/shard_map/ppermute | solution.py:62
  75.1 7.6 %collective-permute-start.13 = (bf16[8,3072]{1,0:T(8,128)(2,1)S(1)}, bf16[8,3072]{1,0:T(8,128)(2,1)S(1)}, u32[]{:S(2)}, u32[]{:S(2)}) collective-permute-start(bf16[8,3072]{1,0:T(8,128)(2,1)S(1)} %get-tuple-element.114), channel_id=1, source_target_pairs={{0,192},{1,193},{2,194},{3,195},{4,196},{5,197},{6,198},{7,199},{8... | collective-permute-start | bytes 147464 | tf_op jit(solution)/shard_map/ppermute | solution.py:62
  79.1 7.4 %collective-permute-start.14 = (bf16[8,3072]{1,0:T(8,128)(2,1)S(1)}, bf16[8,3072]{1,0:T(8,128)(2,1)S(1)}, u32[]{:S(2)}, u32[]{:S(2)}) collective-permute-start(bf16[8,3072]{1,0:T(8,128)(2,1)S(1)} %get-tuple-element.115), channel_id=1, source_target_pairs={{0,128},{1,129},{2,130},{3,131},{4,132},{5,133},{6,134},{7,135},{8... | collective-permute-start | bytes 147464 | tf_op jit(solution)/shard_map/ppermute | solution.py:62
  87.2 6.3 %collective-permute-start.16 = (bf16[128,512]{1,0:T(8,128)(2,1)S(1)}, bf16[128,512]{1,0:T(8,128)(2,1)S(1)}, u32[]{:S(2)}, u32[]{:S(2)}) collective-permute-start(bf16[128,512]{1,0:T(8,128)(2,1)S(1)} %get-tuple-element.121), channel_id=1, source_target_pairs={{0,1},{1,0},{2,3},{3,2},{4,5},{5,4},{6,7},{7,6},{8,9},{9,8},{10,11... | collective-permute-start | bytes 393224 | tf_op jit(solution)/shard_map/ppermute | solution.py:45
  91.1 4.4 %collective-permute-start.17 = (bf16[4,3072]{1,0:T(4,128)(2,1)S(1)}, bf16[4,3072]{1,0:T(4,128)(2,1)S(1)}, u32[]{:S(2)}, u32[]{:S(2)}) collective-permute-start(bf16[4,3072]{1,0:T(4,128)(2,1)S(1)} %get-tuple-element.123), channel_id=1, source_target_pairs={{0,32},{1,33},{2,34},{3,35},{4,36},{5,37},{6,38},{7,39},{8,40},{9,... | collective-permute-start | bytes 73736 | tf_op jit(solution)/shard_map/ppermute | solution.py:62

commit v8 on v7

--- a/solution.py
+++ b/solution.py
@@ -534,8 +534,8 @@
     back, near_one = met(after(place, base), hand_keep, to_mate(hand_give))
     own, *sends = folded(after(own, base, back), *ring_one)
     ring_two = ring([None, *sends], 1)
+    back = jnp.stack([passed_along(after(back[i], own), -2) for i in range(2)])
     own, *sends = folded(own, *ring_two)
-    back = passed_along(after(back, own), -2)
     ring_three = [along_z(sends[d - 1], 2 * d) for d in (1, 3, 2)]
     own, send = halved(own, *ring_three)
     got = along_z(send, 1)

time: 96.5 us -> 93.1 us (0.965)
  the two profiles are of different devices: /device:TPU:1 before, /device:TPU:24 now
where the time goes in v8:
time: 93.1 us; the launch traced here: 91.8 us
  starting transfers between devices  39.2 us (42%)
  Pallas kernels  32.1 us (34%)
  waiting for transfers between devices  19.4 us (21%)
    ppermute x4, starting transfers between devices, along_z(): lax.ppermute(block, AXIS, route_of(lambda z, x, y, c: ((z + distance) % 8...  17.8 us
    pallas_call x2, Pallas kernels, attention(): pl.pallas_call(attention_kernel, grid=(steps,), out_shape=(struct(ROWS, Q...  15 us
    ppermute x6, waiting for transfers between devices, ring(): lax.ppermute(blocks[d], AXIS, route_of(functools.partial(plane_step, phas...  15 us
    ppermute x5, starting transfers between devices, passed_along(): lax.ppermute(block, AXIS, [(i, i + distance) for i in sources if i + dist...  12.4 us
    ppermute x6, starting transfers between devices, ring(): lax.ppermute(blocks[d], AXIS, route_of(functools.partial(plane_step, phas...  8.26 us
    pallas_call x1, Pallas kernels, middle(): pl.pallas_call(middle_kernel, grid=(STEPS,), out_shape=(jax.ShapeDtypeStr...  4.36 us
    pallas_call x1, Pallas kernels, early(): pl.pallas_call(early_kernel, grid=(STEPS,), out_shape=(jax.ShapeDtypeStru...  3.9 us
    ppermute x4, waiting for transfers between devices, along_z(): lax.ppermute(block, AXIS, route_of(lambda z, x, y, c: ((z + distance) % 8...  3.79 us
  transfers between devices with their start and end apart: 19, of which 9 were waited for; matrix products, arithmetic and copies ran while one was open for 0% of the time, Pallas kernels for 20%

profile of v8, /device:TPU:24, one launch (start us, length us, event | category | flops | bytes accessed | tf_op | source)
XLA Modules:
  0.0 91.8 jit_solution(1591427160082837632)
XLA Ops:
  0.7 2.1 %collective-permute-start = (bf16[128,1024]{1,0:T(8,128)(2,1)}, bf16[128,1024]{1,0:T(8,128)(2,1)S(1)}, u32[]{:S(2)}, u32[]{:S(2)}) collective-permute-start(bf16[128,1024]{1,0:T(8,128)(2,1)} %own_ref.3), channel_id=1, source_target_pairs={{0,1},{1,2},{2,3},{3,4},{4,5},{5,6},{6,7},{7,8},{8,9},{9,10},{10,1... | collective-permute-start | bytes 786440 | tf_op jit(solution)/shard_map/ppermute | solution.py:68
  2.7 3.1 %collective-permute-start.1 = (bf16[128,1024]{1,0:T(8,128)(2,1)}, bf16[128,1024]{1,0:T(8,128)(2,1)S(1)}, u32[]{:S(2)}, u32[]{:S(2)}) collective-permute-start(bf16[128,1024]{1,0:T(8,128)(2,1)} %own_ref.3), channel_id=1, source_target_pairs={{0,2},{2,4},{4,6},{6,8},{8,10},{10,12},{12,14},{14,16},{16,18},{18... | collective-permute-start | bytes 786440 | tf_op jit(solution)/shard_map/ppermute | solution.py:68
  5.8 3.9 %early.1 = (bf16[128,1024]{1,0:T(8,128)(2,1)S(1)}, bf16[128,1024]{1,0:T(8,128)(2,1)S(1)}) custom-call(bf16[128,1024]{1,0:T(8,128)(2,1)} %own_ref.3, bf16[128,1024]{1,0:T(8,128)(2,1)} %b_ref.1, bf16[1024,1024]{1,0:T(8,128)(2,1)} %wq_ref.3, bf16[1024,1024]{1,0:T(8,128)(2,1)} %wo_ref.3), custom_call_target="tpu_custom_call" | custom-call | tf_op jit(solution)/shard_map/early/pallas_call | solution.py:109
  9.7 1.3 %collective-permute-start.2 = (bf16[128,1024]{1,0:T(8,128)(2,1)S(1)}, bf16[128,1024]{1,0:T(8,128)(2,1)S(1)}, u32[]{:S(2)}, u32[]{:S(2)}) collective-permute-start(bf16[128,1024]{1,0:T(8,128)(2,1)S(1)} %collective-permute-done.near_ref), channel_id=1, source_target_pairs={{0,1},{2,3},{4,5},{6,7},{8,9},{10,11},{12,13},{14,15},{16,17},{18,... | collective-permute-start | bytes 786440 | tf_op jit(solution)/shard_map/ppermute | solution.py:68
  12.4 1.2 %prep.3 = (bf16[2,512,256]{2,1,0:T(8,128)(2,1)S(1)}, bf16[128,1024]{1,0:T(8,128)(2,1)S(1)}) custom-call(s32[5]{0:T(128)S(1)} %stack.32.place, bf16[128,1024]{1,0:T(8,128)(2,1)S(1)} %collective-permute-done.1.far_ref, bf16[128,1024]{1,0:T(8,128)(2,1)S(1)} %collective-permute-done.2.mate_ref, bf16[128,1024]{1,0:T(8,128)(2,1)S(1)} %collective-permute-done.near_ref), custom_call_target="tpu_custom_call" | custom-call | tf_op jit(solution)/shard_map/prep/pallas_call | solution.py:148
  13.6 10.9 %attention.2 = (bf16[128,768]{1,0:T(8,128)(2,1)S(1)}, bf16[128,768]{1,0:T(8,128)(2,1)S(1)}, f32[2,128,384]{2,1,0:T(8,128)S(1)}, bf16[2,128,384]{2,1,0:T(8,128)(2...) custom-call(s32[5]{0:T(128)S(1)} %stack.32.place, ...), custom_call_target="tpu_custom_call" | custom-call | flops 1000 | bytes 1000 | tf_op jit(solution)/shard_map/attention/pallas_call | solution.py:255
  24.8 4.1 %attention.3 = (bf16[128,256]{1,0:T(8,128)(2,1)S(1)}, bf16[128,256]{1,0:T(8,128)(2,1)S(1)}, f32[2,128,128]{2,1,0:T(8,128)S(1)}, bf16[2,128,128]{2,1,0:T(8,128)(2...) custom-call(s32[5]{0:T(128)S(1)} %stack.32.place, ...), custom_call_target="tpu_custom_call" | custom-call | flops 1000 | bytes 1000 | tf_op jit(solution)/shard_map/attention/pallas_call | solution.py:255
  31.5 1.6 %collective-permute-start.6 = (bf16[128,3072]{1,0:T(8,128)(2,1)S(1)}, bf16[128,3072]{1,0:T(8,128)(2,1)S(1)}, u32[]{:S(2)}, u32[]{:S(2)}) collective-permute-start(bf16[128,3072]{1,0:T(8,128)(2,1)S(1)} %get-tuple-element.106), channel_id=1, source_target_pairs={{0,8},{1,3},{2,10},{3,5},{4,12},{5,7},{6,14},{7,1},{8,16},{9,11},{... | collective-permute-start | bytes 2359304 | tf_op jit(solution)/shard_map/ppermute | solution.py:56
  33.0 1.7 %collective-permute-start.7 = (bf16[128,3072]{1,0:T(8,128)(2,1)S(1)}, bf16[128,3072]{1,0:T(8,128)(2,1)S(1)}, u32[]{:S(2)}, u32[]{:S(2)}) collective-permute-start(bf16[128,3072]{1,0:T(8,128)(2,1)S(1)} %get-tuple-element.107), channel_id=1, source_target_pairs={{0,24},{1,7},{2,26},{3,1},{4,28},{5,3},{6,30},{7,5},{8,0},{9,15},{... | collective-permute-start | bytes 2359304 | tf_op jit(solution)/shard_map/ppermute | solution.py:56
  34.8 1.5 %collective-permute-start.8 = (bf16[128,3072]{1,0:T(8,128)(2,1)S(1)}, bf16[128,3072]{1,0:T(8,128)(2,1)S(1)}, u32[]{:S(2)}, u32[]{:S(2)}) collective-permute-start(bf16[128,3072]{1,0:T(8,128)(2,1)S(1)} %get-tuple-element.108), channel_id=1, source_target_pairs={{0,16},{1,5},{2,18},{3,7},{4,20},{5,1},{6,22},{7,3},{8,24},{9,13},... | collective-permute-start | bytes 2359304 | tf_op jit(solution)/shard_map/ppermute | solution.py:56
  36.3 4.4 %middle.1 = (bf16[128,1024]{1,0:T(8,128)(2,1)}, f32[128,1024]{1,0:T(8,128)S(1)}) custom-call(bf16[128,768]{1,0:T(8,128)(2,1)S(1)} %get-tuple-element.75.att_one, bf16[128,256]{1,0:T(8,128)(2,1)S(1)} %get-tuple-element.95.att_two, bf16[128,768]{1,0:T(8,128)(2,1)S(1)} %get-tuple-element.96.dq_one, bf16[128,256]{1,0:T(8,128)(2,1)S(1)} %get-tuple-element.97.dq_two, ...), custom_call_target="tpu_custom_call" | custom-call | tf_op jit(solution)/shard_map/middle/pallas_call | solution.py:401
  41.4 3.3 %collective-permute-done.6.refs_1_ = bf16[128,3072]{1,0:T(8,128)(2,1)S(1)} collective-permute-done((bf16[128,3072]{1,0:T(8,128)(2,1)S(1)}, bf16[128,3072]{1,0:T(8,128)(2,1)S(1)}, u32[]{:S(2)}, u32[]{:S(2)}) %collective-permute-start.6) | collective-permute-done | bytes 786464 | tf_op jit(solution)/shard_map/ppermute | solution.py:56
  45.0 9.5 %collective-permute-done.8.refs_3_ = bf16[128,3072]{1,0:T(8,128)(2,1)S(1)} collective-permute-done((bf16[128,3072]{1,0:T(8,128)(2,1)S(1)}, bf16[128,3072]{1,0:T(8,128)(2,1)S(1)}, u32[]{:S(2)}, u32[]{:S(2)}) %collective-permute-start.8) | collective-permute-done | bytes 786464 | tf_op jit(solution)/shard_map/ppermute | solution.py:56
  54.9 1.3 %collective-permute-start.9 = (bf16[32,3072]{1,0:T(8,128)(2,1)S(1)}, bf16[32,3072]{1,0:T(8,128)(2,1)S(1)}, u32[]{:S(2)}, u32[]{:S(2)}) collective-permute-start(bf16[32,3072]{1,0:T(8,128)(2,1)S(1)} %get-tuple-element.110), channel_id=1, source_target_pairs={{0,2},{1,9},{2,4},{3,11},{4,6},{5,13},{6,0},{7,15},{8,10},{9,17},{... | collective-permute-start | bytes 589832 | tf_op jit(solution)/shard_map/ppermute | solution.py:56
  57.0 1.3 %collective-permute-start.11 = (bf16[32,3072]{1,0:T(8,128)(2,1)S(1)}, bf16[32,3072]{1,0:T(8,128)(2,1)S(1)}, u32[]{:S(2)}, u32[]{:S(2)}) collective-permute-start(bf16[32,3072]{1,0:T(8,128)(2,1)S(1)} %get-tuple-element.112), channel_id=1, source_target_pairs={{0,4},{1,17},{2,6},{3,19},{4,0},{5,21},{6,2},{7,23},{8,12},{9,25},... | collective-permute-start | bytes 589832 | tf_op jit(solution)/shard_map/ppermute | solution.py:56
  58.3 3.9 %collective-permute-start.15 = (bf16[128,512]{1,0:T(8,128)(2,1)S(1)}, bf16[128,512]{1,0:T(8,128)(2,1)S(1)}, u32[]{:S(2)}, u32[]{:S(2)}) collective-permute-start(bf16[128,512]{1,0:T(8,128)(2,1)S(1)} %get-tuple-element.119), channel_id=1, source_target_pairs={{2,0},{3,1},{4,2},{5,3},{6,4},{7,5},{8,6},{9,7},{10,8},{11,9},{12,... | collective-permute-start | bytes 393224 | tf_op jit(solution)/shard_map/ppermute | solution.py:68
  62.2 2.1 %collective-permute-start.16 = (bf16[128,512]{1,0:T(8,128)(2,1)S(1)}, bf16[128,512]{1,0:T(8,128)(2,1)S(1)}, u32[]{:S(2)}, u32[]{:S(2)}) collective-permute-start(bf16[128,512]{1,0:T(8,128)(2,1)S(1)} %get-tuple-element.120), channel_id=1, source_target_pairs={{2,0},{3,1},{4,2},{5,3},{6,4},{7,5},{8,6},{9,7},{10,8},{11,9},{12,... | collective-permute-start | bytes 393224 | tf_op jit(solution)/shard_map/ppermute | solution.py:68
  64.4 1.8 %collective-permute-done.11.refs_3_ = bf16[32,3072]{1,0:T(8,128)(2,1)S(1)} collective-permute-done((bf16[32,3072]{1,0:T(8,128)(2,1)S(1)}, bf16[32,3072]{1,0:T(8,128)(2,1)S(1)}, u32[]{:S(2)}, u32[]{:S(2)}) %collective-permute-start.11) | collective-permute-done | bytes 196640 | tf_op jit(solution)/shard_map/ppermute | solution.py:56
  66.3 7.6 %collective-permute-start.12 = (bf16[8,3072]{1,0:T(8,128)(2,1)S(1)}, bf16[8,3072]{1,0:T(8,128)(2,1)S(1)}, u32[]{:S(2)}, u32[]{:S(2)}) collective-permute-start(bf16[8,3072]{1,0:T(8,128)(2,1)S(1)} %get-tuple-element.114), channel_id=1, source_target_pairs={{0,64},{1,65},{2,66},{3,67},{4,68},{5,69},{6,70},{7,71},{8,72},{9,... | collective-permute-start | bytes 147464 | tf_op jit(solution)/shard_map/ppermute | solution.py:62
  73.9 3.1 %collective-permute-start.13 = (bf16[8,3072]{1,0:T(8,128)(2,1)S(1)}, bf16[8,3072]{1,0:T(8,128)(2,1)S(1)}, u32[]{:S(2)}, u32[]{:S(2)}) collective-permute-start(bf16[8,3072]{1,0:T(8,128)(2,1)S(1)} %get-tuple-element.115), channel_id=1, source_target_pairs={{0,192},{1,193},{2,194},{3,195},{4,196},{5,197},{6,198},{7,199},{8... | collective-permute-start | bytes 147464 | tf_op jit(solution)/shard_map/ppermute | solution.py:62
  77.0 6.2 %collective-permute-start.14 = (bf16[8,3072]{1,0:T(8,128)(2,1)S(1)}, bf16[8,3072]{1,0:T(8,128)(2,1)S(1)}, u32[]{:S(2)}, u32[]{:S(2)}) collective-permute-start(bf16[8,3072]{1,0:T(8,128)(2,1)S(1)} %get-tuple-element.116), channel_id=1, source_target_pairs={{0,128},{1,129},{2,130},{3,131},{4,132},{5,133},{6,134},{7,135},{8... | collective-permute-start | bytes 147464 | tf_op jit(solution)/shard_map/ppermute | solution.py:62
  83.3 2.1 %collective-permute-done.14.c_ref = bf16[8,3072]{1,0:T(8,128)(2,1)S(1)} collective-permute-done((bf16[8,3072]{1,0:T(8,128)(2,1)S(1)}, bf16[8,3072]{1,0:T(8,128)(2,1)S(1)}, u32[]{:S(2)}, u32[]{:S(2)}) %collective-permute-start.14) | collective-permute-done | bytes 49184 | tf_op jit(solution)/shard_map/ppermute | solution.py:62
  87.4 2.1 %tail.1 = bf16[128,1024]{1,0:T(8,128)(2,1)} custom-call(s32[5]{0:T(128)S(1)} %stack.32.place, f32[128,1024]{1,0:T(8,128)S(1)} %get-tuple-element.99.base_ref, f32[2,128,384]{2,1,0:T(8,128)S(1)} %get-tuple-element.100.own_one, f32[2,128,128]{2,1,0:T(8,128)S(1)} %get-tuple-element.101.own_two, f32[128,512]{1,0:T(8,128)S(1)} %get-tuple-element.122.mine_ref, ...), custom_call_target="tpu_custom_call" | custom-call | tf_op jit(solution)/shard_map/tail/pallas_call | solution.py:429
  89.5 1.7 %collective-permute-done.18.got_ref = bf16[4,3072]{1,0:T(4,128)(2,1)S(1)} collective-permute-done((bf16[4,3072]{1,0:T(4,128)(2,1)S(1)}, bf16[4,3072]{1,0:T(4,128)(2,1)S(1)}, u32[]{:S(2)}, u32[]{:S(2)}) %collective-permute-start.18) | collective-permute-done | bytes 24608 | tf_op jit(solution)/shard_map/ppermute | solution.py:62
  (41 shorter events, 9.3 us)
Async XLA Ops:
  0.6 10.5 %copy-start.2 = (bf16[128,1024]{1,0:T(8,128)(2,1)S(1)}, bf16[128,1024]{1,0:T(8,128)(2,1)}, u32[]{:S(2)}) copy-start(bf16[128,1024]{1,0:T(8,128)(2,1)} %own_ref.3) | copy-start | bytes 786436
  0.6 10.5 %copy-start.3 = (bf16[128,1024]{1,0:T(8,128)(2,1)S(1)}, bf16[128,1024]{1,0:T(8,128)(2,1)}, u32[]{:S(2)}) copy-start(bf16[128,1024]{1,0:T(8,128)(2,1)} %b_ref.1) | copy-start | bytes 786436
  0.7 9.0 %collective-permute-start = (bf16[128,1024]{1,0:T(8,128)(2,1)}, bf16[128,1024]{1,0:T(8,128)(2,1)S(1)}, u32[]{:S(2)}, u32[]{:S(2)}) collective-permute-start(bf16[128,1024]{1,0:T(8,128)(2,1)} %own_ref.3), channel_id=1, source_target_pairs={{0,1},{1,2},{2,3},{3,4},{4,5},{5,6},{6,7},{7,8},{8,9},{9,10},{10,1... | collective-permute-start | bytes 786440 | tf_op jit(solution)/shard_map/ppermute | solution.py:68
  2.7 9.7 %collective-permute-start.1 = (bf16[128,1024]{1,0:T(8,128)(2,1)}, bf16[128,1024]{1,0:T(8,128)(2,1)S(1)}, u32[]{:S(2)}, u32[]{:S(2)}) collective-permute-start(bf16[128,1024]{1,0:T(8,128)(2,1)} %own_ref.3), channel_id=1, source_target_pairs={{0,2},{2,4},{4,6},{6,8},{8,10},{10,12},{12,14},{14,16},{16,18},{18... | collective-permute-start | bytes 786440 | tf_op jit(solution)/shard_map/ppermute | solution.py:68
  9.7 2.7 %collective-permute-start.2 = (bf16[128,1024]{1,0:T(8,128)(2,1)S(1)}, bf16[128,1024]{1,0:T(8,128)(2,1)S(1)}, u32[]{:S(2)}, u32[]{:S(2)}) collective-permute-start(bf16[128,1024]{1,0:T(8,128)(2,1)S(1)} %collective-permute-done.near_ref), channel_id=1, source_target_pairs={{0,1},{2,3},{4,5},{6,7},{8,9},{10,11},{12,13},{14,15},{16,17},{18,... | collective-permute-start | bytes 786440 | tf_op jit(solution)/shard_map/ppermute | solution.py:68
  24.6 4.8 %collective-permute-start.4 = (bf16[512,2304]{1,0:T(8,128)(2,1)S(1)}, bf16[512,2304]{1,0:T(8,128)(2,1)S(1)}, u32[]{:S(2)}, u32[]{:S(2)}) collective-permute-start(bf16[512,2304]{1,0:T(8,128)(2,1)S(1)} %get-tuple-element.81), channel_id=1, source_target_pairs={{0,1},{1,0},{2,3},{3,2},{4,5},{5,4},{6,7},{7,6},{8,9},{9,8},{10,11... | collective-permute-start | bytes 7077896 | tf_op jit(solution)/shard_map/ppermute | solution.py:45
  28.9 2.4 %collective-permute-start.3 = (bf16[512,768]{1,0:T(8,128)(2,1)S(1)}, bf16[512,768]{1,0:T(8,128)(2,1)S(1)}, u32[]{:S(2)}, u32[]{:S(2)}) collective-permute-start(bf16[512,768]{1,0:T(8,128)(2,1)S(1)} %get-tuple-element.80), channel_id=1, source_target_pairs={{0,1},{1,0},{2,3},{3,2},{4,5},{5,4},{6,7},{7,6},{8,9},{9,8},{10,11... | collective-permute-start | bytes 2359304 | tf_op jit(solution)/shard_map/ppermute | solution.py:45
  31.5 13.3 %collective-permute-start.6 = (bf16[128,3072]{1,0:T(8,128)(2,1)S(1)}, bf16[128,3072]{1,0:T(8,128)(2,1)S(1)}, u32[]{:S(2)}, u32[]{:S(2)}) collective-permute-start(bf16[128,3072]{1,0:T(8,128)(2,1)S(1)} %get-tuple-element.106), channel_id=1, source_target_pairs={{0,8},{1,3},{2,10},{3,5},{4,12},{5,7},{6,14},{7,1},{8,16},{9,11},{... | collective-permute-start | bytes 2359304 | tf_op jit(solution)/shard_map/ppermute | solution.py:56
  33.0 12.0 %collective-permute-start.7 = (bf16[128,3072]{1,0:T(8,128)(2,1)S(1)}, bf16[128,3072]{1,0:T(8,128)(2,1)S(1)}, u32[]{:S(2)}, u32[]{:S(2)}) collective-permute-start(bf16[128,3072]{1,0:T(8,128)(2,1)S(1)} %get-tuple-element.107), channel_id=1, source_target_pairs={{0,24},{1,7},{2,26},{3,1},{4,28},{5,3},{6,30},{7,5},{8,0},{9,15},{... | collective-permute-start | bytes 2359304 | tf_op jit(solution)/shard_map/ppermute | solution.py:56
  34.8 19.7 %collective-permute-start.8 = (bf16[128,3072]{1,0:T(8,128)(2,1)S(1)}, bf16[128,3072]{1,0:T(8,128)(2,1)S(1)}, u32[]{:S(2)}, u32[]{:S(2)}) collective-permute-start(bf16[128,3072]{1,0:T(8,128)(2,1)S(1)} %get-tuple-element.108), channel_id=1, source_target_pairs={{0,16},{1,5},{2,18},{3,7},{4,20},{5,1},{6,22},{7,3},{8,24},{9,13},... | collective-permute-start | bytes 2359304 | tf_op jit(solution)/shard_map/ppermute | solution.py:56
  36.3 4.4 %collective-permute-start.5 = (bf16[2,128,512]{2,1,0:T(8,128)(2,1)S(1)}, bf16[2,128,512]{2,1,0:T(8,128)(2,1)S(1)}, u32[]{:S(2)}, u32[]{:S(2)}) collective-permute-start(bf16[2,128,512]{2,1,0:T(8,128)(2,1)S(1)} %get-tuple-element.103), channel_id=1, source_target_pairs={{0,1},{1,0},{2,3},{3,2},{4,5},{5,4},{6,7},{7,6},{8,9},{9,8},{10,11... | collective-permute-start | bytes 786440 | tf_op jit(solution)/shard_map/ppermute | solution.py:45
  54.8 32.6 %copy-start = (bf16[1024,512]{1,0:T(8,128)(2,1)S(1)}, bf16[1024,512]{1,0:T(8,128)(2,1)}, u32[]{:S(2)}) copy-start(bf16[1024,512]{1,0:T(8,128)(2,1)} %wk_ref.5) | copy-start | bytes 3145732
  54.8 32.6 %copy-start.1 = (bf16[1024,512]{1,0:T(8,128)(2,1)S(1)}, bf16[1024,512]{1,0:T(8,128)(2,1)}, u32[]{:S(2)}) copy-start(bf16[1024,512]{1,0:T(8,128)(2,1)} %wv_ref.5) | copy-start | bytes 3145732
  54.9 9.4 %collective-permute-start.9 = (bf16[32,3072]{1,0:T(8,128)(2,1)S(1)}, bf16[32,3072]{1,0:T(8,128)(2,1)S(1)}, u32[]{:S(2)}, u32[]{:S(2)}) collective-permute-start(bf16[32,3072]{1,0:T(8,128)(2,1)S(1)} %get-tuple-element.110), channel_id=1, source_target_pairs={{0,2},{1,9},{2,4},{3,11},{4,6},{5,13},{6,0},{7,15},{8,10},{9,17},{... | collective-permute-start | bytes 589832 | tf_op jit(solution)/shard_map/ppermute | solution.py:56
  56.1 8.3 %collective-permute-start.10 = (bf16[32,3072]{1,0:T(8,128)(2,1)S(1)}, bf16[32,3072]{1,0:T(8,128)(2,1)S(1)}, u32[]{:S(2)}, u32[]{:S(2)}) collective-permute-start(bf16[32,3072]{1,0:T(8,128)(2,1)S(1)} %get-tuple-element.111), channel_id=1, source_target_pairs={{0,6},{1,25},{2,0},{3,27},{4,2},{5,29},{6,4},{7,31},{8,14},{9,1},{... | collective-permute-start | bytes 589832 | tf_op jit(solution)/shard_map/ppermute | solution.py:56
  57.0 9.3 %collective-permute-start.11 = (bf16[32,3072]{1,0:T(8,128)(2,1)S(1)}, bf16[32,3072]{1,0:T(8,128)(2,1)S(1)}, u32[]{:S(2)}, u32[]{:S(2)}) collective-permute-start(bf16[32,3072]{1,0:T(8,128)(2,1)S(1)} %get-tuple-element.112), channel_id=1, source_target_pairs={{0,4},{1,17},{2,6},{3,19},{4,0},{5,21},{6,2},{7,23},{8,12},{9,25},... | collective-permute-start | bytes 589832 | tf_op jit(solution)/shard_map/ppermute | solution.py:56
  58.3 24.9 %collective-permute-start.15 = (bf16[128,512]{1,0:T(8,128)(2,1)S(1)}, bf16[128,512]{1,0:T(8,128)(2,1)S(1)}, u32[]{:S(2)}, u32[]{:S(2)}) collective-permute-start(bf16[128,512]{1,0:T(8,128)(2,1)S(1)} %get-tuple-element.119), channel_id=1, source_target_pairs={{2,0},{3,1},{4,2},{5,3},{6,4},{7,5},{8,6},{9,7},{10,8},{11,9},{12,... | collective-permute-start | bytes 393224 | tf_op jit(solution)/shard_map/ppermute | solution.py:68
  62.2 21.0 %collective-permute-start.16 = (bf16[128,512]{1,0:T(8,128)(2,1)S(1)}, bf16[128,512]{1,0:T(8,128)(2,1)S(1)}, u32[]{:S(2)}, u32[]{:S(2)}) collective-permute-start(bf16[128,512]{1,0:T(8,128)(2,1)S(1)} %get-tuple-element.120), channel_id=1, source_target_pairs={{2,0},{3,1},{4,2},{5,3},{6,4},{7,5},{8,6},{9,7},{10,8},{11,9},{12,... | collective-permute-start | bytes 393224 | tf_op jit(solution)/shard_map/ppermute | solution.py:68
  66.3 16.9 %collective-permute-start.12 = (bf16[8,3072]{1,0:T(8,128)(2,1)S(1)}, bf16[8,3072]{1,0:T(8,128)(2,1)S(1)}, u32[]{:S(2)}, u32[]{:S(2)}) collective-permute-start(bf16[8,3072]{1,0:T(8,128)(2,1)S(1)} %get-tuple-element.114), channel_id=1, source_target_pairs={{0,64},{1,65},{2,66},{3,67},{4,68},{5,69},{6,70},{7,71},{8,72},{9,... | collective-permute-start | bytes 147464 | tf_op jit(solution)/shard_map/ppermute | solution.py:62
  73.9 9.3 %collective-permute-start.13 = (bf16[8,3072]{1,0:T(8,128)(2,1)S(1)}, bf16[8,3072]{1,0:T(8,128)(2,1)S(1)}, u32[]{:S(2)}, u32[]{:S(2)}) collective-permute-start(bf16[8,3072]{1,0:T(8,128)(2,1)S(1)} %get-tuple-element.115), channel_id=1, source_target_pairs={{0,192},{1,193},{2,194},{3,195},{4,196},{5,197},{6,198},{7,199},{8... | collective-permute-start | bytes 147464 | tf_op jit(solution)/shard_map/ppermute | solution.py:62
  77.0 8.3 %collective-permute-start.14 = (bf16[8,3072]{1,0:T(8,128)(2,1)S(1)}, bf16[8,3072]{1,0:T(8,128)(2,1)S(1)}, u32[]{:S(2)}, u32[]{:S(2)}) collective-permute-start(bf16[8,3072]{1,0:T(8,128)(2,1)S(1)} %get-tuple-element.116), channel_id=1, source_target_pairs={{0,128},{1,129},{2,130},{3,131},{4,132},{5,133},{6,134},{7,135},{8... | collective-permute-start | bytes 147464 | tf_op jit(solution)/shard_map/ppermute | solution.py:62
  86.0 1.4 %collective-permute-start.17 = (bf16[128,512]{1,0:T(8,128)(2,1)S(1)}, bf16[128,512]{1,0:T(8,128)(2,1)S(1)}, u32[]{:S(2)}, u32[]{:S(2)}) collective-permute-start(bf16[128,512]{1,0:T(8,128)(2,1)S(1)} %get-tuple-element.123), channel_id=1, source_target_pairs={{0,1},{1,0},{2,3},{3,2},{4,5},{5,4},{6,7},{7,6},{8,9},{9,8},{10,11... | collective-permute-start | bytes 393224 | tf_op jit(solution)/shard_map/ppermute | solution.py:45
  86.1 5.1 %collective-permute-start.18 = (bf16[4,3072]{1,0:T(4,128)(2,1)S(1)}, bf16[4,3072]{1,0:T(4,128)(2,1)S(1)}, u32[]{:S(2)}, u32[]{:S(2)}) collective-permute-start(bf16[4,3072]{1,0:T(4,128)(2,1)S(1)} %get-tuple-element.125), channel_id=1, source_target_pairs={{0,32},{1,33},{2,34},{3,35},{4,36},{5,37},{6,38},{7,39},{8,40},{9,... | collective-permute-start | bytes 73736 | tf_op jit(solution)/shard_map/ppermute | solution.py:62

commit v9 on v8

--- a/solution.py
+++ b/solution.py
@@ -54,7 +54,7 @@
 def ring(blocks, phase):
     return [
         lax.ppermute(blocks[d], AXIS, route_of(functools.partial(plane_step, phase, d)))
-        for d in (1, 3, 2)
+        for d in (2, 1, 3)
     ]
 
 
@@ -539,8 +539,8 @@
     ring_three = [along_z(sends[d - 1], 2 * d) for d in (1, 3, 2)]
     own, send = halved(own, *ring_three)
     got = along_z(send, 1)
-    mine, other = turned(after(place, own), back, near_one)
-    other = to_mate(other)
+    mine, other = turned(place, back, near_one)
+    other = to_mate(after(other, own))
     tokens_grad = tail(place, base, one[2], two[2], mine, other, key_weight, value_matrix)
     query_rows, key_rows, value_rows, out_rows = summed_last(after(own, tokens_grad), got)
     return attn_out, tokens_grad, query_rows, key_rows, value_rows, out_rows.T

time: 93.1 us -> 90.9 us (0.976)
  the two profiles are of different devices: /device:TPU:24 before, /device:TPU:26 now
where the time goes in v9:
time: 90.9 us; the launch traced here: 90.5 us
  starting transfers between devices  33.7 us (37%)
  Pallas kernels  32.2 us (35%)
  waiting for transfers between devices  23.6 us (26%)
  between operations  0.94 us (1%)
    ppermute x6, waiting for transfers between devices, ring(): lax.ppermute(blocks[d], AXIS, route_of(functools.partial(plane_step, phas...  19 us
    pallas_call x2, Pallas kernels, attention(): pl.pallas_call(attention_kernel, grid=(steps,), out_shape=(struct(ROWS, Q...  15 us
    ppermute x4, starting transfers between devices, along_z(): lax.ppermute(block, AXIS, route_of(lambda z, x, y, c: ((z + distance) % 8...  12.5 us
    ppermute x5, starting transfers between devices, passed_along(): lax.ppermute(block, AXIS, [(i, i + distance) for i in sources if i + dist...  12 us
    ppermute x6, starting transfers between devices, ring(): lax.ppermute(blocks[d], AXIS, route_of(functools.partial(plane_step, phas...  8.43 us
    pallas_call x1, Pallas kernels, middle(): pl.pallas_call(middle_kernel, grid=(STEPS,), out_shape=(jax.ShapeDtypeStr...  4.36 us
    ppermute x4, waiting for transfers between devices, along_z(): lax.ppermute(block, AXIS, route_of(lambda z, x, y, c: ((z + distance) % 8...  4.11 us
    pallas_call x1, Pallas kernels, early(): pl.pallas_call(early_kernel, grid=(STEPS,), out_shape=(jax.ShapeDtypeStru...  3.9 us
  transfers between devices with their start and end apart: 19, of which 8 were waited for; matrix products, arithmetic and copies ran while one was open for 0% of the time, Pallas kernels for 21%

profile of v9, /device:TPU:26, one launch (start us, length us, event | category | flops | bytes accessed | tf_op | source)
XLA Modules:
  0.0 90.5 jit_solution(16045958013688804820)
XLA Ops:
  0.7 2.1 %collective-permute-start = (bf16[128,1024]{1,0:T(8,128)(2,1)}, bf16[128,1024]{1,0:T(8,128)(2,1)S(1)}, u32[]{:S(2)}, u32[]{:S(2)}) collective-permute-start(bf16[128,1024]{1,0:T(8,128)(2,1)} %own_ref.3), channel_id=1, source_target_pairs={{0,1},{1,2},{2,3},{3,4},{4,5},{5,6},{6,7},{7,8},{8,9},{9,10},{10,1... | collective-permute-start | bytes 786440 | tf_op jit(solution)/shard_map/ppermute | solution.py:68
  2.7 3.1 %collective-permute-start.1 = (bf16[128,1024]{1,0:T(8,128)(2,1)}, bf16[128,1024]{1,0:T(8,128)(2,1)S(1)}, u32[]{:S(2)}, u32[]{:S(2)}) collective-permute-start(bf16[128,1024]{1,0:T(8,128)(2,1)} %own_ref.3), channel_id=1, source_target_pairs={{0,2},{2,4},{4,6},{6,8},{8,10},{10,12},{12,14},{14,16},{16,18},{18... | collective-permute-start | bytes 786440 | tf_op jit(solution)/shard_map/ppermute | solution.py:68
  5.8 3.9 %early.1 = (bf16[128,1024]{1,0:T(8,128)(2,1)S(1)}, bf16[128,1024]{1,0:T(8,128)(2,1)S(1)}) custom-call(bf16[128,1024]{1,0:T(8,128)(2,1)} %own_ref.3, bf16[128,1024]{1,0:T(8,128)(2,1)} %b_ref.1, bf16[1024,1024]{1,0:T(8,128)(2,1)} %wq_ref.3, bf16[1024,1024]{1,0:T(8,128)(2,1)} %wo_ref.3), custom_call_target="tpu_custom_call" | custom-call | tf_op jit(solution)/shard_map/early/pallas_call | solution.py:109
  9.7 1.3 %collective-permute-start.2 = (bf16[128,1024]{1,0:T(8,128)(2,1)S(1)}, bf16[128,1024]{1,0:T(8,128)(2,1)S(1)}, u32[]{:S(2)}, u32[]{:S(2)}) collective-permute-start(bf16[128,1024]{1,0:T(8,128)(2,1)S(1)} %collective-permute-done.near_ref), channel_id=1, source_target_pairs={{0,1},{2,3},{4,5},{6,7},{8,9},{10,11},{12,13},{14,15},{16,17},{18,... | collective-permute-start | bytes 786440 | tf_op jit(solution)/shard_map/ppermute | solution.py:68
  11.2 1.2 %prep.2.tp_ref = bf16[2,512,256]{2,1,0:T(8,128)(2,1)S(1)} custom-call(s32[5]{0:T(128)S(1)} %stack.32.place, bf16[128,1024]{1,0:T(8,128)(2,1)S(1)} %copy-done.2, bf16[128,1024]{1,0:T(8,128)(2,1)S(1)} %copy-done.3), custom_call_target="tpu_custom_call" | custom-call | tf_op jit(solution)/shard_map/prep/pallas_call | solution.py:148
  12.4 1.2 %prep.3 = (bf16[2,512,256]{2,1,0:T(8,128)(2,1)S(1)}, bf16[128,1024]{1,0:T(8,128)(2,1)S(1)}) custom-call(s32[5]{0:T(128)S(1)} %stack.32.place, bf16[128,1024]{1,0:T(8,128)(2,1)S(1)} %collective-permute-done.1.far_ref, bf16[128,1024]{1,0:T(8,128)(2,1)S(1)} %collective-permute-done.2.mate_ref, bf16[128,1024]{1,0:T(8,128)(2,1)S(1)} %collective-permute-done.near_ref), custom_call_target="tpu_custom_call" | custom-call | tf_op jit(solution)/shard_map/prep/pallas_call | solution.py:148
  13.6 10.9 %attention.2 = (bf16[128,768]{1,0:T(8,128)(2,1)S(1)}, bf16[128,768]{1,0:T(8,128)(2,1)S(1)}, f32[2,128,384]{2,1,0:T(8,128)S(1)}, bf16[2,128,384]{2,1,0:T(8,128)(2...) custom-call(s32[5]{0:T(128)S(1)} %stack.32.place, ...), custom_call_target="tpu_custom_call" | custom-call | flops 1000 | bytes 1000 | tf_op jit(solution)/shard_map/attention/pallas_call | solution.py:255
  24.8 4.1 %attention.3 = (bf16[128,256]{1,0:T(8,128)(2,1)S(1)}, bf16[128,256]{1,0:T(8,128)(2,1)S(1)}, f32[2,128,128]{2,1,0:T(8,128)S(1)}, bf16[2,128,128]{2,1,0:T(8,128)(2...) custom-call(s32[5]{0:T(128)S(1)} %stack.32.place, ...), custom_call_target="tpu_custom_call" | custom-call | flops 1000 | bytes 1000 | tf_op jit(solution)/shard_map/attention/pallas_call | solution.py:255
  31.5 2.6 %collective-permute-start.6 = (bf16[128,3072]{1,0:T(8,128)(2,1)S(1)}, bf16[128,3072]{1,0:T(8,128)(2,1)S(1)}, u32[]{:S(2)}, u32[]{:S(2)}) collective-permute-start(bf16[128,3072]{1,0:T(8,128)(2,1)S(1)} %get-tuple-element.106), channel_id=1, source_target_pairs={{0,16},{1,5},{2,18},{3,7},{4,20},{5,1},{6,22},{7,3},{8,24},{9,13},... | collective-permute-start | bytes 2359304 | tf_op jit(solution)/shard_map/ppermute | solution.py:56
  34.0 2.0 %collective-permute-start.8 = (bf16[128,3072]{1,0:T(8,128)(2,1)S(1)}, bf16[128,3072]{1,0:T(8,128)(2,1)S(1)}, u32[]{:S(2)}, u32[]{:S(2)}) collective-permute-start(bf16[128,3072]{1,0:T(8,128)(2,1)S(1)} %get-tuple-element.108), channel_id=1, source_target_pairs={{0,24},{1,7},{2,26},{3,1},{4,28},{5,3},{6,30},{7,5},{8,0},{9,15},{... | collective-permute-start | bytes 2359304 | tf_op jit(solution)/shard_map/ppermute | solution.py:56
  36.1 4.4 %middle.1 = (bf16[128,1024]{1,0:T(8,128)(2,1)}, f32[128,1024]{1,0:T(8,128)S(1)}) custom-call(bf16[128,768]{1,0:T(8,128)(2,1)S(1)} %get-tuple-element.75.att_one, bf16[128,256]{1,0:T(8,128)(2,1)S(1)} %get-tuple-element.95.att_two, bf16[128,768]{1,0:T(8,128)(2,1)S(1)} %get-tuple-element.96.dq_one, bf16[128,256]{1,0:T(8,128)(2,1)S(1)} %get-tuple-element.97.dq_two, ...), custom_call_target="tpu_custom_call" | custom-call | tf_op jit(solution)/shard_map/middle/pallas_call | solution.py:401
  41.2 4.0 %collective-permute-done.6.refs_1_ = bf16[128,3072]{1,0:T(8,128)(2,1)S(1)} collective-permute-done((bf16[128,3072]{1,0:T(8,128)(2,1)S(1)}, bf16[128,3072]{1,0:T(8,128)(2,1)S(1)}, u32[]{:S(2)}, u32[]{:S(2)}) %collective-permute-start.6) | collective-permute-done | bytes 786464 | tf_op jit(solution)/shard_map/ppermute | solution.py:56
  45.2 8.1 %collective-permute-done.7.refs_2_ = bf16[128,3072]{1,0:T(8,128)(2,1)S(1)} collective-permute-done((bf16[128,3072]{1,0:T(8,128)(2,1)S(1)}, bf16[128,3072]{1,0:T(8,128)(2,1)S(1)}, u32[]{:S(2)}, u32[]{:S(2)}) %collective-permute-start.7) | collective-permute-done | bytes 786464 | tf_op jit(solution)/shard_map/ppermute | solution.py:56
  53.8 1.8 %collective-permute-start.11 = (bf16[32,3072]{1,0:T(8,128)(2,1)S(1)}, bf16[32,3072]{1,0:T(8,128)(2,1)S(1)}, u32[]{:S(2)}, u32[]{:S(2)}) collective-permute-start(bf16[32,3072]{1,0:T(8,128)(2,1)S(1)} %get-tuple-element.115), channel_id=1, source_target_pairs={{0,4},{1,17},{2,6},{3,19},{4,0},{5,21},{6,2},{7,23},{8,12},{9,25},... | collective-permute-start | bytes 589832 | tf_op jit(solution)/shard_map/ppermute | solution.py:56
  55.7 1.9 %collective-permute-start.12 = (bf16[32,3072]{1,0:T(8,128)(2,1)S(1)}, bf16[32,3072]{1,0:T(8,128)(2,1)S(1)}, u32[]{:S(2)}, u32[]{:S(2)}) collective-permute-start(bf16[32,3072]{1,0:T(8,128)(2,1)S(1)} %get-tuple-element.116), channel_id=1, source_target_pairs={{0,2},{1,9},{2,4},{3,11},{4,6},{5,13},{6,0},{7,15},{8,10},{9,17},{... | collective-permute-start | bytes 589832 | tf_op jit(solution)/shard_map/ppermute | solution.py:56
  57.7 2.6 %collective-permute-start.9 = (bf16[128,512]{1,0:T(8,128)(2,1)S(1)}, bf16[128,512]{1,0:T(8,128)(2,1)S(1)}, u32[]{:S(2)}, u32[]{:S(2)}) collective-permute-start(bf16[128,512]{1,0:T(8,128)(2,1)S(1)} %get-tuple-element.110), channel_id=1, source_target_pairs={{2,0},{3,1},{4,2},{5,3},{6,4},{7,5},{8,6},{9,7},{10,8},{11,9},{12,... | collective-permute-start | bytes 393224 | tf_op jit(solution)/shard_map/ppermute | solution.py:68
  60.4 2.9 %collective-permute-start.10 = (bf16[128,512]{1,0:T(8,128)(2,1)S(1)}, bf16[128,512]{1,0:T(8,128)(2,1)S(1)}, u32[]{:S(2)}, u32[]{:S(2)}) collective-permute-start(bf16[128,512]{1,0:T(8,128)(2,1)S(1)} %get-tuple-element.111), channel_id=1, source_target_pairs={{2,0},{3,1},{4,2},{5,3},{6,4},{7,5},{8,6},{9,7},{10,8},{11,9},{12,... | collective-permute-start | bytes 393224 | tf_op jit(solution)/shard_map/ppermute | solution.py:68
  63.3 6.7 %collective-permute-done.13.refs_3_ = bf16[32,3072]{1,0:T(8,128)(2,1)S(1)} collective-permute-done((bf16[32,3072]{1,0:T(8,128)(2,1)S(1)}, bf16[32,3072]{1,0:T(8,128)(2,1)S(1)}, u32[]{:S(2)}, u32[]{:S(2)}) %collective-permute-start.13) | collective-permute-done | bytes 196640 | tf_op jit(solution)/shard_map/ppermute | solution.py:56
  70.2 3.3 %collective-permute-start.14 = (bf16[8,3072]{1,0:T(8,128)(2,1)S(1)}, bf16[8,3072]{1,0:T(8,128)(2,1)S(1)}, u32[]{:S(2)}, u32[]{:S(2)}) collective-permute-start(bf16[8,3072]{1,0:T(8,128)(2,1)S(1)} %get-tuple-element.119), channel_id=1, source_target_pairs={{0,64},{1,65},{2,66},{3,67},{4,68},{5,69},{6,70},{7,71},{8,72},{9,... | collective-permute-start | bytes 147464 | tf_op jit(solution)/shard_map/ppermute | solution.py:62
  73.5 3.1 %collective-permute-start.15 = (bf16[8,3072]{1,0:T(8,128)(2,1)S(1)}, bf16[8,3072]{1,0:T(8,128)(2,1)S(1)}, u32[]{:S(2)}, u32[]{:S(2)}) collective-permute-start(bf16[8,3072]{1,0:T(8,128)(2,1)S(1)} %get-tuple-element.120), channel_id=1, source_target_pairs={{0,192},{1,193},{2,194},{3,195},{4,196},{5,197},{6,198},{7,199},{8... | collective-permute-start | bytes 147464 | tf_op jit(solution)/shard_map/ppermute | solution.py:62
  76.6 4.9 %collective-permute-start.16 = (bf16[8,3072]{1,0:T(8,128)(2,1)S(1)}, bf16[8,3072]{1,0:T(8,128)(2,1)S(1)}, u32[]{:S(2)}, u32[]{:S(2)}) collective-permute-start(bf16[8,3072]{1,0:T(8,128)(2,1)S(1)} %get-tuple-element.121), channel_id=1, source_target_pairs={{0,128},{1,129},{2,130},{3,131},{4,132},{5,133},{6,134},{7,135},{8... | collective-permute-start | bytes 147464 | tf_op jit(solution)/shard_map/ppermute | solution.py:62
  82.2 2.4 %collective-permute-done.16.c_ref = bf16[8,3072]{1,0:T(8,128)(2,1)S(1)} collective-permute-done((bf16[8,3072]{1,0:T(8,128)(2,1)S(1)}, bf16[8,3072]{1,0:T(8,128)(2,1)S(1)}, u32[]{:S(2)}, u32[]{:S(2)}) %collective-permute-start.16) | collective-permute-done | bytes 49184 | tf_op jit(solution)/shard_map/ppermute | solution.py:62
  86.1 2.1 %tail.1 = bf16[128,1024]{1,0:T(8,128)(2,1)} custom-call(s32[5]{0:T(128)S(1)} %stack.32.place, f32[128,1024]{1,0:T(8,128)S(1)} %get-tuple-element.99.base_ref, f32[2,128,384]{2,1,0:T(8,128)S(1)} %get-tuple-element.100.own_one, f32[2,128,128]{2,1,0:T(8,128)S(1)} %get-tuple-element.101.own_two, f32[128,512]{1,0:T(8,128)S(1)} %get-tuple-element.113.mine_ref, ...), custom_call_target="tpu_custom_call" | custom-call | tf_op jit(solution)/shard_map/tail/pallas_call | solution.py:429
  88.2 1.7 %collective-permute-done.18.got_ref = bf16[4,3072]{1,0:T(4,128)(2,1)S(1)} collective-permute-done((bf16[4,3072]{1,0:T(4,128)(2,1)S(1)}, bf16[4,3072]{1,0:T(4,128)(2,1)S(1)}, u32[]{:S(2)}, u32[]{:S(2)}) %collective-permute-start.18) | collective-permute-done | bytes 24608 | tf_op jit(solution)/shard_map/ppermute | solution.py:62
  (41 shorter events, 7.2 us)
Async XLA Ops:
  0.6 10.5 %copy-start.2 = (bf16[128,1024]{1,0:T(8,128)(2,1)S(1)}, bf16[128,1024]{1,0:T(8,128)(2,1)}, u32[]{:S(2)}) copy-start(bf16[128,1024]{1,0:T(8,128)(2,1)} %own_ref.3) | copy-start | bytes 786436
  0.6 10.5 %copy-start.3 = (bf16[128,1024]{1,0:T(8,128)(2,1)S(1)}, bf16[128,1024]{1,0:T(8,128)(2,1)}, u32[]{:S(2)}) copy-start(bf16[128,1024]{1,0:T(8,128)(2,1)} %b_ref.1) | copy-start | bytes 786436
  0.7 9.0 %collective-permute-start = (bf16[128,1024]{1,0:T(8,128)(2,1)}, bf16[128,1024]{1,0:T(8,128)(2,1)S(1)}, u32[]{:S(2)}, u32[]{:S(2)}) collective-permute-start(bf16[128,1024]{1,0:T(8,128)(2,1)} %own_ref.3), channel_id=1, source_target_pairs={{0,1},{1,2},{2,3},{3,4},{4,5},{5,6},{6,7},{7,8},{8,9},{9,10},{10,1... | collective-permute-start | bytes 786440 | tf_op jit(solution)/shard_map/ppermute | solution.py:68
  2.7 9.7 %collective-permute-start.1 = (bf16[128,1024]{1,0:T(8,128)(2,1)}, bf16[128,1024]{1,0:T(8,128)(2,1)S(1)}, u32[]{:S(2)}, u32[]{:S(2)}) collective-permute-start(bf16[128,1024]{1,0:T(8,128)(2,1)} %own_ref.3), channel_id=1, source_target_pairs={{0,2},{2,4},{4,6},{6,8},{8,10},{10,12},{12,14},{14,16},{16,18},{18... | collective-permute-start | bytes 786440 | tf_op jit(solution)/shard_map/ppermute | solution.py:68
  9.7 2.7 %collective-permute-start.2 = (bf16[128,1024]{1,0:T(8,128)(2,1)S(1)}, bf16[128,1024]{1,0:T(8,128)(2,1)S(1)}, u32[]{:S(2)}, u32[]{:S(2)}) collective-permute-start(bf16[128,1024]{1,0:T(8,128)(2,1)S(1)} %collective-permute-done.near_ref), channel_id=1, source_target_pairs={{0,1},{2,3},{4,5},{6,7},{8,9},{10,11},{12,13},{14,15},{16,17},{18,... | collective-permute-start | bytes 786440 | tf_op jit(solution)/shard_map/ppermute | solution.py:68
  24.6 4.8 %collective-permute-start.4 = (bf16[512,2304]{1,0:T(8,128)(2,1)S(1)}, bf16[512,2304]{1,0:T(8,128)(2,1)S(1)}, u32[]{:S(2)}, u32[]{:S(2)}) collective-permute-start(bf16[512,2304]{1,0:T(8,128)(2,1)S(1)} %get-tuple-element.81), channel_id=1, source_target_pairs={{0,1},{1,0},{2,3},{3,2},{4,5},{5,4},{6,7},{7,6},{8,9},{9,8},{10,11... | collective-permute-start | bytes 7077896 | tf_op jit(solution)/shard_map/ppermute | solution.py:45
  28.9 2.4 %collective-permute-start.3 = (bf16[512,768]{1,0:T(8,128)(2,1)S(1)}, bf16[512,768]{1,0:T(8,128)(2,1)S(1)}, u32[]{:S(2)}, u32[]{:S(2)}) collective-permute-start(bf16[512,768]{1,0:T(8,128)(2,1)S(1)} %get-tuple-element.80), channel_id=1, source_target_pairs={{0,1},{1,0},{2,3},{3,2},{4,5},{5,4},{6,7},{7,6},{8,9},{9,8},{10,11... | collective-permute-start | bytes 2359304 | tf_op jit(solution)/shard_map/ppermute | solution.py:45
  31.5 13.7 %collective-permute-start.6 = (bf16[128,3072]{1,0:T(8,128)(2,1)S(1)}, bf16[128,3072]{1,0:T(8,128)(2,1)S(1)}, u32[]{:S(2)}, u32[]{:S(2)}) collective-permute-start(bf16[128,3072]{1,0:T(8,128)(2,1)S(1)} %get-tuple-element.106), channel_id=1, source_target_pairs={{0,16},{1,5},{2,18},{3,7},{4,20},{5,1},{6,22},{7,3},{8,24},{9,13},... | collective-permute-start | bytes 2359304 | tf_op jit(solution)/shard_map/ppermute | solution.py:56
  34.0 19.2 %collective-permute-start.7 = (bf16[128,3072]{1,0:T(8,128)(2,1)S(1)}, bf16[128,3072]{1,0:T(8,128)(2,1)S(1)}, u32[]{:S(2)}, u32[]{:S(2)}) collective-permute-start(bf16[128,3072]{1,0:T(8,128)(2,1)S(1)} %get-tuple-element.107), channel_id=1, source_target_pairs={{0,8},{1,3},{2,10},{3,5},{4,12},{5,7},{6,14},{7,1},{8,16},{9,11},{... | collective-permute-start | bytes 2359304 | tf_op jit(solution)/shard_map/ppermute | solution.py:56
  34.0 19.5 %collective-permute-start.8 = (bf16[128,3072]{1,0:T(8,128)(2,1)S(1)}, bf16[128,3072]{1,0:T(8,128)(2,1)S(1)}, u32[]{:S(2)}, u32[]{:S(2)}) collective-permute-start(bf16[128,3072]{1,0:T(8,128)(2,1)S(1)} %get-tuple-element.108), channel_id=1, source_target_pairs={{0,24},{1,7},{2,26},{3,1},{4,28},{5,3},{6,30},{7,5},{8,0},{9,15},{... | collective-permute-start | bytes 2359304 | tf_op jit(solution)/shard_map/ppermute | solution.py:56
  36.1 4.4 %collective-permute-start.5 = (bf16[2,128,512]{2,1,0:T(8,128)(2,1)S(1)}, bf16[2,128,512]{2,1,0:T(8,128)(2,1)S(1)}, u32[]{:S(2)}, u32[]{:S(2)}) collective-permute-start(bf16[2,128,512]{2,1,0:T(8,128)(2,1)S(1)} %get-tuple-element.103), channel_id=1, source_target_pairs={{0,1},{1,0},{2,3},{3,2},{4,5},{5,4},{6,7},{7,6},{8,9},{9,8},{10,11... | collective-permute-start | bytes 786440 | tf_op jit(solution)/shard_map/ppermute | solution.py:45
  53.8 32.3 %copy-start = (bf16[1024,512]{1,0:T(8,128)(2,1)S(1)}, bf16[1024,512]{1,0:T(8,128)(2,1)}, u32[]{:S(2)}) copy-start(bf16[1024,512]{1,0:T(8,128)(2,1)} %wk_ref.5) | copy-start | bytes 3145732
  53.8 32.3 %copy-start.1 = (bf16[1024,512]{1,0:T(8,128)(2,1)S(1)}, bf16[1024,512]{1,0:T(8,128)(2,1)}, u32[]{:S(2)}) copy-start(bf16[1024,512]{1,0:T(8,128)(2,1)} %wv_ref.5) | copy-start | bytes 3145732
  53.8 9.5 %collective-permute-start.11 = (bf16[32,3072]{1,0:T(8,128)(2,1)S(1)}, bf16[32,3072]{1,0:T(8,128)(2,1)S(1)}, u32[]{:S(2)}, u32[]{:S(2)}) collective-permute-start(bf16[32,3072]{1,0:T(8,128)(2,1)S(1)} %get-tuple-element.115), channel_id=1, source_target_pairs={{0,4},{1,17},{2,6},{3,19},{4,0},{5,21},{6,2},{7,23},{8,12},{9,25},... | collective-permute-start | bytes 589832 | tf_op jit(solution)/shard_map/ppermute | solution.py:56
  55.7 7.6 %collective-permute-start.12 = (bf16[32,3072]{1,0:T(8,128)(2,1)S(1)}, bf16[32,3072]{1,0:T(8,128)(2,1)S(1)}, u32[]{:S(2)}, u32[]{:S(2)}) collective-permute-start(bf16[32,3072]{1,0:T(8,128)(2,1)S(1)} %get-tuple-element.116), channel_id=1, source_target_pairs={{0,2},{1,9},{2,4},{3,11},{4,6},{5,13},{6,0},{7,15},{8,10},{9,17},{... | collective-permute-start | bytes 589832 | tf_op jit(solution)/shard_map/ppermute | solution.py:56
  57.6 12.5 %collective-permute-start.13 = (bf16[32,3072]{1,0:T(8,128)(2,1)S(1)}, bf16[32,3072]{1,0:T(8,128)(2,1)S(1)}, u32[]{:S(2)}, u32[]{:S(2)}) collective-permute-start(bf16[32,3072]{1,0:T(8,128)(2,1)S(1)} %get-tuple-element.117), channel_id=1, source_target_pairs={{0,6},{1,25},{2,0},{3,27},{4,2},{5,29},{6,4},{7,31},{8,14},{9,1},{... | collective-permute-start | bytes 589832 | tf_op jit(solution)/shard_map/ppermute | solution.py:56
  57.7 23.9 %collective-permute-start.9 = (bf16[128,512]{1,0:T(8,128)(2,1)S(1)}, bf16[128,512]{1,0:T(8,128)(2,1)S(1)}, u32[]{:S(2)}, u32[]{:S(2)}) collective-permute-start(bf16[128,512]{1,0:T(8,128)(2,1)S(1)} %get-tuple-element.110), channel_id=1, source_target_pairs={{2,0},{3,1},{4,2},{5,3},{6,4},{7,5},{8,6},{9,7},{10,8},{11,9},{12,... | collective-permute-start | bytes 393224 | tf_op jit(solution)/shard_map/ppermute | solution.py:68
  60.4 21.2 %collective-permute-start.10 = (bf16[128,512]{1,0:T(8,128)(2,1)S(1)}, bf16[128,512]{1,0:T(8,128)(2,1)S(1)}, u32[]{:S(2)}, u32[]{:S(2)}) collective-permute-start(bf16[128,512]{1,0:T(8,128)(2,1)S(1)} %get-tuple-element.111), channel_id=1, source_target_pairs={{2,0},{3,1},{4,2},{5,3},{6,4},{7,5},{8,6},{9,7},{10,8},{11,9},{12,... | collective-permute-start | bytes 393224 | tf_op jit(solution)/shard_map/ppermute | solution.py:68
  70.2 12.1 %collective-permute-start.14 = (bf16[8,3072]{1,0:T(8,128)(2,1)S(1)}, bf16[8,3072]{1,0:T(8,128)(2,1)S(1)}, u32[]{:S(2)}, u32[]{:S(2)}) collective-permute-start(bf16[8,3072]{1,0:T(8,128)(2,1)S(1)} %get-tuple-element.119), channel_id=1, source_target_pairs={{0,64},{1,65},{2,66},{3,67},{4,68},{5,69},{6,70},{7,71},{8,72},{9,... | collective-permute-start | bytes 147464 | tf_op jit(solution)/shard_map/ppermute | solution.py:62
  73.5 8.7 %collective-permute-start.15 = (bf16[8,3072]{1,0:T(8,128)(2,1)S(1)}, bf16[8,3072]{1,0:T(8,128)(2,1)S(1)}, u32[]{:S(2)}, u32[]{:S(2)}) collective-permute-start(bf16[8,3072]{1,0:T(8,128)(2,1)S(1)} %get-tuple-element.120), channel_id=1, source_target_pairs={{0,192},{1,193},{2,194},{3,195},{4,196},{5,197},{6,198},{7,199},{8... | collective-permute-start | bytes 147464 | tf_op jit(solution)/shard_map/ppermute | solution.py:62
  76.6 8.0 %collective-permute-start.16 = (bf16[8,3072]{1,0:T(8,128)(2,1)S(1)}, bf16[8,3072]{1,0:T(8,128)(2,1)S(1)}, u32[]{:S(2)}, u32[]{:S(2)}) collective-permute-start(bf16[8,3072]{1,0:T(8,128)(2,1)S(1)} %get-tuple-element.121), channel_id=1, source_target_pairs={{0,128},{1,129},{2,130},{3,131},{4,132},{5,133},{6,134},{7,135},{8... | collective-permute-start | bytes 147464 | tf_op jit(solution)/shard_map/ppermute | solution.py:62
  84.7 1.4 %collective-permute-start.17 = (bf16[128,512]{1,0:T(8,128)(2,1)S(1)}, bf16[128,512]{1,0:T(8,128)(2,1)S(1)}, u32[]{:S(2)}, u32[]{:S(2)}) collective-permute-start(bf16[128,512]{1,0:T(8,128)(2,1)S(1)} %get-tuple-element.123), channel_id=1, source_target_pairs={{0,1},{1,0},{2,3},{3,2},{4,5},{5,4},{6,7},{7,6},{8,9},{9,8},{10,11... | collective-permute-start | bytes 393224 | tf_op jit(solution)/shard_map/ppermute | solution.py:45
  84.8 5.1 %collective-permute-start.18 = (bf16[4,3072]{1,0:T(4,128)(2,1)S(1)}, bf16[4,3072]{1,0:T(4,128)(2,1)S(1)}, u32[]{:S(2)}, u32[]{:S(2)}) collective-permute-start(bf16[4,3072]{1,0:T(4,128)(2,1)S(1)} %get-tuple-element.125), channel_id=1, source_target_pairs={{0,32},{1,33},{2,34},{3,35},{4,36},{5,37},{6,38},{7,39},{8,40},{9,... | collective-permute-start | bytes 73736 | tf_op jit(solution)/shard_map/ppermute | solution.py:62

commit v10 on v9

--- a/solution.py
+++ b/solution.py
@@ -536,7 +536,7 @@
     ring_two = ring([None, *sends], 1)
     back = jnp.stack([passed_along(after(back[i], own), -2) for i in range(2)])
     own, *sends = folded(own, *ring_two)
-    ring_three = [along_z(sends[d - 1], 2 * d) for d in (1, 3, 2)]
+    ring_three = [along_z(sends[d - 1], 2 * d) for d in (2, 1, 3)]
     own, send = halved(own, *ring_three)
     got = along_z(send, 1)
     mine, other = turned(place, back, near_one)

time: 90.9 us -> 90.4 us (level)
  waiting for transfers between devices: 23.6 us -> 22.6 us
where the time goes in v10:
time: 90.4 us; the launch traced here: 90 us
  starting transfers between devices  34.2 us (38%)
  Pallas kernels  32.1 us (36%)
  waiting for transfers between devices  22.6 us (25%)
  between operations  0.93 us (1%)
    ppermute x6, waiting for transfers between devices, ring(): lax.ppermute(blocks[d], AXIS, route_of(functools.partial(plane_step, phas...  19 us
    pallas_call x2, Pallas kernels, attention(): pl.pallas_call(attention_kernel, grid=(steps,), out_shape=(struct(ROWS, Q...  15 us
    ppermute x4, starting transfers between devices, along_z(): lax.ppermute(block, AXIS, route_of(lambda z, x, y, c: ((z + distance) % 8...  13 us
    ppermute x5, starting transfers between devices, passed_along(): lax.ppermute(block, AXIS, [(i, i + distance) for i in sources if i + dist...  12 us
    ppermute x6, starting transfers between devices, ring(): lax.ppermute(blocks[d], AXIS, route_of(functools.partial(plane_step, phas...  8.43 us
    pallas_call x1, Pallas kernels, middle(): pl.pallas_call(middle_kernel, grid=(STEPS,), out_shape=(jax.ShapeDtypeStr...  4.36 us
    pallas_call x1, Pallas kernels, early(): pl.pallas_call(early_kernel, grid=(STEPS,), out_shape=(jax.ShapeDtypeStru...  3.9 us
    ppermute x4, waiting for transfers between devices, along_z(): lax.ppermute(block, AXIS, route_of(lambda z, x, y, c: ((z + distance) % 8...  3.37 us
  transfers between devices with their start and end apart: 19, of which 8 were waited for; matrix products, arithmetic and copies ran while one was open for 0% of the time, Pallas kernels for 21%

profile of v10, /device:TPU:26, one launch (start us, length us, event | category | flops | bytes accessed | tf_op | source)
XLA Modules:
  0.0 90.0 jit_solution(10905024939727409615)
XLA Ops:
  0.7 2.1 %collective-permute-start = (bf16[128,1024]{1,0:T(8,128)(2,1)}, bf16[128,1024]{1,0:T(8,128)(2,1)S(1)}, u32[]{:S(2)}, u32[]{:S(2)}) collective-permute-start(bf16[128,1024]{1,0:T(8,128)(2,1)} %own_ref.3), channel_id=1, source_target_pairs={{0,1},{1,2},{2,3},{3,4},{4,5},{5,6},{6,7},{7,8},{8,9},{9,10},{10,1... | collective-permute-start | bytes 786440 | tf_op jit(solution)/shard_map/ppermute | solution.py:68
  2.7 3.1 %collective-permute-start.1 = (bf16[128,1024]{1,0:T(8,128)(2,1)}, bf16[128,1024]{1,0:T(8,128)(2,1)S(1)}, u32[]{:S(2)}, u32[]{:S(2)}) collective-permute-start(bf16[128,1024]{1,0:T(8,128)(2,1)} %own_ref.3), channel_id=1, source_target_pairs={{0,2},{2,4},{4,6},{6,8},{8,10},{10,12},{12,14},{14,16},{16,18},{18... | collective-permute-start | bytes 786440 | tf_op jit(solution)/shard_map/ppermute | solution.py:68
  5.8 3.9 %early.1 = (bf16[128,1024]{1,0:T(8,128)(2,1)S(1)}, bf16[128,1024]{1,0:T(8,128)(2,1)S(1)}) custom-call(bf16[128,1024]{1,0:T(8,128)(2,1)} %own_ref.3, bf16[128,1024]{1,0:T(8,128)(2,1)} %b_ref.1, bf16[1024,1024]{1,0:T(8,128)(2,1)} %wq_ref.3, bf16[1024,1024]{1,0:T(8,128)(2,1)} %wo_ref.3), custom_call_target="tpu_custom_call" | custom-call | tf_op jit(solution)/shard_map/early/pallas_call | solution.py:109
  9.7 1.3 %collective-permute-start.2 = (bf16[128,1024]{1,0:T(8,128)(2,1)S(1)}, bf16[128,1024]{1,0:T(8,128)(2,1)S(1)}, u32[]{:S(2)}, u32[]{:S(2)}) collective-permute-start(bf16[128,1024]{1,0:T(8,128)(2,1)S(1)} %collective-permute-done.near_ref), channel_id=1, source_target_pairs={{0,1},{2,3},{4,5},{6,7},{8,9},{10,11},{12,13},{14,15},{16,17},{18,... | collective-permute-start | bytes 786440 | tf_op jit(solution)/shard_map/ppermute | solution.py:68
  12.4 1.2 %prep.3 = (bf16[2,512,256]{2,1,0:T(8,128)(2,1)S(1)}, bf16[128,1024]{1,0:T(8,128)(2,1)S(1)}) custom-call(s32[5]{0:T(128)S(1)} %stack.32.place, bf16[128,1024]{1,0:T(8,128)(2,1)S(1)} %collective-permute-done.1.far_ref, bf16[128,1024]{1,0:T(8,128)(2,1)S(1)} %collective-permute-done.2.mate_ref, bf16[128,1024]{1,0:T(8,128)(2,1)S(1)} %collective-permute-done.near_ref), custom_call_target="tpu_custom_call" | custom-call | tf_op jit(solution)/shard_map/prep/pallas_call | solution.py:148
  13.6 10.9 %attention.2 = (bf16[128,768]{1,0:T(8,128)(2,1)S(1)}, bf16[128,768]{1,0:T(8,128)(2,1)S(1)}, f32[2,128,384]{2,1,0:T(8,128)S(1)}, bf16[2,128,384]{2,1,0:T(8,128)(2...) custom-call(s32[5]{0:T(128)S(1)} %stack.32.place, ...), custom_call_target="tpu_custom_call" | custom-call | flops 1000 | bytes 1000 | tf_op jit(solution)/shard_map/attention/pallas_call | solution.py:255
  24.8 4.1 %attention.3 = (bf16[128,256]{1,0:T(8,128)(2,1)S(1)}, bf16[128,256]{1,0:T(8,128)(2,1)S(1)}, f32[2,128,128]{2,1,0:T(8,128)S(1)}, bf16[2,128,128]{2,1,0:T(8,128)(2...) custom-call(s32[5]{0:T(128)S(1)} %stack.32.place, ...), custom_call_target="tpu_custom_call" | custom-call | flops 1000 | bytes 1000 | tf_op jit(solution)/shard_map/attention/pallas_call | solution.py:255
  31.5 2.6 %collective-permute-start.6 = (bf16[128,3072]{1,0:T(8,128)(2,1)S(1)}, bf16[128,3072]{1,0:T(8,128)(2,1)S(1)}, u32[]{:S(2)}, u32[]{:S(2)}) collective-permute-start(bf16[128,3072]{1,0:T(8,128)(2,1)S(1)} %get-tuple-element.106), channel_id=1, source_target_pairs={{0,16},{1,5},{2,18},{3,7},{4,20},{5,1},{6,22},{7,3},{8,24},{9,13},... | collective-permute-start | bytes 2359304 | tf_op jit(solution)/shard_map/ppermute | solution.py:56
  34.0 2.0 %collective-permute-start.8 = (bf16[128,3072]{1,0:T(8,128)(2,1)S(1)}, bf16[128,3072]{1,0:T(8,128)(2,1)S(1)}, u32[]{:S(2)}, u32[]{:S(2)}) collective-permute-start(bf16[128,3072]{1,0:T(8,128)(2,1)S(1)} %get-tuple-element.108), channel_id=1, source_target_pairs={{0,24},{1,7},{2,26},{3,1},{4,28},{5,3},{6,30},{7,5},{8,0},{9,15},{... | collective-permute-start | bytes 2359304 | tf_op jit(solution)/shard_map/ppermute | solution.py:56
  36.1 4.4 %middle.1 = (bf16[128,1024]{1,0:T(8,128)(2,1)}, f32[128,1024]{1,0:T(8,128)S(1)}) custom-call(bf16[128,768]{1,0:T(8,128)(2,1)S(1)} %get-tuple-element.75.att_one, bf16[128,256]{1,0:T(8,128)(2,1)S(1)} %get-tuple-element.95.att_two, bf16[128,768]{1,0:T(8,128)(2,1)S(1)} %get-tuple-element.96.dq_one, bf16[128,256]{1,0:T(8,128)(2,1)S(1)} %get-tuple-element.97.dq_two, ...), custom_call_target="tpu_custom_call" | custom-call | tf_op jit(solution)/shard_map/middle/pallas_call | solution.py:401
  41.2 4.0 %collective-permute-done.6.refs_1_ = bf16[128,3072]{1,0:T(8,128)(2,1)S(1)} collective-permute-done((bf16[128,3072]{1,0:T(8,128)(2,1)S(1)}, bf16[128,3072]{1,0:T(8,128)(2,1)S(1)}, u32[]{:S(2)}, u32[]{:S(2)}) %collective-permute-start.6) | collective-permute-done | bytes 786464 | tf_op jit(solution)/shard_map/ppermute | solution.py:56
  45.2 8.1 %collective-permute-done.7.refs_2_ = bf16[128,3072]{1,0:T(8,128)(2,1)S(1)} collective-permute-done((bf16[128,3072]{1,0:T(8,128)(2,1)S(1)}, bf16[128,3072]{1,0:T(8,128)(2,1)S(1)}, u32[]{:S(2)}, u32[]{:S(2)}) %collective-permute-start.7) | collective-permute-done | bytes 786464 | tf_op jit(solution)/shard_map/ppermute | solution.py:56
  53.8 1.8 %collective-permute-start.11 = (bf16[32,3072]{1,0:T(8,128)(2,1)S(1)}, bf16[32,3072]{1,0:T(8,128)(2,1)S(1)}, u32[]{:S(2)}, u32[]{:S(2)}) collective-permute-start(bf16[32,3072]{1,0:T(8,128)(2,1)S(1)} %get-tuple-element.115), channel_id=1, source_target_pairs={{0,4},{1,17},{2,6},{3,19},{4,0},{5,21},{6,2},{7,23},{8,12},{9,25},... | collective-permute-start | bytes 589832 | tf_op jit(solution)/shard_map/ppermute | solution.py:56
  55.7 1.9 %collective-permute-start.12 = (bf16[32,3072]{1,0:T(8,128)(2,1)S(1)}, bf16[32,3072]{1,0:T(8,128)(2,1)S(1)}, u32[]{:S(2)}, u32[]{:S(2)}) collective-permute-start(bf16[32,3072]{1,0:T(8,128)(2,1)S(1)} %get-tuple-element.116), channel_id=1, source_target_pairs={{0,2},{1,9},{2,4},{3,11},{4,6},{5,13},{6,0},{7,15},{8,10},{9,17},{... | collective-permute-start | bytes 589832 | tf_op jit(solution)/shard_map/ppermute | solution.py:56
  57.7 2.6 %collective-permute-start.9 = (bf16[128,512]{1,0:T(8,128)(2,1)S(1)}, bf16[128,512]{1,0:T(8,128)(2,1)S(1)}, u32[]{:S(2)}, u32[]{:S(2)}) collective-permute-start(bf16[128,512]{1,0:T(8,128)(2,1)S(1)} %get-tuple-element.110), channel_id=1, source_target_pairs={{2,0},{3,1},{4,2},{5,3},{6,4},{7,5},{8,6},{9,7},{10,8},{11,9},{12,... | collective-permute-start | bytes 393224 | tf_op jit(solution)/shard_map/ppermute | solution.py:68
  60.4 2.9 %collective-permute-start.10 = (bf16[128,512]{1,0:T(8,128)(2,1)S(1)}, bf16[128,512]{1,0:T(8,128)(2,1)S(1)}, u32[]{:S(2)}, u32[]{:S(2)}) collective-permute-start(bf16[128,512]{1,0:T(8,128)(2,1)S(1)} %get-tuple-element.111), channel_id=1, source_target_pairs={{2,0},{3,1},{4,2},{5,3},{6,4},{7,5},{8,6},{9,7},{10,8},{11,9},{12,... | collective-permute-start | bytes 393224 | tf_op jit(solution)/shard_map/ppermute | solution.py:68
  63.3 6.7 %collective-permute-done.13.refs_3_ = bf16[32,3072]{1,0:T(8,128)(2,1)S(1)} collective-permute-done((bf16[32,3072]{1,0:T(8,128)(2,1)S(1)}, bf16[32,3072]{1,0:T(8,128)(2,1)S(1)}, u32[]{:S(2)}, u32[]{:S(2)}) %collective-permute-start.13) | collective-permute-done | bytes 196640 | tf_op jit(solution)/shard_map/ppermute | solution.py:56
  70.2 7.3 %collective-permute-start.14 = (bf16[8,3072]{1,0:T(8,128)(2,1)S(1)}, bf16[8,3072]{1,0:T(8,128)(2,1)S(1)}, u32[]{:S(2)}, u32[]{:S(2)}) collective-permute-start(bf16[8,3072]{1,0:T(8,128)(2,1)S(1)} %get-tuple-element.119), channel_id=1, source_target_pairs={{0,128},{1,129},{2,130},{3,131},{4,132},{5,133},{6,134},{7,135},{8... | collective-permute-start | bytes 147464 | tf_op jit(solution)/shard_map/ppermute | solution.py:62
  77.4 1.5 %collective-permute-start.15 = (bf16[8,3072]{1,0:T(8,128)(2,1)S(1)}, bf16[8,3072]{1,0:T(8,128)(2,1)S(1)}, u32[]{:S(2)}, u32[]{:S(2)}) collective-permute-start(bf16[8,3072]{1,0:T(8,128)(2,1)S(1)} %get-tuple-element.120), channel_id=1, source_target_pairs={{0,64},{1,65},{2,66},{3,67},{4,68},{5,69},{6,70},{7,71},{8,72},{9,... | collective-permute-start | bytes 147464 | tf_op jit(solution)/shard_map/ppermute | solution.py:62
  78.9 2.7 %collective-permute-start.16 = (bf16[8,3072]{1,0:T(8,128)(2,1)S(1)}, bf16[8,3072]{1,0:T(8,128)(2,1)S(1)}, u32[]{:S(2)}, u32[]{:S(2)}) collective-permute-start(bf16[8,3072]{1,0:T(8,128)(2,1)S(1)} %get-tuple-element.121), channel_id=1, source_target_pairs={{0,192},{1,193},{2,194},{3,195},{4,196},{5,197},{6,198},{7,199},{8... | collective-permute-start | bytes 147464 | tf_op jit(solution)/shard_map/ppermute | solution.py:62
  82.2 1.5 %collective-permute-done.15.b_ref = bf16[8,3072]{1,0:T(8,128)(2,1)S(1)} collective-permute-done((bf16[8,3072]{1,0:T(8,128)(2,1)S(1)}, bf16[8,3072]{1,0:T(8,128)(2,1)S(1)}, u32[]{:S(2)}, u32[]{:S(2)}) %collective-permute-start.15) | collective-permute-done | bytes 49184 | tf_op jit(solution)/shard_map/ppermute | solution.py:62
  84.0 1.6 %collective-permute-start.18 = (bf16[4,3072]{1,0:T(4,128)(2,1)S(1)}, bf16[4,3072]{1,0:T(4,128)(2,1)S(1)}, u32[]{:S(2)}, u32[]{:S(2)}) collective-permute-start(bf16[4,3072]{1,0:T(4,128)(2,1)S(1)} %get-tuple-element.125), channel_id=1, source_target_pairs={{0,32},{1,33},{2,34},{3,35},{4,36},{5,37},{6,38},{7,39},{8,40},{9,... | collective-permute-start | bytes 73736 | tf_op jit(solution)/shard_map/ppermute | solution.py:62
  85.7 2.1 %tail.1 = bf16[128,1024]{1,0:T(8,128)(2,1)} custom-call(s32[5]{0:T(128)S(1)} %stack.32.place, f32[128,1024]{1,0:T(8,128)S(1)} %get-tuple-element.99.base_ref, f32[2,128,384]{2,1,0:T(8,128)S(1)} %get-tuple-element.100.own_one, f32[2,128,128]{2,1,0:T(8,128)S(1)} %get-tuple-element.101.own_two, f32[128,512]{1,0:T(8,128)S(1)} %get-tuple-element.113.mine_ref, ...), custom_call_target="tpu_custom_call" | custom-call | tf_op jit(solution)/shard_map/tail/pallas_call | solution.py:429
  87.7 1.7 %collective-permute-done.18.got_ref = bf16[4,3072]{1,0:T(4,128)(2,1)S(1)} collective-permute-done((bf16[4,3072]{1,0:T(4,128)(2,1)S(1)}, bf16[4,3072]{1,0:T(4,128)(2,1)S(1)}, u32[]{:S(2)}, u32[]{:S(2)}) %collective-permute-start.18) | collective-permute-done | bytes 24608 | tf_op jit(solution)/shard_map/ppermute | solution.py:62
  (41 shorter events, 7.2 us)
Async XLA Ops:
  0.6 10.5 %copy-start.2 = (bf16[128,1024]{1,0:T(8,128)(2,1)S(1)}, bf16[128,1024]{1,0:T(8,128)(2,1)}, u32[]{:S(2)}) copy-start(bf16[128,1024]{1,0:T(8,128)(2,1)} %own_ref.3) | copy-start | bytes 786436
  0.6 10.5 %copy-start.3 = (bf16[128,1024]{1,0:T(8,128)(2,1)S(1)}, bf16[128,1024]{1,0:T(8,128)(2,1)}, u32[]{:S(2)}) copy-start(bf16[128,1024]{1,0:T(8,128)(2,1)} %b_ref.1) | copy-start | bytes 786436
  0.7 9.0 %collective-permute-start = (bf16[128,1024]{1,0:T(8,128)(2,1)}, bf16[128,1024]{1,0:T(8,128)(2,1)S(1)}, u32[]{:S(2)}, u32[]{:S(2)}) collective-permute-start(bf16[128,1024]{1,0:T(8,128)(2,1)} %own_ref.3), channel_id=1, source_target_pairs={{0,1},{1,2},{2,3},{3,4},{4,5},{5,6},{6,7},{7,8},{8,9},{9,10},{10,1... | collective-permute-start | bytes 786440 | tf_op jit(solution)/shard_map/ppermute | solution.py:68
  2.7 9.7 %collective-permute-start.1 = (bf16[128,1024]{1,0:T(8,128)(2,1)}, bf16[128,1024]{1,0:T(8,128)(2,1)S(1)}, u32[]{:S(2)}, u32[]{:S(2)}) collective-permute-start(bf16[128,1024]{1,0:T(8,128)(2,1)} %own_ref.3), channel_id=1, source_target_pairs={{0,2},{2,4},{4,6},{6,8},{8,10},{10,12},{12,14},{14,16},{16,18},{18... | collective-permute-start | bytes 786440 | tf_op jit(solution)/shard_map/ppermute | solution.py:68
  9.7 2.7 %collective-permute-start.2 = (bf16[128,1024]{1,0:T(8,128)(2,1)S(1)}, bf16[128,1024]{1,0:T(8,128)(2,1)S(1)}, u32[]{:S(2)}, u32[]{:S(2)}) collective-permute-start(bf16[128,1024]{1,0:T(8,128)(2,1)S(1)} %collective-permute-done.near_ref), channel_id=1, source_target_pairs={{0,1},{2,3},{4,5},{6,7},{8,9},{10,11},{12,13},{14,15},{16,17},{18,... | collective-permute-start | bytes 786440 | tf_op jit(solution)/shard_map/ppermute | solution.py:68
  24.6 4.8 %collective-permute-start.4 = (bf16[512,2304]{1,0:T(8,128)(2,1)S(1)}, bf16[512,2304]{1,0:T(8,128)(2,1)S(1)}, u32[]{:S(2)}, u32[]{:S(2)}) collective-permute-start(bf16[512,2304]{1,0:T(8,128)(2,1)S(1)} %get-tuple-element.81), channel_id=1, source_target_pairs={{0,1},{1,0},{2,3},{3,2},{4,5},{5,4},{6,7},{7,6},{8,9},{9,8},{10,11... | collective-permute-start | bytes 7077896 | tf_op jit(solution)/shard_map/ppermute | solution.py:45
  28.9 2.4 %collective-permute-start.3 = (bf16[512,768]{1,0:T(8,128)(2,1)S(1)}, bf16[512,768]{1,0:T(8,128)(2,1)S(1)}, u32[]{:S(2)}, u32[]{:S(2)}) collective-permute-start(bf16[512,768]{1,0:T(8,128)(2,1)S(1)} %get-tuple-element.80), channel_id=1, source_target_pairs={{0,1},{1,0},{2,3},{3,2},{4,5},{5,4},{6,7},{7,6},{8,9},{9,8},{10,11... | collective-permute-start | bytes 2359304 | tf_op jit(solution)/shard_map/ppermute | solution.py:45
  31.5 13.7 %collective-permute-start.6 = (bf16[128,3072]{1,0:T(8,128)(2,1)S(1)}, bf16[128,3072]{1,0:T(8,128)(2,1)S(1)}, u32[]{:S(2)}, u32[]{:S(2)}) collective-permute-start(bf16[128,3072]{1,0:T(8,128)(2,1)S(1)} %get-tuple-element.106), channel_id=1, source_target_pairs={{0,16},{1,5},{2,18},{3,7},{4,20},{5,1},{6,22},{7,3},{8,24},{9,13},... | collective-permute-start | bytes 2359304 | tf_op jit(solution)/shard_map/ppermute | solution.py:56
  34.0 19.2 %collective-permute-start.7 = (bf16[128,3072]{1,0:T(8,128)(2,1)S(1)}, bf16[128,3072]{1,0:T(8,128)(2,1)S(1)}, u32[]{:S(2)}, u32[]{:S(2)}) collective-permute-start(bf16[128,3072]{1,0:T(8,128)(2,1)S(1)} %get-tuple-element.107), channel_id=1, source_target_pairs={{0,8},{1,3},{2,10},{3,5},{4,12},{5,7},{6,14},{7,1},{8,16},{9,11},{... | collective-permute-start | bytes 2359304 | tf_op jit(solution)/shard_map/ppermute | solution.py:56
  34.0 19.5 %collective-permute-start.8 = (bf16[128,3072]{1,0:T(8,128)(2,1)S(1)}, bf16[128,3072]{1,0:T(8,128)(2,1)S(1)}, u32[]{:S(2)}, u32[]{:S(2)}) collective-permute-start(bf16[128,3072]{1,0:T(8,128)(2,1)S(1)} %get-tuple-element.108), channel_id=1, source_target_pairs={{0,24},{1,7},{2,26},{3,1},{4,28},{5,3},{6,30},{7,5},{8,0},{9,15},{... | collective-permute-start | bytes 2359304 | tf_op jit(solution)/shard_map/ppermute | solution.py:56
  36.1 4.4 %collective-permute-start.5 = (bf16[2,128,512]{2,1,0:T(8,128)(2,1)S(1)}, bf16[2,128,512]{2,1,0:T(8,128)(2,1)S(1)}, u32[]{:S(2)}, u32[]{:S(2)}) collective-permute-start(bf16[2,128,512]{2,1,0:T(8,128)(2,1)S(1)} %get-tuple-element.103), channel_id=1, source_target_pairs={{0,1},{1,0},{2,3},{3,2},{4,5},{5,4},{6,7},{7,6},{8,9},{9,8},{10,11... | collective-permute-start | bytes 786440 | tf_op jit(solution)/shard_map/ppermute | solution.py:45
  53.8 31.8 %copy-start = (bf16[1024,512]{1,0:T(8,128)(2,1)S(1)}, bf16[1024,512]{1,0:T(8,128)(2,1)}, u32[]{:S(2)}) copy-start(bf16[1024,512]{1,0:T(8,128)(2,1)} %wk_ref.5) | copy-start | bytes 3145732
  53.8 31.8 %copy-start.1 = (bf16[1024,512]{1,0:T(8,128)(2,1)S(1)}, bf16[1024,512]{1,0:T(8,128)(2,1)}, u32[]{:S(2)}) copy-start(bf16[1024,512]{1,0:T(8,128)(2,1)} %wv_ref.5) | copy-start | bytes 3145732
  53.8 9.5 %collective-permute-start.11 = (bf16[32,3072]{1,0:T(8,128)(2,1)S(1)}, bf16[32,3072]{1,0:T(8,128)(2,1)S(1)}, u32[]{:S(2)}, u32[]{:S(2)}) collective-permute-start(bf16[32,3072]{1,0:T(8,128)(2,1)S(1)} %get-tuple-element.115), channel_id=1, source_target_pairs={{0,4},{1,17},{2,6},{3,19},{4,0},{5,21},{6,2},{7,23},{8,12},{9,25},... | collective-permute-start | bytes 589832 | tf_op jit(solution)/shard_map/ppermute | solution.py:56
  55.7 7.6 %collective-permute-start.12 = (bf16[32,3072]{1,0:T(8,128)(2,1)S(1)}, bf16[32,3072]{1,0:T(8,128)(2,1)S(1)}, u32[]{:S(2)}, u32[]{:S(2)}) collective-permute-start(bf16[32,3072]{1,0:T(8,128)(2,1)S(1)} %get-tuple-element.116), channel_id=1, source_target_pairs={{0,2},{1,9},{2,4},{3,11},{4,6},{5,13},{6,0},{7,15},{8,10},{9,17},{... | collective-permute-start | bytes 589832 | tf_op jit(solution)/shard_map/ppermute | solution.py:56
  57.6 12.5 %collective-permute-start.13 = (bf16[32,3072]{1,0:T(8,128)(2,1)S(1)}, bf16[32,3072]{1,0:T(8,128)(2,1)S(1)}, u32[]{:S(2)}, u32[]{:S(2)}) collective-permute-start(bf16[32,3072]{1,0:T(8,128)(2,1)S(1)} %get-tuple-element.117), channel_id=1, source_target_pairs={{0,6},{1,25},{2,0},{3,27},{4,2},{5,29},{6,4},{7,31},{8,14},{9,1},{... | collective-permute-start | bytes 589832 | tf_op jit(solution)/shard_map/ppermute | solution.py:56
  57.7 23.9 %collective-permute-start.9 = (bf16[128,512]{1,0:T(8,128)(2,1)S(1)}, bf16[128,512]{1,0:T(8,128)(2,1)S(1)}, u32[]{:S(2)}, u32[]{:S(2)}) collective-permute-start(bf16[128,512]{1,0:T(8,128)(2,1)S(1)} %get-tuple-element.110), channel_id=1, source_target_pairs={{2,0},{3,1},{4,2},{5,3},{6,4},{7,5},{8,6},{9,7},{10,8},{11,9},{12,... | collective-permute-start | bytes 393224 | tf_op jit(solution)/shard_map/ppermute | solution.py:68
  60.4 21.2 %collective-permute-start.10 = (bf16[128,512]{1,0:T(8,128)(2,1)S(1)}, bf16[128,512]{1,0:T(8,128)(2,1)S(1)}, u32[]{:S(2)}, u32[]{:S(2)}) collective-permute-start(bf16[128,512]{1,0:T(8,128)(2,1)S(1)} %get-tuple-element.111), channel_id=1, source_target_pairs={{2,0},{3,1},{4,2},{5,3},{6,4},{7,5},{8,6},{9,7},{10,8},{11,9},{12,... | collective-permute-start | bytes 393224 | tf_op jit(solution)/shard_map/ppermute | solution.py:68
  70.2 12.1 %collective-permute-start.14 = (bf16[8,3072]{1,0:T(8,128)(2,1)S(1)}, bf16[8,3072]{1,0:T(8,128)(2,1)S(1)}, u32[]{:S(2)}, u32[]{:S(2)}) collective-permute-start(bf16[8,3072]{1,0:T(8,128)(2,1)S(1)} %get-tuple-element.119), channel_id=1, source_target_pairs={{0,128},{1,129},{2,130},{3,131},{4,132},{5,133},{6,134},{7,135},{8... | collective-permute-start | bytes 147464 | tf_op jit(solution)/shard_map/ppermute | solution.py:62
  77.4 6.3 %collective-permute-start.15 = (bf16[8,3072]{1,0:T(8,128)(2,1)S(1)}, bf16[8,3072]{1,0:T(8,128)(2,1)S(1)}, u32[]{:S(2)}, u32[]{:S(2)}) collective-permute-start(bf16[8,3072]{1,0:T(8,128)(2,1)S(1)} %get-tuple-element.120), channel_id=1, source_target_pairs={{0,64},{1,65},{2,66},{3,67},{4,68},{5,69},{6,70},{7,71},{8,72},{9,... | collective-permute-start | bytes 147464 | tf_op jit(solution)/shard_map/ppermute | solution.py:62
  78.9 5.0 %collective-permute-start.16 = (bf16[8,3072]{1,0:T(8,128)(2,1)S(1)}, bf16[8,3072]{1,0:T(8,128)(2,1)S(1)}, u32[]{:S(2)}, u32[]{:S(2)}) collective-permute-start(bf16[8,3072]{1,0:T(8,128)(2,1)S(1)} %get-tuple-element.121), channel_id=1, source_target_pairs={{0,192},{1,193},{2,194},{3,195},{4,196},{5,197},{6,198},{7,199},{8... | collective-permute-start | bytes 147464 | tf_op jit(solution)/shard_map/ppermute | solution.py:62
  83.9 1.7 %collective-permute-start.17 = (bf16[128,512]{1,0:T(8,128)(2,1)S(1)}, bf16[128,512]{1,0:T(8,128)(2,1)S(1)}, u32[]{:S(2)}, u32[]{:S(2)}) collective-permute-start(bf16[128,512]{1,0:T(8,128)(2,1)S(1)} %get-tuple-element.123), channel_id=1, source_target_pairs={{0,1},{1,0},{2,3},{3,2},{4,5},{5,4},{6,7},{7,6},{8,9},{9,8},{10,11... | collective-permute-start | bytes 393224 | tf_op jit(solution)/shard_map/ppermute | solution.py:45
  84.0 5.4 %collective-permute-start.18 = (bf16[4,3072]{1,0:T(4,128)(2,1)S(1)}, bf16[4,3072]{1,0:T(4,128)(2,1)S(1)}, u32[]{:S(2)}, u32[]{:S(2)}) collective-permute-start(bf16[4,3072]{1,0:T(4,128)(2,1)S(1)} %get-tuple-element.125), channel_id=1, source_target_pairs={{0,32},{1,33},{2,34},{3,35},{4,36},{5,37},{6,38},{7,39},{8,40},{9,... | collective-permute-start | bytes 73736 | tf_op jit(solution)/shard_map/ppermute | solution.py:62
